TPU v7x, 32 devices: a whole 2x2x4 slice. The times are simulated.
32 devices in a mesh: parts: 2 (over y), rows: 4 (over z), cols: 2 (over x), rank: 2 (over core).
Axes of the slice: x: 2, y: 2, z: 4, core: 2. Of those that a mesh axis runs over, the one named last changes fastest.
Arguments:
- probes: bfloat16 [32768, 128], P(('parts', 'rows', 'cols')), parts along dimension 0, may hold values from -6 to 6
- basis_one: bfloat16 [32768, 256], P(('parts', 'rows', 'cols'), 'rank'), parts along dimension 0, may hold values from -0.375 to 0.375
- basis_two: bfloat16 [32768, 256], P(('parts', 'rows', 'cols'), 'rank'), parts along dimension 0, may hold values from -0.375 to 0.375
- basis_three: bfloat16 [32768, 256], P(('parts', 'rows', 'cols'), 'rank'), parts along dimension 0, may hold values from -0.375 to 0.375
- coeff_one: bfloat16 [32768, 256], P(('parts', 'rows', 'cols'), 'rank'), parts along dimension 0, may hold values from -0.0625 to 0.0625
- coeff_two: bfloat16 [32768, 256], P(('parts', 'rows', 'cols'), 'rank'), parts along dimension 0, may hold values from -0.09375 to 0.09375
- coeff_three: bfloat16 [32768, 256], P(('parts', 'rows', 'cols'), 'rank'), parts along dimension 0, may hold values from -0.125 to 0.125
- leaves: bfloat16 [128, 256, 256], P(('parts', 'rows', 'cols', 'rank')), parts along dimension 0, may hold values from -0.375 to 0.375
Outputs:
- covariance_power: bfloat16 [32768, 128], P(('parts', 'rows', 'cols', 'rank')), parts along dimension 0
There are 2 independent parts, one for each index of `parts`. A program takes and returns all parts, laid end to end along the dimension named above; each array names one. Nothing has to cross between parts.
All inputs are finite; a program needn't handle non-finite values.
Results may differ from a plain program's by a relative error of at most 0.017.
Values may be sent and summed in bfloat16 or wider, within the bound.
No kernel may reach another device: no remote copies, remote signals or barrier semaphores. Data moves between devices by JAX's collectives and lax.ppermute only.
A program may use at most 64 MiB of HBM per device.

v0:
```python
import jax
import jax.numpy as jnp
from jax import lax
from jax.sharding import PartitionSpec as P

C = 128
LEAF = 256
PASSES = 2


def as_sent(x):
    return jax.tree.map(lambda a: a.astype(jnp.bfloat16) if a.dtype == jnp.float32 else a, x)


def partner(value, axis, stride):
    mask = 2**stride
    pairs = [(source, source ^ mask) for source in range(lax.axis_size(axis))]
    return lax.ppermute(value, axis, pairs)


def combine_levels(projections):
    total_bits = lax.axis_size(("rows", "cols")).bit_length() - 1
    partial_value = list(projections)
    sibling = [projections[0], projections[1], projections[2]]
    for bit_number in range(total_bits):
        received = partner(
            (as_sent(partial_value[0]), as_sent(partial_value[1]), as_sent(partial_value[2])),
            ("rows", "cols"),
            bit_number,
        )
        for rung_index in range(3):
            target_bit = total_bits - 1 - rung_index
            if bit_number < target_bit:
                partial_value[rung_index] = partial_value[rung_index] + received[rung_index]
            elif bit_number == target_bit:
                sibling[rung_index] = received[rung_index]
    return [entry.astype(jnp.bfloat16) for entry in sibling]


def local(probes, basis_one, basis_two, basis_three, coeff_one, coeff_two, coeff_three, leaves):
    rank_count = lax.axis_size("rank")
    rank_place = lax.axis_index("rank")
    rows_here = probes.shape[0]
    half_rows = rows_here // rank_count
    uppers = (basis_one, basis_two, basis_three)
    lowers = (coeff_one, coeff_two, coeff_three)
    current = probes
    applies = 2 * PASSES
    halfway = None
    for step_number in range(applies):
        flipped = step_number % 2 == 0
        outside = lowers if flipped else uppers
        inside = uppers if flipped else lowers
        projections = [
            jnp.einsum("nk,nc->kc", factor, current, preferred_element_type=jnp.float32)
            for factor in inside
        ]
        siblings = combine_levels(projections)
        own_rows = lax.dynamic_slice_in_dim(current, rank_place * half_rows, half_rows, 0).reshape(
            -1, LEAF, C
        )
        pattern = "bji,bjc->bic" if flipped else "bij,bjc->bic"
        leaf_term = jnp.einsum(
            pattern, leaves, own_rows, preferred_element_type=jnp.float32
        ).reshape(half_rows, C)

        def term_rows(start, count, outside=outside, siblings=siblings):
            result = jnp.dot(outside[0], siblings[0], preferred_element_type=jnp.float32)
            result = result + jnp.dot(outside[1], siblings[1], preferred_element_type=jnp.float32)
            result = result + jnp.dot(outside[2], siblings[2], preferred_element_type=jnp.float32)
            return result

        summed = lax.psum_scatter(
            term_rows(jnp.int32(0), half_rows * lax.axis_size("rank")).astype(jnp.bfloat16),
            "rank",
            scatter_dimension=0,
            tiled=True,
        ).astype(jnp.float32)
        halfway = (summed + leaf_term).astype(jnp.bfloat16)
        if step_number + 1 < applies:
            current = lax.all_gather(halfway, "rank", axis=0, tiled=True)
    return halfway


def solution(mesh):
    in_specs = (
        P(("parts", "rows", "cols"), None),
        P(("parts", "rows", "cols"), "rank"),
        P(("parts", "rows", "cols"), "rank"),
        P(("parts", "rows", "cols"), "rank"),
        P(("parts", "rows", "cols"), "rank"),
        P(("parts", "rows", "cols"), "rank"),
        P(("parts", "rows", "cols"), "rank"),
        P(("parts", "rows", "cols", "rank"), None, None),
    )
    out_specs = P(("parts", "rows", "cols", "rank"), None)
    return jax.shard_map(local, mesh=mesh, in_specs=in_specs, out_specs=out_specs, check_vma=False)
```

profile of v0, /device:TPU:0, one launch (start us, length us, event | category | flops | bytes accessed | tf_op | source)
XLA Modules:
  0.0 132.8 jit_solution(5686425325117326454)
XLA Ops:
  6.5 1.7 %convolution_convert_fusion.3 = bf16[128,128]{1,0:T(8,128)(2,1)S(1)} fusion(bf16[2048,128]{1,0:T(8,128)(2,1)} %param.11, bf16[2048,128]{1,0:T(8,128)(2,1)} %param.8), kind=kOutput, calls=%fused_computation.29 | convolution fusion | flops 67125248 | bytes 1081344 | tf_op jit(solution)/shard_map/nk,nc->kc/dot_general | solution.py:55
  8.2 3.0 %collective-permute-start.5 = (bf16[128,128]{1,0:T(8,128)(2,1)S(1)}, bf16[128,128]{1,0:T(8,128)(2,1)S(1)}, u32[]{:S(2)}, u32[]{:S(2)}) collective-permute-start(bf16[128,128]{1,0:T(8,128)(2,1)S(1)} %convolution_convert_fusion.3), channel_id=1, source_target_pairs={{0,2},{2,0},{4,6},{6,4},{8,10},{10,8},{12,14},{14,12},{1,3},{3,1},... | collective-permute-start | bytes 98312 | tf_op jit(solution)/shard_map/ppermute | solution.py:18
  12.0 2.1 %collective-permute-start.3 = (bf16[128,128]{1,0:T(8,128)(2,1)S(1)}, bf16[128,128]{1,0:T(8,128)(2,1)S(1)}, u32[]{:S(2)}, u32[]{:S(2)}) collective-permute-start(bf16[128,128]{1,0:T(8,128)(2,1)S(1)} %get-tuple-element.5), channel_id=1, source_target_pairs={{0,2},{2,0},{4,6},{6,4},{8,10},{10,8},{12,14},{14,12},{1,3},{3,1},... | collective-permute-start | bytes 98312 | tf_op jit(solution)/shard_map/ppermute | solution.py:18
  14.1 1.5 %collective-permute-done = bf16[128,128]{1,0:T(8,128)(2,1)S(1)} collective-permute-done((bf16[128,128]{1,0:T(8,128)(2,1)S(1)}, bf16[128,128]{1,0:T(8,128)(2,1)S(1)}, u32[]{:S(2)}, u32[]{:S(2)}) %collective-permute-start) | collective-permute-done | bytes 32800 | tf_op jit(solution)/shard_map/ppermute | solution.py:18
  15.6 1.6 %collective-permute-start.1 = (bf16[128,128]{1,0:T(8,128)(2,1)S(1)}, bf16[128,128]{1,0:T(8,128)(2,1)S(1)}, u32[]{:S(2)}, u32[]{:S(2)}) collective-permute-start(bf16[128,128]{1,0:T(8,128)(2,1)S(1)} %fusion.15), channel_id=1, source_target_pairs={{0,4},{2,6},{4,0},{6,2},{8,12},{10,14},{12,8},{14,10},{1,5},{3,7},... | collective-permute-start | bytes 98312 | tf_op jit(solution)/shard_map/ppermute | solution.py:18
  17.3 0.9 collective-permute-start.4
  18.5 1.1 collective-permute-done.1
  19.6 2.8 %collective-permute-start.2 = (bf16[128,128]{1,0:T(8,128)(2,1)S(1)}, bf16[128,128]{1,0:T(8,128)(2,1)S(1)}, u32[]{:S(2)}, u32[]{:S(2)}) collective-permute-start(bf16[128,128]{1,0:T(8,128)(2,1)S(1)} %add_convert_fusion.11), channel_id=1, source_target_pairs={{0,8},{2,10},{4,12},{6,14},{8,0},{10,2},{12,4},{14,6},{1,9},{3,11}... | collective-permute-start | bytes 98312 | tf_op jit(solution)/shard_map/ppermute | solution.py:18
  22.8 1.7 %collective-permute-done.2 = bf16[128,128]{1,0:T(8,128)(2,1)S(1)} collective-permute-done((bf16[128,128]{1,0:T(8,128)(2,1)S(1)}, bf16[128,128]{1,0:T(8,128)(2,1)S(1)}, u32[]{:S(2)}, u32[]{:S(2)}) %collective-permute-start.2) | collective-permute-done | bytes 32800 | tf_op jit(solution)/shard_map/ppermute | solution.py:18
  24.5 1.1 fusion.11
  25.7 0.9 copy-done.9
  27.0 7.5 %reduce-scatter.5.cloned.1.call-done = bf16[1024,128]{0,1:T(8,128)(2,1)} async-done(((bf16[2048,128]{0,1:T(8,128)(2,1)}), bf16[1024,128]{0,1:T(8,128)(2,1)}) %reduce-scatter.5.cloned.1.call-update) | async-done | bytes 262160 | tf_op jit(solution)/shard_map/reduce_scatter | solution.py:73
  34.5 1.0 add_convert_fusion.3
  35.5 2.2 %all_gather.9 = bf16[2048,128]{0,1:T(8,128)(2,1)S(1)} all-gather(bf16[1024,128]{0,1:T(8,128)(2,1)S(1)} %add_convert_fusion.3), channel_id=1, replica_groups=mesh['parts'=2,'rows'=4,'cols'=2,'rank'=2] {'rank'}, dimensions={0}, use_global_device_ids=true | all-gather | bytes 786432 | tf_op jit(solution)/shard_map/all_gather | solution.py:81
  38.3 1.8 %collective-permute-start.9 = (bf16[128,128]{0,1:T(8,128)(2,1)S(1)}, bf16[128,128]{0,1:T(8,128)(2,1)S(1)}, u32[]{:S(2)}, u32[]{:S(2)}) collective-permute-start(bf16[128,128]{0,1:T(8,128)(2,1)S(1)} %get-tuple-element.9), channel_id=1, source_target_pairs={{0,2},{2,0},{4,6},{6,4},{8,10},{10,8},{12,14},{14,12},{1,3},{3,1},... | collective-permute-start | bytes 98312 | tf_op jit(solution)/shard_map/ppermute | solution.py:18
  40.8 1.7 %collective-permute-start.6 = (bf16[128,128]{0,1:T(8,128)(2,1)S(1)}, bf16[128,128]{0,1:T(8,128)(2,1)S(1)}, u32[]{:S(2)}, u32[]{:S(2)}) collective-permute-start(bf16[128,128]{0,1:T(8,128)(2,1)S(1)} %get-tuple-element.11), channel_id=1, source_target_pairs={{0,2},{2,0},{4,6},{6,4},{8,10},{10,8},{12,14},{14,12},{1,3},{3,1},... | collective-permute-start | bytes 98312 | tf_op jit(solution)/shard_map/ppermute | solution.py:18
  42.5 1.6 %collective-permute-start.10 = (bf16[128,128]{0,1:T(8,128)(2,1)S(1)}, bf16[128,128]{0,1:T(8,128)(2,1)S(1)}, u32[]{:S(2)}, u32[]{:S(2)}) collective-permute-start(bf16[128,128]{0,1:T(8,128)(2,1)S(1)} %add_convert_fusion.8), channel_id=1, source_target_pairs={{0,4},{2,6},{4,0},{6,2},{8,12},{10,14},{12,8},{14,10},{1,5},{3,7},... | collective-permute-start | bytes 98312 | tf_op jit(solution)/shard_map/ppermute | solution.py:18
  44.7 1.7 %collective-permute-start.7 = (bf16[128,128]{0,1:T(8,128)(2,1)S(1)}, bf16[128,128]{0,1:T(8,128)(2,1)S(1)}, u32[]{:S(2)}, u32[]{:S(2)}) collective-permute-start(bf16[128,128]{0,1:T(8,128)(2,1)S(1)} %fusion.16), channel_id=1, source_target_pairs={{0,4},{2,6},{4,0},{6,2},{8,12},{10,14},{12,8},{14,10},{1,5},{3,7},... | collective-permute-start | bytes 98312 | tf_op jit(solution)/shard_map/ppermute | solution.py:18
  46.8 1.9 %collective-permute-done.7 = bf16[128,128]{0,1:T(8,128)(2,1)S(1)} collective-permute-done((bf16[128,128]{0,1:T(8,128)(2,1)S(1)}, bf16[128,128]{0,1:T(8,128)(2,1)S(1)}, u32[]{:S(2)}, u32[]{:S(2)}) %collective-permute-start.7) | collective-permute-done | bytes 32800 | tf_op jit(solution)/shard_map/ppermute | solution.py:18
  48.7 2.7 %collective-permute-start.8 = (bf16[128,128]{0,1:T(8,128)(2,1)S(1)}, bf16[128,128]{0,1:T(8,128)(2,1)S(1)}, u32[]{:S(2)}, u32[]{:S(2)}) collective-permute-start(bf16[128,128]{0,1:T(8,128)(2,1)S(1)} %add_convert_fusion.9), channel_id=1, source_target_pairs={{0,8},{2,10},{4,12},{6,14},{8,0},{10,2},{12,4},{14,6},{1,9},{3,11}... | collective-permute-start | bytes 98312 | tf_op jit(solution)/shard_map/ppermute | solution.py:18
  51.7 1.9 %collective-permute-done.8 = bf16[128,128]{0,1:T(8,128)(2,1)S(1)} collective-permute-done((bf16[128,128]{0,1:T(8,128)(2,1)S(1)}, bf16[128,128]{0,1:T(8,128)(2,1)S(1)}, u32[]{:S(2)}, u32[]{:S(2)}) %collective-permute-start.8) | collective-permute-done | bytes 32800 | tf_op jit(solution)/shard_map/ppermute | solution.py:18
  53.6 1.1 fusion.10
  55.5 1.2 copy.16
  57.1 7.2 %reduce-scatter.7.cloned.1.call-done = bf16[1024,128]{0,1:T(8,128)(2,1)} async-done(((bf16[2048,128]{0,1:T(8,128)(2,1)}), bf16[1024,128]{0,1:T(8,128)(2,1)}) %reduce-scatter.7.cloned.1.call-update) | async-done | bytes 262160 | tf_op jit(solution)/shard_map/reduce_scatter | solution.py:73
  64.2 1.0 add_convert_fusion.2
  65.2 2.2 %all_gather.10 = bf16[2048,128]{0,1:T(8,128)(2,1)S(1)} all-gather(bf16[1024,128]{0,1:T(8,128)(2,1)S(1)} %add_convert_fusion.2), channel_id=1, replica_groups=mesh['parts'=2,'rows'=4,'cols'=2,'rank'=2] {'rank'}, dimensions={0}, use_global_device_ids=true | all-gather | bytes 786432 | tf_op jit(solution)/shard_map/all_gather | solution.py:81
  68.8 1.7 %collective-permute-start.15 = (bf16[128,128]{0,1:T(8,128)(2,1)S(1)}, bf16[128,128]{0,1:T(8,128)(2,1)S(1)}, u32[]{:S(2)}, u32[]{:S(2)}) collective-permute-start(bf16[128,128]{0,1:T(8,128)(2,1)S(1)} %get-tuple-element.13), channel_id=1, source_target_pairs={{0,2},{2,0},{4,6},{6,4},{8,10},{10,8},{12,14},{14,12},{1,3},{3,1},... | collective-permute-start | bytes 98312 | tf_op jit(solution)/shard_map/ppermute | solution.py:18
  71.2 1.7 %collective-permute-start.12 = (bf16[128,128]{0,1:T(8,128)(2,1)S(1)}, bf16[128,128]{0,1:T(8,128)(2,1)S(1)}, u32[]{:S(2)}, u32[]{:S(2)}) collective-permute-start(bf16[128,128]{0,1:T(8,128)(2,1)S(1)} %get-tuple-element.15), channel_id=1, source_target_pairs={{0,2},{2,0},{4,6},{6,4},{8,10},{10,8},{12,14},{14,12},{1,3},{3,1},... | collective-permute-start | bytes 98312 | tf_op jit(solution)/shard_map/ppermute | solution.py:18
  72.9 1.6 %collective-permute-start.16 = (bf16[128,128]{0,1:T(8,128)(2,1)S(1)}, bf16[128,128]{0,1:T(8,128)(2,1)S(1)}, u32[]{:S(2)}, u32[]{:S(2)}) collective-permute-start(bf16[128,128]{0,1:T(8,128)(2,1)S(1)} %add_convert_fusion.6), channel_id=1, source_target_pairs={{0,4},{2,6},{4,0},{6,2},{8,12},{10,14},{12,8},{14,10},{1,5},{3,7},... | collective-permute-start | bytes 98312 | tf_op jit(solution)/shard_map/ppermute | solution.py:18
  75.1 1.8 %collective-permute-start.13 = (bf16[128,128]{0,1:T(8,128)(2,1)S(1)}, bf16[128,128]{0,1:T(8,128)(2,1)S(1)}, u32[]{:S(2)}, u32[]{:S(2)}) collective-permute-start(bf16[128,128]{0,1:T(8,128)(2,1)S(1)} %fusion.17), channel_id=1, source_target_pairs={{0,4},{2,6},{4,0},{6,2},{8,12},{10,14},{12,8},{14,10},{1,5},{3,7},... | collective-permute-start | bytes 98312 | tf_op jit(solution)/shard_map/ppermute | solution.py:18
  77.2 1.9 %collective-permute-done.13 = bf16[128,128]{0,1:T(8,128)(2,1)S(1)} collective-permute-done((bf16[128,128]{0,1:T(8,128)(2,1)S(1)}, bf16[128,128]{0,1:T(8,128)(2,1)S(1)}, u32[]{:S(2)}, u32[]{:S(2)}) %collective-permute-start.13) | collective-permute-done | bytes 32800 | tf_op jit(solution)/shard_map/ppermute | solution.py:18
  79.1 2.7 %collective-permute-start.14 = (bf16[128,128]{0,1:T(8,128)(2,1)S(1)}, bf16[128,128]{0,1:T(8,128)(2,1)S(1)}, u32[]{:S(2)}, u32[]{:S(2)}) collective-permute-start(bf16[128,128]{0,1:T(8,128)(2,1)S(1)} %add_convert_fusion.7), channel_id=1, source_target_pairs={{0,8},{2,10},{4,12},{6,14},{8,0},{10,2},{12,4},{14,6},{1,9},{3,11}... | collective-permute-start | bytes 98312 | tf_op jit(solution)/shard_map/ppermute | solution.py:18
  82.1 1.9 %collective-permute-done.14 = bf16[128,128]{0,1:T(8,128)(2,1)S(1)} collective-permute-done((bf16[128,128]{0,1:T(8,128)(2,1)S(1)}, bf16[128,128]{0,1:T(8,128)(2,1)S(1)}, u32[]{:S(2)}, u32[]{:S(2)}) %collective-permute-start.14) | collective-permute-done | bytes 32800 | tf_op jit(solution)/shard_map/ppermute | solution.py:18
  84.0 1.1 fusion.9
  85.9 1.2 copy.19
  87.5 7.2 %reduce-scatter.9.cloned.1.call-done = bf16[1024,128]{0,1:T(8,128)(2,1)} async-done(((bf16[2048,128]{0,1:T(8,128)(2,1)}), bf16[1024,128]{0,1:T(8,128)(2,1)}) %reduce-scatter.9.cloned.1.call-update) | async-done | bytes 262160 | tf_op jit(solution)/shard_map/reduce_scatter | solution.py:73
  94.7 1.0 add_convert_fusion.1
  95.7 2.2 %all_gather.11 = bf16[2048,128]{0,1:T(8,128)(2,1)S(1)} all-gather(bf16[1024,128]{0,1:T(8,128)(2,1)S(1)} %add_convert_fusion.1), channel_id=1, replica_groups=mesh['parts'=2,'rows'=4,'cols'=2,'rank'=2] {'rank'}, dimensions={0}, use_global_device_ids=true | all-gather | bytes 786432 | tf_op jit(solution)/shard_map/all_gather | solution.py:81
  98.5 1.7 %collective-permute-start.21 = (bf16[128,128]{0,1:T(8,128)(2,1)S(1)}, bf16[128,128]{0,1:T(8,128)(2,1)S(1)}, u32[]{:S(2)}, u32[]{:S(2)}) collective-permute-start(bf16[128,128]{0,1:T(8,128)(2,1)S(1)} %get-tuple-element.17), channel_id=1, source_target_pairs={{0,2},{2,0},{4,6},{6,4},{8,10},{10,8},{12,14},{14,12},{1,3},{3,1},... | collective-permute-start | bytes 98312 | tf_op jit(solution)/shard_map/ppermute | solution.py:18
  100.9 1.7 %collective-permute-start.18 = (bf16[128,128]{0,1:T(8,128)(2,1)S(1)}, bf16[128,128]{0,1:T(8,128)(2,1)S(1)}, u32[]{:S(2)}, u32[]{:S(2)}) collective-permute-start(bf16[128,128]{0,1:T(8,128)(2,1)S(1)} %get-tuple-element.19), channel_id=1, source_target_pairs={{0,2},{2,0},{4,6},{6,4},{8,10},{10,8},{12,14},{14,12},{1,3},{3,1},... | collective-permute-start | bytes 98312 | tf_op jit(solution)/shard_map/ppermute | solution.py:18
  102.6 1.6 %collective-permute-start.22 = (bf16[128,128]{0,1:T(8,128)(2,1)S(1)}, bf16[128,128]{0,1:T(8,128)(2,1)S(1)}, u32[]{:S(2)}, u32[]{:S(2)}) collective-permute-start(bf16[128,128]{0,1:T(8,128)(2,1)S(1)} %add_convert_fusion.4), channel_id=1, source_target_pairs={{0,4},{2,6},{4,0},{6,2},{8,12},{10,14},{12,8},{14,10},{1,5},{3,7},... | collective-permute-start | bytes 98312 | tf_op jit(solution)/shard_map/ppermute | solution.py:18
  104.8 1.7 %collective-permute-start.19 = (bf16[128,128]{0,1:T(8,128)(2,1)S(1)}, bf16[128,128]{0,1:T(8,128)(2,1)S(1)}, u32[]{:S(2)}, u32[]{:S(2)}) collective-permute-start(bf16[128,128]{0,1:T(8,128)(2,1)S(1)} %fusion.18), channel_id=1, source_target_pairs={{0,4},{2,6},{4,0},{6,2},{8,12},{10,14},{12,8},{14,10},{1,5},{3,7},... | collective-permute-start | bytes 98312 | tf_op jit(solution)/shard_map/ppermute | solution.py:18
  106.9 1.9 %collective-permute-done.19 = bf16[128,128]{0,1:T(8,128)(2,1)S(1)} collective-permute-done((bf16[128,128]{0,1:T(8,128)(2,1)S(1)}, bf16[128,128]{0,1:T(8,128)(2,1)S(1)}, u32[]{:S(2)}, u32[]{:S(2)}) %collective-permute-start.19) | collective-permute-done | bytes 32800 | tf_op jit(solution)/shard_map/ppermute | solution.py:18
  108.9 2.7 %collective-permute-start.20 = (bf16[128,128]{0,1:T(8,128)(2,1)S(1)}, bf16[128,128]{0,1:T(8,128)(2,1)S(1)}, u32[]{:S(2)}, u32[]{:S(2)}) collective-permute-start(bf16[128,128]{0,1:T(8,128)(2,1)S(1)} %add_convert_fusion.5), channel_id=1, source_target_pairs={{0,8},{2,10},{4,12},{6,14},{8,0},{10,2},{12,4},{14,6},{1,9},{3,11}... | collective-permute-start | bytes 98312 | tf_op jit(solution)/shard_map/ppermute | solution.py:18
  111.8 1.9 %collective-permute-done.20 = bf16[128,128]{0,1:T(8,128)(2,1)S(1)} collective-permute-done((bf16[128,128]{0,1:T(8,128)(2,1)S(1)}, bf16[128,128]{0,1:T(8,128)(2,1)S(1)}, u32[]{:S(2)}, u32[]{:S(2)}) %collective-permute-start.20) | collective-permute-done | bytes 32800 | tf_op jit(solution)/shard_map/ppermute | solution.py:18
  113.7 1.1 fusion.8
  116.3 8.1 %reduce-scatter.11.cloned.1.call-done = bf16[1024,128]{0,1:T(8,128)(2,1)} async-done(((bf16[2048,128]{0,1:T(8,128)(2,1)}), bf16[1024,128]{0,1:T(8,128)(2,1)}) %reduce-scatter.11.cloned.1.call-update) | async-done | bytes 262160 | tf_op jit(solution)/shard_map/reduce_scatter | solution.py:73
  124.4 1.0 add_convert_fusion
  (99 shorter events, 14.7 us)
Async XLA Ops:
  6.5 15.9 %copy-start = (bf16[2048,128]{1,0:T(8,128)(2,1)S(1)}, bf16[2048,128]{1,0:T(8,128)(2,1)}, u32[]{:S(2)}) copy-start(bf16[2048,128]{1,0:T(8,128)(2,1)} %param.13) | copy-start | bytes 1572868
  6.5 4.7 %copy-start.13 = (bf16[2048,128]{1,0:T(8,128)(2,1)S(1)}, bf16[2048,128]{1,0:T(8,128)(2,1)}, u32[]{:S(2)}) copy-start(bf16[2048,128]{1,0:T(8,128)(2,1)} %param.8) | copy-start | bytes 1572868
  6.5 4.7 %copy-start.5 = (bf16[2048,128]{1,0:T(8,128)(2,1)S(1)}, bf16[2048,128]{1,0:T(8,128)(2,1)}, u32[]{:S(2)}) copy-start(bf16[2048,128]{1,0:T(8,128)(2,1)} %param.9) | copy-start | bytes 1572868
  6.5 28.0 %reduce-scatter.5.cloned.1.call-start = ((), (), s32[]{:S(2)}) async-start(), calls=%async_computation.4 | async-start | bytes 786432 | tf_op jit(solution)/shard_map/reduce_scatter | solution.py:73
  8.2 3.5 %copy-start.4 = (bf16[2048,128]{1,0:T(8,128)(2,1)S(1)}, bf16[2048,128]{1,0:T(8,128)(2,1)}, u32[]{:S(2)}) copy-start(bf16[2048,128]{1,0:T(8,128)(2,1)} %param.10) | copy-start | bytes 1572868
  8.2 10.0 %collective-permute-start.5 = (bf16[128,128]{1,0:T(8,128)(2,1)S(1)}, bf16[128,128]{1,0:T(8,128)(2,1)S(1)}, u32[]{:S(2)}, u32[]{:S(2)}) collective-permute-start(bf16[128,128]{1,0:T(8,128)(2,1)S(1)} %convolution_convert_fusion.3), channel_id=1, source_target_pairs={{0,2},{2,0},{4,6},{6,4},{8,10},{10,8},{12,14},{14,12},{1,3},{3,1},... | collective-permute-start | bytes 98312 | tf_op jit(solution)/shard_map/ppermute | solution.py:18
  11.6 6.6 %copy-start.2 = (bf16[2048,128]{1,0:T(8,128)(2,1)S(1)}, bf16[2048,128]{1,0:T(8,128)(2,1)}, u32[]{:S(2)}) copy-start(bf16[2048,128]{1,0:T(8,128)(2,1)} %param.14) | copy-start | bytes 1572868
  11.6 4.0 %collective-permute-start = (bf16[128,128]{1,0:T(8,128)(2,1)S(1)}, bf16[128,128]{1,0:T(8,128)(2,1)S(1)}, u32[]{:S(2)}, u32[]{:S(2)}) collective-permute-start(bf16[128,128]{1,0:T(8,128)(2,1)S(1)} %get-tuple-element.7), channel_id=1, source_target_pairs={{0,2},{2,0},{4,6},{6,4},{8,10},{10,8},{12,14},{14,12},{1,3},{3,1},... | collective-permute-start | bytes 98312 | tf_op jit(solution)/shard_map/ppermute | solution.py:18
  12.0 5.2 %collective-permute-start.3 = (bf16[128,128]{1,0:T(8,128)(2,1)S(1)}, bf16[128,128]{1,0:T(8,128)(2,1)S(1)}, u32[]{:S(2)}, u32[]{:S(2)}) collective-permute-start(bf16[128,128]{1,0:T(8,128)(2,1)S(1)} %get-tuple-element.5), channel_id=1, source_target_pairs={{0,2},{2,0},{4,6},{6,4},{8,10},{10,8},{12,14},{14,12},{1,3},{3,1},... | collective-permute-start | bytes 98312 | tf_op jit(solution)/shard_map/ppermute | solution.py:18
  15.6 4.0 %collective-permute-start.1 = (bf16[128,128]{1,0:T(8,128)(2,1)S(1)}, bf16[128,128]{1,0:T(8,128)(2,1)S(1)}, u32[]{:S(2)}, u32[]{:S(2)}) collective-permute-start(bf16[128,128]{1,0:T(8,128)(2,1)S(1)} %fusion.15), channel_id=1, source_target_pairs={{0,4},{2,6},{4,0},{6,2},{8,12},{10,14},{12,8},{14,10},{1,5},{3,7},... | collective-permute-start | bytes 98312 | tf_op jit(solution)/shard_map/ppermute | solution.py:18
  17.3 5.2 %collective-permute-start.4 = (bf16[128,128]{1,0:T(8,128)(2,1)S(1)}, bf16[128,128]{1,0:T(8,128)(2,1)S(1)}, u32[]{:S(2)}, u32[]{:S(2)}) collective-permute-start(bf16[128,128]{1,0:T(8,128)(2,1)S(1)} %add_convert_fusion.10), channel_id=1, source_target_pairs={{0,4},{2,6},{4,0},{6,2},{8,12},{10,14},{12,8},{14,10},{1,5},{3,7},... | collective-permute-start | bytes 98312 | tf_op jit(solution)/shard_map/ppermute | solution.py:18
  19.6 4.9 %copy-start.1 = (bf16[2048,128]{1,0:T(8,128)(2,1)S(1)}, bf16[2048,128]{1,0:T(8,128)(2,1)}, u32[]{:S(2)}) copy-start(bf16[2048,128]{1,0:T(8,128)(2,1)} %param.12) | copy-start | bytes 1572868
  19.6 4.9 %collective-permute-start.2 = (bf16[128,128]{1,0:T(8,128)(2,1)S(1)}, bf16[128,128]{1,0:T(8,128)(2,1)S(1)}, u32[]{:S(2)}, u32[]{:S(2)}) collective-permute-start(bf16[128,128]{1,0:T(8,128)(2,1)S(1)} %add_convert_fusion.11), channel_id=1, source_target_pairs={{0,8},{2,10},{4,12},{6,14},{8,0},{10,2},{12,4},{14,6},{1,9},{3,11}... | collective-permute-start | bytes 98312 | tf_op jit(solution)/shard_map/ppermute | solution.py:18
  25.6 1.0 copy-start.9
  25.7 38.6 %reduce-scatter.7.cloned.1.call-start = ((), (), s32[]{:S(2)}) async-start(), calls=%async_computation.5 | async-start | bytes 786432 | tf_op jit(solution)/shard_map/reduce_scatter | solution.py:73
  38.3 8.1 %copy-start.3 = (bf16[2048,128]{1,0:T(8,128)(2,1)S(1)}, bf16[2048,128]{1,0:T(8,128)(2,1)}, u32[]{:S(2)}) copy-start(bf16[2048,128]{1,0:T(8,128)(2,1)} %param.11) | copy-start | bytes 1572868
  38.3 4.1 %collective-permute-start.9 = (bf16[128,128]{0,1:T(8,128)(2,1)S(1)}, bf16[128,128]{0,1:T(8,128)(2,1)S(1)}, u32[]{:S(2)}, u32[]{:S(2)}) collective-permute-start(bf16[128,128]{0,1:T(8,128)(2,1)S(1)} %get-tuple-element.9), channel_id=1, source_target_pairs={{0,2},{2,0},{4,6},{6,4},{8,10},{10,8},{12,14},{14,12},{1,3},{3,1},... | collective-permute-start | bytes 98312 | tf_op jit(solution)/shard_map/ppermute | solution.py:18
  40.4 6.1 %collective-permute-start.11 = (bf16[128,128]{0,1:T(8,128)(2,1)S(1)}, bf16[128,128]{0,1:T(8,128)(2,1)S(1)}, u32[]{:S(2)}, u32[]{:S(2)}) collective-permute-start(bf16[128,128]{0,1:T(8,128)(2,1)S(1)} %fusion.12), channel_id=1, source_target_pairs={{0,2},{2,0},{4,6},{6,4},{8,10},{10,8},{12,14},{14,12},{1,3},{3,1},... | collective-permute-start | bytes 98312 | tf_op jit(solution)/shard_map/ppermute | solution.py:18
  40.8 3.9 %collective-permute-start.6 = (bf16[128,128]{0,1:T(8,128)(2,1)S(1)}, bf16[128,128]{0,1:T(8,128)(2,1)S(1)}, u32[]{:S(2)}, u32[]{:S(2)}) collective-permute-start(bf16[128,128]{0,1:T(8,128)(2,1)S(1)} %get-tuple-element.11), channel_id=1, source_target_pairs={{0,2},{2,0},{4,6},{6,4},{8,10},{10,8},{12,14},{14,12},{1,3},{3,1},... | collective-permute-start | bytes 98312 | tf_op jit(solution)/shard_map/ppermute | solution.py:18
  42.5 8.9 %collective-permute-start.10 = (bf16[128,128]{0,1:T(8,128)(2,1)S(1)}, bf16[128,128]{0,1:T(8,128)(2,1)S(1)}, u32[]{:S(2)}, u32[]{:S(2)}) collective-permute-start(bf16[128,128]{0,1:T(8,128)(2,1)S(1)} %add_convert_fusion.8), channel_id=1, source_target_pairs={{0,4},{2,6},{4,0},{6,2},{8,12},{10,14},{12,8},{14,10},{1,5},{3,7},... | collective-permute-start | bytes 98312 | tf_op jit(solution)/shard_map/ppermute | solution.py:18
  44.7 4.0 %collective-permute-start.7 = (bf16[128,128]{0,1:T(8,128)(2,1)S(1)}, bf16[128,128]{0,1:T(8,128)(2,1)S(1)}, u32[]{:S(2)}, u32[]{:S(2)}) collective-permute-start(bf16[128,128]{0,1:T(8,128)(2,1)S(1)} %fusion.16), channel_id=1, source_target_pairs={{0,4},{2,6},{4,0},{6,2},{8,12},{10,14},{12,8},{14,10},{1,5},{3,7},... | collective-permute-start | bytes 98312 | tf_op jit(solution)/shard_map/ppermute | solution.py:18
  48.7 4.9 %copy-start.6 = (bf16[2048,128]{1,0:T(8,128)(2,1)S(1)}, bf16[2048,128]{1,0:T(8,128)(2,1)}, u32[]{:S(2)}) copy-start(bf16[2048,128]{1,0:T(8,128)(2,1)} %param.9) | copy-start | bytes 1572868
  48.7 4.9 %collective-permute-start.8 = (bf16[128,128]{0,1:T(8,128)(2,1)S(1)}, bf16[128,128]{0,1:T(8,128)(2,1)S(1)}, u32[]{:S(2)}, u32[]{:S(2)}) collective-permute-start(bf16[128,128]{0,1:T(8,128)(2,1)S(1)} %add_convert_fusion.9), channel_id=1, source_target_pairs={{0,8},{2,10},{4,12},{6,14},{8,0},{10,2},{12,4},{14,6},{1,9},{3,11}... | collective-permute-start | bytes 98312 | tf_op jit(solution)/shard_map/ppermute | solution.py:18
  54.7 40.0 %reduce-scatter.9.cloned.1.call-start = ((), (), s32[]{:S(2)}) async-start(), calls=%async_computation.6 | async-start | bytes 786432 | tf_op jit(solution)/shard_map/reduce_scatter | solution.py:73
  55.5 1.2 copy-start.10
  67.4 1.0 copy-start.7
  68.8 4.1 %collective-permute-start.15 = (bf16[128,128]{0,1:T(8,128)(2,1)S(1)}, bf16[128,128]{0,1:T(8,128)(2,1)S(1)}, u32[]{:S(2)}, u32[]{:S(2)}) collective-permute-start(bf16[128,128]{0,1:T(8,128)(2,1)S(1)} %get-tuple-element.13), channel_id=1, source_target_pairs={{0,2},{2,0},{4,6},{6,4},{8,10},{10,8},{12,14},{14,12},{1,3},{3,1},... | collective-permute-start | bytes 98312 | tf_op jit(solution)/shard_map/ppermute | solution.py:18
  70.8 6.1 %collective-permute-start.17 = (bf16[128,128]{0,1:T(8,128)(2,1)S(1)}, bf16[128,128]{0,1:T(8,128)(2,1)S(1)}, u32[]{:S(2)}, u32[]{:S(2)}) collective-permute-start(bf16[128,128]{0,1:T(8,128)(2,1)S(1)} %fusion.13), channel_id=1, source_target_pairs={{0,2},{2,0},{4,6},{6,4},{8,10},{10,8},{12,14},{14,12},{1,3},{3,1},... | collective-permute-start | bytes 98312 | tf_op jit(solution)/shard_map/ppermute | solution.py:18
  71.2 3.9 %collective-permute-start.12 = (bf16[128,128]{0,1:T(8,128)(2,1)S(1)}, bf16[128,128]{0,1:T(8,128)(2,1)S(1)}, u32[]{:S(2)}, u32[]{:S(2)}) collective-permute-start(bf16[128,128]{0,1:T(8,128)(2,1)S(1)} %get-tuple-element.15), channel_id=1, source_target_pairs={{0,2},{2,0},{4,6},{6,4},{8,10},{10,8},{12,14},{14,12},{1,3},{3,1},... | collective-permute-start | bytes 98312 | tf_op jit(solution)/shard_map/ppermute | solution.py:18
  72.9 8.9 %collective-permute-start.16 = (bf16[128,128]{0,1:T(8,128)(2,1)S(1)}, bf16[128,128]{0,1:T(8,128)(2,1)S(1)}, u32[]{:S(2)}, u32[]{:S(2)}) collective-permute-start(bf16[128,128]{0,1:T(8,128)(2,1)S(1)} %add_convert_fusion.6), channel_id=1, source_target_pairs={{0,4},{2,6},{4,0},{6,2},{8,12},{10,14},{12,8},{14,10},{1,5},{3,7},... | collective-permute-start | bytes 98312 | tf_op jit(solution)/shard_map/ppermute | solution.py:18
  75.1 4.0 %collective-permute-start.13 = (bf16[128,128]{0,1:T(8,128)(2,1)S(1)}, bf16[128,128]{0,1:T(8,128)(2,1)S(1)}, u32[]{:S(2)}, u32[]{:S(2)}) collective-permute-start(bf16[128,128]{0,1:T(8,128)(2,1)S(1)} %fusion.17), channel_id=1, source_target_pairs={{0,4},{2,6},{4,0},{6,2},{8,12},{10,14},{12,8},{14,10},{1,5},{3,7},... | collective-permute-start | bytes 98312 | tf_op jit(solution)/shard_map/ppermute | solution.py:18
  79.1 4.9 %collective-permute-start.14 = (bf16[128,128]{0,1:T(8,128)(2,1)S(1)}, bf16[128,128]{0,1:T(8,128)(2,1)S(1)}, u32[]{:S(2)}, u32[]{:S(2)}) collective-permute-start(bf16[128,128]{0,1:T(8,128)(2,1)S(1)} %add_convert_fusion.7), channel_id=1, source_target_pairs={{0,8},{2,10},{4,12},{6,14},{8,0},{10,2},{12,4},{14,6},{1,9},{3,11}... | collective-permute-start | bytes 98312 | tf_op jit(solution)/shard_map/ppermute | solution.py:18
  85.2 39.2 %reduce-scatter.11.cloned.1.call-start = ((), (), s32[]{:S(2)}) async-start(), calls=%async_computation.7 | async-start | bytes 786432 | tf_op jit(solution)/shard_map/reduce_scatter | solution.py:73
  85.9 1.2 copy-start.11
  98.5 4.1 %collective-permute-start.21 = (bf16[128,128]{0,1:T(8,128)(2,1)S(1)}, bf16[128,128]{0,1:T(8,128)(2,1)S(1)}, u32[]{:S(2)}, u32[]{:S(2)}) collective-permute-start(bf16[128,128]{0,1:T(8,128)(2,1)S(1)} %get-tuple-element.17), channel_id=1, source_target_pairs={{0,2},{2,0},{4,6},{6,4},{8,10},{10,8},{12,14},{14,12},{1,3},{3,1},... | collective-permute-start | bytes 98312 | tf_op jit(solution)/shard_map/ppermute | solution.py:18
  100.5 6.1 %collective-permute-start.23 = (bf16[128,128]{0,1:T(8,128)(2,1)S(1)}, bf16[128,128]{0,1:T(8,128)(2,1)S(1)}, u32[]{:S(2)}, u32[]{:S(2)}) collective-permute-start(bf16[128,128]{0,1:T(8,128)(2,1)S(1)} %fusion.14), channel_id=1, source_target_pairs={{0,2},{2,0},{4,6},{6,4},{8,10},{10,8},{12,14},{14,12},{1,3},{3,1},... | collective-permute-start | bytes 98312 | tf_op jit(solution)/shard_map/ppermute | solution.py:18
  100.9 3.9 %collective-permute-start.18 = (bf16[128,128]{0,1:T(8,128)(2,1)S(1)}, bf16[128,128]{0,1:T(8,128)(2,1)S(1)}, u32[]{:S(2)}, u32[]{:S(2)}) collective-permute-start(bf16[128,128]{0,1:T(8,128)(2,1)S(1)} %get-tuple-element.19), channel_id=1, source_target_pairs={{0,2},{2,0},{4,6},{6,4},{8,10},{10,8},{12,14},{14,12},{1,3},{3,1},... | collective-permute-start | bytes 98312 | tf_op jit(solution)/shard_map/ppermute | solution.py:18
  102.6 8.9 %collective-permute-start.22 = (bf16[128,128]{0,1:T(8,128)(2,1)S(1)}, bf16[128,128]{0,1:T(8,128)(2,1)S(1)}, u32[]{:S(2)}, u32[]{:S(2)}) collective-permute-start(bf16[128,128]{0,1:T(8,128)(2,1)S(1)} %add_convert_fusion.4), channel_id=1, source_target_pairs={{0,4},{2,6},{4,0},{6,2},{8,12},{10,14},{12,8},{14,10},{1,5},{3,7},... | collective-permute-start | bytes 98312 | tf_op jit(solution)/shard_map/ppermute | solution.py:18
  104.8 4.0 %collective-permute-start.19 = (bf16[128,128]{0,1:T(8,128)(2,1)S(1)}, bf16[128,128]{0,1:T(8,128)(2,1)S(1)}, u32[]{:S(2)}, u32[]{:S(2)}) collective-permute-start(bf16[128,128]{0,1:T(8,128)(2,1)S(1)} %fusion.18), channel_id=1, source_target_pairs={{0,4},{2,6},{4,0},{6,2},{8,12},{10,14},{12,8},{14,10},{1,5},{3,7},... | collective-permute-start | bytes 98312 | tf_op jit(solution)/shard_map/ppermute | solution.py:18
  108.8 4.9 %copy-start.8 = (bf16[2048,128]{1,0:T(8,128)(2,1)S(1)}, bf16[2048,128]{1,0:T(8,128)(2,1)}, u32[]{:S(2)}) copy-start(bf16[2048,128]{1,0:T(8,128)(2,1)} %param.9) | copy-start | bytes 1572868
  108.9 4.9 %collective-permute-start.20 = (bf16[128,128]{0,1:T(8,128)(2,1)S(1)}, bf16[128,128]{0,1:T(8,128)(2,1)S(1)}, u32[]{:S(2)}, u32[]{:S(2)}) collective-permute-start(bf16[128,128]{0,1:T(8,128)(2,1)S(1)} %add_convert_fusion.5), channel_id=1, source_target_pairs={{0,8},{2,10},{4,12},{6,14},{8,0},{10,2},{12,4},{14,6},{1,9},{3,11}... | collective-permute-start | bytes 98312 | tf_op jit(solution)/shard_map/ppermute | solution.py:18
  114.9 1.0 copy-start.12
Sparse Core Ops, SparseCore 0:
  25.8 8.6 reduce-scatter.4
  54.8 9.3 reduce-scatter.6
  85.3 9.3 reduce-scatter.8
  115.0 9.3 reduce-scatter.10
where the time goes:
time: 133 us
  waiting for transfers between devices  47.7 us (36%)
  starting transfers between devices  40.3 us (30%)
  between operations  13.5 us (10%)
  matrix products  12.9 us (10%)
  local copies, waits for them, and re-layouts  7.63 us (6%)
  blocking collectives  6.54 us (5%)
  other arithmetic  4.14 us (3%)
    ppermute x24, starting transfers between devices, partner(): return lax.ppermute(value, axis, pairs)  40.1 us
    reduce_scatter x4, waiting for transfers between devices, local(): lax.psum_scatter(term_rows(jnp.int32(0), half_rows * lax.axis_size('rank'...  30 us
    ppermute x24, waiting for transfers between devices, partner(): return lax.ppermute(value, axis, pairs)  17.7 us
    all_gather x3, blocking collectives, local(): current = lax.all_gather(halfway, 'rank', axis=0, tiled=True)  6.54 us
    dot_general x12, matrix products, local(): jnp.einsum('nk,nc->kc', factor, current, preferred_element_type=jnp.float32)  4.9 us
    dot_general x4, matrix products, term_rows(): jnp.dot(outside[0], siblings[0], preferred_element_type=jnp.float32)  4.45 us
    dynamic_slice x7, local copies, waits for them, and re-layouts, local(): lax.dynamic_slice_in_dim(current, rank_place * half_rows, half_rows, 0)  4.03 us
    convert_element_type x4, other arithmetic, local(): halfway = (summed + leaf_term).astype(jnp.bfloat16)  4 us
  transfers between devices with their start and end apart: 28, of which 16 were waited for; matrix products, arithmetic and copies ran while one was open for 7% of the time, Pallas kernels for 0%

commit v1 on v0

v1 whole, which is shorter than its diff:
```python
import jax
import jax.numpy as jnp
from jax import lax
from jax.sharding import PartitionSpec as P

LEAF = 256
PASSES = 2
BF = jnp.bfloat16
F32 = jnp.float32


def over_chips(value, stride):
    axes = ("rows", "cols")
    mask = 2**stride
    return lax.ppermute(value, axes, [(s, s ^ mask) for s in range(lax.axis_size(axes))])


def over_rank(value):
    n = lax.axis_size("rank")
    return lax.ppermute(value, "rank", [(s, (s + 1) % n) for s in range(n)])


def siblings_of(partials):
    bits = lax.axis_size(("rows", "cols")).bit_length() - 1
    depth = len(partials)
    k = partials[0].shape[0]
    found = [None] * depth
    live = list(partials)
    for bit in range(bits):
        count = min(depth, bits - bit)
        received = over_chips(jnp.concatenate(live[:count], 0), bit)
        for level in range(count):
            piece = received[level * k : (level + 1) * k]
            if bit == bits - 1 - level:
                found[level] = piece
            else:
                live[level] = (live[level].astype(F32) + piece.astype(F32)).astype(BF)
    return found


def local(probes, basis_one, basis_two, basis_three, coeff_one, coeff_two, coeff_three, leaves):
    place = lax.axis_index("rank")
    rows, cols = probes.shape
    half = rows // lax.axis_size("rank")
    uppers = (basis_one, basis_two, basis_three)
    lowers = (coeff_one, coeff_two, coeff_three)
    other = over_rank(leaves)
    dense = jnp.where(place == 0, jnp.concatenate([leaves, other], 0), jnp.concatenate([other, leaves], 0))
    field = probes
    applies = 2 * PASSES
    for step in range(applies):
        flipped = step % 2 == 0
        outside, inside = (lowers, uppers) if flipped else (uppers, lowers)
        partials = [
            jnp.einsum("nk,nc->kc", factor, field, preferred_element_type=F32).astype(BF) for factor in inside
        ]
        siblings = siblings_of(partials)
        pattern = "bji,bjc->bic" if flipped else "bij,bjc->bic"
        last = step + 1 == applies
        if last:
            mine = lax.dynamic_slice_in_dim(field, place * half, half, 0)
            blocks = leaves
        else:
            mine, blocks = field, dense
        leaf_term = jnp.einsum(
            pattern, blocks, mine.reshape(-1, LEAF, cols), preferred_element_type=F32
        ).reshape(-1, cols)
        term = jnp.dot(outside[0], siblings[0], preferred_element_type=F32)
        for factor, sibling in zip(outside[1:], siblings[1:]):
            term = term + jnp.dot(factor, sibling, preferred_element_type=F32)
        term = term.astype(BF)
        if last:
            keep = lax.dynamic_slice_in_dim(term, place * half, half, 0)
            send = lax.dynamic_slice_in_dim(term, (1 - place) * half, half, 0)
        else:
            keep = send = term
        field = (keep.astype(F32) + over_rank(send).astype(F32) + leaf_term).astype(BF)
    return field


def solution(mesh):
    rows = P(("parts", "rows", "cols"), None)
    split = P(("parts", "rows", "cols"), "rank")
    every = ("parts", "rows", "cols", "rank")
    in_specs = (rows,) + (split,) * 6 + (P(every, None, None),)
    return jax.shard_map(local, mesh=mesh, in_specs=in_specs, out_specs=P(every, None), check_vma=False)
```

time: 133 us -> 97.3 us (0.73)
  waiting for transfers between devices: 47.7 us -> 27.9 us
  between operations: 13.5 us -> 0.4 us
  starting transfers between devices: 40.3 us -> 28.1 us
  matrix products: 12.9 us -> 21.6 us
  blocking collectives: 6.54 us -> 0 us
  local copies, waits for them, and re-layouts: 7.63 us -> 13.2 us
    reduce_scatter x4 -> x0, waiting for transfers between devices: 30 us -> none  [local(): lax.psum_scatter(term_rows(jnp.int32(0), half_rows * lax.axis_size('rank'...]
    ppermute x24 -> x17, starting transfers between devices: 40.1 us -> 28.1 us  [the longest x12 28 us: over_chips(): lax.ppermute(value, axes, [(s, s ^ mask) for s in range(lax.axis_size(axe...]
    ppermute x24 -> x17, waiting for transfers between devices: 17.7 us -> 27.9 us  [the longest x12 27.9 us: over_chips(): lax.ppermute(value, axes, [(s, s ^ mask) for s in range(lax.axis_size(axe...]
    reshape x4 -> x6, local copies, waits for them, and re-layouts: 0.2 us -> 9.65 us  [the longest x4 7.65 us: local(): leaf_term = jnp.einsum(pattern, blocks, mine.reshape(-1, LEAF, cols), pre...]
    dot_general x28, matrix products: 12.9 us -> 21.6 us  [the longest x4 11 us: local(): jnp.einsum(pattern, blocks, mine.reshape(-1, LEAF, cols), preferred_eleme...]
    all_gather x3 -> x0, blocking collectives: 6.54 us -> none  [local(): current = lax.all_gather(halfway, 'rank', axis=0, tiled=True)]
    dynamic_slice x7 -> x3, local copies, waits for them, and re-layouts: 4.03 us -> 0.22 us  [the longest x2 0.2 us: local(): mine = lax.dynamic_slice_in_dim(field, place * half, half, 0)]
    convert_element_type x16 -> x12, other arithmetic: 4.14 us -> 5.37 us  [the longest x4 5.24 us: local(): (keep.astype(F32) + over_rank(send).astype(F32) + leaf_term).astype(BF)]
  transfers between devices with their start and end apart: 28 -> 17, of which waited for: 16 -> 12; matrix products, arithmetic and copies ran while one was open for 7% -> 25% of each run, Pallas kernels for 0% -> 0%
where the time goes in v1:
time: 97.3 us; the launch traced here: 96.7 us
  starting transfers between devices  28.1 us (29%)
  waiting for transfers between devices  27.9 us (29%)
  matrix products  21.6 us (22%)
  local copies, waits for them, and re-layouts  13.2 us (14%)
  other arithmetic  5.44 us (6%)
    ppermute x12, starting transfers between devices, over_chips(): lax.ppermute(value, axes, [(s, s ^ mask) for s in range(lax.axis_size(axe...  28 us
    ppermute x12, waiting for transfers between devices, over_chips(): lax.ppermute(value, axes, [(s, s ^ mask) for s in range(lax.axis_size(axe...  27.9 us
    dot_general x4, matrix products, local(): jnp.einsum(pattern, blocks, mine.reshape(-1, LEAF, cols), preferred_eleme...  11 us
    reshape x4, local copies, waits for them, and re-layouts, local(): leaf_term = jnp.einsum(pattern, blocks, mine.reshape(-1, LEAF, cols), pre...  7.65 us
    convert_element_type x4, other arithmetic, local(): (keep.astype(F32) + over_rank(send).astype(F32) + leaf_term).astype(BF)  5.24 us
    dot_general x12, matrix products, local(): jnp.einsum('nk,nc->kc', factor, field, preferred_element_type=F32)  5.21 us
    dot_general x4, matrix products, local(): term = jnp.dot(outside[0], siblings[0], preferred_element_type=F32)  2.88 us
    dot_general x8, matrix products, local(): term = term + jnp.dot(factor, sibling, preferred_element_type=F32)  2.54 us
  transfers between devices with their start and end apart: 17, of which 12 were waited for; matrix products, arithmetic and copies ran while one was open for 25% of the time, Pallas kernels for 0%

profile of v1, /device:TPU:0, one launch (start us, length us, event | category | flops | bytes accessed | tf_op | source)
XLA Modules:
  0.0 96.7 jit_solution(7722307405031646090)
XLA Ops:
  0.0 1.0 %copy-done = bf16[2048,128]{1,0:T(8,128)(2,1)S(1)} copy-done((bf16[2048,128]{1,0:T(8,128)(2,1)S(1)}, bf16[2048,128]{1,0:T(8,128)(2,1)}, u32[]{:S(2)}) %copy-start) | copy-done | bytes 524312
  1.0 1.4 %convolution_convert_fusion.10 = bf16[128,128]{1,0:T(8,128)(2,1)S(1)} fusion(bf16[2048,128]{1,0:T(8,128)(2,1)} %param.10, bf16[2048,128]{1,0:T(8,128)(2,1)S(1)} %copy-done), kind=kOutput, calls=%fused_computation.26 | convolution fusion | flops 67125248 | bytes 1081344 | tf_op jit(solution)/shard_map/nk,nc->kc/dot_general | solution.py:55
  2.8 0.7 copy-done.4
  3.9 3.0 %collective-permute-start = (bf16[384,128]{1,0:T(8,128)(2,1)S(1)}, bf16[384,128]{1,0:T(8,128)(2,1)S(1)}, u32[]{:S(2)}, u32[]{:S(2)}) collective-permute-start(bf16[384,128]{1,0:T(8,128)(2,1)S(1)} %pad_maximum_fusion), channel_id=1, source_target_pairs={{0,2},{2,0},{4,6},{6,4},{8,10},{10,8},{12,14},{14,12},{1,3},{3,1},... | collective-permute-start | bytes 294920 | tf_op jit(solution)/shard_map/ppermute | solution.py:15
  6.9 2.8 %collective-permute-done = bf16[384,128]{1,0:T(8,128)(2,1)S(1)} collective-permute-done((bf16[384,128]{1,0:T(8,128)(2,1)S(1)}, bf16[384,128]{1,0:T(8,128)(2,1)S(1)}, u32[]{:S(2)}, u32[]{:S(2)}) %collective-permute-start) | collective-permute-done | bytes 98336 | tf_op jit(solution)/shard_map/ppermute | solution.py:15
  9.7 2.0 %collective-permute-start.1 = (bf16[256,128]{1,0:T(8,128)(2,1)S(1)}, bf16[256,128]{1,0:T(8,128)(2,1)S(1)}, u32[]{:S(2)}, u32[]{:S(2)}) collective-permute-start(bf16[256,128]{1,0:T(8,128)(2,1)S(1)} %pad_maximum_fusion.4), channel_id=1, source_target_pairs={{0,4},{2,6},{4,0},{6,2},{8,12},{10,14},{12,8},{14,10},{1,5},{3,7},... | collective-permute-start | bytes 196616 | tf_op jit(solution)/shard_map/ppermute | solution.py:15
  12.0 2.0 %collective-permute-done.1 = bf16[256,128]{1,0:T(8,128)(2,1)S(1)} collective-permute-done((bf16[256,128]{1,0:T(8,128)(2,1)S(1)}, bf16[256,128]{1,0:T(8,128)(2,1)S(1)}, u32[]{:S(2)}, u32[]{:S(2)}) %collective-permute-start.1) | collective-permute-done | bytes 65568 | tf_op jit(solution)/shard_map/ppermute | solution.py:15
  14.1 3.0 %collective-permute-start.2 = (bf16[128,128]{1,0:T(8,128)(2,1)S(1)}, bf16[128,128]{1,0:T(8,128)(2,1)S(1)}, u32[]{:S(2)}, u32[]{:S(2)}) collective-permute-start(bf16[128,128]{1,0:T(8,128)(2,1)S(1)} %add_convert_fusion.12), channel_id=1, source_target_pairs={{0,8},{2,10},{4,12},{6,14},{8,0},{10,2},{12,4},{14,6},{1,9},{3,11}... | collective-permute-start | bytes 98312 | tf_op jit(solution)/shard_map/ppermute | solution.py:15
  17.4 1.6 %collective-permute-done.2 = bf16[128,128]{1,0:T(8,128)(2,1)S(1)} collective-permute-done((bf16[128,128]{1,0:T(8,128)(2,1)S(1)}, bf16[128,128]{1,0:T(8,128)(2,1)S(1)}, u32[]{:S(2)}, u32[]{:S(2)}) %collective-permute-start.2) | collective-permute-done | bytes 32800 | tf_op jit(solution)/shard_map/ppermute | solution.py:15
  19.4 3.2 %fusion.40 = f32[8,256,128]{2,1,0:T(8,128)} fusion(bf16[8,256,128]{2,1,0:T(8,128)(2,1)S(1)} %bitcast.88, bf16[4,256,256]{2,1,0:T(8,128)(2,1)} %collective-permute-done.4, bf16[4,256,256]{2,1,0:T(8,128)(2,1)} %param.15, pred[]{:T(512)S(6)} %eq.3), kind=kOutput, calls=%fused_computation.84 | convolution fusion | flops 135790592 | bytes 2621441 | tf_op jit(solution)/shard_map/bji,bjc->bic/dot_general | solution.py:65
  22.6 2.5 %copy.32 = f32[2048,128]{0,1:T(8,128)} copy(f32[2048,128]{1,0:T(8,128)} %bitcast.93) | data formatting | bytes 2097152 | tf_op jit(solution)/shard_map/reshape | solution.py:67
  25.2 1.7 %add_convert_fusion.2 = bf16[2048,128]{0,1:T(8,128)(2,1)S(1)} fusion(f32[2048,128]{0,1:T(8,128)} %copy.32, bf16[2048,128]{0,1:T(8,128)(2,1)} %collective-permute-done.3, bf16[2048,128]{0,1:T(8,128)(2,1)} %copy-done.12), kind=kLoop, calls=%fused_computation.40 | loop fusion | flops 1310720 | bytes 2621440 | tf_op jit(solution)/shard_map/convert_element_type | solution.py:77
  27.2 0.4 fusion.12
  27.6 0.3 fusion.13
  27.9 1.9 %collective-permute-start.5 = (bf16[384,128]{1,0:T(8,128)(2,1)S(1)}, bf16[384,128]{1,0:T(8,128)(2,1)S(1)}, u32[]{:S(2)}, u32[]{:S(2)}) collective-permute-start(bf16[384,128]{1,0:T(8,128)(2,1)S(1)} %pad_maximum_fusion.1), channel_id=1, source_target_pairs={{0,2},{2,0},{4,6},{6,4},{8,10},{10,8},{12,14},{14,12},{1,3},{3,1},... | collective-permute-start | bytes 294920 | tf_op jit(solution)/shard_map/ppermute | solution.py:15
  29.8 3.4 %collective-permute-done.5 = bf16[384,128]{1,0:T(8,128)(2,1)S(1)} collective-permute-done((bf16[384,128]{1,0:T(8,128)(2,1)S(1)}, bf16[384,128]{1,0:T(8,128)(2,1)S(1)}, u32[]{:S(2)}, u32[]{:S(2)}) %collective-permute-start.5) | collective-permute-done | bytes 98336 | tf_op jit(solution)/shard_map/ppermute | solution.py:15
  33.2 1.9 %collective-permute-start.6 = (bf16[256,128]{1,0:T(8,128)(2,1)S(1)}, bf16[256,128]{1,0:T(8,128)(2,1)S(1)}, u32[]{:S(2)}, u32[]{:S(2)}) collective-permute-start(bf16[256,128]{1,0:T(8,128)(2,1)S(1)} %pad_maximum_fusion.5), channel_id=1, source_target_pairs={{0,4},{2,6},{4,0},{6,2},{8,12},{10,14},{12,8},{14,10},{1,5},{3,7},... | collective-permute-start | bytes 196616 | tf_op jit(solution)/shard_map/ppermute | solution.py:15
  35.4 2.1 %collective-permute-done.6 = bf16[256,128]{1,0:T(8,128)(2,1)S(1)} collective-permute-done((bf16[256,128]{1,0:T(8,128)(2,1)S(1)}, bf16[256,128]{1,0:T(8,128)(2,1)S(1)}, u32[]{:S(2)}, u32[]{:S(2)}) %collective-permute-start.6) | collective-permute-done | bytes 65568 | tf_op jit(solution)/shard_map/ppermute | solution.py:15
  37.6 2.9 %collective-permute-start.7 = (bf16[128,128]{1,0:T(8,128)(2,1)S(1)}, bf16[128,128]{1,0:T(8,128)(2,1)S(1)}, u32[]{:S(2)}, u32[]{:S(2)}) collective-permute-start(bf16[128,128]{1,0:T(8,128)(2,1)S(1)} %add_convert_fusion.9), channel_id=1, source_target_pairs={{0,8},{2,10},{4,12},{6,14},{8,0},{10,2},{12,4},{14,6},{1,9},{3,11}... | collective-permute-start | bytes 98312 | tf_op jit(solution)/shard_map/ppermute | solution.py:15
  40.8 1.6 %collective-permute-done.7 = bf16[128,128]{1,0:T(8,128)(2,1)S(1)} collective-permute-done((bf16[128,128]{1,0:T(8,128)(2,1)S(1)}, bf16[128,128]{1,0:T(8,128)(2,1)S(1)}, u32[]{:S(2)}, u32[]{:S(2)}) %collective-permute-start.7) | collective-permute-done | bytes 32800 | tf_op jit(solution)/shard_map/ppermute | solution.py:15
  42.5 1.1 %fusion.9 = bf16[2048,128]{0,1:T(8,128)(2,1)} fusion(f32[128,2048]{1,0:T(8,128)S(1)} %fusion.30, f32[128,2048]{1,0:T(8,128)S(1)} %fusion.32, bf16[128,128]{1,0:T(8,128)(2,1)S(1)} %collective-permute-done.7, bf16[2048,128]{1,0:T(8,128)(2,1)S(1)} %copy-done.9), kind=kOutput, calls=%fused_computation.13 | convolution fusion | flops 67895296 | bytes 3178496 | tf_op jit(solution)/shard_map/dot_general | solution.py:68
  43.6 1.0 %copy.33 = bf16[2048,128]{1,0:T(8,128)(2,1)} copy(bf16[2048,128]{0,1:T(8,128)(2,1)S(1)} %add_convert_fusion.2) | data formatting | bytes 1048576 | tf_op jit(solution)/shard_map/reshape | solution.py:66
  44.6 3.1 %fusion.39 = f32[8,256,128]{2,1,0:T(8,128)} fusion(bf16[8,256,128]{2,1,0:T(8,128)(2,1)} %bitcast.95, bf16[4,256,256]{2,1,0:T(8,128)(2,1)} %collective-permute-done.4, bf16[4,256,256]{2,1,0:T(8,128)(2,1)} %param.15, pred[]{:T(512)S(6)} %eq.3), kind=kOutput, calls=%fused_computation.83 | convolution fusion | flops 135790592 | bytes 2621441 | tf_op jit(solution)/shard_map/bij,bjc->bic/dot_general | solution.py:65
  47.7 2.5 %copy.34 = f32[2048,128]{0,1:T(8,128)} copy(f32[2048,128]{1,0:T(8,128)} %bitcast.92) | data formatting | bytes 2097152 | tf_op jit(solution)/shard_map/reshape | solution.py:67
  50.3 1.8 %add_convert_fusion.1 = bf16[2048,128]{0,1:T(8,128)(2,1)S(1)} fusion(f32[2048,128]{0,1:T(8,128)} %copy.34, bf16[2048,128]{0,1:T(8,128)(2,1)} %collective-permute-done.8, bf16[2048,128]{0,1:T(8,128)(2,1)} %fusion.9), kind=kLoop, calls=%fused_computation.39 | loop fusion | flops 1310720 | bytes 2621440 | tf_op jit(solution)/shard_map/convert_element_type | solution.py:77
  52.0 0.4 fusion.14
  52.4 0.7 copy-done.6
  53.4 0.3 fusion.16
  53.8 1.8 %collective-permute-start.9 = (bf16[384,128]{1,0:T(8,128)(2,1)S(1)}, bf16[384,128]{1,0:T(8,128)(2,1)S(1)}, u32[]{:S(2)}, u32[]{:S(2)}) collective-permute-start(bf16[384,128]{1,0:T(8,128)(2,1)S(1)} %pad_maximum_fusion.2), channel_id=1, source_target_pairs={{0,2},{2,0},{4,6},{6,4},{8,10},{10,8},{12,14},{14,12},{1,3},{3,1},... | collective-permute-start | bytes 294920 | tf_op jit(solution)/shard_map/ppermute | solution.py:15
  55.6 3.5 %collective-permute-done.9 = bf16[384,128]{1,0:T(8,128)(2,1)S(1)} collective-permute-done((bf16[384,128]{1,0:T(8,128)(2,1)S(1)}, bf16[384,128]{1,0:T(8,128)(2,1)S(1)}, u32[]{:S(2)}, u32[]{:S(2)}) %collective-permute-start.9) | collective-permute-done | bytes 98336 | tf_op jit(solution)/shard_map/ppermute | solution.py:15
  59.1 1.9 %collective-permute-start.10 = (bf16[256,128]{1,0:T(8,128)(2,1)S(1)}, bf16[256,128]{1,0:T(8,128)(2,1)S(1)}, u32[]{:S(2)}, u32[]{:S(2)}) collective-permute-start(bf16[256,128]{1,0:T(8,128)(2,1)S(1)} %pad_maximum_fusion.6), channel_id=1, source_target_pairs={{0,4},{2,6},{4,0},{6,2},{8,12},{10,14},{12,8},{14,10},{1,5},{3,7},... | collective-permute-start | bytes 196616 | tf_op jit(solution)/shard_map/ppermute | solution.py:15
  61.3 2.1 %collective-permute-done.10 = bf16[256,128]{1,0:T(8,128)(2,1)S(1)} collective-permute-done((bf16[256,128]{1,0:T(8,128)(2,1)S(1)}, bf16[256,128]{1,0:T(8,128)(2,1)S(1)}, u32[]{:S(2)}, u32[]{:S(2)}) %collective-permute-start.10) | collective-permute-done | bytes 65568 | tf_op jit(solution)/shard_map/ppermute | solution.py:15
  63.5 2.9 %collective-permute-start.11 = (bf16[128,128]{1,0:T(8,128)(2,1)S(1)}, bf16[128,128]{1,0:T(8,128)(2,1)S(1)}, u32[]{:S(2)}, u32[]{:S(2)}) collective-permute-start(bf16[128,128]{1,0:T(8,128)(2,1)S(1)} %add_convert_fusion.6), channel_id=1, source_target_pairs={{0,8},{2,10},{4,12},{6,14},{8,0},{10,2},{12,4},{14,6},{1,9},{3,11}... | collective-permute-start | bytes 98312 | tf_op jit(solution)/shard_map/ppermute | solution.py:15
  66.7 1.6 %collective-permute-done.11 = bf16[128,128]{1,0:T(8,128)(2,1)S(1)} collective-permute-done((bf16[128,128]{1,0:T(8,128)(2,1)S(1)}, bf16[128,128]{1,0:T(8,128)(2,1)S(1)}, u32[]{:S(2)}, u32[]{:S(2)}) %collective-permute-start.11) | collective-permute-done | bytes 32800 | tf_op jit(solution)/shard_map/ppermute | solution.py:15
  68.3 1.1 %fusion.8 = bf16[2048,128]{0,1:T(8,128)(2,1)} fusion(f32[128,2048]{1,0:T(8,128)S(1)} %fusion.26, f32[128,2048]{1,0:T(8,128)S(1)} %fusion.28, bf16[128,128]{1,0:T(8,128)(2,1)S(1)} %collective-permute-done.11, bf16[2048,128]{1,0:T(8,128)(2,1)S(1)} %copy-done.1), kind=kOutput, calls=%fused_computation.12 | convolution fusion | flops 67895296 | bytes 3178496 | tf_op jit(solution)/shard_map/dot_general | solution.py:68
  69.5 1.0 %copy.35 = bf16[2048,128]{1,0:T(8,128)(2,1)} copy(bf16[2048,128]{0,1:T(8,128)(2,1)S(1)} %add_convert_fusion.1) | data formatting | bytes 1048576 | tf_op jit(solution)/shard_map/reshape | solution.py:66
  70.5 3.3 %fusion.38 = f32[8,256,128]{2,1,0:T(8,128)} fusion(bf16[8,256,128]{2,1,0:T(8,128)(2,1)} %bitcast.94, bf16[4,256,256]{2,1,0:T(8,128)(2,1)} %collective-permute-done.4, bf16[4,256,256]{2,1,0:T(8,128)(2,1)} %param.15, pred[]{:T(512)S(6)} %eq.3), kind=kOutput, calls=%fused_computation.82 | convolution fusion | flops 135790592 | bytes 2621441 | tf_op jit(solution)/shard_map/bji,bjc->bic/dot_general | solution.py:65
  73.8 2.5 %copy.36 = f32[2048,128]{0,1:T(8,128)} copy(f32[2048,128]{1,0:T(8,128)} %bitcast.91) | data formatting | bytes 2097152 | tf_op jit(solution)/shard_map/reshape | solution.py:67
  76.3 1.7 %add_convert_fusion = bf16[2048,128]{0,1:T(8,128)(2,1)S(1)} fusion(f32[2048,128]{0,1:T(8,128)} %copy.36, bf16[2048,128]{0,1:T(8,128)(2,1)} %collective-permute-done.12, bf16[2048,128]{0,1:T(8,128)(2,1)} %fusion.8), kind=kLoop, calls=%fused_computation.38 | loop fusion | flops 1310720 | bytes 2621440 | tf_op jit(solution)/shard_map/convert_element_type | solution.py:77
  78.0 0.4 fusion.17
  79.1 1.8 %collective-permute-start.13 = (bf16[384,128]{1,0:T(8,128)(2,1)S(1)}, bf16[384,128]{1,0:T(8,128)(2,1)S(1)}, u32[]{:S(2)}, u32[]{:S(2)}) collective-permute-start(bf16[384,128]{1,0:T(8,128)(2,1)S(1)} %pad_maximum_fusion.3), channel_id=1, source_target_pairs={{0,2},{2,0},{4,6},{6,4},{8,10},{10,8},{12,14},{14,12},{1,3},{3,1},... | collective-permute-start | bytes 294920 | tf_op jit(solution)/shard_map/ppermute | solution.py:15
  80.9 3.5 %collective-permute-done.13 = bf16[384,128]{1,0:T(8,128)(2,1)S(1)} collective-permute-done((bf16[384,128]{1,0:T(8,128)(2,1)S(1)}, bf16[384,128]{1,0:T(8,128)(2,1)S(1)}, u32[]{:S(2)}, u32[]{:S(2)}) %collective-permute-start.13) | collective-permute-done | bytes 98336 | tf_op jit(solution)/shard_map/ppermute | solution.py:15
  84.4 1.9 %collective-permute-start.14 = (bf16[256,128]{1,0:T(8,128)(2,1)S(1)}, bf16[256,128]{1,0:T(8,128)(2,1)S(1)}, u32[]{:S(2)}, u32[]{:S(2)}) collective-permute-start(bf16[256,128]{1,0:T(8,128)(2,1)S(1)} %pad_maximum_fusion.7), channel_id=1, source_target_pairs={{0,4},{2,6},{4,0},{6,2},{8,12},{10,14},{12,8},{14,10},{1,5},{3,7},... | collective-permute-start | bytes 196616 | tf_op jit(solution)/shard_map/ppermute | solution.py:15
  86.6 2.1 %collective-permute-done.14 = bf16[256,128]{1,0:T(8,128)(2,1)S(1)} collective-permute-done((bf16[256,128]{1,0:T(8,128)(2,1)S(1)}, bf16[256,128]{1,0:T(8,128)(2,1)S(1)}, u32[]{:S(2)}, u32[]{:S(2)}) %collective-permute-start.14) | collective-permute-done | bytes 65568 | tf_op jit(solution)/shard_map/ppermute | solution.py:15
  88.8 2.9 %collective-permute-start.15 = (bf16[128,128]{1,0:T(8,128)(2,1)S(1)}, bf16[128,128]{1,0:T(8,128)(2,1)S(1)}, u32[]{:S(2)}, u32[]{:S(2)}) collective-permute-start(bf16[128,128]{1,0:T(8,128)(2,1)S(1)} %add_convert_fusion.3), channel_id=1, source_target_pairs={{0,8},{2,10},{4,12},{6,14},{8,0},{10,2},{12,4},{14,6},{1,9},{3,11}... | collective-permute-start | bytes 98312 | tf_op jit(solution)/shard_map/ppermute | solution.py:15
  92.0 1.6 %collective-permute-done.15 = bf16[128,128]{1,0:T(8,128)(2,1)S(1)} collective-permute-done((bf16[128,128]{1,0:T(8,128)(2,1)S(1)}, bf16[128,128]{1,0:T(8,128)(2,1)S(1)}, u32[]{:S(2)}, u32[]{:S(2)}) %collective-permute-start.15) | collective-permute-done | bytes 32800 | tf_op jit(solution)/shard_map/ppermute | solution.py:15
  94.3 1.4 %convolution_bitcast_fusion = f32[4,16,8,256]{3,2,1,0:T(8,128)S(1)} fusion(bf16[4,256,128]{2,1,0:T(8,128)(2,1)S(1)} %bitcast.90, bf16[4,256,256]{2,1,0:T(8,128)(2,1)} %param.15), kind=kOutput, calls=%fused_computation.15 | convolution fusion | flops 67108864 | bytes 1310720 | tf_op jit(solution)/shard_map/bij,bjc->bic/dot_general | solution.py:65
  95.8 0.8 copy.28
  (70 shorter events, 6.1 us)
Async XLA Ops:
  0.0 1.0 %copy-start = (bf16[2048,128]{1,0:T(8,128)(2,1)S(1)}, bf16[2048,128]{1,0:T(8,128)(2,1)}, u32[]{:S(2)}) copy-start(bf16[2048,128]{1,0:T(8,128)(2,1)} %param.8) | copy-start | bytes 1572868
  0.0 2.4 %copy-start.8 = (bf16[2048,128]{1,0:T(8,128)(2,1)S(1)}, bf16[2048,128]{1,0:T(8,128)(2,1)}, u32[]{:S(2)}) copy-start(bf16[2048,128]{1,0:T(8,128)(2,1)} %param.9) | copy-start | bytes 1572868
  2.4 1.0 %copy-start.4 = (bf16[2048,128]{1,0:T(8,128)(2,1)S(1)}, bf16[2048,128]{1,0:T(8,128)(2,1)}, u32[]{:S(2)}) copy-start(bf16[2048,128]{1,0:T(8,128)(2,1)} %param.11) | copy-start | bytes 1572868
  3.8 7.9 %copy-start.3 = (bf16[2048,128]{1,0:T(8,128)(2,1)S(1)}, bf16[2048,128]{1,0:T(8,128)(2,1)}, u32[]{:S(2)}) copy-start(bf16[2048,128]{1,0:T(8,128)(2,1)} %param.14) | copy-start | bytes 1572868
  3.9 5.8 %collective-permute-start = (bf16[384,128]{1,0:T(8,128)(2,1)S(1)}, bf16[384,128]{1,0:T(8,128)(2,1)S(1)}, u32[]{:S(2)}, u32[]{:S(2)}) collective-permute-start(bf16[384,128]{1,0:T(8,128)(2,1)S(1)} %pad_maximum_fusion), channel_id=1, source_target_pairs={{0,2},{2,0},{4,6},{6,4},{8,10},{10,8},{12,14},{14,12},{1,3},{3,1},... | collective-permute-start | bytes 294920 | tf_op jit(solution)/shard_map/ppermute | solution.py:15
  6.9 12.5 %collective-permute-start.4 = (bf16[4,256,256]{2,1,0:T(8,128)(2,1)}, bf16[4,256,256]{2,1,0:T(8,128)(2,1)}, u32[]{:S(2)}, u32[]{:S(2)}) collective-permute-start(bf16[4,256,256]{2,1,0:T(8,128)(2,1)} %param.15), channel_id=1, source_target_pairs={{0,1},{1,0},{2,3},{3,2},{4,5},{5,4},{6,7},{7,6},{8,9},{9,8},{10,11... | collective-permute-start | bytes 1572872 | tf_op jit(solution)/shard_map/ppermute | solution.py:20
  9.7 7.4 %copy-start.2 = (bf16[2048,128]{1,0:T(8,128)(2,1)S(1)}, bf16[2048,128]{1,0:T(8,128)(2,1)}, u32[]{:S(2)}) copy-start(bf16[2048,128]{1,0:T(8,128)(2,1)} %param.13) | copy-start | bytes 1572868
  9.7 4.3 %collective-permute-start.1 = (bf16[256,128]{1,0:T(8,128)(2,1)S(1)}, bf16[256,128]{1,0:T(8,128)(2,1)S(1)}, u32[]{:S(2)}, u32[]{:S(2)}) collective-permute-start(bf16[256,128]{1,0:T(8,128)(2,1)S(1)} %pad_maximum_fusion.4), channel_id=1, source_target_pairs={{0,4},{2,6},{4,0},{6,2},{8,12},{10,14},{12,8},{14,10},{1,5},{3,7},... | collective-permute-start | bytes 196616 | tf_op jit(solution)/shard_map/ppermute | solution.py:15
  14.1 4.9 %copy-start.1 = (bf16[2048,128]{1,0:T(8,128)(2,1)S(1)}, bf16[2048,128]{1,0:T(8,128)(2,1)}, u32[]{:S(2)}) copy-start(bf16[2048,128]{1,0:T(8,128)(2,1)} %param.12) | copy-start | bytes 1572868
  14.1 4.9 %collective-permute-start.2 = (bf16[128,128]{1,0:T(8,128)(2,1)S(1)}, bf16[128,128]{1,0:T(8,128)(2,1)S(1)}, u32[]{:S(2)}, u32[]{:S(2)}) collective-permute-start(bf16[128,128]{1,0:T(8,128)(2,1)S(1)} %add_convert_fusion.12), channel_id=1, source_target_pairs={{0,8},{2,10},{4,12},{6,14},{8,0},{10,2},{12,4},{14,6},{1,9},{3,11}... | collective-permute-start | bytes 98312 | tf_op jit(solution)/shard_map/ppermute | solution.py:15
  19.3 3.3 %copy-start.12 = (bf16[2048,128]{0,1:T(8,128)(2,1)}, bf16[2048,128]{0,1:T(8,128)(2,1)S(1)}, u32[]{:S(2)}) copy-start(bf16[2048,128]{0,1:T(8,128)(2,1)S(1)} %fusion.10) | copy-start | bytes 1572868
  19.3 5.8 %collective-permute-start.3 = (bf16[2048,128]{0,1:T(8,128)(2,1)S(1)}, bf16[2048,128]{0,1:T(8,128)(2,1)}, u32[]{:S(2)}, u32[]{:S(2)}) collective-permute-start(bf16[2048,128]{0,1:T(8,128)(2,1)S(1)} %fusion.10), channel_id=1, source_target_pairs={{0,1},{1,0},{2,3},{3,2},{4,5},{5,4},{6,7},{7,6},{8,9},{9,8},{10,11... | collective-permute-start | bytes 1572872 | tf_op jit(solution)/shard_map/ppermute | solution.py:20
  27.9 5.2 %collective-permute-start.5 = (bf16[384,128]{1,0:T(8,128)(2,1)S(1)}, bf16[384,128]{1,0:T(8,128)(2,1)S(1)}, u32[]{:S(2)}, u32[]{:S(2)}) collective-permute-start(bf16[384,128]{1,0:T(8,128)(2,1)S(1)} %pad_maximum_fusion.1), channel_id=1, source_target_pairs={{0,2},{2,0},{4,6},{6,4},{8,10},{10,8},{12,14},{14,12},{1,3},{3,1},... | collective-permute-start | bytes 294920 | tf_op jit(solution)/shard_map/ppermute | solution.py:15
  33.2 7.3 %copy-start.5 = (bf16[2048,128]{1,0:T(8,128)(2,1)S(1)}, bf16[2048,128]{1,0:T(8,128)(2,1)}, u32[]{:S(2)}) copy-start(bf16[2048,128]{1,0:T(8,128)(2,1)} %param.10) | copy-start | bytes 1572868
  33.2 4.3 %collective-permute-start.6 = (bf16[256,128]{1,0:T(8,128)(2,1)S(1)}, bf16[256,128]{1,0:T(8,128)(2,1)S(1)}, u32[]{:S(2)}, u32[]{:S(2)}) collective-permute-start(bf16[256,128]{1,0:T(8,128)(2,1)S(1)} %pad_maximum_fusion.5), channel_id=1, source_target_pairs={{0,4},{2,6},{4,0},{6,2},{8,12},{10,14},{12,8},{14,10},{1,5},{3,7},... | collective-permute-start | bytes 196616 | tf_op jit(solution)/shard_map/ppermute | solution.py:15
  37.6 4.9 %copy-start.9 = (bf16[2048,128]{1,0:T(8,128)(2,1)S(1)}, bf16[2048,128]{1,0:T(8,128)(2,1)}, u32[]{:S(2)}) copy-start(bf16[2048,128]{1,0:T(8,128)(2,1)} %param.9) | copy-start | bytes 1572868
  37.6 4.9 %collective-permute-start.7 = (bf16[128,128]{1,0:T(8,128)(2,1)S(1)}, bf16[128,128]{1,0:T(8,128)(2,1)S(1)}, u32[]{:S(2)}, u32[]{:S(2)}) collective-permute-start(bf16[128,128]{1,0:T(8,128)(2,1)S(1)} %add_convert_fusion.9), channel_id=1, source_target_pairs={{0,8},{2,10},{4,12},{6,14},{8,0},{10,2},{12,4},{14,6},{1,9},{3,11}... | collective-permute-start | bytes 98312 | tf_op jit(solution)/shard_map/ppermute | solution.py:15
  43.6 6.7 %collective-permute-start.8 = (bf16[2048,128]{0,1:T(8,128)(2,1)}, bf16[2048,128]{0,1:T(8,128)(2,1)}, u32[]{:S(2)}, u32[]{:S(2)}) collective-permute-start(bf16[2048,128]{0,1:T(8,128)(2,1)} %fusion.9), channel_id=1, source_target_pairs={{0,1},{1,0},{2,3},{3,2},{4,5},{5,4},{6,7},{7,6},{8,9},{9,8},{10,11... | collective-permute-start | bytes 1572872 | tf_op jit(solution)/shard_map/ppermute | solution.py:20
  50.3 1.8 %copy-start.10 = (bf16[2048,128]{1,0:T(8,128)(2,1)S(1)}, bf16[2048,128]{1,0:T(8,128)(2,1)}, u32[]{:S(2)}) copy-start(bf16[2048,128]{1,0:T(8,128)(2,1)} %param.9) | copy-start | bytes 1572868
  52.0 1.0 %copy-start.6 = (bf16[2048,128]{1,0:T(8,128)(2,1)S(1)}, bf16[2048,128]{1,0:T(8,128)(2,1)}, u32[]{:S(2)}) copy-start(bf16[2048,128]{1,0:T(8,128)(2,1)} %param.10) | copy-start | bytes 1572868
  53.8 5.3 %collective-permute-start.9 = (bf16[384,128]{1,0:T(8,128)(2,1)S(1)}, bf16[384,128]{1,0:T(8,128)(2,1)S(1)}, u32[]{:S(2)}, u32[]{:S(2)}) collective-permute-start(bf16[384,128]{1,0:T(8,128)(2,1)S(1)} %pad_maximum_fusion.2), channel_id=1, source_target_pairs={{0,2},{2,0},{4,6},{6,4},{8,10},{10,8},{12,14},{14,12},{1,3},{3,1},... | collective-permute-start | bytes 294920 | tf_op jit(solution)/shard_map/ppermute | solution.py:15
  59.1 4.3 %collective-permute-start.10 = (bf16[256,128]{1,0:T(8,128)(2,1)S(1)}, bf16[256,128]{1,0:T(8,128)(2,1)S(1)}, u32[]{:S(2)}, u32[]{:S(2)}) collective-permute-start(bf16[256,128]{1,0:T(8,128)(2,1)S(1)} %pad_maximum_fusion.6), channel_id=1, source_target_pairs={{0,4},{2,6},{4,0},{6,2},{8,12},{10,14},{12,8},{14,10},{1,5},{3,7},... | collective-permute-start | bytes 196616 | tf_op jit(solution)/shard_map/ppermute | solution.py:15
  63.5 4.9 %collective-permute-start.11 = (bf16[128,128]{1,0:T(8,128)(2,1)S(1)}, bf16[128,128]{1,0:T(8,128)(2,1)S(1)}, u32[]{:S(2)}, u32[]{:S(2)}) collective-permute-start(bf16[128,128]{1,0:T(8,128)(2,1)S(1)} %add_convert_fusion.6), channel_id=1, source_target_pairs={{0,8},{2,10},{4,12},{6,14},{8,0},{10,2},{12,4},{14,6},{1,9},{3,11}... | collective-permute-start | bytes 98312 | tf_op jit(solution)/shard_map/ppermute | solution.py:15
  69.5 6.9 %collective-permute-start.12 = (bf16[2048,128]{0,1:T(8,128)(2,1)}, bf16[2048,128]{0,1:T(8,128)(2,1)}, u32[]{:S(2)}, u32[]{:S(2)}) collective-permute-start(bf16[2048,128]{0,1:T(8,128)(2,1)} %fusion.8), channel_id=1, source_target_pairs={{0,1},{1,0},{2,3},{3,2},{4,5},{5,4},{6,7},{7,6},{8,9},{9,8},{10,11... | collective-permute-start | bytes 1572872 | tf_op jit(solution)/shard_map/ppermute | solution.py:20
  79.1 5.3 %collective-permute-start.13 = (bf16[384,128]{1,0:T(8,128)(2,1)S(1)}, bf16[384,128]{1,0:T(8,128)(2,1)S(1)}, u32[]{:S(2)}, u32[]{:S(2)}) collective-permute-start(bf16[384,128]{1,0:T(8,128)(2,1)S(1)} %pad_maximum_fusion.3), channel_id=1, source_target_pairs={{0,2},{2,0},{4,6},{6,4},{8,10},{10,8},{12,14},{14,12},{1,3},{3,1},... | collective-permute-start | bytes 294920 | tf_op jit(solution)/shard_map/ppermute | solution.py:15
  84.4 7.3 %copy-start.7 = (bf16[2048,128]{1,0:T(8,128)(2,1)S(1)}, bf16[2048,128]{1,0:T(8,128)(2,1)}, u32[]{:S(2)}) copy-start(bf16[2048,128]{1,0:T(8,128)(2,1)} %param.10) | copy-start | bytes 1572868
  84.4 4.3 %collective-permute-start.14 = (bf16[256,128]{1,0:T(8,128)(2,1)S(1)}, bf16[256,128]{1,0:T(8,128)(2,1)S(1)}, u32[]{:S(2)}, u32[]{:S(2)}) collective-permute-start(bf16[256,128]{1,0:T(8,128)(2,1)S(1)} %pad_maximum_fusion.7), channel_id=1, source_target_pairs={{0,4},{2,6},{4,0},{6,2},{8,12},{10,14},{12,8},{14,10},{1,5},{3,7},... | collective-permute-start | bytes 196616 | tf_op jit(solution)/shard_map/ppermute | solution.py:15
  88.8 4.9 %copy-start.11 = (bf16[2048,128]{1,0:T(8,128)(2,1)S(1)}, bf16[2048,128]{1,0:T(8,128)(2,1)}, u32[]{:S(2)}) copy-start(bf16[2048,128]{1,0:T(8,128)(2,1)} %param.9) | copy-start | bytes 1572868
  88.8 4.9 %collective-permute-start.15 = (bf16[128,128]{1,0:T(8,128)(2,1)S(1)}, bf16[128,128]{1,0:T(8,128)(2,1)S(1)}, u32[]{:S(2)}, u32[]{:S(2)}) collective-permute-start(bf16[128,128]{1,0:T(8,128)(2,1)S(1)} %add_convert_fusion.3), channel_id=1, source_target_pairs={{0,8},{2,10},{4,12},{6,14},{8,0},{10,2},{12,4},{14,6},{1,9},{3,11}... | collective-permute-start | bytes 98312 | tf_op jit(solution)/shard_map/ppermute | solution.py:15
  94.0 1.7 %collective-permute-start.16 = (bf16[1024,128]{0,1:T(8,128)(2,1)S(1)}, bf16[1024,128]{0,1:T(8,128)(2,1)S(1)}, u32[]{:S(2)}, u32[]{:S(2)}) collective-permute-start(bf16[1024,128]{0,1:T(8,128)(2,1)S(1)} %dynamic-slice_bitcast_fusion), channel_id=1, source_target_pairs={{0,1},{1,0},{2,3},{3,2},{4,5},{5,4},{6,7},{7,6},{8,9},{9,8},{10,11... | collective-permute-start | bytes 786440 | tf_op jit(solution)/shard_map/ppermute | solution.py:20

commit v2 on v1

v2 whole, which is shorter than its diff:
```python
import jax
import jax.numpy as jnp
from jax import lax
from jax.experimental import pallas as pl
from jax.experimental.pallas import tpu as pltpu
from jax.sharding import PartitionSpec as P

PASSES = 2
LEVELS = 3
BF = jnp.bfloat16
F32 = jnp.float32
VMEM_BYTES = 12 * 2**20


def mm(a, b, ca, cb):
    return lax.dot_general(a, b, (((ca,), (cb,)), ((), ())), preferred_element_type=F32)


def call(kernel, outs, args, flops, scratch=()):
    vm = pl.BlockSpec(memory_space=pltpu.VMEM)
    moved = sum(a.size * a.dtype.itemsize for a in args[1:]) + sum(o.size * o.dtype.itemsize for o in outs)
    return pl.pallas_call(
        kernel,
        out_shape=outs,
        in_specs=[pl.BlockSpec(memory_space=pltpu.SMEM)] + [vm] * (len(args) - 1),
        out_specs=[vm] * len(outs),
        scratch_shapes=list(scratch),
        cost_estimate=pl.CostEstimate(flops=flops, bytes_accessed=moved, transcendentals=0),
        compiler_params=pltpu.CompilerParams(vmem_limit_bytes=VMEM_BYTES),
    )(*args)


def at(start, size):
    return pl.ds(pl.multiple_of(start, size), size)


def first_kernel(place, z, *refs):
    factors, out = refs[:LEVELS], refs[LEVELS]
    zt = z[...].T
    c = zt.shape[0]
    for level, factor in enumerate(factors):
        out[level * c : (level + 1) * c, :] = mm(zt, factor[...], 1, 0).astype(BF)


def gram_kernel(place, *refs):
    own, (other, full, gram) = refs[:LEVELS], refs[LEVELS:]
    half, k = other.shape[0] // LEVELS, other.shape[1]
    me = place[0]
    for level in range(LEVELS):
        full[:, at((2 * level + me) * k, k)] = own[level][at(me * half, half), :]
        full[:, at((2 * level + 1 - me) * k, k)] = other[level * half : (level + 1) * half, :]
    for i in range(LEVELS):
        rows = slice(2 * k * i, 2 * k * (i + 1))
        left = full[:, rows].T
        for j in range(i + 1):
            cols = slice(2 * k * j, 2 * k * (j + 1))
            block = mm(left, full[:, cols], 1, 0).astype(BF)
            gram[rows, cols] = block
            if j < i:
                gram[cols, rows] = block.T


def join(place, own, other, joined):
    c, k = own.shape[0] // LEVELS, own.shape[1]
    me = place[0]
    for level in range(LEVELS):
        joined[:, at((2 * level + me) * k, k)] = own[level * c : (level + 1) * c, :]
        joined[:, at((2 * level + 1 - me) * k, k)] = other[level * c : (level + 1) * c, :]


def next_kernel(place, own, other, gram, here, there, out, joined):
    join(place, own, other, joined)
    c, k = own.shape[0] // LEVELS, own.shape[1]
    me = place[0]
    q = joined[...]
    for level in range(LEVELS):
        cols = at((2 * level + me) * k, k)
        base = here[:, cols].astype(F32) + there[:, cols].astype(F32)
        out[level * c : (level + 1) * c, :] = (mm(q, gram[:, cols], 1, 0) + base).astype(BF)


def leaf_terms(z, leaves, flipped, out):
    size = leaves.shape[1]
    for q in range(leaves.shape[0]):
        rows = slice(q * size, (q + 1) * size)
        out[rows, :] = mm(leaves[q], z[rows, :], 0 if flipped else 1, 0)


def start_kernel(place, z, leaves, after, y, s):
    half = y.shape[0]
    leaf_terms(z[at(place[0] * half, half), :], leaves, True, y)
    s[...] = mm(y[...].astype(BF).T, after[...], 1, 0).astype(BF)


def field_kernel(flipped, place, q, factor, was, leaves, after, y, s):
    z = (mm(factor[...], q[...], 1, 1) + was[...]).astype(BF)
    leaf_terms(z, leaves, flipped, y)
    s[...] = mm(y[...].astype(BF).T, after[...], 1, 0).astype(BF)


def late_kernel(flipped, place, q, factor, was, leaves, y):
    z = (mm(factor[...], q[...], 1, 1) + was[...]).astype(BF)
    leaf_terms(z, leaves, flipped, y)


def last_kernel(place, own, other, factor, was, out, joined):
    join(place, own, other, joined)
    out[...] = (mm(factor[...], joined[...], 1, 1) + was[...]).astype(BF)


def over_chips(value, stride):
    axes = ("rows", "cols")
    mask = 2**stride
    return lax.ppermute(value, axes, [(s, s ^ mask) for s in range(lax.axis_size(axes))])


def over_rank(value):
    return lax.ppermute(value, "rank", [(0, 1), (1, 0)])


def siblings_of(packed):
    bits = lax.axis_size(("rows", "cols")).bit_length() - 1
    c = packed.shape[0] // LEVELS
    found = [None] * LEVELS
    for bit in range(bits):
        received = over_chips(packed, bit)
        count = min(LEVELS, bits - bit)
        if bit == bits - count:
            found[count - 1] = received[(count - 1) * c :]
            count -= 1
            packed, received = packed[: count * c], received[: count * c]
        packed = (packed.astype(F32) + received.astype(F32)).astype(BF)
    return found


def local(probes, basis_one, basis_two, basis_three, coeff_one, coeff_two, coeff_three, leaves):
    rank = lax.axis_index("rank")
    place = rank.reshape(1)
    n, c = probes.shape
    half = n // 2
    k = basis_one.shape[1]
    wide = 2 * k * LEVELS
    S = jax.ShapeDtypeStruct
    uppers = (basis_one, basis_two, basis_three)
    lowers = (coeff_one, coeff_two, coeff_three)

    def swapped(factors):
        return over_rank(
            jnp.concatenate([lax.dynamic_slice_in_dim(f, (1 - rank) * half, half, 0) for f in factors], 0)
        )

    def prepared(factors, other):
        full, gram = call(
            gram_kernel, [S((half, wide), BF), S((wide, wide), BF)], (place, *factors, other), half * wide * wide * 3 // 2
        )
        return full, (gram.astype(F32) + over_rank(gram).astype(F32)).astype(BF)

    (packed,) = call(first_kernel, [S((LEVELS * c, k), BF)], (place, probes, *uppers), 2 * n * LEVELS * k * c)
    lower, lower_gram = prepared(lowers, swapped(lowers))
    upper, upper_gram = prepared(uppers, swapped(uppers))
    y_shape, s_shape = S((half, c), F32), S((c, wide), BF)
    field_flops = 4 * half * wide * c
    y, s = call(start_kernel, [y_shape, s_shape], (place, probes, leaves, lower), field_flops // 2)
    applies = 2 * PASSES
    for step in range(applies):
        flipped = step % 2 == 0
        factor, gram, after = (lower, lower_gram, upper) if flipped else (upper, upper_gram, lower)
        found = siblings_of(packed)
        own = jnp.concatenate(found, 0)
        other = over_rank(own)
        joined = pltpu.VMEM((c, wide), BF)
        if step + 1 == applies:
            (out,) = call(last_kernel, [S((half, c), BF)], (place, own, other, factor, y), field_flops // 2, [joined])
            return out
        packed, q = call(
            next_kernel,
            [S((LEVELS * c, k), BF), s_shape],
            (place, own, other, gram, s, over_rank(s)),
            wide * wide * c,
        )
        if step + 2 == applies:
            (y,) = call(lambda *r: late_kernel(not flipped, *r), [y_shape], (place, q, factor, y, leaves), field_flops // 2)
        else:
            y, s = call(
                lambda *r: field_kernel(not flipped, *r), [y_shape, s_shape], (place, q, factor, y, leaves, after), field_flops
            )


def solution(mesh):
    rows = P(("parts", "rows", "cols"), None)
    split = P(("parts", "rows", "cols"), "rank")
    every = ("parts", "rows", "cols", "rank")
    in_specs = (rows,) + (split,) * 6 + (P(every, None, None),)
    return jax.shard_map(local, mesh=mesh, in_specs=in_specs, out_specs=P(every, None), check_vma=False)
```

time: 97.3 us -> 75.1 us (0.77)
  matrix products: 21.6 us -> 0 us
  local copies, waits for them, and re-layouts: 13.2 us -> 2.65 us
  Pallas kernels: 0 us -> 10.4 us
  other arithmetic: 5.44 us -> 0.87 us
  waiting for transfers between devices: 27.9 us -> 31.1 us
  starting transfers between devices: 28.1 us -> 29.5 us
    dot_general x28 -> x0, matrix products: 21.6 us -> none  [the longest x4 11 us: local(): jnp.einsum(pattern, blocks, mine.reshape(-1, LEAF, cols), preferred_eleme...]
    pallas_call x0 -> x11, Pallas kernels: none -> 10.4 us  [call(): pl.pallas_call(kernel, out_shape=outs, in_specs=[pl.BlockSpec(memory_spac...]
    reshape x6 -> x0, local copies, waits for them, and re-layouts: 9.65 us -> none  [the longest x4 7.65 us: local(): leaf_term = jnp.einsum(pattern, blocks, mine.reshape(-1, LEAF, cols), pre...]
    ppermute x5 -> x11, waiting for transfers between devices: 0.01 us -> 5.28 us  [over_rank(): return lax.ppermute(value, 'rank', [(0, 1), (1, 0)])]
    convert_element_type x12 -> x10, other arithmetic: 5.37 us -> 0.73 us  [the longest x2 0.6 us: prepared(): return (full, (gram.astype(F32) + over_rank(gram).astype(F32)).astype(BF))]
    ppermute x5 -> x11, starting transfers between devices: 0.15 us -> 2.52 us  [over_rank(): return lax.ppermute(value, 'rank', [(0, 1), (1, 0)])]
    unnamed x26 -> x16, local copies, waits for them, and re-layouts: 2.47 us -> 0.38 us
    ppermute x12, waiting for transfers between devices: 27.9 us -> 25.8 us  [over_chips(): lax.ppermute(value, axes, [(s, s ^ mask) for s in range(lax.axis_size(axe...]
  transfers between devices with their start and end apart: 17 -> 23, of which waited for: 12 -> 20; matrix products, arithmetic and copies ran while one was open for 25% -> 1% of each run, Pallas kernels for 0% -> 9%
where the time goes in v2:
time: 75.1 us; the launch traced here: 74.9 us
  waiting for transfers between devices  31.1 us (41%)
  starting transfers between devices  29.5 us (39%)
  Pallas kernels  10.4 us (14%)
  local copies, waits for them, and re-layouts  2.65 us (4%)
  other arithmetic  0.87 us (1%)
    ppermute x12, starting transfers between devices, over_chips(): lax.ppermute(value, axes, [(s, s ^ mask) for s in range(lax.axis_size(axe...  27 us
    ppermute x12, waiting for transfers between devices, over_chips(): lax.ppermute(value, axes, [(s, s ^ mask) for s in range(lax.axis_size(axe...  25.8 us
    pallas_call x11, Pallas kernels, call(): pl.pallas_call(kernel, out_shape=outs, in_specs=[pl.BlockSpec(memory_spac...  10.4 us
    ppermute x11, waiting for transfers between devices, over_rank(): return lax.ppermute(value, 'rank', [(0, 1), (1, 0)])  5.28 us
    ppermute x11, starting transfers between devices, over_rank(): return lax.ppermute(value, 'rank', [(0, 1), (1, 0)])  2.52 us
    dynamic_slice x4, local copies, waits for them, and re-layouts, swapped(): lax.dynamic_slice_in_dim(f, (1 - rank) * half, half, 0)  2.24 us
  transfers between devices with their start and end apart: 23, of which 20 were waited for; matrix products, arithmetic and copies ran while one was open for 1% of the time, Pallas kernels for 9%

profile of v2, /device:TPU:0, one launch (start us, length us, event | category | flops | bytes accessed | tf_op | source)
XLA Modules:
  0.0 74.9 jit_solution(15416468317913360132)
XLA Ops:
  0.0 1.0 %constant_dynamic-slice_fusion.5 = bf16[1024,128]{1,0:T(8,128)(2,1)S(1)} fusion(bf16[2048,128]{1,0:T(8,128)(2,1)} %refs_0_.4, s32[]{:T(128)S(6)} %select_n.2), kind=kLoop, calls=%fused_computation.21 | loop fusion | bytes 524292 | tf_op jit(solution)/shard_map/dynamic_slice | solution.py:149
  1.1 1.2 %constant_dynamic-slice_fusion.3 = (bf16[1024,128]{1,0:T(8,128)(2,1)S(1)}, bf16[1024,128]{1,0:T(8,128)(2,1)S(1)}) fusion(bf16[2048,128]{1,0:T(8,128)(2,1)} %refs_2_.4, s32[]{:T(128)S(6)} %select_n.2, bf16[2048,128]{1,0:T(8,128)(2,1)} %refs_1_.4), kind=kLoop, calls=%fused_computation.19 | loop fusion | bytes 1048580 | tf_op jit(solution)/shard_map/dynamic_slice | solution.py:149
  2.3 0.6 collective-permute-start.4
  3.0 1.8 %collective-permute-done.4.refs_3_ = bf16[3072,128]{1,0:T(8,128)(2,1)S(1)} collective-permute-done((bf16[3072,128]{1,0:T(8,128)(2,1)S(1)}, bf16[3072,128]{1,0:T(8,128)(2,1)S(1)}, u32[]{:S(2)}, u32[]{:S(2)}) %collective-permute-start.4) | collective-permute-done | bytes 786464 | tf_op jit(solution)/shard_map/ppermute | solution.py:118
  4.8 1.4 %shard_map.83 = (bf16[1024,768]{1,0:T(8,128)(2,1)S(1)}, bf16[768,768]{1,0:T(8,128)(2,1)S(1)}) custom-call(s32[1]{0:T(128)} %bitcast.place.r_0_, bf16[2048,128]{1,0:T(8,128)(2,1)S(1)} %copy-done.5, bf16[2048,128]{1,0:T(8,128)(2,1)S(1)} %copy-done.6, bf16[2048,128]{1,0:T(8,128)(2,1)S(1)} %copy-done.7, bf16[3072,128]{1,0:T(8,128)(2,1)S(1)} %collective-permute-done.4.refs_3_), custom_call_target="tpu_custom_call" | custom-call | flops 905969664 | bytes 5111808 | tf_op jit(solution)/shard_map/pallas_call | solution.py:22
  6.2 0.4 collective-permute-start.5
  6.9 0.3 copy-done.1
  7.2 0.6 shard_map.82
  7.9 2.9 %collective-permute-start = (bf16[384,128]{1,0:T(8,128)(2,1)S(1)}, bf16[384,128]{1,0:T(8,128)(2,1)S(1)}, u32[]{:S(2)}, u32[]{:S(2)}) collective-permute-start(bf16[384,128]{1,0:T(8,128)(2,1)S(1)} %shard_map.82), channel_id=1, source_target_pairs={{0,2},{2,0},{4,6},{6,4},{8,10},{10,8},{12,14},{14,12},{1,3},{3,1},... | collective-permute-start | bytes 294920 | tf_op jit(solution)/shard_map/ppermute | solution.py:114
  10.8 3.1 %collective-permute-done = bf16[384,128]{1,0:T(8,128)(2,1)S(1)} collective-permute-done((bf16[384,128]{1,0:T(8,128)(2,1)S(1)}, bf16[384,128]{1,0:T(8,128)(2,1)S(1)}, u32[]{:S(2)}, u32[]{:S(2)}) %collective-permute-start) | collective-permute-done | bytes 98336 | tf_op jit(solution)/shard_map/ppermute | solution.py:114
  13.9 1.9 %collective-permute-start.1 = (bf16[256,128]{1,0:T(8,128)(2,1)S(1)}, bf16[256,128]{1,0:T(8,128)(2,1)S(1)}, u32[]{:S(2)}, u32[]{:S(2)}) collective-permute-start(bf16[256,128]{1,0:T(8,128)(2,1)S(1)} %add_convert_fusion.5), channel_id=1, source_target_pairs={{0,4},{2,6},{4,0},{6,2},{8,12},{10,14},{12,8},{14,10},{1,5},{3,7},... | collective-permute-start | bytes 196616 | tf_op jit(solution)/shard_map/ppermute | solution.py:114
  15.8 2.4 %collective-permute-done.1 = bf16[256,128]{1,0:T(8,128)(2,1)S(1)} collective-permute-done((bf16[256,128]{1,0:T(8,128)(2,1)S(1)}, bf16[256,128]{1,0:T(8,128)(2,1)S(1)}, u32[]{:S(2)}, u32[]{:S(2)}) %collective-permute-start.1) | collective-permute-done | bytes 65568 | tf_op jit(solution)/shard_map/ppermute | solution.py:114
  18.2 2.9 %collective-permute-start.2 = (bf16[128,128]{1,0:T(8,128)(2,1)S(1)}, bf16[128,128]{1,0:T(8,128)(2,1)S(1)}, u32[]{:S(2)}, u32[]{:S(2)}) collective-permute-start(bf16[128,128]{1,0:T(8,128)(2,1)S(1)} %add_convert_fusion.9), channel_id=1, source_target_pairs={{0,8},{2,10},{4,12},{6,14},{8,0},{10,2},{12,4},{14,6},{1,9},{3,11}... | collective-permute-start | bytes 98312 | tf_op jit(solution)/shard_map/ppermute | solution.py:114
  21.1 1.4 %shard_map.86 = (bf16[1024,768]{1,0:T(8,128)(2,1)S(1)}, bf16[768,768]{1,0:T(8,128)(2,1)S(1)}) custom-call(s32[1]{0:T(128)} %bitcast.place.r_0_, bf16[2048,128]{1,0:T(8,128)(2,1)S(1)} %copy-done.2, bf16[2048,128]{1,0:T(8,128)(2,1)S(1)} %copy-done.3, bf16[2048,128]{1,0:T(8,128)(2,1)S(1)} %copy-done.4, bf16[3072,128]{1,0:T(8,128)(2,1)S(1)} %collective-permute-done.11.refs_3_), custom_call_target="tpu_custom_call" | custom-call | flops 905969664 | bytes 5111808 | tf_op jit(solution)/shard_map/pallas_call | solution.py:22
  22.6 0.5 collective-permute-done.2
  23.2 0.7 shard_map.84
  24.0 0.6 collective-permute-start.6
  24.8 0.8 %collective-permute-done.3.other = bf16[384,128]{1,0:T(8,128)(2,1)S(1)} collective-permute-done((bf16[384,128]{1,0:T(8,128)(2,1)S(1)}, bf16[384,128]{1,0:T(8,128)(2,1)S(1)}, u32[]{:S(2)}, u32[]{:S(2)}) %collective-permute-start.3) | collective-permute-done | bytes 98336 | tf_op jit(solution)/shard_map/ppermute | solution.py:118
  25.9 0.3 shard_map.85
  26.2 1.6 %collective-permute-start.7 = (bf16[384,128]{1,0:T(8,128)(2,1)S(1)}, bf16[384,128]{1,0:T(8,128)(2,1)S(1)}, u32[]{:S(2)}, u32[]{:S(2)}) collective-permute-start(bf16[384,128]{1,0:T(8,128)(2,1)S(1)} %get-tuple-element.24), channel_id=1, source_target_pairs={{0,2},{2,0},{4,6},{6,4},{8,10},{10,8},{12,14},{14,12},{1,3},{3,1},... | collective-permute-start | bytes 294920 | tf_op jit(solution)/shard_map/ppermute | solution.py:114
  27.8 3.4 %collective-permute-done.7 = bf16[384,128]{1,0:T(8,128)(2,1)S(1)} collective-permute-done((bf16[384,128]{1,0:T(8,128)(2,1)S(1)}, bf16[384,128]{1,0:T(8,128)(2,1)S(1)}, u32[]{:S(2)}, u32[]{:S(2)}) %collective-permute-start.7) | collective-permute-done | bytes 98336 | tf_op jit(solution)/shard_map/ppermute | solution.py:114
  31.1 1.8 %collective-permute-start.8 = (bf16[256,128]{1,0:T(8,128)(2,1)S(1)}, bf16[256,128]{1,0:T(8,128)(2,1)S(1)}, u32[]{:S(2)}, u32[]{:S(2)}) collective-permute-start(bf16[256,128]{1,0:T(8,128)(2,1)S(1)} %add_convert_fusion.4), channel_id=1, source_target_pairs={{0,4},{2,6},{4,0},{6,2},{8,12},{10,14},{12,8},{14,10},{1,5},{3,7},... | collective-permute-start | bytes 196616 | tf_op jit(solution)/shard_map/ppermute | solution.py:114
  33.0 2.5 %collective-permute-done.8 = bf16[256,128]{1,0:T(8,128)(2,1)S(1)} collective-permute-done((bf16[256,128]{1,0:T(8,128)(2,1)S(1)}, bf16[256,128]{1,0:T(8,128)(2,1)S(1)}, u32[]{:S(2)}, u32[]{:S(2)}) %collective-permute-start.8) | collective-permute-done | bytes 65568 | tf_op jit(solution)/shard_map/ppermute | solution.py:114
  35.5 2.9 %collective-permute-start.9 = (bf16[128,128]{1,0:T(8,128)(2,1)S(1)}, bf16[128,128]{1,0:T(8,128)(2,1)S(1)}, u32[]{:S(2)}, u32[]{:S(2)}) collective-permute-start(bf16[128,128]{1,0:T(8,128)(2,1)S(1)} %add_convert_fusion.8), channel_id=1, source_target_pairs={{0,8},{2,10},{4,12},{6,14},{8,0},{10,2},{12,4},{14,6},{1,9},{3,11}... | collective-permute-start | bytes 98312 | tf_op jit(solution)/shard_map/ppermute | solution.py:114
  38.4 1.5 %shard_map.87 = (f32[1024,128]{1,0:T(8,128)S(1)}, bf16[128,768]{1,0:T(8,128)(2,1)S(1)}) custom-call(s32[1]{0:T(128)} %bitcast.place.r_0_, bf16[128,768]{1,0:T(8,128)(2,1)S(1)} %get-tuple-element.26.r_1_, bf16[1024,768]{1,0:T(8,128)(2,1)S(1)} %get-tuple-element.22.after.r_2_.r_5_, f32[1024,128]{1,0:T(8,128)S(1)} %get-tuple-element.27.r_3_, ...), custom_call_target="tpu_custom_call" | custom-call | flops 402653184 | bytes 5111808 | tf_op jit(solution)/shard_map/pallas_call | solution.py:22
  40.0 0.3 collective-permute-done.9
  40.9 0.5 collective-permute-done.13.there
  41.4 0.3 collective-permute-done.10.other
  41.7 0.3 shard_map.88
  42.1 1.8 %collective-permute-start.14 = (bf16[384,128]{1,0:T(8,128)(2,1)S(1)}, bf16[384,128]{1,0:T(8,128)(2,1)S(1)}, u32[]{:S(2)}, u32[]{:S(2)}) collective-permute-start(bf16[384,128]{1,0:T(8,128)(2,1)S(1)} %get-tuple-element.30), channel_id=1, source_target_pairs={{0,2},{2,0},{4,6},{6,4},{8,10},{10,8},{12,14},{14,12},{1,3},{3,1},... | collective-permute-start | bytes 294920 | tf_op jit(solution)/shard_map/ppermute | solution.py:114
  43.9 3.2 %collective-permute-done.14 = bf16[384,128]{1,0:T(8,128)(2,1)S(1)} collective-permute-done((bf16[384,128]{1,0:T(8,128)(2,1)S(1)}, bf16[384,128]{1,0:T(8,128)(2,1)S(1)}, u32[]{:S(2)}, u32[]{:S(2)}) %collective-permute-start.14) | collective-permute-done | bytes 98336 | tf_op jit(solution)/shard_map/ppermute | solution.py:114
  47.0 1.9 %collective-permute-start.15 = (bf16[256,128]{1,0:T(8,128)(2,1)S(1)}, bf16[256,128]{1,0:T(8,128)(2,1)S(1)}, u32[]{:S(2)}, u32[]{:S(2)}) collective-permute-start(bf16[256,128]{1,0:T(8,128)(2,1)S(1)} %add_convert_fusion.3), channel_id=1, source_target_pairs={{0,4},{2,6},{4,0},{6,2},{8,12},{10,14},{12,8},{14,10},{1,5},{3,7},... | collective-permute-start | bytes 196616 | tf_op jit(solution)/shard_map/ppermute | solution.py:114
  48.9 2.5 %collective-permute-done.15 = bf16[256,128]{1,0:T(8,128)(2,1)S(1)} collective-permute-done((bf16[256,128]{1,0:T(8,128)(2,1)S(1)}, bf16[256,128]{1,0:T(8,128)(2,1)S(1)}, u32[]{:S(2)}, u32[]{:S(2)}) %collective-permute-start.15) | collective-permute-done | bytes 65568 | tf_op jit(solution)/shard_map/ppermute | solution.py:114
  51.4 2.9 %collective-permute-start.16 = (bf16[128,128]{1,0:T(8,128)(2,1)S(1)}, bf16[128,128]{1,0:T(8,128)(2,1)S(1)}, u32[]{:S(2)}, u32[]{:S(2)}) collective-permute-start(bf16[128,128]{1,0:T(8,128)(2,1)S(1)} %add_convert_fusion.7), channel_id=1, source_target_pairs={{0,8},{2,10},{4,12},{6,14},{8,0},{10,2},{12,4},{14,6},{1,9},{3,11}... | collective-permute-start | bytes 98312 | tf_op jit(solution)/shard_map/ppermute | solution.py:114
  54.3 1.5 %shard_map.89 = (f32[1024,128]{1,0:T(8,128)S(1)}, bf16[128,768]{1,0:T(8,128)(2,1)S(1)}) custom-call(s32[1]{0:T(128)} %bitcast.place.r_0_, bf16[128,768]{1,0:T(8,128)(2,1)S(1)} %get-tuple-element.31.r_1_, bf16[1024,768]{1,0:T(8,128)(2,1)S(1)} %get-tuple-element.28.r_5_.r_2_.factor, f32[1024,128]{1,0:T(8,128)S(1)} %get-tuple-element.32.r_3_, ...), custom_call_target="tpu_custom_call" | custom-call | flops 402653184 | bytes 5111808 | tf_op jit(solution)/shard_map/pallas_call | solution.py:22
  55.9 0.3 collective-permute-done.16
  56.5 0.8 %collective-permute-done.18.there = bf16[128,768]{1,0:T(8,128)(2,1)S(1)} collective-permute-done((bf16[128,768]{1,0:T(8,128)(2,1)S(1)}, bf16[128,768]{1,0:T(8,128)(2,1)S(1)}, u32[]{:S(2)}, u32[]{:S(2)}) %collective-permute-start.18) | collective-permute-done | bytes 196640 | tf_op jit(solution)/shard_map/ppermute | solution.py:118
  57.3 0.3 collective-permute-done.17.other
  57.6 0.3 shard_map.90
  58.0 1.8 %collective-permute-start.19 = (bf16[384,128]{1,0:T(8,128)(2,1)S(1)}, bf16[384,128]{1,0:T(8,128)(2,1)S(1)}, u32[]{:S(2)}, u32[]{:S(2)}) collective-permute-start(bf16[384,128]{1,0:T(8,128)(2,1)S(1)} %get-tuple-element.34), channel_id=1, source_target_pairs={{0,2},{2,0},{4,6},{6,4},{8,10},{10,8},{12,14},{14,12},{1,3},{3,1},... | collective-permute-start | bytes 294920 | tf_op jit(solution)/shard_map/ppermute | solution.py:114
  59.8 3.2 %collective-permute-done.19 = bf16[384,128]{1,0:T(8,128)(2,1)S(1)} collective-permute-done((bf16[384,128]{1,0:T(8,128)(2,1)S(1)}, bf16[384,128]{1,0:T(8,128)(2,1)S(1)}, u32[]{:S(2)}, u32[]{:S(2)}) %collective-permute-start.19) | collective-permute-done | bytes 98336 | tf_op jit(solution)/shard_map/ppermute | solution.py:114
  62.9 1.9 %collective-permute-start.20 = (bf16[256,128]{1,0:T(8,128)(2,1)S(1)}, bf16[256,128]{1,0:T(8,128)(2,1)S(1)}, u32[]{:S(2)}, u32[]{:S(2)}) collective-permute-start(bf16[256,128]{1,0:T(8,128)(2,1)S(1)} %add_convert_fusion.2), channel_id=1, source_target_pairs={{0,4},{2,6},{4,0},{6,2},{8,12},{10,14},{12,8},{14,10},{1,5},{3,7},... | collective-permute-start | bytes 196616 | tf_op jit(solution)/shard_map/ppermute | solution.py:114
  64.8 2.5 %collective-permute-done.20 = bf16[256,128]{1,0:T(8,128)(2,1)S(1)} collective-permute-done((bf16[256,128]{1,0:T(8,128)(2,1)S(1)}, bf16[256,128]{1,0:T(8,128)(2,1)S(1)}, u32[]{:S(2)}, u32[]{:S(2)}) %collective-permute-start.20) | collective-permute-done | bytes 65568 | tf_op jit(solution)/shard_map/ppermute | solution.py:114
  67.3 2.9 %collective-permute-start.21 = (bf16[128,128]{1,0:T(8,128)(2,1)S(1)}, bf16[128,128]{1,0:T(8,128)(2,1)S(1)}, u32[]{:S(2)}, u32[]{:S(2)}) collective-permute-start(bf16[128,128]{1,0:T(8,128)(2,1)S(1)} %add_convert_fusion.6), channel_id=1, source_target_pairs={{0,8},{2,10},{4,12},{6,14},{8,0},{10,2},{12,4},{14,6},{1,9},{3,11}... | collective-permute-start | bytes 98312 | tf_op jit(solution)/shard_map/ppermute | solution.py:114
  70.2 2.0 %collective-permute-done.21 = bf16[128,128]{1,0:T(8,128)(2,1)S(1)} collective-permute-done((bf16[128,128]{1,0:T(8,128)(2,1)S(1)}, bf16[128,128]{1,0:T(8,128)(2,1)S(1)}, u32[]{:S(2)}, u32[]{:S(2)}) %collective-permute-start.21) | collective-permute-done | bytes 32800 | tf_op jit(solution)/shard_map/ppermute | solution.py:114
  72.3 0.9 %shard_map.91.was = f32[1024,128]{1,0:T(8,128)S(1)} custom-call(s32[1]{0:T(128)} %bitcast.place.r_0_, bf16[128,768]{1,0:T(8,128)(2,1)S(1)} %get-tuple-element.35.r_1_, bf16[1024,768]{1,0:T(8,128)(2,1)S(1)} %get-tuple-element.22.after.r_2_.r_5_, f32[1024,128]{1,0:T(8,128)S(1)} %get-tuple-element.36.r_3_, bf16[4,256,256]{2,1,0:T(8,128)(2,1)S(1)} %copy-done), custom_call_target="tpu_custom_call" | custom-call | flops 201326592 | bytes 3342336 | tf_op jit(solution)/shard_map/pallas_call | solution.py:22
  73.1 0.4 collective-permute-done.22.other
  73.5 1.3 %shard_map.92 = bf16[1024,128]{1,0:T(8,128)(2,1)} custom-call(s32[1]{0:T(128)} %bitcast.place.r_0_, bf16[384,128]{1,0:T(8,128)(2,1)S(1)} %pad_maximum_fusion.5.own, bf16[384,128]{1,0:T(8,128)(2,1)S(1)} %collective-permute-done.22.other, bf16[1024,768]{1,0:T(8,128)(2,1)S(1)} %get-tuple-element.28.r_5_.r_2_.factor, f32[1024,128]{1,0:T(8,128)S(1)} %shard_map.91.was), custom_call_target="tpu_custom_call" | custom-call | flops 201326592 | bytes 2555904 | tf_op jit(solution)/shard_map/pallas_call | solution.py:22
  (53 shorter events, 2.3 us)
Async XLA Ops:
  0.0 2.9 %copy-start.2 = (bf16[2048,128]{1,0:T(8,128)(2,1)S(1)}, bf16[2048,128]{1,0:T(8,128)(2,1)}, u32[]{:S(2)}) copy-start(bf16[2048,128]{1,0:T(8,128)(2,1)} %refs_0_.5) | copy-start | bytes 1572868
  1.0 1.9 %copy-start.3 = (bf16[2048,128]{1,0:T(8,128)(2,1)S(1)}, bf16[2048,128]{1,0:T(8,128)(2,1)}, u32[]{:S(2)}) copy-start(bf16[2048,128]{1,0:T(8,128)(2,1)} %refs_1_.5) | copy-start | bytes 1572868
  1.0 1.9 %copy-start.4 = (bf16[2048,128]{1,0:T(8,128)(2,1)S(1)}, bf16[2048,128]{1,0:T(8,128)(2,1)}, u32[]{:S(2)}) copy-start(bf16[2048,128]{1,0:T(8,128)(2,1)} %refs_2_.5) | copy-start | bytes 1572868
  2.2 2.6 %copy-start.5 = (bf16[2048,128]{1,0:T(8,128)(2,1)S(1)}, bf16[2048,128]{1,0:T(8,128)(2,1)}, u32[]{:S(2)}) copy-start(bf16[2048,128]{1,0:T(8,128)(2,1)} %refs_0_.4) | copy-start | bytes 1572868
  2.2 2.6 %copy-start.6 = (bf16[2048,128]{1,0:T(8,128)(2,1)S(1)}, bf16[2048,128]{1,0:T(8,128)(2,1)}, u32[]{:S(2)}) copy-start(bf16[2048,128]{1,0:T(8,128)(2,1)} %refs_1_.4) | copy-start | bytes 1572868
  2.2 2.6 %copy-start.7 = (bf16[2048,128]{1,0:T(8,128)(2,1)S(1)}, bf16[2048,128]{1,0:T(8,128)(2,1)}, u32[]{:S(2)}) copy-start(bf16[2048,128]{1,0:T(8,128)(2,1)} %refs_2_.4) | copy-start | bytes 1572868
  2.3 2.5 %collective-permute-start.4 = (bf16[3072,128]{1,0:T(8,128)(2,1)S(1)}, bf16[3072,128]{1,0:T(8,128)(2,1)S(1)}, u32[]{:S(2)}, u32[]{:S(2)}) collective-permute-start(bf16[3072,128]{1,0:T(8,128)(2,1)S(1)} %pad_maximum_fusion), channel_id=1, source_target_pairs={{0,1},{1,0},{2,3},{3,2},{4,5},{5,4},{6,7},{7,6},{8,9},{9,8},{10,11... | collective-permute-start | bytes 2359304 | tf_op jit(solution)/shard_map/ppermute | solution.py:118
  6.2 1.0 %copy-start.1 = (bf16[2048,128]{1,0:T(8,128)(2,1)S(1)}, bf16[2048,128]{1,0:T(8,128)(2,1)}, u32[]{:S(2)}) copy-start(bf16[2048,128]{1,0:T(8,128)(2,1)} %z.3) | copy-start | bytes 1572868
  6.2 18.3 %collective-permute-start.5 = (bf16[768,768]{1,0:T(8,128)(2,1)S(1)}, bf16[768,768]{1,0:T(8,128)(2,1)S(1)}, u32[]{:S(2)}, u32[]{:S(2)}) collective-permute-start(bf16[768,768]{1,0:T(8,128)(2,1)S(1)} %get-tuple-element.21), channel_id=1, source_target_pairs={{0,1},{1,0},{2,3},{3,2},{4,5},{5,4},{6,7},{7,6},{8,9},{9,8},{10,11... | collective-permute-start | bytes 3538952 | tf_op jit(solution)/shard_map/ppermute | solution.py:118
  6.7 14.5 %collective-permute-start.11 = (bf16[3072,128]{1,0:T(8,128)(2,1)S(1)}, bf16[3072,128]{1,0:T(8,128)(2,1)S(1)}, u32[]{:S(2)}, u32[]{:S(2)}) collective-permute-start(bf16[3072,128]{1,0:T(8,128)(2,1)S(1)} %pad_maximum_fusion.1), channel_id=1, source_target_pairs={{0,1},{1,0},{2,3},{3,2},{4,5},{5,4},{6,7},{7,6},{8,9},{9,8},{10,11... | collective-permute-start | bytes 2359304 | tf_op jit(solution)/shard_map/ppermute | solution.py:118
  7.9 6.0 %collective-permute-start = (bf16[384,128]{1,0:T(8,128)(2,1)S(1)}, bf16[384,128]{1,0:T(8,128)(2,1)S(1)}, u32[]{:S(2)}, u32[]{:S(2)}) collective-permute-start(bf16[384,128]{1,0:T(8,128)(2,1)S(1)} %shard_map.82), channel_id=1, source_target_pairs={{0,2},{2,0},{4,6},{6,4},{8,10},{10,8},{12,14},{14,12},{1,3},{3,1},... | collective-permute-start | bytes 294920 | tf_op jit(solution)/shard_map/ppermute | solution.py:114
  13.9 4.3 %collective-permute-start.1 = (bf16[256,128]{1,0:T(8,128)(2,1)S(1)}, bf16[256,128]{1,0:T(8,128)(2,1)S(1)}, u32[]{:S(2)}, u32[]{:S(2)}) collective-permute-start(bf16[256,128]{1,0:T(8,128)(2,1)S(1)} %add_convert_fusion.5), channel_id=1, source_target_pairs={{0,4},{2,6},{4,0},{6,2},{8,12},{10,14},{12,8},{14,10},{1,5},{3,7},... | collective-permute-start | bytes 196616 | tf_op jit(solution)/shard_map/ppermute | solution.py:114
  18.2 4.9 %collective-permute-start.2 = (bf16[128,128]{1,0:T(8,128)(2,1)S(1)}, bf16[128,128]{1,0:T(8,128)(2,1)S(1)}, u32[]{:S(2)}, u32[]{:S(2)}) collective-permute-start(bf16[128,128]{1,0:T(8,128)(2,1)S(1)} %add_convert_fusion.9), channel_id=1, source_target_pairs={{0,8},{2,10},{4,12},{6,14},{8,0},{10,2},{12,4},{14,6},{1,9},{3,11}... | collective-permute-start | bytes 98312 | tf_op jit(solution)/shard_map/ppermute | solution.py:114
  21.1 2.1 %copy-start = (bf16[4,256,256]{2,1,0:T(8,128)(2,1)S(1)}, bf16[4,256,256]{2,1,0:T(8,128)(2,1)}, u32[]{:S(2)}) copy-start(bf16[4,256,256]{2,1,0:T(8,128)(2,1)} %r_4_.5) | copy-start | bytes 1572868
  22.5 18.1 %collective-permute-start.12 = (bf16[768,768]{1,0:T(8,128)(2,1)S(1)}, bf16[768,768]{1,0:T(8,128)(2,1)S(1)}, u32[]{:S(2)}, u32[]{:S(2)}) collective-permute-start(bf16[768,768]{1,0:T(8,128)(2,1)S(1)} %get-tuple-element.25), channel_id=1, source_target_pairs={{0,1},{1,0},{2,3},{3,2},{4,5},{5,4},{6,7},{7,6},{8,9},{9,8},{10,11... | collective-permute-start | bytes 3538952 | tf_op jit(solution)/shard_map/ppermute | solution.py:118
  23.1 2.5 %collective-permute-start.3 = (bf16[384,128]{1,0:T(8,128)(2,1)S(1)}, bf16[384,128]{1,0:T(8,128)(2,1)S(1)}, u32[]{:S(2)}, u32[]{:S(2)}) collective-permute-start(bf16[384,128]{1,0:T(8,128)(2,1)S(1)} %pad_maximum_fusion.2.own), channel_id=1, source_target_pairs={{0,1},{1,0},{2,3},{3,2},{4,5},{5,4},{6,7},{7,6},{8,9},{9,8},{10,11... | collective-permute-start | bytes 294920 | tf_op jit(solution)/shard_map/ppermute | solution.py:118
  24.0 1.9 %collective-permute-start.6 = (bf16[128,768]{1,0:T(8,128)(2,1)S(1)}, bf16[128,768]{1,0:T(8,128)(2,1)S(1)}, u32[]{:S(2)}, u32[]{:S(2)}) collective-permute-start(bf16[128,768]{1,0:T(8,128)(2,1)S(1)} %get-tuple-element.23.here), channel_id=1, source_target_pairs={{0,1},{1,0},{2,3},{3,2},{4,5},{5,4},{6,7},{7,6},{8,9},{9,8},{10,11... | collective-permute-start | bytes 589832 | tf_op jit(solution)/shard_map/ppermute | solution.py:118
  26.2 4.9 %collective-permute-start.7 = (bf16[384,128]{1,0:T(8,128)(2,1)S(1)}, bf16[384,128]{1,0:T(8,128)(2,1)S(1)}, u32[]{:S(2)}, u32[]{:S(2)}) collective-permute-start(bf16[384,128]{1,0:T(8,128)(2,1)S(1)} %get-tuple-element.24), channel_id=1, source_target_pairs={{0,2},{2,0},{4,6},{6,4},{8,10},{10,8},{12,14},{14,12},{1,3},{3,1},... | collective-permute-start | bytes 294920 | tf_op jit(solution)/shard_map/ppermute | solution.py:114
  31.1 4.3 %collective-permute-start.8 = (bf16[256,128]{1,0:T(8,128)(2,1)S(1)}, bf16[256,128]{1,0:T(8,128)(2,1)S(1)}, u32[]{:S(2)}, u32[]{:S(2)}) collective-permute-start(bf16[256,128]{1,0:T(8,128)(2,1)S(1)} %add_convert_fusion.4), channel_id=1, source_target_pairs={{0,4},{2,6},{4,0},{6,2},{8,12},{10,14},{12,8},{14,10},{1,5},{3,7},... | collective-permute-start | bytes 196616 | tf_op jit(solution)/shard_map/ppermute | solution.py:114
  35.5 4.9 %collective-permute-start.9 = (bf16[128,128]{1,0:T(8,128)(2,1)S(1)}, bf16[128,128]{1,0:T(8,128)(2,1)S(1)}, u32[]{:S(2)}, u32[]{:S(2)}) collective-permute-start(bf16[128,128]{1,0:T(8,128)(2,1)S(1)} %add_convert_fusion.8), channel_id=1, source_target_pairs={{0,8},{2,10},{4,12},{6,14},{8,0},{10,2},{12,4},{14,6},{1,9},{3,11}... | collective-permute-start | bytes 98312 | tf_op jit(solution)/shard_map/ppermute | solution.py:114
  39.9 1.5 %collective-permute-start.13 = (bf16[128,768]{1,0:T(8,128)(2,1)S(1)}, bf16[128,768]{1,0:T(8,128)(2,1)S(1)}, u32[]{:S(2)}, u32[]{:S(2)}) collective-permute-start(bf16[128,768]{1,0:T(8,128)(2,1)S(1)} %get-tuple-element.29.here), channel_id=1, source_target_pairs={{0,1},{1,0},{2,3},{3,2},{4,5},{5,4},{6,7},{7,6},{8,9},{9,8},{10,11... | collective-permute-start | bytes 589832 | tf_op jit(solution)/shard_map/ppermute | solution.py:118
  40.4 1.4 %collective-permute-start.10 = (bf16[384,128]{1,0:T(8,128)(2,1)S(1)}, bf16[384,128]{1,0:T(8,128)(2,1)S(1)}, u32[]{:S(2)}, u32[]{:S(2)}) collective-permute-start(bf16[384,128]{1,0:T(8,128)(2,1)S(1)} %pad_maximum_fusion.3.own), channel_id=1, source_target_pairs={{0,1},{1,0},{2,3},{3,2},{4,5},{5,4},{6,7},{7,6},{8,9},{9,8},{10,11... | collective-permute-start | bytes 294920 | tf_op jit(solution)/shard_map/ppermute | solution.py:118
  42.1 4.9 %collective-permute-start.14 = (bf16[384,128]{1,0:T(8,128)(2,1)S(1)}, bf16[384,128]{1,0:T(8,128)(2,1)S(1)}, u32[]{:S(2)}, u32[]{:S(2)}) collective-permute-start(bf16[384,128]{1,0:T(8,128)(2,1)S(1)} %get-tuple-element.30), channel_id=1, source_target_pairs={{0,2},{2,0},{4,6},{6,4},{8,10},{10,8},{12,14},{14,12},{1,3},{3,1},... | collective-permute-start | bytes 294920 | tf_op jit(solution)/shard_map/ppermute | solution.py:114
  47.0 4.3 %collective-permute-start.15 = (bf16[256,128]{1,0:T(8,128)(2,1)S(1)}, bf16[256,128]{1,0:T(8,128)(2,1)S(1)}, u32[]{:S(2)}, u32[]{:S(2)}) collective-permute-start(bf16[256,128]{1,0:T(8,128)(2,1)S(1)} %add_convert_fusion.3), channel_id=1, source_target_pairs={{0,4},{2,6},{4,0},{6,2},{8,12},{10,14},{12,8},{14,10},{1,5},{3,7},... | collective-permute-start | bytes 196616 | tf_op jit(solution)/shard_map/ppermute | solution.py:114
  51.4 4.9 %collective-permute-start.16 = (bf16[128,128]{1,0:T(8,128)(2,1)S(1)}, bf16[128,128]{1,0:T(8,128)(2,1)S(1)}, u32[]{:S(2)}, u32[]{:S(2)}) collective-permute-start(bf16[128,128]{1,0:T(8,128)(2,1)S(1)} %add_convert_fusion.7), channel_id=1, source_target_pairs={{0,8},{2,10},{4,12},{6,14},{8,0},{10,2},{12,4},{14,6},{1,9},{3,11}... | collective-permute-start | bytes 98312 | tf_op jit(solution)/shard_map/ppermute | solution.py:114
  55.8 1.5 %collective-permute-start.18 = (bf16[128,768]{1,0:T(8,128)(2,1)S(1)}, bf16[128,768]{1,0:T(8,128)(2,1)S(1)}, u32[]{:S(2)}, u32[]{:S(2)}) collective-permute-start(bf16[128,768]{1,0:T(8,128)(2,1)S(1)} %get-tuple-element.33.here), channel_id=1, source_target_pairs={{0,1},{1,0},{2,3},{3,2},{4,5},{5,4},{6,7},{7,6},{8,9},{9,8},{10,11... | collective-permute-start | bytes 589832 | tf_op jit(solution)/shard_map/ppermute | solution.py:118
  56.3 1.4 %collective-permute-start.17 = (bf16[384,128]{1,0:T(8,128)(2,1)S(1)}, bf16[384,128]{1,0:T(8,128)(2,1)S(1)}, u32[]{:S(2)}, u32[]{:S(2)}) collective-permute-start(bf16[384,128]{1,0:T(8,128)(2,1)S(1)} %pad_maximum_fusion.4.own), channel_id=1, source_target_pairs={{0,1},{1,0},{2,3},{3,2},{4,5},{5,4},{6,7},{7,6},{8,9},{9,8},{10,11... | collective-permute-start | bytes 294920 | tf_op jit(solution)/shard_map/ppermute | solution.py:118
  58.0 4.9 %collective-permute-start.19 = (bf16[384,128]{1,0:T(8,128)(2,1)S(1)}, bf16[384,128]{1,0:T(8,128)(2,1)S(1)}, u32[]{:S(2)}, u32[]{:S(2)}) collective-permute-start(bf16[384,128]{1,0:T(8,128)(2,1)S(1)} %get-tuple-element.34), channel_id=1, source_target_pairs={{0,2},{2,0},{4,6},{6,4},{8,10},{10,8},{12,14},{14,12},{1,3},{3,1},... | collective-permute-start | bytes 294920 | tf_op jit(solution)/shard_map/ppermute | solution.py:114
  62.9 4.3 %collective-permute-start.20 = (bf16[256,128]{1,0:T(8,128)(2,1)S(1)}, bf16[256,128]{1,0:T(8,128)(2,1)S(1)}, u32[]{:S(2)}, u32[]{:S(2)}) collective-permute-start(bf16[256,128]{1,0:T(8,128)(2,1)S(1)} %add_convert_fusion.2), channel_id=1, source_target_pairs={{0,4},{2,6},{4,0},{6,2},{8,12},{10,14},{12,8},{14,10},{1,5},{3,7},... | collective-permute-start | bytes 196616 | tf_op jit(solution)/shard_map/ppermute | solution.py:114
  67.3 4.9 %collective-permute-start.21 = (bf16[128,128]{1,0:T(8,128)(2,1)S(1)}, bf16[128,128]{1,0:T(8,128)(2,1)S(1)}, u32[]{:S(2)}, u32[]{:S(2)}) collective-permute-start(bf16[128,128]{1,0:T(8,128)(2,1)S(1)} %add_convert_fusion.6), channel_id=1, source_target_pairs={{0,8},{2,10},{4,12},{6,14},{8,0},{10,2},{12,4},{14,6},{1,9},{3,11}... | collective-permute-start | bytes 98312 | tf_op jit(solution)/shard_map/ppermute | solution.py:114
  72.2 1.4 %collective-permute-start.22 = (bf16[384,128]{1,0:T(8,128)(2,1)S(1)}, bf16[384,128]{1,0:T(8,128)(2,1)S(1)}, u32[]{:S(2)}, u32[]{:S(2)}) collective-permute-start(bf16[384,128]{1,0:T(8,128)(2,1)S(1)} %pad_maximum_fusion.5.own), channel_id=1, source_target_pairs={{0,1},{1,0},{2,3},{3,2},{4,5},{5,4},{6,7},{7,6},{8,9},{9,8},{10,11... | collective-permute-start | bytes 294920 | tf_op jit(solution)/shard_map/ppermute | solution.py:118

commit v3 on v2

--- a/solution.py
+++ b/solution.py
@@ -40,6 +40,13 @@
     c = zt.shape[0]
     for level, factor in enumerate(factors):
         out[level * c : (level + 1) * c, :] = mm(zt, factor[...], 1, 0).astype(BF)
+
+
+def join_kernel(place, own, other, out):
+    k = own.shape[1]
+    me = place[0]
+    out[:, at(me * k, k)] = own[...]
+    out[:, at((1 - me) * k, k)] = other[...]
 
 
 def gram_kernel(place, *refs):
@@ -60,23 +67,40 @@
                 gram[cols, rows] = block.T
 
 
-def join(place, own, other, joined):
-    c, k = own.shape[0] // LEVELS, own.shape[1]
-    me = place[0]
+def next_kernel(place, *refs):
+    found, (gram, here, there, out) = refs[:LEVELS], refs[LEVELS:]
+    c, k = found[0].shape
     for level in range(LEVELS):
-        joined[:, at((2 * level + me) * k, k)] = own[level * c : (level + 1) * c, :]
-        joined[:, at((2 * level + 1 - me) * k, k)] = other[level * c : (level + 1) * c, :]
-
-
-def next_kernel(place, own, other, gram, here, there, out, joined):
-    join(place, own, other, joined)
-    c, k = own.shape[0] // LEVELS, own.shape[1]
-    me = place[0]
-    q = joined[...]
+        cols = slice(level * k, (level + 1) * k)
+        total = here[:, cols].astype(F32) + there[:, cols].astype(F32)
+        for i, q in enumerate(found):
+            total = total + mm(q[...], gram[i * k : (i + 1) * k, cols], 1, 0)
+        out[level * c : (level + 1) * c, :] = total.astype(BF)
+
+
+def chosen(place, holders, refs, joined):
+    k = refs[0].shape[1]
+    for level, holder in enumerate(holders):
+        received, relayed = refs[2 * level], refs[2 * level + 1]
+        cols = slice(level * k, (level + 1) * k)
+
+        @pl.when(place[0] == holder)
+        def _():
+            joined[:, cols] = received[...]
+
+        @pl.when(place[0] != holder)
+        def _():
+            joined[:, cols] = relayed[...]
+
+
+def again_kernel(holders, place, *refs):
+    pieces, (gram, here, there, out, joined) = refs[: 2 * LEVELS], refs[2 * LEVELS :]
+    chosen(place, holders, pieces, joined)
+    c, k = pieces[0].shape
     for level in range(LEVELS):
-        cols = at((2 * level + me) * k, k)
-        base = here[:, cols].astype(F32) + there[:, cols].astype(F32)
-        out[level * c : (level + 1) * c, :] = (mm(q, gram[:, cols], 1, 0) + base).astype(BF)
+        cols = slice(level * k, (level + 1) * k)
+        total = here[:, cols].astype(F32) + there[:, cols].astype(F32) + mm(joined[...], gram[:, cols], 1, 0)
+        out[level * c : (level + 1) * c, :] = total.astype(BF)
 
 
 def leaf_terms(z, leaves, flipped, out):
@@ -103,34 +127,51 @@
     leaf_terms(z, leaves, flipped, y)
 
 
-def last_kernel(place, own, other, factor, was, out, joined):
-    join(place, own, other, joined)
+def last_kernel(holders, place, *refs):
+    pieces, (factor, was, out, joined) = refs[: 2 * LEVELS], refs[2 * LEVELS :]
+    chosen(place, holders, pieces, joined)
     out[...] = (mm(factor[...], joined[...], 1, 1) + was[...]).astype(BF)
 
 
-def over_chips(value, stride):
-    axes = ("rows", "cols")
+def one_way(value, stride, source):
     mask = 2**stride
-    return lax.ppermute(value, axes, [(s, s ^ mask) for s in range(lax.axis_size(axes))])
+    chips = lax.axis_size(("rows", "cols"))
+    away = [(2 * p + source, 2 * (p ^ mask) + 1 - source) for p in range(chips)]
+    home = [(2 * p + 1 - source, 2 * p + source) for p in range(chips)]
+    return lax.ppermute(value, ("rows", "cols", "rank"), away + home)
 
 
 def over_rank(value):
     return lax.ppermute(value, "rank", [(0, 1), (1, 0)])
 
 
-def siblings_of(packed):
+def add(a, b):
+    return (a.astype(F32) + b.astype(F32)).astype(BF)
+
+
+def siblings_of(packed, summed, source):
+    rank = lax.axis_index("rank")
     bits = lax.axis_size(("rows", "cols")).bit_length() - 1
     c = packed.shape[0] // LEVELS
     found = [None] * LEVELS
     for bit in range(bits):
-        received = over_chips(packed, bit)
         count = min(LEVELS, bits - bit)
-        if bit == bits - count:
-            found[count - 1] = received[(count - 1) * c :]
+        received = one_way(packed[: count * c], bit, source)
+        done = bit == bits - count
+        onward = min(LEVELS, max(bits - bit - 2, 0))
+        relay = [l for l in range(count) if l < onward or (done and l == count - 1)]
+        if relay:
+            sent = jnp.concatenate([received[l * c : (l + 1) * c] for l in relay], 0)
+            relayed = over_rank(sent)
+        if done:
+            found[count - 1] = (received[(count - 1) * c :], relayed[(len(relay) - 1) * c :], 1 - source)
             count -= 1
-            packed, received = packed[: count * c], received[: count * c]
-        packed = (packed.astype(F32) + received.astype(F32)).astype(BF)
-    return found
+        packed = add(summed[: count * c], received[: count * c])
+        if onward:
+            got = jnp.where(rank == source, relayed[: onward * c], received[: onward * c])
+            summed = add(summed[: onward * c], got)
+        source = 1 - source
+    return found, source
 
 
 def local(probes, basis_one, basis_two, basis_three, coeff_one, coeff_two, coeff_three, leaves):
@@ -141,6 +182,7 @@
     k = basis_one.shape[1]
     wide = 2 * k * LEVELS
     S = jax.ShapeDtypeStruct
+    p_shape, y_shape, s_shape = S((LEVELS * c, 2 * k), BF), S((half, c), F32), S((c, wide), BF)
     uppers = (basis_one, basis_two, basis_three)
     lowers = (coeff_one, coeff_two, coeff_three)
 
@@ -153,36 +195,44 @@
         full, gram = call(
             gram_kernel, [S((half, wide), BF), S((wide, wide), BF)], (place, *factors, other), half * wide * wide * 3 // 2
         )
-        return full, (gram.astype(F32) + over_rank(gram).astype(F32)).astype(BF)
-
-    (packed,) = call(first_kernel, [S((LEVELS * c, k), BF)], (place, probes, *uppers), 2 * n * LEVELS * k * c)
+        return full, add(gram, over_rank(gram))
+
+    (own,) = call(first_kernel, [S((LEVELS * c, k), BF)], (place, probes, *uppers), 2 * n * LEVELS * k * c)
+    own, lowers, uppers = lax.optimization_barrier((own, lowers, uppers))
+    (packed,) = call(join_kernel, [p_shape], (place, own, over_rank(own)), 0)
+    summed = packed
     lower, lower_gram = prepared(lowers, swapped(lowers))
     upper, upper_gram = prepared(uppers, swapped(uppers))
-    y_shape, s_shape = S((half, c), F32), S((c, wide), BF)
     field_flops = 4 * half * wide * c
     y, s = call(start_kernel, [y_shape, s_shape], (place, probes, leaves, lower), field_flops // 2)
     applies = 2 * PASSES
+    source = 0
+    joined = pltpu.VMEM((c, wide), BF)
     for step in range(applies):
         flipped = step % 2 == 0
         factor, gram, after = (lower, lower_gram, upper) if flipped else (upper, upper_gram, lower)
-        found = siblings_of(packed)
-        own = jnp.concatenate(found, 0)
-        other = over_rank(own)
-        joined = pltpu.VMEM((c, wide), BF)
+        found, source = siblings_of(packed, summed, source)
+        holders = [f[2] for f in found]
+        pieces = [x for f in found for x in f[:2]]
         if step + 1 == applies:
-            (out,) = call(last_kernel, [S((half, c), BF)], (place, own, other, factor, y), field_flops // 2, [joined])
+            (out,) = call(
+                lambda *r: last_kernel(holders, *r), [S((half, c), BF)], (place, *pieces, factor, y), field_flops // 2, [joined]
+            )
             return out
-        packed, q = call(
-            next_kernel,
-            [S((LEVELS * c, k), BF), s_shape],
-            (place, own, other, gram, s, over_rank(s)),
-            wide * wide * c,
+        there = over_rank(s)
+        early = [f[0] if f[2] == source else f[1] for f in found]
+        (packed,) = call(next_kernel, [p_shape], (place, *early, gram, s, there), 2 * wide * wide * c)
+        summed, q = call(
+            lambda *r: again_kernel(holders, *r), [p_shape, s_shape], (place, *pieces, gram, s, there), 2 * wide * wide * c
         )
         if step + 2 == applies:
             (y,) = call(lambda *r: late_kernel(not flipped, *r), [y_shape], (place, q, factor, y, leaves), field_flops // 2)
         else:
             y, s = call(
-                lambda *r: field_kernel(not flipped, *r), [y_shape, s_shape], (place, q, factor, y, leaves, after), field_flops
+                lambda *r: field_kernel(not flipped, *r),
+                [y_shape, s_shape],
+                (place, q, factor, y, leaves, after),
+                field_flops,
             )
 
 

time: 75.1 us -> 77.6 us (1.033)
  starting transfers between devices: 29.5 us -> 16.2 us
  local copies, waits for them, and re-layouts: 2.65 us -> 11.6 us
  other arithmetic: 0.87 us -> 9.63 us
  waiting for transfers between devices: 31.1 us -> 24.3 us
  Pallas kernels: 10.4 us -> 14.7 us
    ppermute x12, starting transfers between devices: 27 us -> 8.15 us  [one_way(): return lax.ppermute(value, ('rows', 'cols', 'rank'), away + home)]
    unnamed x16 -> x52, local copies, waits for them, and re-layouts: 0.38 us -> 8.92 us
    convert_element_type x10, other arithmetic: 0.73 us -> 7.31 us  [add(): return (a.astype(F32) + b.astype(F32)).astype(BF)]
    ppermute x12, waiting for transfers between devices: 25.8 us -> 20 us  [one_way(): return lax.ppermute(value, ('rows', 'cols', 'rank'), away + home)]
    ppermute x11 -> x20, starting transfers between devices: 2.52 us -> 8.07 us  [over_rank(): return lax.ppermute(value, 'rank', [(0, 1), (1, 0)])]
    pallas_call x11 -> x15, Pallas kernels: 10.4 us -> 14.7 us  [call(): pl.pallas_call(kernel, out_shape=outs, in_specs=[pl.BlockSpec(memory_spac...]
    slice x8 -> x12, local copies, waits for them, and re-layouts: 0.03 us -> 2.6 us  [the longest x4 1.7 us: siblings_of(): received[(count - 1) * c:]]
    dynamic_slice x4, local copies, waits for them, and re-layouts: 2.24 us -> 0.11 us  [swapped(): lax.dynamic_slice_in_dim(f, (1 - rank) * half, half, 0)]
  transfers between devices with their start and end apart: 23 -> 32, of which waited for: 20 -> 14; matrix products, arithmetic and copies ran while one was open for 1% -> 16% of each run, Pallas kernels for 9% -> 16%
where the time goes in v3:
time: 77.6 us; the launch traced here: 76.8 us
  waiting for transfers between devices  24.3 us (31%)
  starting transfers between devices  16.2 us (21%)
  Pallas kernels  14.7 us (19%)
  local copies, waits for them, and re-layouts  11.6 us (15%)
  other arithmetic  9.63 us (12%)
    ppermute x12, waiting for transfers between devices, one_way(): return lax.ppermute(value, ('rows', 'cols', 'rank'), away + home)  20 us
    pallas_call x15, Pallas kernels, call(): pl.pallas_call(kernel, out_shape=outs, in_specs=[pl.BlockSpec(memory_spac...  14.7 us
    unnamed x52, local copies, waits for them, and re-layouts  8.92 us
    ppermute x12, starting transfers between devices, one_way(): return lax.ppermute(value, ('rows', 'cols', 'rank'), away + home)  8.15 us
    ppermute x20, starting transfers between devices, over_rank(): return lax.ppermute(value, 'rank', [(0, 1), (1, 0)])  8.07 us
    convert_element_type x10, other arithmetic, add(): return (a.astype(F32) + b.astype(F32)).astype(BF)  7.31 us
    ppermute x20, waiting for transfers between devices, over_rank(): return lax.ppermute(value, 'rank', [(0, 1), (1, 0)])  4.31 us
    slice x4, local copies, waits for them, and re-layouts, siblings_of(): received[(count - 1) * c:]  1.7 us
  transfers between devices with their start and end apart: 32, of which 14 were waited for; matrix products, arithmetic and copies ran while one was open for 16% of the time, Pallas kernels for 16%

profile of v3, /device:TPU:0, one launch (start us, length us, event | category | flops | bytes accessed | tf_op | source)
XLA Modules:
  0.0 76.8 jit_solution(11357991716979151185)
XLA Ops:
  0.0 1.0 %copy-done.4 = bf16[2048,128]{1,0:T(8,128)(2,1)S(1)} copy-done((bf16[2048,128]{1,0:T(8,128)(2,1)S(1)}, bf16[2048,128]{1,0:T(8,128)(2,1)}, u32[]{:S(2)}) %copy-start.4) | copy-done | bytes 524312
  1.0 1.0 %copy-done.6 = bf16[2048,128]{1,0:T(8,128)(2,1)S(1)} copy-done((bf16[2048,128]{1,0:T(8,128)(2,1)S(1)}, bf16[2048,128]{1,0:T(8,128)(2,1)}, u32[]{:S(2)}) %copy-start.6) | copy-done | bytes 524312
  2.1 1.0 %copy-done.8 = bf16[2048,128]{1,0:T(8,128)(2,1)S(1)} copy-done((bf16[2048,128]{1,0:T(8,128)(2,1)S(1)}, bf16[2048,128]{1,0:T(8,128)(2,1)}, u32[]{:S(2)}) %copy-start.8) | copy-done | bytes 524312
  3.1 1.0 %copy-done.11 = bf16[2048,128]{1,0:T(8,128)(2,1)S(1)} copy-done((bf16[2048,128]{1,0:T(8,128)(2,1)S(1)}, bf16[2048,128]{1,0:T(8,128)(2,1)}, u32[]{:S(2)}) %copy-start.11) | copy-done | bytes 524312
  4.2 0.6 shard_map.82.own
  5.7 0.6 collective-permute-start.7
  6.7 1.6 %collective-permute-done.other = bf16[384,128]{1,0:T(8,128)(2,1)S(1)} collective-permute-done((bf16[384,128]{1,0:T(8,128)(2,1)S(1)}, bf16[384,128]{1,0:T(8,128)(2,1)S(1)}, u32[]{:S(2)}, u32[]{:S(2)}) %collective-permute-start) | collective-permute-done | bytes 98336 | tf_op jit(solution)/shard_map/ppermute | solution.py:145
  8.3 2.6 %collective-permute-start.1 = (bf16[384,256]{1,0:T(8,128)(2,1)S(1)}, bf16[384,256]{1,0:T(8,128)(2,1)S(1)}, u32[]{:S(2)}, u32[]{:S(2)}) collective-permute-start(bf16[384,256]{1,0:T(8,128)(2,1)S(1)} %shard_map.83), channel_id=1, source_target_pairs={{0,3},{2,1},{4,7},{6,5},{8,11},{10,9},{12,15},{14,13},{1,0},{3,2},... | collective-permute-start | bytes 589832 | tf_op jit(solution)/shard_map/ppermute | solution.py:141
  11.0 2.4 %shard_map.84 = (bf16[1024,768]{1,0:T(8,128)(2,1)S(1)}, bf16[768,768]{1,0:T(8,128)(2,1)}) custom-call(s32[1]{0:T(128)} %bitcast.place.r_0_, bf16[2048,128]{1,0:T(8,128)(2,1)S(1)} %copy-done.17, bf16[2048,128]{1,0:T(8,128)(2,1)S(1)} %copy-done.19, bf16[2048,128]{1,0:T(8,128)(2,1)S(1)} %copy-done.21, bf16[3072,128]{1,0:T(8,128)(2,1)S(1)} %collective-permute-done.7.refs_3_), custom_call_target="tpu_custom_call" | custom-call | flops 905969664 | bytes 5111808 | tf_op jit(solution)/shard_map/pallas_call | solution.py:22
  13.4 0.9 %pad_maximum_fusion.1 = bf16[3072,128]{1,0:T(8,128)(2,1)} fusion(bf16[1024,128]{1,0:T(8,128)(2,1)S(1)} %get-tuple-element.59, bf16[1024,128]{1,0:T(8,128)(2,1)S(1)} %get-tuple-element.60, bf16[1024,128]{1,0:T(8,128)(2,1)S(1)} %constant_dynamic-slice_fusion.2), kind=kLoop, calls=%fused_computation.3 | loop fusion | flops 2359296 | bytes 1572864 | tf_op jit(solution)/shard_map/concatenate | solution.py:191
  14.8 0.7 add_convert_fusion.5
  15.6 0.7 pad_maximum_fusion.2
  16.2 1.7 %collective-permute-start.2 = (bf16[256,256]{1,0:T(8,128)(2,1)}, bf16[256,256]{1,0:T(8,128)(2,1)S(1)}, u32[]{:S(2)}, u32[]{:S(2)}) collective-permute-start(bf16[256,256]{1,0:T(8,128)(2,1)} %pad_maximum_fusion.2), channel_id=1, source_target_pairs={{0,1},{1,0},{2,3},{3,2},{4,5},{5,4},{6,7},{7,6},{8,9},{9,8},{10,11... | collective-permute-start | bytes 393224 | tf_op jit(solution)/shard_map/ppermute | solution.py:145
  17.9 2.3 %collective-permute-done.3 = bf16[256,256]{1,0:T(8,128)(2,1)} collective-permute-done((bf16[256,256]{1,0:T(8,128)(2,1)}, bf16[256,256]{1,0:T(8,128)(2,1)}, u32[]{:S(2)}, u32[]{:S(2)}) %collective-permute-start.3) | collective-permute-done | bytes 131104 | tf_op jit(solution)/shard_map/ppermute | solution.py:141
  20.2 1.0 %add_convert_fusion.12 = bf16[128,256]{1,0:T(8,128)(2,1)S(1)} fusion(bf16[256,256]{1,0:T(8,128)(2,1)} %collective-permute-done.3, bf16[256,256]{1,0:T(8,128)(2,1)S(1)} %collective-permute-done.2, bf16[384,256]{1,0:T(8,128)(2,1)S(1)} %shard_map.83, pred[]{:T(512)S(6)} %eq.8, bf16[384,256]{1,0:T(8,128)(2,1)} %copy-done.23), kind=kLoop, calls=%fused_computation.18 | loop fusion | flops 294912 | bytes 327681 | tf_op jit(solution)/shard_map/convert_element_type | solution.py:149
  21.2 1.5 %collective-permute-start.4 = (bf16[128,256]{1,0:T(8,128)(2,1)S(1)}, bf16[128,256]{1,0:T(8,128)(2,1)S(1)}, u32[]{:S(2)}, u32[]{:S(2)}) collective-permute-start(bf16[128,256]{1,0:T(8,128)(2,1)S(1)} %add_convert_fusion.12), channel_id=1, source_target_pairs={{0,9},{2,11},{4,13},{6,15},{8,1},{10,3},{12,5},{14,7},{1,0},{3,2},... | collective-permute-start | bytes 196616 | tf_op jit(solution)/shard_map/ppermute | solution.py:141
  22.7 0.8 %slice.163.r_3_ = bf16[128,256]{1,0:T(8,128)(2,1)S(1)} slice(bf16[256,256]{1,0:T(8,128)(2,1)} %collective-permute-done.3), slice={[128:256], [0:256]} | slice | bytes 131072 | tf_op jit(solution)/shard_map/slice | solution.py:167
  23.6 0.7 shard_map.85
  24.3 0.6 collective-permute-start.9
  24.9 3.6 %shard_map.88 = (bf16[1024,768]{1,0:T(8,128)(2,1)S(1)}, bf16[768,768]{1,0:T(8,128)(2,1)}) custom-call(s32[1]{0:T(128)} %bitcast.place.r_0_, bf16[2048,128]{1,0:T(8,128)(2,1)S(1)} %copy-done.7, bf16[2048,128]{1,0:T(8,128)(2,1)S(1)} %copy-done.10, bf16[2048,128]{1,0:T(8,128)(2,1)S(1)} %copy-done.13, bf16[3072,128]{1,0:T(8,128)(2,1)} %collective-permute-done.16.refs_3_), custom_call_target="tpu_custom_call" | custom-call | flops 905969664 | bytes 5111808 | tf_op jit(solution)/shard_map/pallas_call | solution.py:22
  28.5 1.2 %copy-done = bf16[1024,768]{1,0:T(8,128)(2,1)} copy-done((bf16[1024,768]{1,0:T(8,128)(2,1)}, bf16[1024,768]{1,0:T(8,128)(2,1)S(1)}, u32[]{:S(2)}) %copy-start) | copy-done | bytes 1572888
  29.8 1.9 %add_convert_fusion.1.r_7_.refs_3_ = bf16[768,768]{1,0:T(8,128)(2,1)S(1)} fusion(bf16[768,768]{1,0:T(8,128)(2,1)} %collective-permute-done.8, bf16[768,768]{1,0:T(8,128)(2,1)} %get-tuple-element.32), kind=kLoop, calls=%fused_computation.1 | loop fusion | flops 2359296 | bytes 3538944 | tf_op jit(solution)/shard_map/convert_element_type | solution.py:149
  32.8 1.0 %collective-permute-done.5.r_2_ = bf16[128,256]{1,0:T(8,128)(2,1)S(1)} collective-permute-done((bf16[128,256]{1,0:T(8,128)(2,1)S(1)}, bf16[128,256]{1,0:T(8,128)(2,1)S(1)}, u32[]{:S(2)}, u32[]{:S(2)}) %collective-permute-start.5) | collective-permute-done | bytes 65568 | tf_op jit(solution)/shard_map/ppermute | solution.py:145
  34.1 3.1 %collective-permute-done.10 = bf16[384,256]{1,0:T(8,128)(2,1)S(1)} collective-permute-done((bf16[384,256]{1,0:T(8,128)(2,1)S(1)}, bf16[384,256]{1,0:T(8,128)(2,1)S(1)}, u32[]{:S(2)}, u32[]{:S(2)}) %collective-permute-start.10) | collective-permute-done | bytes 196640 | tf_op jit(solution)/shard_map/ppermute | solution.py:141
  37.2 0.7 add_convert_fusion.4
  38.0 0.6 pad_maximum_fusion.3
  39.1 1.4 %copy-done.1 = bf16[1024,768]{1,0:T(8,128)(2,1)S(1)} copy-done((bf16[1024,768]{1,0:T(8,128)(2,1)S(1)}, bf16[1024,768]{1,0:T(8,128)(2,1)}, u32[]{:S(2)}) %copy-start.1) | copy-done | bytes 1572888
  40.5 1.0 %copy-done.15 = f32[1024,128]{1,0:T(8,128)S(1)} copy-done((f32[1024,128]{1,0:T(8,128)S(1)}, f32[1024,128]{1,0:T(8,128)}, u32[]{:S(2)}) %copy-start.15) | copy-done | bytes 524312
  41.6 1.5 %shard_map.89 = (f32[1024,128]{1,0:T(8,128)S(1)}, bf16[128,768]{1,0:T(8,128)(2,1)S(1)}) custom-call(s32[1]{0:T(128)} %bitcast.place.r_0_, bf16[128,768]{1,0:T(8,128)(2,1)S(1)} %get-tuple-element.40.r_1_, bf16[1024,768]{1,0:T(8,128)(2,1)S(1)} %get-tuple-element.33.after.r_2_.r_5_, f32[1024,128]{1,0:T(8,128)S(1)} %copy-done.15, ...), custom_call_target="tpu_custom_call" | custom-call | flops 402653184 | bytes 5111808 | tf_op jit(solution)/shard_map/pallas_call | solution.py:22
  43.2 1.0 %add_convert_fusion.10 = bf16[128,256]{1,0:T(8,128)(2,1)S(1)} fusion(bf16[256,256]{1,0:T(8,128)(2,1)} %collective-permute-done.12, bf16[256,256]{1,0:T(8,128)(2,1)} %collective-permute-done.11, bf16[384,256]{1,0:T(8,128)(2,1)} %copy-done.16, pred[]{:T(512)S(6)} %eq.9, bf16[384,256]{1,0:T(8,128)(2,1)} %copy-done.22), kind=kLoop, calls=%fused_computation.16 | loop fusion | flops 294912 | bytes 327681 | tf_op jit(solution)/shard_map/convert_element_type | solution.py:149
  44.7 0.8 %slice.170.r_3_ = bf16[128,256]{1,0:T(8,128)(2,1)S(1)} slice(bf16[256,256]{1,0:T(8,128)(2,1)} %collective-permute-done.12), slice={[128:256], [0:256]} | slice | bytes 131072 | tf_op jit(solution)/shard_map/slice | solution.py:167
  45.6 1.2 %collective-permute-start.15 = (bf16[128,256]{1,0:T(8,128)(2,1)S(1)}, bf16[128,256]{1,0:T(8,128)(2,1)S(1)}, u32[]{:S(2)}, u32[]{:S(2)}) collective-permute-start(bf16[128,256]{1,0:T(8,128)(2,1)S(1)} %slice.170.r_3_), channel_id=1, source_target_pairs={{0,1},{1,0},{2,3},{3,2},{4,5},{5,4},{6,7},{7,6},{8,9},{9,8},{10,11... | collective-permute-start | bytes 196616 | tf_op jit(solution)/shard_map/ppermute | solution.py:145
  46.7 1.9 %add_convert_fusion.r_7_.refs_3_ = bf16[768,768]{1,0:T(8,128)(2,1)S(1)} fusion(bf16[768,768]{1,0:T(8,128)(2,1)} %collective-permute-done.17, bf16[768,768]{1,0:T(8,128)(2,1)} %get-tuple-element.39), kind=kLoop, calls=%fused_computation | loop fusion | flops 2359296 | bytes 3538944 | tf_op jit(solution)/shard_map/convert_element_type | solution.py:149
  48.7 0.9 %collective-permute-done.13.r_1_.refs_0_ = bf16[128,256]{1,0:T(8,128)(2,1)S(1)} collective-permute-done((bf16[128,256]{1,0:T(8,128)(2,1)S(1)}, bf16[128,256]{1,0:T(8,128)(2,1)S(1)}, u32[]{:S(2)}, u32[]{:S(2)}) %collective-permute-start.13) | collective-permute-done | bytes 65568 | tf_op jit(solution)/shard_map/ppermute | solution.py:141
  50.4 0.8 %slice.171.r_6_ = bf16[128,256]{1,0:T(8,128)(2,1)S(1)} slice(bf16[256,256]{1,0:T(8,128)(2,1)} %collective-permute-done.11), slice={[128:256], [0:256]} | slice | bytes 131072 | tf_op jit(solution)/shard_map/slice | solution.py:167
  51.8 1.3 %collective-permute-done.19 = bf16[384,256]{1,0:T(8,128)(2,1)S(1)} collective-permute-done((bf16[384,256]{1,0:T(8,128)(2,1)S(1)}, bf16[384,256]{1,0:T(8,128)(2,1)S(1)}, u32[]{:S(2)}, u32[]{:S(2)}) %collective-permute-start.19) | collective-permute-done | bytes 196640 | tf_op jit(solution)/shard_map/ppermute | solution.py:141
  53.2 1.1 %collective-permute-start.21 = (bf16[256,256]{1,0:T(8,128)(2,1)S(1)}, bf16[256,256]{1,0:T(8,128)(2,1)S(1)}, u32[]{:S(2)}, u32[]{:S(2)}) collective-permute-start(bf16[256,256]{1,0:T(8,128)(2,1)S(1)} %add_convert_fusion.3), channel_id=1, source_target_pairs={{1,4},{3,6},{5,0},{7,2},{9,12},{11,14},{13,8},{15,10},{0,1},{2,3},... | collective-permute-start | bytes 393224 | tf_op jit(solution)/shard_map/ppermute | solution.py:141
  54.4 1.5 %shard_map.92 = (f32[1024,128]{1,0:T(8,128)S(1)}, bf16[128,768]{1,0:T(8,128)(2,1)S(1)}) custom-call(s32[1]{0:T(128)} %bitcast.place.r_0_, bf16[128,768]{1,0:T(8,128)(2,1)S(1)} %get-tuple-element.45.r_1_, bf16[1024,768]{1,0:T(8,128)(2,1)S(1)} %copy-done.2, f32[1024,128]{1,0:T(8,128)S(1)} %get-tuple-element.46.r_3_, bf16[4,256,256]{2,1,0:T(8,128)(2,1)S(1)} %copy-done.3, ...), custom_call_target="tpu_custom_call" | custom-call | flops 402653184 | bytes 5111808 | tf_op jit(solution)/shard_map/pallas_call | solution.py:22
  56.5 1.6 %collective-permute-done.21 = bf16[256,256]{1,0:T(8,128)(2,1)S(1)} collective-permute-done((bf16[256,256]{1,0:T(8,128)(2,1)S(1)}, bf16[256,256]{1,0:T(8,128)(2,1)S(1)}, u32[]{:S(2)}, u32[]{:S(2)}) %collective-permute-start.21) | collective-permute-done | bytes 131104 | tf_op jit(solution)/shard_map/ppermute | solution.py:141
  58.7 1.4 %collective-permute-done.22.r_1_.refs_0_ = bf16[128,256]{1,0:T(8,128)(2,1)S(1)} collective-permute-done((bf16[128,256]{1,0:T(8,128)(2,1)S(1)}, bf16[128,256]{1,0:T(8,128)(2,1)S(1)}, u32[]{:S(2)}, u32[]{:S(2)}) %collective-permute-start.22) | collective-permute-done | bytes 65568 | tf_op jit(solution)/shard_map/ppermute | solution.py:141
  60.5 1.4 %collective-permute-start.26 = (bf16[384,256]{1,0:T(8,128)(2,1)S(1)}, bf16[384,256]{1,0:T(8,128)(2,1)S(1)}, u32[]{:S(2)}, u32[]{:S(2)}) collective-permute-start(bf16[384,256]{1,0:T(8,128)(2,1)S(1)} %shard_map.94), channel_id=1, source_target_pairs={{1,2},{3,0},{5,6},{7,4},{9,10},{11,8},{13,14},{15,12},{0,1},{2,3},... | collective-permute-start | bytes 589832 | tf_op jit(solution)/shard_map/ppermute | solution.py:141
  62.0 1.2 %collective-permute-done.23.r_2_ = bf16[128,256]{1,0:T(8,128)(2,1)S(1)} collective-permute-done((bf16[128,256]{1,0:T(8,128)(2,1)S(1)}, bf16[128,256]{1,0:T(8,128)(2,1)S(1)}, u32[]{:S(2)}, u32[]{:S(2)}) %collective-permute-start.23) | collective-permute-done | bytes 65568 | tf_op jit(solution)/shard_map/ppermute | solution.py:145
  63.6 3.3 %collective-permute-done.26 = bf16[384,256]{1,0:T(8,128)(2,1)S(1)} collective-permute-done((bf16[384,256]{1,0:T(8,128)(2,1)S(1)}, bf16[384,256]{1,0:T(8,128)(2,1)S(1)}, u32[]{:S(2)}, u32[]{:S(2)}) %collective-permute-start.26) | collective-permute-done | bytes 196640 | tf_op jit(solution)/shard_map/ppermute | solution.py:141
  67.1 0.6 collective-permute-start.27
  67.6 1.9 %collective-permute-done.28 = bf16[256,256]{1,0:T(8,128)(2,1)S(1)} collective-permute-done((bf16[256,256]{1,0:T(8,128)(2,1)S(1)}, bf16[256,256]{1,0:T(8,128)(2,1)S(1)}, u32[]{:S(2)}, u32[]{:S(2)}) %collective-permute-start.28) | collective-permute-done | bytes 131104 | tf_op jit(solution)/shard_map/ppermute | solution.py:141
  70.1 4.1 %collective-permute-done.29.r_1_ = bf16[128,256]{1,0:T(8,128)(2,1)S(1)} collective-permute-done((bf16[128,256]{1,0:T(8,128)(2,1)S(1)}, bf16[128,256]{1,0:T(8,128)(2,1)S(1)}, u32[]{:S(2)}, u32[]{:S(2)}) %collective-permute-start.29) | collective-permute-done | bytes 65568 | tf_op jit(solution)/shard_map/ppermute | solution.py:141
  74.3 0.9 %shard_map.95.r_8_ = f32[1024,128]{1,0:T(8,128)S(1)} custom-call(s32[1]{0:T(128)} %bitcast.place.r_0_, bf16[128,768]{1,0:T(8,128)(2,1)S(1)} %get-tuple-element.49.r_1_, bf16[1024,768]{1,0:T(8,128)(2,1)S(1)} %get-tuple-element.33.after.r_2_.r_5_, f32[1024,128]{1,0:T(8,128)S(1)} %get-tuple-element.50.r_3_, bf16[4,256,256]{2,1,0:T(8,128)(2,1)S(1)} %copy-done.3), custom_call_target="tpu_custom_call" | custom-call | flops 201326592 | bytes 3342336 | tf_op jit(solution)/shard_map/pallas_call | solution.py:22
  75.5 1.3 %shard_map.96 = bf16[1024,128]{1,0:T(8,128)(2,1)} custom-call(s32[1]{0:T(128)} %bitcast.place.r_0_, bf16[128,256]{1,0:T(8,128)(2,1)S(1)} %collective-permute-done.29.r_1_, bf16[128,256]{1,0:T(8,128)(2,1)S(1)} %collective-permute-done.30.r_2_, bf16[128,256]{1,0:T(8,128)(2,1)S(1)} %slice.184.r_3_, bf16[128,256]{1,0:T(8,128)(2,1)S(1)} %collective-permute-done.31.r_4_, ...), custom_call_target="tpu_custom_call" | custom-call | flops 201326592 | bytes 2752512 | tf_op jit(solution)/shard_map/pallas_call | solution.py:22
  (115 shorter events, 9.1 us)
Async XLA Ops:
  4.2 1.2 %copy-start.18 = (bf16[2048,128]{1,0:T(8,128)(2,1)S(1)}, bf16[2048,128]{1,0:T(8,128)(2,1)}, u32[]{:S(2)}) copy-start(bf16[2048,128]{1,0:T(8,128)(2,1)} %refs_1_.2) | copy-start | bytes 1572868
  4.2 1.4 %copy-start.20 = (bf16[2048,128]{1,0:T(8,128)(2,1)S(1)}, bf16[2048,128]{1,0:T(8,128)(2,1)}, u32[]{:S(2)}) copy-start(bf16[2048,128]{1,0:T(8,128)(2,1)} %refs_2_.2) | copy-start | bytes 1572868
  5.2 1.1 %copy-start.9 = (bf16[2048,128]{1,0:T(8,128)(2,1)S(1)}, bf16[2048,128]{1,0:T(8,128)(2,1)}, u32[]{:S(2)}) copy-start(bf16[2048,128]{1,0:T(8,128)(2,1)} %refs_1_.3) | copy-start | bytes 1572868
  5.2 1.3 %copy-start.12 = (bf16[2048,128]{1,0:T(8,128)(2,1)S(1)}, bf16[2048,128]{1,0:T(8,128)(2,1)}, u32[]{:S(2)}) copy-start(bf16[2048,128]{1,0:T(8,128)(2,1)} %refs_2_.3) | copy-start | bytes 1572868
  5.6 5.4 %copy-start.19 = (bf16[2048,128]{1,0:T(8,128)(2,1)S(1)}, bf16[2048,128]{1,0:T(8,128)(2,1)}, u32[]{:S(2)}) copy-start(bf16[2048,128]{1,0:T(8,128)(2,1)} %refs_1_.2) | copy-start | bytes 1572868
  5.6 5.4 %copy-start.21 = (bf16[2048,128]{1,0:T(8,128)(2,1)S(1)}, bf16[2048,128]{1,0:T(8,128)(2,1)}, u32[]{:S(2)}) copy-start(bf16[2048,128]{1,0:T(8,128)(2,1)} %refs_2_.2) | copy-start | bytes 1572868
  5.7 5.3 %collective-permute-start.7 = (bf16[3072,128]{1,0:T(8,128)(2,1)S(1)}, bf16[3072,128]{1,0:T(8,128)(2,1)S(1)}, u32[]{:S(2)}, u32[]{:S(2)}) collective-permute-start(bf16[3072,128]{1,0:T(8,128)(2,1)S(1)} %pad_maximum_fusion), channel_id=1, source_target_pairs={{0,1},{1,0},{2,3},{3,2},{4,5},{5,4},{6,7},{7,6},{8,9},{9,8},{10,11... | collective-permute-start | bytes 2359304 | tf_op jit(solution)/shard_map/ppermute | solution.py:145
  6.2 2.1 %collective-permute-start = (bf16[384,128]{1,0:T(8,128)(2,1)S(1)}, bf16[384,128]{1,0:T(8,128)(2,1)S(1)}, u32[]{:S(2)}, u32[]{:S(2)}) collective-permute-start(bf16[384,128]{1,0:T(8,128)(2,1)S(1)} %shard_map.82.own), channel_id=1, source_target_pairs={{0,1},{1,0},{2,3},{3,2},{4,5},{5,4},{6,7},{7,6},{8,9},{9,8},{10,11... | collective-permute-start | bytes 294920 | tf_op jit(solution)/shard_map/ppermute | solution.py:145
  8.3 6.5 %collective-permute-start.1 = (bf16[384,256]{1,0:T(8,128)(2,1)S(1)}, bf16[384,256]{1,0:T(8,128)(2,1)S(1)}, u32[]{:S(2)}, u32[]{:S(2)}) collective-permute-start(bf16[384,256]{1,0:T(8,128)(2,1)S(1)} %shard_map.83), channel_id=1, source_target_pairs={{0,3},{2,1},{4,7},{6,5},{8,11},{10,9},{12,15},{14,13},{1,0},{3,2},... | collective-permute-start | bytes 589832 | tf_op jit(solution)/shard_map/ppermute | solution.py:141
  13.4 10.2 %copy-start.3 = (bf16[4,256,256]{2,1,0:T(8,128)(2,1)S(1)}, bf16[4,256,256]{2,1,0:T(8,128)(2,1)}, u32[]{:S(2)}) copy-start(bf16[4,256,256]{2,1,0:T(8,128)(2,1)} %r_4_.5) | copy-start | bytes 1572868
  13.4 10.2 %copy-start.5 = (bf16[2048,128]{1,0:T(8,128)(2,1)S(1)}, bf16[2048,128]{1,0:T(8,128)(2,1)}, u32[]{:S(2)}) copy-start(bf16[2048,128]{1,0:T(8,128)(2,1)} %z.3) | copy-start | bytes 1572868
  13.4 16.4 %collective-permute-start.8 = (bf16[768,768]{1,0:T(8,128)(2,1)}, bf16[768,768]{1,0:T(8,128)(2,1)}, u32[]{:S(2)}, u32[]{:S(2)}) collective-permute-start(bf16[768,768]{1,0:T(8,128)(2,1)} %get-tuple-element.32), channel_id=1, source_target_pairs={{0,1},{1,0},{2,3},{3,2},{4,5},{5,4},{6,7},{7,6},{8,9},{9,8},{10,11... | collective-permute-start | bytes 3538952 | tf_op jit(solution)/shard_map/ppermute | solution.py:145
  14.3 10.6 %collective-permute-start.16 = (bf16[3072,128]{1,0:T(8,128)(2,1)}, bf16[3072,128]{1,0:T(8,128)(2,1)}, u32[]{:S(2)}, u32[]{:S(2)}) collective-permute-start(bf16[3072,128]{1,0:T(8,128)(2,1)} %pad_maximum_fusion.1), channel_id=1, source_target_pairs={{0,1},{1,0},{2,3},{3,2},{4,5},{5,4},{6,7},{7,6},{8,9},{9,8},{10,11... | collective-permute-start | bytes 2359304 | tf_op jit(solution)/shard_map/ppermute | solution.py:145
  15.5 4.7 %collective-permute-start.3 = (bf16[256,256]{1,0:T(8,128)(2,1)}, bf16[256,256]{1,0:T(8,128)(2,1)}, u32[]{:S(2)}, u32[]{:S(2)}) collective-permute-start(bf16[256,256]{1,0:T(8,128)(2,1)} %add_convert_fusion.5), channel_id=1, source_target_pairs={{1,4},{3,6},{5,0},{7,2},{9,12},{11,14},{13,8},{15,10},{0,1},{2,3},... | collective-permute-start | bytes 393224 | tf_op jit(solution)/shard_map/ppermute | solution.py:141
  16.2 4.0 %collective-permute-start.2 = (bf16[256,256]{1,0:T(8,128)(2,1)}, bf16[256,256]{1,0:T(8,128)(2,1)S(1)}, u32[]{:S(2)}, u32[]{:S(2)}) collective-permute-start(bf16[256,256]{1,0:T(8,128)(2,1)} %pad_maximum_fusion.2), channel_id=1, source_target_pairs={{0,1},{1,0},{2,3},{3,2},{4,5},{5,4},{6,7},{7,6},{8,9},{9,8},{10,11... | collective-permute-start | bytes 393224 | tf_op jit(solution)/shard_map/ppermute | solution.py:145
  17.9 7.0 %copy-start.10 = (bf16[2048,128]{1,0:T(8,128)(2,1)S(1)}, bf16[2048,128]{1,0:T(8,128)(2,1)}, u32[]{:S(2)}) copy-start(bf16[2048,128]{1,0:T(8,128)(2,1)} %refs_1_.3) | copy-start | bytes 1572868
  17.9 7.0 %copy-start.13 = (bf16[2048,128]{1,0:T(8,128)(2,1)S(1)}, bf16[2048,128]{1,0:T(8,128)(2,1)}, u32[]{:S(2)}) copy-start(bf16[2048,128]{1,0:T(8,128)(2,1)} %refs_2_.3) | copy-start | bytes 1572868
  20.2 3.3 %copy-start.24 = (bf16[256,256]{1,0:T(8,128)(2,1)}, bf16[256,256]{1,0:T(8,128)(2,1)S(1)}, u32[]{:S(2)}) copy-start(bf16[256,256]{1,0:T(8,128)(2,1)S(1)} %collective-permute-done.2) | copy-start | bytes 393220
  21.2 10.5 %collective-permute-start.4 = (bf16[128,256]{1,0:T(8,128)(2,1)S(1)}, bf16[128,256]{1,0:T(8,128)(2,1)S(1)}, u32[]{:S(2)}, u32[]{:S(2)}) collective-permute-start(bf16[128,256]{1,0:T(8,128)(2,1)S(1)} %add_convert_fusion.12), channel_id=1, source_target_pairs={{0,9},{2,11},{4,13},{6,15},{8,1},{10,3},{12,5},{14,7},{1,0},{3,2},... | collective-permute-start | bytes 196616 | tf_op jit(solution)/shard_map/ppermute | solution.py:141
  23.5 8.2 %collective-permute-start.6 = (bf16[128,256]{1,0:T(8,128)(2,1)S(1)}, bf16[128,256]{1,0:T(8,128)(2,1)S(1)}, u32[]{:S(2)}, u32[]{:S(2)}) collective-permute-start(bf16[128,256]{1,0:T(8,128)(2,1)S(1)} %slice.163.r_3_), channel_id=1, source_target_pairs={{0,1},{1,0},{2,3},{3,2},{4,5},{5,4},{6,7},{7,6},{8,9},{9,8},{10,11... | collective-permute-start | bytes 196616 | tf_op jit(solution)/shard_map/ppermute | solution.py:145
  24.3 4.1 %copy-start.14 = (f32[1024,128]{1,0:T(8,128)}, f32[1024,128]{1,0:T(8,128)S(1)}, u32[]{:S(2)}) copy-start(f32[1024,128]{1,0:T(8,128)S(1)} %get-tuple-element.41.r_3_) | copy-start | bytes 1572868
  24.3 7.4 %collective-permute-start.9 = (bf16[128,768]{1,0:T(8,128)(2,1)S(1)}, bf16[128,768]{1,0:T(8,128)(2,1)S(1)}, u32[]{:S(2)}, u32[]{:S(2)}) collective-permute-start(bf16[128,768]{1,0:T(8,128)(2,1)S(1)} %get-tuple-element.34.r_8_.refs_4_), channel_id=1, source_target_pairs={{0,1},{1,0},{2,3},{3,2},{4,5},{5,4},{6,7},{7,6},{8,9},{9,8},{10,11... | collective-permute-start | bytes 589832 | tf_op jit(solution)/shard_map/ppermute | solution.py:145
  28.5 1.2 %copy-start = (bf16[1024,768]{1,0:T(8,128)(2,1)}, bf16[1024,768]{1,0:T(8,128)(2,1)S(1)}, u32[]{:S(2)}) copy-start(bf16[1024,768]{1,0:T(8,128)(2,1)S(1)} %get-tuple-element.42.r_5_.r_2_.r_7_) | copy-start | bytes 4718596
  29.7 17.1 %collective-permute-start.17 = (bf16[768,768]{1,0:T(8,128)(2,1)}, bf16[768,768]{1,0:T(8,128)(2,1)}, u32[]{:S(2)}, u32[]{:S(2)}) collective-permute-start(bf16[768,768]{1,0:T(8,128)(2,1)} %get-tuple-element.39), channel_id=1, source_target_pairs={{0,1},{1,0},{2,3},{3,2},{4,5},{5,4},{6,7},{7,6},{8,9},{9,8},{10,11... | collective-permute-start | bytes 3538952 | tf_op jit(solution)/shard_map/ppermute | solution.py:145
  32.1 5.1 %collective-permute-start.10 = (bf16[384,256]{1,0:T(8,128)(2,1)S(1)}, bf16[384,256]{1,0:T(8,128)(2,1)S(1)}, u32[]{:S(2)}, u32[]{:S(2)}) collective-permute-start(bf16[384,256]{1,0:T(8,128)(2,1)S(1)} %shard_map.87), channel_id=1, source_target_pairs={{1,2},{3,0},{5,6},{7,4},{9,10},{11,8},{13,14},{15,12},{0,1},{2,3},... | collective-permute-start | bytes 589832 | tf_op jit(solution)/shard_map/ppermute | solution.py:141
  32.5 1.3 %collective-permute-start.5 = (bf16[128,256]{1,0:T(8,128)(2,1)S(1)}, bf16[128,256]{1,0:T(8,128)(2,1)S(1)}, u32[]{:S(2)}, u32[]{:S(2)}) collective-permute-start(bf16[128,256]{1,0:T(8,128)(2,1)S(1)} %collective-permute-done.4.r_1_.refs_0_), channel_id=1, source_target_pairs={{0,1},{1,0},{2,3},{3,2},{4,5},{5,4},{6,7},{7,6},{8,9},{9,8},{10,11... | collective-permute-start | bytes 196616 | tf_op jit(solution)/shard_map/ppermute | solution.py:145
  34.1 3.8 %copy-start.16 = (bf16[384,256]{1,0:T(8,128)(2,1)}, bf16[384,256]{1,0:T(8,128)(2,1)S(1)}, u32[]{:S(2)}) copy-start(bf16[384,256]{1,0:T(8,128)(2,1)S(1)} %get-tuple-element.35) | copy-start | bytes 589828
  37.9 5.3 %collective-permute-start.12 = (bf16[256,256]{1,0:T(8,128)(2,1)}, bf16[256,256]{1,0:T(8,128)(2,1)}, u32[]{:S(2)}, u32[]{:S(2)}) collective-permute-start(bf16[256,256]{1,0:T(8,128)(2,1)} %add_convert_fusion.4), channel_id=1, source_target_pairs={{0,5},{2,7},{4,1},{6,3},{8,13},{10,15},{12,9},{14,11},{1,0},{3,2},... | collective-permute-start | bytes 393224 | tf_op jit(solution)/shard_map/ppermute | solution.py:141
  38.6 4.6 %collective-permute-start.11 = (bf16[256,256]{1,0:T(8,128)(2,1)}, bf16[256,256]{1,0:T(8,128)(2,1)}, u32[]{:S(2)}, u32[]{:S(2)}) collective-permute-start(bf16[256,256]{1,0:T(8,128)(2,1)} %pad_maximum_fusion.3), channel_id=1, source_target_pairs={{0,1},{1,0},{2,3},{3,2},{4,5},{5,4},{6,7},{7,6},{8,9},{9,8},{10,11... | collective-permute-start | bytes 393224 | tf_op jit(solution)/shard_map/ppermute | solution.py:145
  39.1 1.4 %copy-start.1 = (bf16[1024,768]{1,0:T(8,128)(2,1)S(1)}, bf16[1024,768]{1,0:T(8,128)(2,1)}, u32[]{:S(2)}) copy-start(bf16[1024,768]{1,0:T(8,128)(2,1)} %copy-done) | copy-start | bytes 4718596
  43.1 5.6 %collective-permute-start.18 = (bf16[128,768]{1,0:T(8,128)(2,1)S(1)}, bf16[128,768]{1,0:T(8,128)(2,1)S(1)}, u32[]{:S(2)}, u32[]{:S(2)}) collective-permute-start(bf16[128,768]{1,0:T(8,128)(2,1)S(1)} %get-tuple-element.43.r_8_.refs_4_), channel_id=1, source_target_pairs={{0,1},{1,0},{2,3},{3,2},{4,5},{5,4},{6,7},{7,6},{8,9},{9,8},{10,11... | collective-permute-start | bytes 589832 | tf_op jit(solution)/shard_map/ppermute | solution.py:145
  44.2 5.3 %collective-permute-start.13 = (bf16[128,256]{1,0:T(8,128)(2,1)S(1)}, bf16[128,256]{1,0:T(8,128)(2,1)S(1)}, u32[]{:S(2)}, u32[]{:S(2)}) collective-permute-start(bf16[128,256]{1,0:T(8,128)(2,1)S(1)} %add_convert_fusion.10), channel_id=1, source_target_pairs={{1,8},{3,10},{5,12},{7,14},{9,0},{11,2},{13,4},{15,6},{0,1},{2,3},... | collective-permute-start | bytes 196616 | tf_op jit(solution)/shard_map/ppermute | solution.py:141
  45.6 4.0 %collective-permute-start.15 = (bf16[128,256]{1,0:T(8,128)(2,1)S(1)}, bf16[128,256]{1,0:T(8,128)(2,1)S(1)}, u32[]{:S(2)}, u32[]{:S(2)}) collective-permute-start(bf16[128,256]{1,0:T(8,128)(2,1)S(1)} %slice.170.r_3_), channel_id=1, source_target_pairs={{0,1},{1,0},{2,3},{3,2},{4,5},{5,4},{6,7},{7,6},{8,9},{9,8},{10,11... | collective-permute-start | bytes 196616 | tf_op jit(solution)/shard_map/ppermute | solution.py:145
  49.9 4.5 %copy-start.2 = (bf16[1024,768]{1,0:T(8,128)(2,1)S(1)}, bf16[1024,768]{1,0:T(8,128)(2,1)}, u32[]{:S(2)}) copy-start(bf16[1024,768]{1,0:T(8,128)(2,1)} %copy-done) | copy-start | bytes 4718596
  49.9 3.2 %collective-permute-start.19 = (bf16[384,256]{1,0:T(8,128)(2,1)S(1)}, bf16[384,256]{1,0:T(8,128)(2,1)S(1)}, u32[]{:S(2)}, u32[]{:S(2)}) collective-permute-start(bf16[384,256]{1,0:T(8,128)(2,1)S(1)} %shard_map.91), channel_id=1, source_target_pairs={{0,3},{2,1},{4,7},{6,5},{8,11},{10,9},{12,15},{14,13},{1,0},{3,2},... | collective-permute-start | bytes 589832 | tf_op jit(solution)/shard_map/ppermute | solution.py:141
  49.9 1.5 %collective-permute-start.14 = (bf16[128,256]{1,0:T(8,128)(2,1)S(1)}, bf16[128,256]{1,0:T(8,128)(2,1)S(1)}, u32[]{:S(2)}, u32[]{:S(2)}) collective-permute-start(bf16[128,256]{1,0:T(8,128)(2,1)S(1)} %collective-permute-done.13.r_1_.refs_0_), channel_id=1, source_target_pairs={{0,1},{1,0},{2,3},{3,2},{4,5},{5,4},{6,7},{7,6},{8,9},{9,8},{10,11... | collective-permute-start | bytes 196616 | tf_op jit(solution)/shard_map/ppermute | solution.py:145
  53.2 5.0 %collective-permute-start.21 = (bf16[256,256]{1,0:T(8,128)(2,1)S(1)}, bf16[256,256]{1,0:T(8,128)(2,1)S(1)}, u32[]{:S(2)}, u32[]{:S(2)}) collective-permute-start(bf16[256,256]{1,0:T(8,128)(2,1)S(1)} %add_convert_fusion.3), channel_id=1, source_target_pairs={{1,4},{3,6},{5,0},{7,2},{9,12},{11,14},{13,8},{15,10},{0,1},{2,3},... | collective-permute-start | bytes 393224 | tf_op jit(solution)/shard_map/ppermute | solution.py:141
  54.3 3.8 %collective-permute-start.20 = (bf16[256,256]{1,0:T(8,128)(2,1)S(1)}, bf16[256,256]{1,0:T(8,128)(2,1)S(1)}, u32[]{:S(2)}, u32[]{:S(2)}) collective-permute-start(bf16[256,256]{1,0:T(8,128)(2,1)S(1)} %pad_maximum_fusion.4), channel_id=1, source_target_pairs={{0,1},{1,0},{2,3},{3,2},{4,5},{5,4},{6,7},{7,6},{8,9},{9,8},{10,11... | collective-permute-start | bytes 393224 | tf_op jit(solution)/shard_map/ppermute | solution.py:145
  56.0 2.8 %collective-permute-start.25 = (bf16[128,768]{1,0:T(8,128)(2,1)S(1)}, bf16[128,768]{1,0:T(8,128)(2,1)S(1)}, u32[]{:S(2)}, u32[]{:S(2)}) collective-permute-start(bf16[128,768]{1,0:T(8,128)(2,1)S(1)} %get-tuple-element.47.r_8_.refs_4_), channel_id=1, source_target_pairs={{0,1},{1,0},{2,3},{3,2},{4,5},{5,4},{6,7},{7,6},{8,9},{9,8},{10,11... | collective-permute-start | bytes 589832 | tf_op jit(solution)/shard_map/ppermute | solution.py:145
  58.2 2.0 %collective-permute-start.22 = (bf16[128,256]{1,0:T(8,128)(2,1)S(1)}, bf16[128,256]{1,0:T(8,128)(2,1)S(1)}, u32[]{:S(2)}, u32[]{:S(2)}) collective-permute-start(bf16[128,256]{1,0:T(8,128)(2,1)S(1)} %add_convert_fusion.8), channel_id=1, source_target_pairs={{0,9},{2,11},{4,13},{6,15},{8,1},{10,3},{12,5},{14,7},{1,0},{3,2},... | collective-permute-start | bytes 196616 | tf_op jit(solution)/shard_map/ppermute | solution.py:141
  58.3 1.9 %collective-permute-start.24 = (bf16[128,256]{1,0:T(8,128)(2,1)S(1)}, bf16[128,256]{1,0:T(8,128)(2,1)S(1)}, u32[]{:S(2)}, u32[]{:S(2)}) collective-permute-start(bf16[128,256]{1,0:T(8,128)(2,1)S(1)} %slice.177.r_3_), channel_id=1, source_target_pairs={{0,1},{1,0},{2,3},{3,2},{4,5},{5,4},{6,7},{7,6},{8,9},{9,8},{10,11... | collective-permute-start | bytes 196616 | tf_op jit(solution)/shard_map/ppermute | solution.py:145
  60.5 6.4 %collective-permute-start.26 = (bf16[384,256]{1,0:T(8,128)(2,1)S(1)}, bf16[384,256]{1,0:T(8,128)(2,1)S(1)}, u32[]{:S(2)}, u32[]{:S(2)}) collective-permute-start(bf16[384,256]{1,0:T(8,128)(2,1)S(1)} %shard_map.94), channel_id=1, source_target_pairs={{1,2},{3,0},{5,6},{7,4},{9,10},{11,8},{13,14},{15,12},{0,1},{2,3},... | collective-permute-start | bytes 589832 | tf_op jit(solution)/shard_map/ppermute | solution.py:141
  62.0 1.3 %collective-permute-start.23 = (bf16[128,256]{1,0:T(8,128)(2,1)S(1)}, bf16[128,256]{1,0:T(8,128)(2,1)S(1)}, u32[]{:S(2)}, u32[]{:S(2)}) collective-permute-start(bf16[128,256]{1,0:T(8,128)(2,1)S(1)} %collective-permute-done.22.r_1_.refs_0_), channel_id=1, source_target_pairs={{0,1},{1,0},{2,3},{3,2},{4,5},{5,4},{6,7},{7,6},{8,9},{9,8},{10,11... | collective-permute-start | bytes 196616 | tf_op jit(solution)/shard_map/ppermute | solution.py:145
  66.9 2.6 %collective-permute-start.28 = (bf16[256,256]{1,0:T(8,128)(2,1)S(1)}, bf16[256,256]{1,0:T(8,128)(2,1)S(1)}, u32[]{:S(2)}, u32[]{:S(2)}) collective-permute-start(bf16[256,256]{1,0:T(8,128)(2,1)S(1)} %add_convert_fusion.2), channel_id=1, source_target_pairs={{0,5},{2,7},{4,1},{6,3},{8,13},{10,15},{12,9},{14,11},{1,0},{3,2},... | collective-permute-start | bytes 393224 | tf_op jit(solution)/shard_map/ppermute | solution.py:141
  67.1 2.5 %collective-permute-start.27 = (bf16[256,256]{1,0:T(8,128)(2,1)S(1)}, bf16[256,256]{1,0:T(8,128)(2,1)S(1)}, u32[]{:S(2)}, u32[]{:S(2)}) collective-permute-start(bf16[256,256]{1,0:T(8,128)(2,1)S(1)} %pad_maximum_fusion.5), channel_id=1, source_target_pairs={{0,1},{1,0},{2,3},{3,2},{4,5},{5,4},{6,7},{7,6},{8,9},{9,8},{10,11... | collective-permute-start | bytes 393224 | tf_op jit(solution)/shard_map/ppermute | solution.py:145
  69.6 4.7 %collective-permute-start.29 = (bf16[128,256]{1,0:T(8,128)(2,1)S(1)}, bf16[128,256]{1,0:T(8,128)(2,1)S(1)}, u32[]{:S(2)}, u32[]{:S(2)}) collective-permute-start(bf16[128,256]{1,0:T(8,128)(2,1)S(1)} %add_convert_fusion.6), channel_id=1, source_target_pairs={{1,8},{3,10},{5,12},{7,14},{9,0},{11,2},{13,4},{15,6},{0,1},{2,3},... | collective-permute-start | bytes 196616 | tf_op jit(solution)/shard_map/ppermute | solution.py:141
  69.8 5.4 %collective-permute-start.31 = (bf16[128,256]{1,0:T(8,128)(2,1)S(1)}, bf16[128,256]{1,0:T(8,128)(2,1)S(1)}, u32[]{:S(2)}, u32[]{:S(2)}) collective-permute-start(bf16[128,256]{1,0:T(8,128)(2,1)S(1)} %slice.184.r_3_), channel_id=1, source_target_pairs={{0,1},{1,0},{2,3},{3,2},{4,5},{5,4},{6,7},{7,6},{8,9},{9,8},{10,11... | collective-permute-start | bytes 196616 | tf_op jit(solution)/shard_map/ppermute | solution.py:145
  74.3 1.3 %collective-permute-start.30 = (bf16[128,256]{1,0:T(8,128)(2,1)S(1)}, bf16[128,256]{1,0:T(8,128)(2,1)S(1)}, u32[]{:S(2)}, u32[]{:S(2)}) collective-permute-start(bf16[128,256]{1,0:T(8,128)(2,1)S(1)} %collective-permute-done.29.r_1_), channel_id=1, source_target_pairs={{0,1},{1,0},{2,3},{3,2},{4,5},{5,4},{6,7},{7,6},{8,9},{9,8},{10,11... | collective-permute-start | bytes 196616 | tf_op jit(solution)/shard_map/ppermute | solution.py:145
  (10 other events, 9.9 us)

commit v4 on v3

--- a/solution.py
+++ b/solution.py
@@ -5,6 +5,7 @@
 from jax.experimental.pallas import tpu as pltpu
 from jax.sharding import PartitionSpec as P
 
+
 PASSES = 2
 LEVELS = 3
 BF = jnp.bfloat16
@@ -16,17 +17,18 @@
     return lax.dot_general(a, b, (((ca,), (cb,)), ((), ())), preferred_element_type=F32)
 
 
-def call(kernel, outs, args, flops, scratch=()):
+def call(kernel, outs, args, flops, scratch=(), far=0, room=VMEM_BYTES):
     vm = pl.BlockSpec(memory_space=pltpu.VMEM)
+    hbm = pl.BlockSpec(memory_space=pltpu.HBM)
     moved = sum(a.size * a.dtype.itemsize for a in args[1:]) + sum(o.size * o.dtype.itemsize for o in outs)
     return pl.pallas_call(
         kernel,
         out_shape=outs,
-        in_specs=[pl.BlockSpec(memory_space=pltpu.SMEM)] + [vm] * (len(args) - 1),
+        in_specs=[pl.BlockSpec(memory_space=pltpu.SMEM)] + [vm] * (len(args) - 1 - far) + [hbm] * far,
         out_specs=[vm] * len(outs),
         scratch_shapes=list(scratch),
         cost_estimate=pl.CostEstimate(flops=flops, bytes_accessed=moved, transcendentals=0),
-        compiler_params=pltpu.CompilerParams(vmem_limit_bytes=VMEM_BYTES),
+        compiler_params=pltpu.CompilerParams(vmem_limit_bytes=room),
     )(*args)
 
 
@@ -34,12 +36,30 @@
     return pl.ds(pl.multiple_of(start, size), size)
 
 
-def first_kernel(place, z, *refs):
-    factors, out = refs[:LEVELS], refs[LEVELS]
-    zt = z[...].T
+def first_kernel(place, *refs):
+    sources, out, buffers, sems = refs[: LEVELS + 1], refs[LEVELS + 1], refs[LEVELS + 2 : -1], refs[-1]
+    copies = [pltpu.make_async_copy(a, b, sems.at[i]) for i, (a, b) in enumerate(zip(sources, buffers))]
+    for copy in copies:
+        copy.start()
+    copies[0].wait()
+    zt = buffers[0][...].T
     c = zt.shape[0]
-    for level, factor in enumerate(factors):
-        out[level * c : (level + 1) * c, :] = mm(zt, factor[...], 1, 0).astype(BF)
+    for level in range(LEVELS):
+        copies[1 + level].wait()
+        out[level * c : (level + 1) * c, :] = mm(zt, buffers[1 + level][...], 1, 0).astype(BF)
+
+
+def pack_kernel(place, *refs):
+    sources, out, sems = refs[:LEVELS], refs[LEVELS], refs[LEVELS + 1]
+    half = out.shape[0] // LEVELS
+    copies = [
+        pltpu.make_async_copy(a.at[at((1 - place[0]) * half, half), :], out.at[pl.ds(i * half, half), :], sems.at[i])
+        for i, a in enumerate(sources)
+    ]
+    for copy in copies:
+        copy.start()
+    for copy in copies:
+        copy.wait()
 
 
 def join_kernel(place, own, other, out):
@@ -49,13 +69,20 @@
     out[:, at((1 - me) * k, k)] = other[...]
 
 
-def gram_kernel(place, *refs):
-    own, (other, full, gram) = refs[:LEVELS], refs[LEVELS:]
+def gram_kernel(place, other, *refs):
+    own, (full, gram, sems) = refs[:LEVELS], refs[LEVELS:]
     half, k = other.shape[0] // LEVELS, other.shape[1]
     me = place[0]
+    copies = [
+        pltpu.make_async_copy(a.at[at(me * half, half), :], full.at[:, at((2 * i + me) * k, k)], sems.at[i])
+        for i, a in enumerate(own)
+    ]
+    for copy in copies:
+        copy.start()
     for level in range(LEVELS):
-        full[:, at((2 * level + me) * k, k)] = own[level][at(me * half, half), :]
         full[:, at((2 * level + 1 - me) * k, k)] = other[level * half : (level + 1) * half, :]
+    for copy in copies:
+        copy.wait()
     for i in range(LEVELS):
         rows = slice(2 * k * i, 2 * k * (i + 1))
         left = full[:, rows].T
@@ -103,6 +130,18 @@
         out[level * c : (level + 1) * c, :] = total.astype(BF)
 
 
+def sum_kernel(source, place, summed, received, relayed, out):
+    n = out.shape[0]
+
+    @pl.when(place[0] == source)
+    def _():
+        out[...] = add(summed[:n, :], relayed[:n, :])
+
+    @pl.when(place[0] != source)
+    def _():
+        out[...] = add(summed[:n, :], received[:n, :])
+
+
 def leaf_terms(z, leaves, flipped, out):
     size = leaves.shape[1]
     for q in range(leaves.shape[0]):
@@ -127,10 +166,15 @@
     leaf_terms(z, leaves, flipped, y)
 
 
-def last_kernel(holders, place, *refs):
-    pieces, (factor, was, out, joined) = refs[: 2 * LEVELS], refs[2 * LEVELS :]
+def most_kernel(holders, place, *refs):
+    pieces, (factor, was, y, joined) = refs[: 2 * LEVELS - 2], refs[2 * LEVELS - 2 :]
     chosen(place, holders, pieces, joined)
-    out[...] = (mm(factor[...], joined[...], 1, 1) + was[...]).astype(BF)
+    y[...] = mm(factor[:, pieces[0].shape[1] :], joined[...], 1, 1) + was[...]
+
+
+def last_kernel(holders, place, received, relayed, factor, was, out, joined):
+    chosen(place, holders, (received, relayed), joined)
+    out[...] = (mm(factor[:, : received.shape[1]], joined[...], 1, 1) + was[...]).astype(BF)
 
 
 def one_way(value, stride, source):
@@ -149,8 +193,7 @@
     return (a.astype(F32) + b.astype(F32)).astype(BF)
 
 
-def siblings_of(packed, summed, source):
-    rank = lax.axis_index("rank")
+def siblings_of(place, packed, summed, source):
     bits = lax.axis_size(("rows", "cols")).bit_length() - 1
     c = packed.shape[0] // LEVELS
     found = [None] * LEVELS
@@ -168,65 +211,89 @@
             count -= 1
         packed = add(summed[: count * c], received[: count * c])
         if onward:
-            got = jnp.where(rank == source, relayed[: onward * c], received[: onward * c])
-            summed = add(summed[: onward * c], got)
+            shape = jax.ShapeDtypeStruct((onward * c, packed.shape[1]), BF)
+            (summed,) = call(
+                lambda *r, source=source: sum_kernel(source, *r), [shape], (place, summed, received, relayed), 0
+            )
         source = 1 - source
     return found, source
 
 
 def local(probes, basis_one, basis_two, basis_three, coeff_one, coeff_two, coeff_three, leaves):
-    rank = lax.axis_index("rank")
-    place = rank.reshape(1)
+    place = lax.axis_index("rank").reshape(1)
     n, c = probes.shape
     half = n // 2
     k = basis_one.shape[1]
     wide = 2 * k * LEVELS
     S = jax.ShapeDtypeStruct
     p_shape, y_shape, s_shape = S((LEVELS * c, 2 * k), BF), S((half, c), F32), S((c, wide), BF)
+    sems = pltpu.SemaphoreType.DMA
     uppers = (basis_one, basis_two, basis_three)
     lowers = (coeff_one, coeff_two, coeff_three)
 
-    def swapped(factors):
-        return over_rank(
-            jnp.concatenate([lax.dynamic_slice_in_dim(f, (1 - rank) * half, half, 0) for f in factors], 0)
-        )
-
-    def prepared(factors, other):
+    def prepared(factors):
+        (sent,) = call(pack_kernel, [S((LEVELS * half, k), BF)], (place, *factors), 0, [sems((LEVELS,))], LEVELS)
         full, gram = call(
-            gram_kernel, [S((half, wide), BF), S((wide, wide), BF)], (place, *factors, other), half * wide * wide * 3 // 2
+            gram_kernel,
+            [S((half, wide), BF), S((wide, wide), BF)],
+            (place, over_rank(sent), *factors),
+            half * wide * wide * 3 // 2,
+            [sems((LEVELS,))],
+            LEVELS,
         )
         return full, add(gram, over_rank(gram))
 
-    (own,) = call(first_kernel, [S((LEVELS * c, k), BF)], (place, probes, *uppers), 2 * n * LEVELS * k * c)
-    own, lowers, uppers = lax.optimization_barrier((own, lowers, uppers))
+    buffers = [pltpu.VMEM(a.shape, BF) for a in (probes, *uppers)]
+    (own,) = call(
+        first_kernel,
+        [S((LEVELS * c, k), BF)],
+        (place, probes, *uppers),
+        2 * n * LEVELS * k * c,
+        [*buffers, sems((LEVELS + 1,))],
+        LEVELS + 1,
+        None,
+    )
     (packed,) = call(join_kernel, [p_shape], (place, own, over_rank(own)), 0)
+    packed, lowers, probes, leaves = lax.optimization_barrier((packed, lowers, probes, leaves))
     summed = packed
-    lower, lower_gram = prepared(lowers, swapped(lowers))
-    upper, upper_gram = prepared(uppers, swapped(uppers))
+    lower, lower_gram = prepared(lowers)
     field_flops = 4 * half * wide * c
     y, s = call(start_kernel, [y_shape, s_shape], (place, probes, leaves, lower), field_flops // 2)
     applies = 2 * PASSES
     source = 0
-    joined = pltpu.VMEM((c, wide), BF)
     for step in range(applies):
         flipped = step % 2 == 0
-        factor, gram, after = (lower, lower_gram, upper) if flipped else (upper, upper_gram, lower)
-        found, source = siblings_of(packed, summed, source)
+        found, source = siblings_of(place, packed, summed, source)
         holders = [f[2] for f in found]
         pieces = [x for f in found for x in f[:2]]
         if step + 1 == applies:
+            rest = pltpu.VMEM((c, wide - 2 * k), BF)
+            (y,) = call(
+                lambda *r: most_kernel(holders[1:], *r), [y_shape], (place, *pieces[2:], upper, y), field_flops // 3, [rest]
+            )
             (out,) = call(
-                lambda *r: last_kernel(holders, *r), [S((half, c), BF)], (place, *pieces, factor, y), field_flops // 2, [joined]
+                lambda *r: last_kernel(holders[:1], *r),
+                [S((half, c), BF)],
+                (place, *pieces[:2], upper, y),
+                field_flops // 6,
+                [pltpu.VMEM((c, 2 * k), BF)],
             )
             return out
         there = over_rank(s)
         early = [f[0] if f[2] == source else f[1] for f in found]
+        gram = lower_gram if flipped else upper_gram
         (packed,) = call(next_kernel, [p_shape], (place, *early, gram, s, there), 2 * wide * wide * c)
+        if step == 0:
+            packed, uppers = lax.optimization_barrier((packed, uppers))
+            upper, upper_gram = prepared(uppers)
+        factor, after = (lower, upper) if flipped else (upper, lower)
         summed, q = call(
             lambda *r: again_kernel(holders, *r), [p_shape, s_shape], (place, *pieces, gram, s, there), 2 * wide * wide * c
         )
         if step + 2 == applies:
-            (y,) = call(lambda *r: late_kernel(not flipped, *r), [y_shape], (place, q, factor, y, leaves), field_flops // 2)
+            (y,) = call(
+                lambda *r: late_kernel(not flipped, *r), [y_shape], (place, q, factor, y, leaves), field_flops // 2
+            )
         else:
             y, s = call(
                 lambda *r: field_kernel(not flipped, *r),
@@ -241,4 +308,5 @@
     split = P(("parts", "rows", "cols"), "rank")
     every = ("parts", "rows", "cols", "rank")
     in_specs = (rows,) + (split,) * 6 + (P(every, None, None),)
+
     return jax.shard_map(local, mesh=mesh, in_specs=in_specs, out_specs=P(every, None), check_vma=False)

time: 77.6 us -> 73.7 us (0.950)
  waiting for transfers between devices: 24.3 us -> 35.1 us
  local copies, waits for them, and re-layouts: 11.6 us -> 1.27 us
  other arithmetic: 9.63 us -> 0.86 us
  starting transfers between devices: 16.2 us -> 21.7 us
    unnamed x52 -> x18, local copies, waits for them, and re-layouts: 8.92 us -> 1.19 us
    convert_element_type x10, other arithmetic: 7.31 us -> 0.81 us  [add(): return (a.astype(F32) + b.astype(F32)).astype(BF)]
    ppermute x20, waiting for transfers between devices: 4.31 us -> 10.8 us  [over_rank(): return lax.ppermute(value, 'rank', [(0, 1), (1, 0)])]
    ppermute x12, waiting for transfers between devices: 20 us -> 24.3 us  [one_way(): return lax.ppermute(value, ('rows', 'cols', 'rank'), away + home)]
    ppermute x12, starting transfers between devices: 8.15 us -> 12.5 us  [one_way(): return lax.ppermute(value, ('rows', 'cols', 'rank'), away + home)]
    slice x4, local copies, waits for them, and re-layouts: 1.7 us -> 0.02 us  [siblings_of(): received[(count - 1) * c:]]
    concatenate x4, other arithmetic: 1.33 us -> 0.04 us  [siblings_of(): sent = jnp.concatenate([received[l * c:(l + 1) * c] for l in relay], 0)]
    ppermute x20, starting transfers between devices: 8.07 us -> 9.26 us  [over_rank(): return lax.ppermute(value, 'rank', [(0, 1), (1, 0)])]
  transfers between devices with their start and end apart: 32 -> 32, of which waited for: 14 -> 21; matrix products, arithmetic and copies ran while one was open for 16% -> 1% of each run, Pallas kernels for 16% -> 9%
where the time goes in v4:
time: 73.7 us; the launch traced here: 73.6 us
  waiting for transfers between devices  35.1 us (48%)
  starting transfers between devices  21.7 us (29%)
  Pallas kernels  14.2 us (19%)
  local copies, waits for them, and re-layouts  1.27 us (2%)
  other arithmetic  0.86 us (1%)
    ppermute x12, waiting for transfers between devices, one_way(): return lax.ppermute(value, ('rows', 'cols', 'rank'), away + home)  24.3 us
    pallas_call x22, Pallas kernels, call(): pl.pallas_call(kernel, out_shape=outs, in_specs=[pl.BlockSpec(memory_spac...  14.2 us
    ppermute x12, starting transfers between devices, one_way(): return lax.ppermute(value, ('rows', 'cols', 'rank'), away + home)  12.5 us
    ppermute x20, waiting for transfers between devices, over_rank(): return lax.ppermute(value, 'rank', [(0, 1), (1, 0)])  10.8 us
    ppermute x20, starting transfers between devices, over_rank(): return lax.ppermute(value, 'rank', [(0, 1), (1, 0)])  9.26 us
  transfers between devices with their start and end apart: 32, of which 21 were waited for; matrix products, arithmetic and copies ran while one was open for 1% of the time, Pallas kernels for 9%

profile of v4, /device:TPU:0, one launch (start us, length us, event | category | flops | bytes accessed | tf_op | source)
XLA Modules:
  0.0 73.6 jit_solution(14179195925910773523)
XLA Ops:
  0.0 2.9 %shard_map.82.own = bf16[384,128]{1,0:T(8,128)(2,1)} custom-call(s32[1]{0:T(128)} %bitcast.place.r_0_, bf16[2048,128]{1,0:T(8,128)(2,1)} %z, bf16[2048,128]{1,0:T(8,128)(2,1)} %refs_0_.5, bf16[2048,128]{1,0:T(8,128)(2,1)} %refs_1_.5, bf16[2048,128]{1,0:T(8,128)(2,1)} %refs_2_.5), custom_call_target="tpu_custom_call" | custom-call | flops 201326592 | bytes 2195456 | tf_op jit(solution)/shard_map/pallas_call | solution.py:24
  2.9 0.6 collective-permute-start
  3.5 1.2 %collective-permute-done.other = bf16[384,128]{1,0:T(8,128)(2,1)S(1)} collective-permute-done((bf16[384,128]{1,0:T(8,128)(2,1)}, bf16[384,128]{1,0:T(8,128)(2,1)S(1)}, u32[]{:S(2)}, u32[]{:S(2)}) %collective-permute-start) | collective-permute-done | bytes 98336 | tf_op jit(solution)/shard_map/ppermute | solution.py:189
  4.6 0.9 %copy-done.8 = bf16[384,128]{1,0:T(8,128)(2,1)S(1)} copy-done((bf16[384,128]{1,0:T(8,128)(2,1)S(1)}, bf16[384,128]{1,0:T(8,128)(2,1)}, u32[]{:S(2)}) %copy-start.8) | copy-done | bytes 98328
  5.7 0.4 collective-permute-start.7
  6.1 1.9 %collective-permute-done.7.other = bf16[3072,128]{1,0:T(8,128)(2,1)S(1)} collective-permute-done((bf16[3072,128]{1,0:T(8,128)(2,1)S(1)}, bf16[3072,128]{1,0:T(8,128)(2,1)S(1)}, u32[]{:S(2)}, u32[]{:S(2)}) %collective-permute-start.7) | collective-permute-done | bytes 786464 | tf_op jit(solution)/shard_map/ppermute | solution.py:189
  8.0 1.4 %shard_map.86 = (bf16[1024,768]{1,0:T(8,128)(2,1)S(1)}, bf16[768,768]{1,0:T(8,128)(2,1)S(1)}) custom-call(s32[1]{0:T(128)} %bitcast.place.r_0_, bf16[3072,128]{1,0:T(8,128)(2,1)S(1)} %collective-permute-done.7.other, bf16[2048,128]{1,0:T(8,128)(2,1)S(1)} %copy-done.5, bf16[2048,128]{1,0:T(8,128)(2,1)S(1)} %copy-done.6, bf16[2048,128]{1,0:T(8,128)(2,1)S(1)} %copy-done.7), custom_call_target="tpu_custom_call" | custom-call | flops 905969664 | bytes 5111808 | tf_op jit(solution)/shard_map/pallas_call | solution.py:24
  9.4 0.4 collective-permute-start.8
  9.9 2.6 %collective-permute-start.1 = (bf16[384,256]{1,0:T(8,128)(2,1)S(1)}, bf16[384,256]{1,0:T(8,128)(2,1)S(1)}, u32[]{:S(2)}, u32[]{:S(2)}) collective-permute-start(bf16[384,256]{1,0:T(8,128)(2,1)S(1)} %shard_map.83.r_1_), channel_id=1, source_target_pairs={{0,3},{2,1},{4,7},{6,5},{8,11},{10,9},{12,15},{14,13},{1,0},{3,2},... | collective-permute-start | bytes 589832 | tf_op jit(solution)/shard_map/ppermute | solution.py:185
  12.5 3.2 %collective-permute-done.1.r_2_ = bf16[384,256]{1,0:T(8,128)(2,1)S(1)} collective-permute-done((bf16[384,256]{1,0:T(8,128)(2,1)S(1)}, bf16[384,256]{1,0:T(8,128)(2,1)S(1)}, u32[]{:S(2)}, u32[]{:S(2)}) %collective-permute-start.1) | collective-permute-done | bytes 196640 | tf_op jit(solution)/shard_map/ppermute | solution.py:185
  15.7 0.4 collective-permute-start.2
  16.3 0.7 %collective-permute-done.2.r_3_ = bf16[256,256]{1,0:T(8,128)(2,1)S(1)} collective-permute-done((bf16[256,256]{1,0:T(8,128)(2,1)S(1)}, bf16[256,256]{1,0:T(8,128)(2,1)S(1)}, u32[]{:S(2)}, u32[]{:S(2)}) %collective-permute-start.2) | collective-permute-done | bytes 131104 | tf_op jit(solution)/shard_map/ppermute | solution.py:189
  17.1 3.4 %collective-permute-done.3 = bf16[256,256]{1,0:T(8,128)(2,1)S(1)} collective-permute-done((bf16[256,256]{1,0:T(8,128)(2,1)S(1)}, bf16[256,256]{1,0:T(8,128)(2,1)S(1)}, u32[]{:S(2)}, u32[]{:S(2)}) %collective-permute-start.3) | collective-permute-done | bytes 131104 | tf_op jit(solution)/shard_map/ppermute | solution.py:185
  20.6 2.0 %collective-permute-start.4 = (bf16[128,256]{1,0:T(8,128)(2,1)S(1)}, bf16[128,256]{1,0:T(8,128)(2,1)S(1)}, u32[]{:S(2)}, u32[]{:S(2)}) collective-permute-start(bf16[128,256]{1,0:T(8,128)(2,1)S(1)} %add_convert_fusion.9), channel_id=1, source_target_pairs={{0,9},{2,11},{4,13},{6,15},{8,1},{10,3},{12,5},{14,7},{1,0},{3,2},... | collective-permute-start | bytes 196616 | tf_op jit(solution)/shard_map/ppermute | solution.py:185
  22.6 0.8 %shard_map.87 = (f32[1024,128]{1,0:T(8,128)S(1)}, bf16[128,768]{1,0:T(8,128)(2,1)S(1)}) custom-call(s32[1]{0:T(128)} %bitcast.place.r_0_, bf16[2048,128]{1,0:T(8,128)(2,1)S(1)} %copy-done.4, bf16[4,256,256]{2,1,0:T(8,128)(2,1)S(1)} %copy-done, bf16[1024,768]{1,0:T(8,128)(2,1)S(1)} %get-tuple-element.38.after.r_2_.r_5_), custom_call_target="tpu_custom_call" | custom-call | flops 201326592 | bytes 3342336 | tf_op jit(solution)/shard_map/pallas_call | solution.py:24
  23.3 0.6 collective-permute-start.9
  24.5 0.5 collective-permute-done.9.r_9_.refs_5_
  25.7 0.6 collective-permute-start.16
  26.3 1.9 %collective-permute-done.16.other = bf16[3072,128]{1,0:T(8,128)(2,1)S(1)} collective-permute-done((bf16[3072,128]{1,0:T(8,128)(2,1)S(1)}, bf16[3072,128]{1,0:T(8,128)(2,1)S(1)}, u32[]{:S(2)}, u32[]{:S(2)}) %collective-permute-start.16) | collective-permute-done | bytes 786464 | tf_op jit(solution)/shard_map/ppermute | solution.py:189
  28.2 1.4 %shard_map.92 = (bf16[1024,768]{1,0:T(8,128)(2,1)S(1)}, bf16[768,768]{1,0:T(8,128)(2,1)S(1)}) custom-call(s32[1]{0:T(128)} %bitcast.place.r_0_, bf16[3072,128]{1,0:T(8,128)(2,1)S(1)} %collective-permute-done.16.other, bf16[2048,128]{1,0:T(8,128)(2,1)S(1)} %copy-done.1, bf16[2048,128]{1,0:T(8,128)(2,1)S(1)} %copy-done.2, bf16[2048,128]{1,0:T(8,128)(2,1)S(1)} %copy-done.3), custom_call_target="tpu_custom_call" | custom-call | flops 905969664 | bytes 5111808 | tf_op jit(solution)/shard_map/pallas_call | solution.py:24
  29.6 0.4 collective-permute-start.17
  30.2 1.5 %collective-permute-start.5 = (bf16[128,256]{1,0:T(8,128)(2,1)S(1)}, bf16[128,256]{1,0:T(8,128)(2,1)S(1)}, u32[]{:S(2)}, u32[]{:S(2)}) collective-permute-start(bf16[128,256]{1,0:T(8,128)(2,1)S(1)} %collective-permute-done.4.r_1_.refs_0_), channel_id=1, source_target_pairs={{0,1},{1,0},{2,3},{3,2},{4,5},{5,4},{6,7},{7,6},{8,9},{9,8},{10,11... | collective-permute-start | bytes 196616 | tf_op jit(solution)/shard_map/ppermute | solution.py:189
  31.6 1.2 %collective-permute-done.5.r_2_ = bf16[128,256]{1,0:T(8,128)(2,1)S(1)} collective-permute-done((bf16[128,256]{1,0:T(8,128)(2,1)S(1)}, bf16[128,256]{1,0:T(8,128)(2,1)S(1)}, u32[]{:S(2)}, u32[]{:S(2)}) %collective-permute-start.5) | collective-permute-done | bytes 65568 | tf_op jit(solution)/shard_map/ppermute | solution.py:189
  33.2 1.9 %collective-permute-done.10.r_2_ = bf16[384,256]{1,0:T(8,128)(2,1)S(1)} collective-permute-done((bf16[384,256]{1,0:T(8,128)(2,1)S(1)}, bf16[384,256]{1,0:T(8,128)(2,1)S(1)}, u32[]{:S(2)}, u32[]{:S(2)}) %collective-permute-start.10) | collective-permute-done | bytes 196640 | tf_op jit(solution)/shard_map/ppermute | solution.py:185
  35.3 1.7 %collective-permute-start.12 = (bf16[256,256]{1,0:T(8,128)(2,1)S(1)}, bf16[256,256]{1,0:T(8,128)(2,1)S(1)}, u32[]{:S(2)}, u32[]{:S(2)}) collective-permute-start(bf16[256,256]{1,0:T(8,128)(2,1)S(1)} %add_convert_fusion.4), channel_id=1, source_target_pairs={{0,5},{2,7},{4,1},{6,3},{8,13},{10,15},{12,9},{14,11},{1,0},{3,2},... | collective-permute-start | bytes 393224 | tf_op jit(solution)/shard_map/ppermute | solution.py:185
  37.0 2.5 %collective-permute-done.12 = bf16[256,256]{1,0:T(8,128)(2,1)S(1)} collective-permute-done((bf16[256,256]{1,0:T(8,128)(2,1)S(1)}, bf16[256,256]{1,0:T(8,128)(2,1)S(1)}, u32[]{:S(2)}, u32[]{:S(2)}) %collective-permute-start.12) | collective-permute-done | bytes 131104 | tf_op jit(solution)/shard_map/ppermute | solution.py:185
  39.5 0.7 %collective-permute-start.13 = (bf16[128,256]{1,0:T(8,128)(2,1)S(1)}, bf16[128,256]{1,0:T(8,128)(2,1)S(1)}, u32[]{:S(2)}, u32[]{:S(2)}) collective-permute-start(bf16[128,256]{1,0:T(8,128)(2,1)S(1)} %add_convert_fusion.8), channel_id=1, source_target_pairs={{1,8},{3,10},{5,12},{7,14},{9,0},{11,2},{13,4},{15,6},{0,1},{2,3},... | collective-permute-start | bytes 196616 | tf_op jit(solution)/shard_map/ppermute | solution.py:185
  40.3 0.5 collective-permute-start.15
  40.8 1.5 %shard_map.93 = (f32[1024,128]{1,0:T(8,128)S(1)}, bf16[128,768]{1,0:T(8,128)(2,1)S(1)}) custom-call(s32[1]{0:T(128)} %bitcast.place.r_0_, bf16[128,768]{1,0:T(8,128)(2,1)S(1)} %get-tuple-element.46.r_1_, bf16[1024,768]{1,0:T(8,128)(2,1)S(1)} %get-tuple-element.38.after.r_2_.r_5_, f32[1024,128]{1,0:T(8,128)S(1)} %get-tuple-element.47.r_3_, ...), custom_call_target="tpu_custom_call" | custom-call | flops 402653184 | bytes 5111808 | tf_op jit(solution)/shard_map/pallas_call | solution.py:24
  42.7 2.0 %collective-permute-done.13.r_1_.refs_0_ = bf16[128,256]{1,0:T(8,128)(2,1)S(1)} collective-permute-done((bf16[128,256]{1,0:T(8,128)(2,1)S(1)}, bf16[128,256]{1,0:T(8,128)(2,1)S(1)}, u32[]{:S(2)}, u32[]{:S(2)}) %collective-permute-start.13) | collective-permute-done | bytes 65568 | tf_op jit(solution)/shard_map/ppermute | solution.py:185
  45.7 1.0 %collective-permute-done.14.r_2_ = bf16[128,256]{1,0:T(8,128)(2,1)S(1)} collective-permute-done((bf16[128,256]{1,0:T(8,128)(2,1)S(1)}, bf16[128,256]{1,0:T(8,128)(2,1)S(1)}, u32[]{:S(2)}, u32[]{:S(2)}) %collective-permute-start.14) | collective-permute-done | bytes 65568 | tf_op jit(solution)/shard_map/ppermute | solution.py:189
  47.1 1.6 %collective-permute-done.19.r_2_ = bf16[384,256]{1,0:T(8,128)(2,1)S(1)} collective-permute-done((bf16[384,256]{1,0:T(8,128)(2,1)S(1)}, bf16[384,256]{1,0:T(8,128)(2,1)S(1)}, u32[]{:S(2)}, u32[]{:S(2)}) %collective-permute-start.19) | collective-permute-done | bytes 196640 | tf_op jit(solution)/shard_map/ppermute | solution.py:185
  48.7 1.5 %collective-permute-start.20 = (bf16[256,256]{1,0:T(8,128)(2,1)S(1)}, bf16[256,256]{1,0:T(8,128)(2,1)S(1)}, u32[]{:S(2)}, u32[]{:S(2)}) collective-permute-start(bf16[256,256]{1,0:T(8,128)(2,1)S(1)} %pad_maximum_fusion.2), channel_id=1, source_target_pairs={{0,1},{1,0},{2,3},{3,2},{4,5},{5,4},{6,7},{7,6},{8,9},{9,8},{10,11... | collective-permute-start | bytes 393224 | tf_op jit(solution)/shard_map/ppermute | solution.py:189
  50.3 1.5 %shard_map.97 = (f32[1024,128]{1,0:T(8,128)S(1)}, bf16[128,768]{1,0:T(8,128)(2,1)S(1)}) custom-call(s32[1]{0:T(128)} %bitcast.place.r_0_, bf16[128,768]{1,0:T(8,128)(2,1)S(1)} %get-tuple-element.51.r_1_, bf16[1024,768]{1,0:T(8,128)(2,1)S(1)} %get-tuple-element.48.r_5_.r_2_.r_3_, f32[1024,128]{1,0:T(8,128)S(1)} %get-tuple-element.52.r_3_, ...), custom_call_target="tpu_custom_call" | custom-call | flops 402653184 | bytes 5111808 | tf_op jit(solution)/shard_map/pallas_call | solution.py:24
  51.9 0.9 %collective-permute-start.25 = (bf16[128,768]{1,0:T(8,128)(2,1)S(1)}, bf16[128,768]{1,0:T(8,128)(2,1)S(1)}, u32[]{:S(2)}, u32[]{:S(2)}) collective-permute-start(bf16[128,768]{1,0:T(8,128)(2,1)S(1)} %get-tuple-element.53.r_8_.refs_4_), channel_id=1, source_target_pairs={{0,1},{1,0},{2,3},{3,2},{4,5},{5,4},{6,7},{7,6},{8,9},{9,8},{10,11... | collective-permute-start | bytes 589832 | tf_op jit(solution)/shard_map/ppermute | solution.py:189
  52.9 1.9 %collective-permute-done.21 = bf16[256,256]{1,0:T(8,128)(2,1)S(1)} collective-permute-done((bf16[256,256]{1,0:T(8,128)(2,1)S(1)}, bf16[256,256]{1,0:T(8,128)(2,1)S(1)}, u32[]{:S(2)}, u32[]{:S(2)}) %collective-permute-start.21) | collective-permute-done | bytes 131104 | tf_op jit(solution)/shard_map/ppermute | solution.py:185
  54.8 0.5 collective-permute-start.24
  55.3 1.4 %collective-permute-done.22.r_1_.refs_0_ = bf16[128,256]{1,0:T(8,128)(2,1)S(1)} collective-permute-done((bf16[128,256]{1,0:T(8,128)(2,1)S(1)}, bf16[128,256]{1,0:T(8,128)(2,1)S(1)}, u32[]{:S(2)}, u32[]{:S(2)}) %collective-permute-start.22) | collective-permute-done | bytes 65568 | tf_op jit(solution)/shard_map/ppermute | solution.py:185
  57.0 2.1 %collective-permute-start.26 = (bf16[384,256]{1,0:T(8,128)(2,1)S(1)}, bf16[384,256]{1,0:T(8,128)(2,1)S(1)}, u32[]{:S(2)}, u32[]{:S(2)}) collective-permute-start(bf16[384,256]{1,0:T(8,128)(2,1)S(1)} %shard_map.99), channel_id=1, source_target_pairs={{1,2},{3,0},{5,6},{7,4},{9,10},{11,8},{13,14},{15,12},{0,1},{2,3},... | collective-permute-start | bytes 589832 | tf_op jit(solution)/shard_map/ppermute | solution.py:185
  59.2 1.2 %collective-permute-done.23.r_2_ = bf16[128,256]{1,0:T(8,128)(2,1)S(1)} collective-permute-done((bf16[128,256]{1,0:T(8,128)(2,1)S(1)}, bf16[128,256]{1,0:T(8,128)(2,1)S(1)}, u32[]{:S(2)}, u32[]{:S(2)}) %collective-permute-start.23) | collective-permute-done | bytes 65568 | tf_op jit(solution)/shard_map/ppermute | solution.py:189
  60.8 2.8 %collective-permute-done.26.r_2_ = bf16[384,256]{1,0:T(8,128)(2,1)S(1)} collective-permute-done((bf16[384,256]{1,0:T(8,128)(2,1)S(1)}, bf16[384,256]{1,0:T(8,128)(2,1)S(1)}, u32[]{:S(2)}, u32[]{:S(2)}) %collective-permute-start.26) | collective-permute-done | bytes 196640 | tf_op jit(solution)/shard_map/ppermute | solution.py:185
  64.0 1.1 %collective-permute-done.27.r_3_ = bf16[256,256]{1,0:T(8,128)(2,1)S(1)} collective-permute-done((bf16[256,256]{1,0:T(8,128)(2,1)S(1)}, bf16[256,256]{1,0:T(8,128)(2,1)S(1)}, u32[]{:S(2)}, u32[]{:S(2)}) %collective-permute-start.27) | collective-permute-done | bytes 131104 | tf_op jit(solution)/shard_map/ppermute | solution.py:189
  65.1 1.4 %collective-permute-done.28 = bf16[256,256]{1,0:T(8,128)(2,1)S(1)} collective-permute-done((bf16[256,256]{1,0:T(8,128)(2,1)S(1)}, bf16[256,256]{1,0:T(8,128)(2,1)S(1)}, u32[]{:S(2)}, u32[]{:S(2)}) %collective-permute-start.28) | collective-permute-done | bytes 131104 | tf_op jit(solution)/shard_map/ppermute | solution.py:185
  66.5 2.2 %collective-permute-start.29 = (bf16[128,256]{1,0:T(8,128)(2,1)S(1)}, bf16[128,256]{1,0:T(8,128)(2,1)S(1)}, u32[]{:S(2)}, u32[]{:S(2)}) collective-permute-start(bf16[128,256]{1,0:T(8,128)(2,1)S(1)} %add_convert_fusion.6), channel_id=1, source_target_pairs={{1,8},{3,10},{5,12},{7,14},{9,0},{11,2},{13,4},{15,6},{0,1},{2,3},... | collective-permute-start | bytes 196616 | tf_op jit(solution)/shard_map/ppermute | solution.py:185
  69.1 2.0 %collective-permute-done.29.r_1_ = bf16[128,256]{1,0:T(8,128)(2,1)S(1)} collective-permute-done((bf16[128,256]{1,0:T(8,128)(2,1)S(1)}, bf16[128,256]{1,0:T(8,128)(2,1)S(1)}, u32[]{:S(2)}, u32[]{:S(2)}) %collective-permute-start.29) | collective-permute-done | bytes 65568 | tf_op jit(solution)/shard_map/ppermute | solution.py:185
  71.2 0.9 %shard_map.101.r_6_ = f32[1024,128]{1,0:T(8,128)S(1)} custom-call(s32[1]{0:T(128)} %bitcast.place.r_0_, bf16[128,768]{1,0:T(8,128)(2,1)S(1)} %get-tuple-element.55.r_1_, bf16[1024,768]{1,0:T(8,128)(2,1)S(1)} %get-tuple-element.38.after.r_2_.r_5_, f32[1024,128]{1,0:T(8,128)S(1)} %get-tuple-element.56.r_3_, bf16[4,256,256]{2,1,0:T(8,128)(2,1)S(1)} %copy-done), custom_call_target="tpu_custom_call" | custom-call | flops 201326592 | bytes 3342336 | tf_op jit(solution)/shard_map/pallas_call | solution.py:24
  72.1 0.5 shard_map.102.r_4_
  72.5 1.0 %shard_map.103 = bf16[1024,128]{1,0:T(8,128)(2,1)} custom-call(s32[1]{0:T(128)} %bitcast.place.r_0_, bf16[128,256]{1,0:T(8,128)(2,1)S(1)} %collective-permute-done.29.r_1_, bf16[128,256]{1,0:T(8,128)(2,1)S(1)} %collective-permute-done.30.r_2_, bf16[1024,768]{1,0:T(8,128)(2,1)S(1)} %get-tuple-element.48.r_5_.r_2_.r_3_, f32[1024,128]{1,0:T(8,128)S(1)} %shard_map.102.r_4_), custom_call_target="tpu_custom_call" | custom-call | flops 67108864 | bytes 2490368 | tf_op jit(solution)/shard_map/pallas_call | solution.py:24
  (82 shorter events, 5.8 us)
Async XLA Ops:
  0.0 5.6 %copy-start.5 = (bf16[2048,128]{1,0:T(8,128)(2,1)S(1)}, bf16[2048,128]{1,0:T(8,128)(2,1)}, u32[]{:S(2)}) copy-start(bf16[2048,128]{1,0:T(8,128)(2,1)} %refs_0_.3) | copy-start | bytes 1572868
  0.0 5.6 %copy-start.6 = (bf16[2048,128]{1,0:T(8,128)(2,1)S(1)}, bf16[2048,128]{1,0:T(8,128)(2,1)}, u32[]{:S(2)}) copy-start(bf16[2048,128]{1,0:T(8,128)(2,1)} %refs_1_.3) | copy-start | bytes 1572868
  0.0 5.6 %copy-start.7 = (bf16[2048,128]{1,0:T(8,128)(2,1)S(1)}, bf16[2048,128]{1,0:T(8,128)(2,1)}, u32[]{:S(2)}) copy-start(bf16[2048,128]{1,0:T(8,128)(2,1)} %refs_2_.3) | copy-start | bytes 1572868
  2.9 1.7 %collective-permute-start = (bf16[384,128]{1,0:T(8,128)(2,1)}, bf16[384,128]{1,0:T(8,128)(2,1)S(1)}, u32[]{:S(2)}, u32[]{:S(2)}) collective-permute-start(bf16[384,128]{1,0:T(8,128)(2,1)} %shard_map.82.own), channel_id=1, source_target_pairs={{0,1},{1,0},{2,3},{3,2},{4,5},{5,4},{6,7},{7,6},{8,9},{9,8},{10,11... | collective-permute-start | bytes 294920 | tf_op jit(solution)/shard_map/ppermute | solution.py:189
  4.6 0.9 %copy-start.8 = (bf16[384,128]{1,0:T(8,128)(2,1)S(1)}, bf16[384,128]{1,0:T(8,128)(2,1)}, u32[]{:S(2)}) copy-start(bf16[384,128]{1,0:T(8,128)(2,1)} %shard_map.82.own) | copy-start | bytes 294916
  5.7 2.4 %collective-permute-start.7 = (bf16[3072,128]{1,0:T(8,128)(2,1)S(1)}, bf16[3072,128]{1,0:T(8,128)(2,1)S(1)}, u32[]{:S(2)}, u32[]{:S(2)}) collective-permute-start(bf16[3072,128]{1,0:T(8,128)(2,1)S(1)} %shard_map.85), channel_id=1, source_target_pairs={{0,1},{1,0},{2,3},{3,2},{4,5},{5,4},{6,7},{7,6},{8,9},{9,8},{10,11... | collective-permute-start | bytes 2359304 | tf_op jit(solution)/shard_map/ppermute | solution.py:189
  9.4 13.1 %copy-start = (bf16[4,256,256]{2,1,0:T(8,128)(2,1)S(1)}, bf16[4,256,256]{2,1,0:T(8,128)(2,1)}, u32[]{:S(2)}) copy-start(bf16[4,256,256]{2,1,0:T(8,128)(2,1)} %r_4_.2) | copy-start | bytes 1572868
  9.4 13.1 %copy-start.4 = (bf16[2048,128]{1,0:T(8,128)(2,1)S(1)}, bf16[2048,128]{1,0:T(8,128)(2,1)}, u32[]{:S(2)}) copy-start(bf16[2048,128]{1,0:T(8,128)(2,1)} %z) | copy-start | bytes 1572868
  9.4 14.5 %collective-permute-start.8 = (bf16[768,768]{1,0:T(8,128)(2,1)S(1)}, bf16[768,768]{1,0:T(8,128)(2,1)S(1)}, u32[]{:S(2)}, u32[]{:S(2)}) collective-permute-start(bf16[768,768]{1,0:T(8,128)(2,1)S(1)} %get-tuple-element.35), channel_id=1, source_target_pairs={{0,1},{1,0},{2,3},{3,2},{4,5},{5,4},{6,7},{7,6},{8,9},{9,8},{10,11... | collective-permute-start | bytes 3538952 | tf_op jit(solution)/shard_map/ppermute | solution.py:189
  9.9 5.8 %collective-permute-start.1 = (bf16[384,256]{1,0:T(8,128)(2,1)S(1)}, bf16[384,256]{1,0:T(8,128)(2,1)S(1)}, u32[]{:S(2)}, u32[]{:S(2)}) collective-permute-start(bf16[384,256]{1,0:T(8,128)(2,1)S(1)} %shard_map.83.r_1_), channel_id=1, source_target_pairs={{0,3},{2,1},{4,7},{6,5},{8,11},{10,9},{12,15},{14,13},{1,0},{3,2},... | collective-permute-start | bytes 589832 | tf_op jit(solution)/shard_map/ppermute | solution.py:185
  15.7 1.4 %collective-permute-start.2 = (bf16[256,256]{1,0:T(8,128)(2,1)S(1)}, bf16[256,256]{1,0:T(8,128)(2,1)S(1)}, u32[]{:S(2)}, u32[]{:S(2)}) collective-permute-start(bf16[256,256]{1,0:T(8,128)(2,1)S(1)} %pad_maximum_fusion), channel_id=1, source_target_pairs={{0,1},{1,0},{2,3},{3,2},{4,5},{5,4},{6,7},{7,6},{8,9},{9,8},{10,11... | collective-permute-start | bytes 393224 | tf_op jit(solution)/shard_map/ppermute | solution.py:189
  16.1 4.4 %collective-permute-start.3 = (bf16[256,256]{1,0:T(8,128)(2,1)S(1)}, bf16[256,256]{1,0:T(8,128)(2,1)S(1)}, u32[]{:S(2)}, u32[]{:S(2)}) collective-permute-start(bf16[256,256]{1,0:T(8,128)(2,1)S(1)} %add_convert_fusion.5), channel_id=1, source_target_pairs={{1,4},{3,6},{5,0},{7,2},{9,12},{11,14},{13,8},{15,10},{0,1},{2,3},... | collective-permute-start | bytes 393224 | tf_op jit(solution)/shard_map/ppermute | solution.py:185
  20.6 3.9 %collective-permute-start.4 = (bf16[128,256]{1,0:T(8,128)(2,1)S(1)}, bf16[128,256]{1,0:T(8,128)(2,1)S(1)}, u32[]{:S(2)}, u32[]{:S(2)}) collective-permute-start(bf16[128,256]{1,0:T(8,128)(2,1)S(1)} %add_convert_fusion.9), channel_id=1, source_target_pairs={{0,9},{2,11},{4,13},{6,15},{8,1},{10,3},{12,5},{14,7},{1,0},{3,2},... | collective-permute-start | bytes 196616 | tf_op jit(solution)/shard_map/ppermute | solution.py:185
  22.6 1.9 %collective-permute-start.6 = (bf16[128,256]{1,0:T(8,128)(2,1)S(1)}, bf16[128,256]{1,0:T(8,128)(2,1)S(1)}, u32[]{:S(2)}, u32[]{:S(2)}) collective-permute-start(bf16[128,256]{1,0:T(8,128)(2,1)S(1)} %slice.124.r_3_), channel_id=1, source_target_pairs={{0,1},{1,0},{2,3},{3,2},{4,5},{5,4},{6,7},{7,6},{8,9},{9,8},{10,11... | collective-permute-start | bytes 196616 | tf_op jit(solution)/shard_map/ppermute | solution.py:189
  23.3 1.6 %collective-permute-start.9 = (bf16[128,768]{1,0:T(8,128)(2,1)S(1)}, bf16[128,768]{1,0:T(8,128)(2,1)S(1)}, u32[]{:S(2)}, u32[]{:S(2)}) collective-permute-start(bf16[128,768]{1,0:T(8,128)(2,1)S(1)} %get-tuple-element.39.r_8_.refs_4_), channel_id=1, source_target_pairs={{0,1},{1,0},{2,3},{3,2},{4,5},{5,4},{6,7},{7,6},{8,9},{9,8},{10,11... | collective-permute-start | bytes 589832 | tf_op jit(solution)/shard_map/ppermute | solution.py:189
  24.2 1.1 %copy-start.1 = (bf16[2048,128]{1,0:T(8,128)(2,1)S(1)}, bf16[2048,128]{1,0:T(8,128)(2,1)}, u32[]{:S(2)}) copy-start(bf16[2048,128]{1,0:T(8,128)(2,1)} %refs_0_.5) | copy-start | bytes 1572868
  24.2 1.2 %copy-start.2 = (bf16[2048,128]{1,0:T(8,128)(2,1)S(1)}, bf16[2048,128]{1,0:T(8,128)(2,1)}, u32[]{:S(2)}) copy-start(bf16[2048,128]{1,0:T(8,128)(2,1)} %refs_1_.5) | copy-start | bytes 1572868
  24.2 1.3 %copy-start.3 = (bf16[2048,128]{1,0:T(8,128)(2,1)S(1)}, bf16[2048,128]{1,0:T(8,128)(2,1)}, u32[]{:S(2)}) copy-start(bf16[2048,128]{1,0:T(8,128)(2,1)} %refs_2_.5) | copy-start | bytes 1572868
  25.7 2.6 %collective-permute-start.16 = (bf16[3072,128]{1,0:T(8,128)(2,1)S(1)}, bf16[3072,128]{1,0:T(8,128)(2,1)S(1)}, u32[]{:S(2)}, u32[]{:S(2)}) collective-permute-start(bf16[3072,128]{1,0:T(8,128)(2,1)S(1)} %shard_map.91), channel_id=1, source_target_pairs={{0,1},{1,0},{2,3},{3,2},{4,5},{5,4},{6,7},{7,6},{8,9},{9,8},{10,11... | collective-permute-start | bytes 2359304 | tf_op jit(solution)/shard_map/ppermute | solution.py:189
  29.6 12.8 %collective-permute-start.17 = (bf16[768,768]{1,0:T(8,128)(2,1)S(1)}, bf16[768,768]{1,0:T(8,128)(2,1)S(1)}, u32[]{:S(2)}, u32[]{:S(2)}) collective-permute-start(bf16[768,768]{1,0:T(8,128)(2,1)S(1)} %get-tuple-element.45), channel_id=1, source_target_pairs={{0,1},{1,0},{2,3},{3,2},{4,5},{5,4},{6,7},{7,6},{8,9},{9,8},{10,11... | collective-permute-start | bytes 3538952 | tf_op jit(solution)/shard_map/ppermute | solution.py:189
  30.0 5.1 %collective-permute-start.10 = (bf16[384,256]{1,0:T(8,128)(2,1)S(1)}, bf16[384,256]{1,0:T(8,128)(2,1)S(1)}, u32[]{:S(2)}, u32[]{:S(2)}) collective-permute-start(bf16[384,256]{1,0:T(8,128)(2,1)S(1)} %shard_map.89), channel_id=1, source_target_pairs={{1,2},{3,0},{5,6},{7,4},{9,10},{11,8},{13,14},{15,12},{0,1},{2,3},... | collective-permute-start | bytes 589832 | tf_op jit(solution)/shard_map/ppermute | solution.py:185
  30.2 2.7 %collective-permute-start.5 = (bf16[128,256]{1,0:T(8,128)(2,1)S(1)}, bf16[128,256]{1,0:T(8,128)(2,1)S(1)}, u32[]{:S(2)}, u32[]{:S(2)}) collective-permute-start(bf16[128,256]{1,0:T(8,128)(2,1)S(1)} %collective-permute-done.4.r_1_.refs_0_), channel_id=1, source_target_pairs={{0,1},{1,0},{2,3},{3,2},{4,5},{5,4},{6,7},{7,6},{8,9},{9,8},{10,11... | collective-permute-start | bytes 196616 | tf_op jit(solution)/shard_map/ppermute | solution.py:189
  35.2 1.9 %collective-permute-start.11 = (bf16[256,256]{1,0:T(8,128)(2,1)S(1)}, bf16[256,256]{1,0:T(8,128)(2,1)S(1)}, u32[]{:S(2)}, u32[]{:S(2)}) collective-permute-start(bf16[256,256]{1,0:T(8,128)(2,1)S(1)} %pad_maximum_fusion.1), channel_id=1, source_target_pairs={{0,1},{1,0},{2,3},{3,2},{4,5},{5,4},{6,7},{7,6},{8,9},{9,8},{10,11... | collective-permute-start | bytes 393224 | tf_op jit(solution)/shard_map/ppermute | solution.py:189
  35.3 4.2 %collective-permute-start.12 = (bf16[256,256]{1,0:T(8,128)(2,1)S(1)}, bf16[256,256]{1,0:T(8,128)(2,1)S(1)}, u32[]{:S(2)}, u32[]{:S(2)}) collective-permute-start(bf16[256,256]{1,0:T(8,128)(2,1)S(1)} %add_convert_fusion.4), channel_id=1, source_target_pairs={{0,5},{2,7},{4,1},{6,3},{8,13},{10,15},{12,9},{14,11},{1,0},{3,2},... | collective-permute-start | bytes 393224 | tf_op jit(solution)/shard_map/ppermute | solution.py:185
  39.5 5.2 %collective-permute-start.13 = (bf16[128,256]{1,0:T(8,128)(2,1)S(1)}, bf16[128,256]{1,0:T(8,128)(2,1)S(1)}, u32[]{:S(2)}, u32[]{:S(2)}) collective-permute-start(bf16[128,256]{1,0:T(8,128)(2,1)S(1)} %add_convert_fusion.8), channel_id=1, source_target_pairs={{1,8},{3,10},{5,12},{7,14},{9,0},{11,2},{13,4},{15,6},{0,1},{2,3},... | collective-permute-start | bytes 196616 | tf_op jit(solution)/shard_map/ppermute | solution.py:185
  40.3 4.5 %collective-permute-start.15 = (bf16[128,256]{1,0:T(8,128)(2,1)S(1)}, bf16[128,256]{1,0:T(8,128)(2,1)S(1)}, u32[]{:S(2)}, u32[]{:S(2)}) collective-permute-start(bf16[128,256]{1,0:T(8,128)(2,1)S(1)} %slice.130.r_3_), channel_id=1, source_target_pairs={{0,1},{1,0},{2,3},{3,2},{4,5},{5,4},{6,7},{7,6},{8,9},{9,8},{10,11... | collective-permute-start | bytes 196616 | tf_op jit(solution)/shard_map/ppermute | solution.py:189
  42.3 2.4 %collective-permute-start.18 = (bf16[128,768]{1,0:T(8,128)(2,1)S(1)}, bf16[128,768]{1,0:T(8,128)(2,1)S(1)}, u32[]{:S(2)}, u32[]{:S(2)}) collective-permute-start(bf16[128,768]{1,0:T(8,128)(2,1)S(1)} %get-tuple-element.49.r_8_.refs_4_), channel_id=1, source_target_pairs={{0,1},{1,0},{2,3},{3,2},{4,5},{5,4},{6,7},{7,6},{8,9},{9,8},{10,11... | collective-permute-start | bytes 589832 | tf_op jit(solution)/shard_map/ppermute | solution.py:189
  45.1 3.5 %collective-permute-start.19 = (bf16[384,256]{1,0:T(8,128)(2,1)S(1)}, bf16[384,256]{1,0:T(8,128)(2,1)S(1)}, u32[]{:S(2)}, u32[]{:S(2)}) collective-permute-start(bf16[384,256]{1,0:T(8,128)(2,1)S(1)} %shard_map.95), channel_id=1, source_target_pairs={{0,3},{2,1},{4,7},{6,5},{8,11},{10,9},{12,15},{14,13},{1,0},{3,2},... | collective-permute-start | bytes 589832 | tf_op jit(solution)/shard_map/ppermute | solution.py:185
  45.5 1.3 %collective-permute-start.14 = (bf16[128,256]{1,0:T(8,128)(2,1)S(1)}, bf16[128,256]{1,0:T(8,128)(2,1)S(1)}, u32[]{:S(2)}, u32[]{:S(2)}) collective-permute-start(bf16[128,256]{1,0:T(8,128)(2,1)S(1)} %collective-permute-done.13.r_1_.refs_0_), channel_id=1, source_target_pairs={{0,1},{1,0},{2,3},{3,2},{4,5},{5,4},{6,7},{7,6},{8,9},{9,8},{10,11... | collective-permute-start | bytes 196616 | tf_op jit(solution)/shard_map/ppermute | solution.py:189
  48.7 4.1 %collective-permute-start.20 = (bf16[256,256]{1,0:T(8,128)(2,1)S(1)}, bf16[256,256]{1,0:T(8,128)(2,1)S(1)}, u32[]{:S(2)}, u32[]{:S(2)}) collective-permute-start(bf16[256,256]{1,0:T(8,128)(2,1)S(1)} %pad_maximum_fusion.2), channel_id=1, source_target_pairs={{0,1},{1,0},{2,3},{3,2},{4,5},{5,4},{6,7},{7,6},{8,9},{9,8},{10,11... | collective-permute-start | bytes 393224 | tf_op jit(solution)/shard_map/ppermute | solution.py:189
  50.3 4.4 %collective-permute-start.21 = (bf16[256,256]{1,0:T(8,128)(2,1)S(1)}, bf16[256,256]{1,0:T(8,128)(2,1)S(1)}, u32[]{:S(2)}, u32[]{:S(2)}) collective-permute-start(bf16[256,256]{1,0:T(8,128)(2,1)S(1)} %add_convert_fusion.3), channel_id=1, source_target_pairs={{1,4},{3,6},{5,0},{7,2},{9,12},{11,14},{13,8},{15,10},{0,1},{2,3},... | collective-permute-start | bytes 393224 | tf_op jit(solution)/shard_map/ppermute | solution.py:185
  51.9 3.4 %collective-permute-start.25 = (bf16[128,768]{1,0:T(8,128)(2,1)S(1)}, bf16[128,768]{1,0:T(8,128)(2,1)S(1)}, u32[]{:S(2)}, u32[]{:S(2)}) collective-permute-start(bf16[128,768]{1,0:T(8,128)(2,1)S(1)} %get-tuple-element.53.r_8_.refs_4_), channel_id=1, source_target_pairs={{0,1},{1,0},{2,3},{3,2},{4,5},{5,4},{6,7},{7,6},{8,9},{9,8},{10,11... | collective-permute-start | bytes 589832 | tf_op jit(solution)/shard_map/ppermute | solution.py:189
  54.7 2.0 %collective-permute-start.22 = (bf16[128,256]{1,0:T(8,128)(2,1)S(1)}, bf16[128,256]{1,0:T(8,128)(2,1)S(1)}, u32[]{:S(2)}, u32[]{:S(2)}) collective-permute-start(bf16[128,256]{1,0:T(8,128)(2,1)S(1)} %add_convert_fusion.7), channel_id=1, source_target_pairs={{0,9},{2,11},{4,13},{6,15},{8,1},{10,3},{12,5},{14,7},{1,0},{3,2},... | collective-permute-start | bytes 196616 | tf_op jit(solution)/shard_map/ppermute | solution.py:185
  54.8 1.9 %collective-permute-start.24 = (bf16[128,256]{1,0:T(8,128)(2,1)S(1)}, bf16[128,256]{1,0:T(8,128)(2,1)S(1)}, u32[]{:S(2)}, u32[]{:S(2)}) collective-permute-start(bf16[128,256]{1,0:T(8,128)(2,1)S(1)} %slice.136.r_3_), channel_id=1, source_target_pairs={{0,1},{1,0},{2,3},{3,2},{4,5},{5,4},{6,7},{7,6},{8,9},{9,8},{10,11... | collective-permute-start | bytes 196616 | tf_op jit(solution)/shard_map/ppermute | solution.py:189
  57.0 6.5 %collective-permute-start.26 = (bf16[384,256]{1,0:T(8,128)(2,1)S(1)}, bf16[384,256]{1,0:T(8,128)(2,1)S(1)}, u32[]{:S(2)}, u32[]{:S(2)}) collective-permute-start(bf16[384,256]{1,0:T(8,128)(2,1)S(1)} %shard_map.99), channel_id=1, source_target_pairs={{1,2},{3,0},{5,6},{7,4},{9,10},{11,8},{13,14},{15,12},{0,1},{2,3},... | collective-permute-start | bytes 589832 | tf_op jit(solution)/shard_map/ppermute | solution.py:185
  59.1 1.3 %collective-permute-start.23 = (bf16[128,256]{1,0:T(8,128)(2,1)S(1)}, bf16[128,256]{1,0:T(8,128)(2,1)S(1)}, u32[]{:S(2)}, u32[]{:S(2)}) collective-permute-start(bf16[128,256]{1,0:T(8,128)(2,1)S(1)} %collective-permute-done.22.r_1_.refs_0_), channel_id=1, source_target_pairs={{0,1},{1,0},{2,3},{3,2},{4,5},{5,4},{6,7},{7,6},{8,9},{9,8},{10,11... | collective-permute-start | bytes 196616 | tf_op jit(solution)/shard_map/ppermute | solution.py:189
  63.6 1.4 %collective-permute-start.27 = (bf16[256,256]{1,0:T(8,128)(2,1)S(1)}, bf16[256,256]{1,0:T(8,128)(2,1)S(1)}, u32[]{:S(2)}, u32[]{:S(2)}) collective-permute-start(bf16[256,256]{1,0:T(8,128)(2,1)S(1)} %pad_maximum_fusion.3), channel_id=1, source_target_pairs={{0,1},{1,0},{2,3},{3,2},{4,5},{5,4},{6,7},{7,6},{8,9},{9,8},{10,11... | collective-permute-start | bytes 393224 | tf_op jit(solution)/shard_map/ppermute | solution.py:189
  63.7 2.7 %collective-permute-start.28 = (bf16[256,256]{1,0:T(8,128)(2,1)S(1)}, bf16[256,256]{1,0:T(8,128)(2,1)S(1)}, u32[]{:S(2)}, u32[]{:S(2)}) collective-permute-start(bf16[256,256]{1,0:T(8,128)(2,1)S(1)} %add_convert_fusion.2), channel_id=1, source_target_pairs={{0,5},{2,7},{4,1},{6,3},{8,13},{10,15},{12,9},{14,11},{1,0},{3,2},... | collective-permute-start | bytes 393224 | tf_op jit(solution)/shard_map/ppermute | solution.py:185
  66.5 4.6 %collective-permute-start.29 = (bf16[128,256]{1,0:T(8,128)(2,1)S(1)}, bf16[128,256]{1,0:T(8,128)(2,1)S(1)}, u32[]{:S(2)}, u32[]{:S(2)}) collective-permute-start(bf16[128,256]{1,0:T(8,128)(2,1)S(1)} %add_convert_fusion.6), channel_id=1, source_target_pairs={{1,8},{3,10},{5,12},{7,14},{9,0},{11,2},{13,4},{15,6},{0,1},{2,3},... | collective-permute-start | bytes 196616 | tf_op jit(solution)/shard_map/ppermute | solution.py:185
  68.8 3.3 %collective-permute-start.31 = (bf16[128,256]{1,0:T(8,128)(2,1)S(1)}, bf16[128,256]{1,0:T(8,128)(2,1)S(1)}, u32[]{:S(2)}, u32[]{:S(2)}) collective-permute-start(bf16[128,256]{1,0:T(8,128)(2,1)S(1)} %slice.142.r_1_), channel_id=1, source_target_pairs={{0,1},{1,0},{2,3},{3,2},{4,5},{5,4},{6,7},{7,6},{8,9},{9,8},{10,11... | collective-permute-start | bytes 196616 | tf_op jit(solution)/shard_map/ppermute | solution.py:189
  71.2 1.4 %collective-permute-start.30 = (bf16[128,256]{1,0:T(8,128)(2,1)S(1)}, bf16[128,256]{1,0:T(8,128)(2,1)S(1)}, u32[]{:S(2)}, u32[]{:S(2)}) collective-permute-start(bf16[128,256]{1,0:T(8,128)(2,1)S(1)} %collective-permute-done.29.r_1_), channel_id=1, source_target_pairs={{0,1},{1,0},{2,3},{3,2},{4,5},{5,4},{6,7},{7,6},{8,9},{9,8},{10,11... | collective-permute-start | bytes 196616 | tf_op jit(solution)/shard_map/ppermute | solution.py:189

commit v5 on v4

--- a/solution.py
+++ b/solution.py
@@ -8,6 +8,7 @@
 
 PASSES = 2
 LEVELS = 3
+CHUNKS = 4
 BF = jnp.bfloat16
 F32 = jnp.float32
 VMEM_BYTES = 12 * 2**20
@@ -17,9 +18,10 @@
     return lax.dot_general(a, b, (((ca,), (cb,)), ((), ())), preferred_element_type=F32)
 
 
-def call(kernel, outs, args, flops, scratch=(), far=0, room=VMEM_BYTES):
+def call(kernel, outs, args, flops, scratch=(), far=0):
     vm = pl.BlockSpec(memory_space=pltpu.VMEM)
     hbm = pl.BlockSpec(memory_space=pltpu.HBM)
+    near, distant = args[: len(args) - far], args[len(args) - far :]
     moved = sum(a.size * a.dtype.itemsize for a in args[1:]) + sum(o.size * o.dtype.itemsize for o in outs)
     return pl.pallas_call(
         kernel,
@@ -28,8 +30,8 @@
         out_specs=[vm] * len(outs),
         scratch_shapes=list(scratch),
         cost_estimate=pl.CostEstimate(flops=flops, bytes_accessed=moved, transcendentals=0),
-        compiler_params=pltpu.CompilerParams(vmem_limit_bytes=room),
-    )(*args)
+        compiler_params=pltpu.CompilerParams(vmem_limit_bytes=VMEM_BYTES),
+    )(*near, *(pltpu.with_memory_space_constraint(a, pltpu.HBM) for a in distant))
 
 
 def at(start, size):
@@ -38,14 +40,24 @@
 
 def first_kernel(place, *refs):
     sources, out, buffers, sems = refs[: LEVELS + 1], refs[LEVELS + 1], refs[LEVELS + 2 : -1], refs[-1]
-    copies = [pltpu.make_async_copy(a, b, sems.at[i]) for i, (a, b) in enumerate(zip(sources, buffers))]
-    for copy in copies:
-        copy.start()
-    copies[0].wait()
+    rows = sources[0].shape[0] // CHUNKS
+    copies = [
+        [
+            pltpu.make_async_copy(a.at[pl.ds(j * rows, rows), :], b.at[pl.ds(j * rows, rows), :], sems.at[i, j])
+            for j in range(CHUNKS)
+        ]
+        for i, (a, b) in enumerate(zip(sources, buffers))
+    ]
+    for group in copies:
+        for copy in group:
+            copy.start()
+    for copy in copies[0]:
+        copy.wait()
     zt = buffers[0][...].T
     c = zt.shape[0]
     for level in range(LEVELS):
-        copies[1 + level].wait()
+        for copy in copies[1 + level]:
+            copy.wait()
         out[level * c : (level + 1) * c, :] = mm(zt, buffers[1 + level][...], 1, 0).astype(BF)
 
 
@@ -233,10 +245,11 @@
 
     def prepared(factors):
         (sent,) = call(pack_kernel, [S((LEVELS * half, k), BF)], (place, *factors), 0, [sems((LEVELS,))], LEVELS)
+        other = over_rank(sent)
         full, gram = call(
             gram_kernel,
             [S((half, wide), BF), S((wide, wide), BF)],
-            (place, over_rank(sent), *factors),
+            (place, other, *factors),
             half * wide * wide * 3 // 2,
             [sems((LEVELS,))],
             LEVELS,
@@ -249,14 +262,14 @@
         [S((LEVELS * c, k), BF)],
         (place, probes, *uppers),
         2 * n * LEVELS * k * c,
-        [*buffers, sems((LEVELS + 1,))],
+        [*buffers, sems((LEVELS + 1, CHUNKS))],
         LEVELS + 1,
-        None,
     )
     (packed,) = call(join_kernel, [p_shape], (place, own, over_rank(own)), 0)
     packed, lowers, probes, leaves = lax.optimization_barrier((packed, lowers, probes, leaves))
     summed = packed
     lower, lower_gram = prepared(lowers)
+    upper, upper_gram = prepared(uppers)
     field_flops = 4 * half * wide * c
     y, s = call(start_kernel, [y_shape, s_shape], (place, probes, leaves, lower), field_flops // 2)
     applies = 2 * PASSES
@@ -283,9 +296,6 @@
         early = [f[0] if f[2] == source else f[1] for f in found]
         gram = lower_gram if flipped else upper_gram
         (packed,) = call(next_kernel, [p_shape], (place, *early, gram, s, there), 2 * wide * wide * c)
-        if step == 0:
-            packed, uppers = lax.optimization_barrier((packed, uppers))
-            upper, upper_gram = prepared(uppers)
         factor, after = (lower, upper) if flipped else (upper, lower)
         summed, q = call(
             lambda *r: again_kernel(holders, *r), [p_shape, s_shape], (place, *pieces, gram, s, there), 2 * wide * wide * c

time: 73.7 us -> 67.9 us (0.921)
  waiting for transfers between devices: 35.1 us -> 26.2 us
  Pallas kernels: 14.2 us -> 17.4 us
  local copies, waits for them, and re-layouts: 1.27 us -> 0.09 us
  starting transfers between devices: 21.7 us -> 22.8 us
    ppermute x12, waiting for transfers between devices: 24.3 us -> 18.3 us  [one_way(): return lax.ppermute(value, ('rows', 'cols', 'rank'), away + home)]
    pallas_call x22, Pallas kernels: 14.2 us -> 17.4 us  [call(): pl.pallas_call(kernel, out_shape=outs, in_specs=[pl.BlockSpec(memory_spac...]
    ppermute x20, waiting for transfers between devices: 10.8 us -> 7.88 us  [over_rank(): return lax.ppermute(value, 'rank', [(0, 1), (1, 0)])]
    ppermute x12, starting transfers between devices: 12.5 us -> 13.8 us  [one_way(): return lax.ppermute(value, ('rows', 'cols', 'rank'), away + home)]
    unnamed x18 -> x4, local copies, waits for them, and re-layouts: 1.19 us -> 0.01 us
  transfers between devices with their start and end apart: 32 -> 32, of which waited for: 21 -> 17; matrix products, arithmetic and copies ran while one was open for 1% -> 1% of each run, Pallas kernels for 9% -> 18%
where the time goes in v5:
time: 67.9 us; the launch traced here: 67.7 us
  waiting for transfers between devices  26.2 us (39%)
  starting transfers between devices  22.8 us (34%)
  Pallas kernels  17.4 us (26%)
  other arithmetic  0.86 us (1%)
    ppermute x12, waiting for transfers between devices, one_way(): return lax.ppermute(value, ('rows', 'cols', 'rank'), away + home)  18.3 us
    pallas_call x22, Pallas kernels, call(): pl.pallas_call(kernel, out_shape=outs, in_specs=[pl.BlockSpec(memory_spac...  17.4 us
    ppermute x12, starting transfers between devices, one_way(): return lax.ppermute(value, ('rows', 'cols', 'rank'), away + home)  13.8 us
    ppermute x20, starting transfers between devices, over_rank(): return lax.ppermute(value, 'rank', [(0, 1), (1, 0)])  9 us
    ppermute x20, waiting for transfers between devices, over_rank(): return lax.ppermute(value, 'rank', [(0, 1), (1, 0)])  7.88 us
  transfers between devices with their start and end apart: 32, of which 17 were waited for; matrix products, arithmetic and copies ran while one was open for 1% of the time, Pallas kernels for 18%

profile of v5, /device:TPU:0, one launch (start us, length us, event | category | flops | bytes accessed | tf_op | source)
XLA Modules:
  0.0 67.7 jit_solution(6843557694727223714)
XLA Ops:
  0.0 2.3 %shard_map.82.own = bf16[384,128]{1,0:T(8,128)(2,1)S(1)} custom-call(s32[1]{0:T(128)} %bitcast.place.r_0_, bf16[2048,128]{1,0:T(8,128)(2,1)} %z, bf16[2048,128]{1,0:T(8,128)(2,1)} %refs_0_.7, bf16[2048,128]{1,0:T(8,128)(2,1)} %refs_1_.7, bf16[2048,128]{1,0:T(8,128)(2,1)} %refs_2_.7), custom_call_target="tpu_custom_call" | custom-call | flops 201326592 | bytes 2195456 | tf_op jit(solution)/shard_map/pallas_call | solution.py:26
  2.3 0.6 collective-permute-start
  2.9 0.9 %collective-permute-done.other = bf16[384,128]{1,0:T(8,128)(2,1)S(1)} collective-permute-done((bf16[384,128]{1,0:T(8,128)(2,1)S(1)}, bf16[384,128]{1,0:T(8,128)(2,1)S(1)}, u32[]{:S(2)}, u32[]{:S(2)}) %collective-permute-start) | collective-permute-done | bytes 98336 | tf_op jit(solution)/shard_map/ppermute | solution.py:201
  3.9 1.1 %shard_map.85 = bf16[3072,128]{1,0:T(8,128)(2,1)S(1)} custom-call(s32[1]{0:T(128)} %bitcast.place.r_0_, bf16[2048,128]{1,0:T(8,128)(2,1)} %refs_0_.5, bf16[2048,128]{1,0:T(8,128)(2,1)} %refs_1_.5, bf16[2048,128]{1,0:T(8,128)(2,1)} %refs_2_.5), custom_call_target="tpu_custom_call" | custom-call | bytes 2359296 | tf_op jit(solution)/shard_map/pallas_call | solution.py:26
  5.0 0.4 collective-permute-start.7
  5.4 2.6 %collective-permute-start.1 = (bf16[384,256]{1,0:T(8,128)(2,1)S(1)}, bf16[384,256]{1,0:T(8,128)(2,1)S(1)}, u32[]{:S(2)}, u32[]{:S(2)}) collective-permute-start(bf16[384,256]{1,0:T(8,128)(2,1)S(1)} %shard_map.83.r_1_), channel_id=1, source_target_pairs={{0,3},{2,1},{4,7},{6,5},{8,11},{10,9},{12,15},{14,13},{1,0},{3,2},... | collective-permute-start | bytes 589832 | tf_op jit(solution)/shard_map/ppermute | solution.py:197
  8.0 2.2 %shard_map.86 = (bf16[1024,768]{1,0:T(8,128)(2,1)S(1)}, bf16[768,768]{1,0:T(8,128)(2,1)S(1)}) custom-call(s32[1]{0:T(128)} %bitcast.place.r_0_, bf16[3072,128]{1,0:T(8,128)(2,1)S(1)} %collective-permute-done.7.other, bf16[2048,128]{1,0:T(8,128)(2,1)} %refs_0_.5, bf16[2048,128]{1,0:T(8,128)(2,1)} %refs_1_.5, bf16[2048,128]{1,0:T(8,128)(2,1)} %refs_2_.5), custom_call_target="tpu_custom_call" | custom-call | flops 905969664 | bytes 5111808 | tf_op jit(solution)/shard_map/pallas_call | solution.py:26
  10.3 1.1 %shard_map.91 = bf16[3072,128]{1,0:T(8,128)(2,1)S(1)} custom-call(s32[1]{0:T(128)} %bitcast.place.r_0_, bf16[2048,128]{1,0:T(8,128)(2,1)} %refs_0_.7, bf16[2048,128]{1,0:T(8,128)(2,1)} %refs_1_.7, bf16[2048,128]{1,0:T(8,128)(2,1)} %refs_2_.7), custom_call_target="tpu_custom_call" | custom-call | bytes 2359296 | tf_op jit(solution)/shard_map/pallas_call | solution.py:26
  11.5 0.6 collective-permute-start.16
  12.2 0.5 collective-permute-start.3
  12.7 1.7 %collective-permute-done.2.r_3_ = bf16[256,256]{1,0:T(8,128)(2,1)S(1)} collective-permute-done((bf16[256,256]{1,0:T(8,128)(2,1)S(1)}, bf16[256,256]{1,0:T(8,128)(2,1)S(1)}, u32[]{:S(2)}, u32[]{:S(2)}) %collective-permute-start.2) | collective-permute-done | bytes 131104 | tf_op jit(solution)/shard_map/ppermute | solution.py:201
  14.5 2.7 %collective-permute-done.3 = bf16[256,256]{1,0:T(8,128)(2,1)S(1)} collective-permute-done((bf16[256,256]{1,0:T(8,128)(2,1)S(1)}, bf16[256,256]{1,0:T(8,128)(2,1)S(1)}, u32[]{:S(2)}, u32[]{:S(2)}) %collective-permute-start.3) | collective-permute-done | bytes 131104 | tf_op jit(solution)/shard_map/ppermute | solution.py:197
  17.2 1.7 %collective-permute-start.4 = (bf16[128,256]{1,0:T(8,128)(2,1)S(1)}, bf16[128,256]{1,0:T(8,128)(2,1)S(1)}, u32[]{:S(2)}, u32[]{:S(2)}) collective-permute-start(bf16[128,256]{1,0:T(8,128)(2,1)S(1)} %add_convert_fusion.9), channel_id=1, source_target_pairs={{0,9},{2,11},{4,13},{6,15},{8,1},{10,3},{12,5},{14,7},{1,0},{3,2},... | collective-permute-start | bytes 196616 | tf_op jit(solution)/shard_map/ppermute | solution.py:197
  19.0 2.3 %shard_map.92 = (bf16[1024,768]{1,0:T(8,128)(2,1)S(1)}, bf16[768,768]{1,0:T(8,128)(2,1)S(1)}) custom-call(s32[1]{0:T(128)} %bitcast.place.r_0_, bf16[3072,128]{1,0:T(8,128)(2,1)S(1)} %collective-permute-done.16.other, bf16[2048,128]{1,0:T(8,128)(2,1)} %refs_0_.7, bf16[2048,128]{1,0:T(8,128)(2,1)} %refs_1_.7, bf16[2048,128]{1,0:T(8,128)(2,1)} %refs_2_.7), custom_call_target="tpu_custom_call" | custom-call | flops 905969664 | bytes 5111808 | tf_op jit(solution)/shard_map/pallas_call | solution.py:26
  21.3 0.5 collective-permute-start.17
  21.8 0.7 %shard_map.87 = (f32[1024,128]{1,0:T(8,128)S(1)}, bf16[128,768]{1,0:T(8,128)(2,1)S(1)}) custom-call(s32[1]{0:T(128)} %bitcast.place.r_0_, bf16[2048,128]{1,0:T(8,128)(2,1)S(1)} %copy-done.1, bf16[4,256,256]{2,1,0:T(8,128)(2,1)S(1)} %copy-done, bf16[1024,768]{1,0:T(8,128)(2,1)S(1)} %get-tuple-element.34.after.r_2_.r_5_), custom_call_target="tpu_custom_call" | custom-call | flops 201326592 | bytes 3342336 | tf_op jit(solution)/shard_map/pallas_call | solution.py:26
  23.0 1.5 %collective-permute-done.9.r_9_.refs_5_ = bf16[128,768]{1,0:T(8,128)(2,1)S(1)} collective-permute-done((bf16[128,768]{1,0:T(8,128)(2,1)S(1)}, bf16[128,768]{1,0:T(8,128)(2,1)S(1)}, u32[]{:S(2)}, u32[]{:S(2)}) %collective-permute-start.9) | collective-permute-done | bytes 196640 | tf_op jit(solution)/shard_map/ppermute | solution.py:201
  24.9 0.4 collective-permute-start.10
  25.3 1.2 %collective-permute-start.5 = (bf16[128,256]{1,0:T(8,128)(2,1)S(1)}, bf16[128,256]{1,0:T(8,128)(2,1)S(1)}, u32[]{:S(2)}, u32[]{:S(2)}) collective-permute-start(bf16[128,256]{1,0:T(8,128)(2,1)S(1)} %collective-permute-done.4.r_1_.refs_0_), channel_id=1, source_target_pairs={{0,1},{1,0},{2,3},{3,2},{4,5},{5,4},{6,7},{7,6},{8,9},{9,8},{10,11... | collective-permute-start | bytes 196616 | tf_op jit(solution)/shard_map/ppermute | solution.py:201
  26.6 0.9 %collective-permute-done.5.r_2_ = bf16[128,256]{1,0:T(8,128)(2,1)S(1)} collective-permute-done((bf16[128,256]{1,0:T(8,128)(2,1)S(1)}, bf16[128,256]{1,0:T(8,128)(2,1)S(1)}, u32[]{:S(2)}, u32[]{:S(2)}) %collective-permute-start.5) | collective-permute-done | bytes 65568 | tf_op jit(solution)/shard_map/ppermute | solution.py:201
  27.5 0.4 shard_map.88
  27.8 2.2 %collective-permute-done.10.r_2_ = bf16[384,256]{1,0:T(8,128)(2,1)S(1)} collective-permute-done((bf16[384,256]{1,0:T(8,128)(2,1)S(1)}, bf16[384,256]{1,0:T(8,128)(2,1)S(1)}, u32[]{:S(2)}, u32[]{:S(2)}) %collective-permute-start.10) | collective-permute-done | bytes 196640 | tf_op jit(solution)/shard_map/ppermute | solution.py:197
  30.2 0.7 %collective-permute-start.12 = (bf16[256,256]{1,0:T(8,128)(2,1)S(1)}, bf16[256,256]{1,0:T(8,128)(2,1)S(1)}, u32[]{:S(2)}, u32[]{:S(2)}) collective-permute-start(bf16[256,256]{1,0:T(8,128)(2,1)S(1)} %add_convert_fusion.4), channel_id=1, source_target_pairs={{0,5},{2,7},{4,1},{6,3},{8,13},{10,15},{12,9},{14,11},{1,0},{3,2},... | collective-permute-start | bytes 393224 | tf_op jit(solution)/shard_map/ppermute | solution.py:197
  30.9 1.5 %shard_map.93 = (f32[1024,128]{1,0:T(8,128)S(1)}, bf16[128,768]{1,0:T(8,128)(2,1)S(1)}) custom-call(s32[1]{0:T(128)} %bitcast.place.r_0_, bf16[128,768]{1,0:T(8,128)(2,1)S(1)} %get-tuple-element.38.r_1_, bf16[1024,768]{1,0:T(8,128)(2,1)S(1)} %get-tuple-element.34.after.r_2_.r_5_, f32[1024,128]{1,0:T(8,128)S(1)} %get-tuple-element.39.r_3_, ...), custom_call_target="tpu_custom_call" | custom-call | flops 402653184 | bytes 5111808 | tf_op jit(solution)/shard_map/pallas_call | solution.py:26
  32.6 0.8 %collective-permute-done.12 = bf16[256,256]{1,0:T(8,128)(2,1)S(1)} collective-permute-done((bf16[256,256]{1,0:T(8,128)(2,1)S(1)}, bf16[256,256]{1,0:T(8,128)(2,1)S(1)}, u32[]{:S(2)}, u32[]{:S(2)}) %collective-permute-start.12) | collective-permute-done | bytes 131104 | tf_op jit(solution)/shard_map/ppermute | solution.py:197
  33.4 1.8 %collective-permute-start.13 = (bf16[128,256]{1,0:T(8,128)(2,1)S(1)}, bf16[128,256]{1,0:T(8,128)(2,1)S(1)}, u32[]{:S(2)}, u32[]{:S(2)}) collective-permute-start(bf16[128,256]{1,0:T(8,128)(2,1)S(1)} %add_convert_fusion.8), channel_id=1, source_target_pairs={{1,8},{3,10},{5,12},{7,14},{9,0},{11,2},{13,4},{15,6},{0,1},{2,3},... | collective-permute-start | bytes 196616 | tf_op jit(solution)/shard_map/ppermute | solution.py:197
  35.2 1.0 %collective-permute-start.15 = (bf16[128,256]{1,0:T(8,128)(2,1)S(1)}, bf16[128,256]{1,0:T(8,128)(2,1)S(1)}, u32[]{:S(2)}, u32[]{:S(2)}) collective-permute-start(bf16[128,256]{1,0:T(8,128)(2,1)S(1)} %slice.130.r_3_), channel_id=1, source_target_pairs={{0,1},{1,0},{2,3},{3,2},{4,5},{5,4},{6,7},{7,6},{8,9},{9,8},{10,11... | collective-permute-start | bytes 196616 | tf_op jit(solution)/shard_map/ppermute | solution.py:201
  36.5 1.8 %collective-permute-done.13.r_1_.refs_0_ = bf16[128,256]{1,0:T(8,128)(2,1)S(1)} collective-permute-done((bf16[128,256]{1,0:T(8,128)(2,1)S(1)}, bf16[128,256]{1,0:T(8,128)(2,1)S(1)}, u32[]{:S(2)}, u32[]{:S(2)}) %collective-permute-start.13) | collective-permute-done | bytes 65568 | tf_op jit(solution)/shard_map/ppermute | solution.py:197
  39.2 1.0 %collective-permute-done.14.r_2_ = bf16[128,256]{1,0:T(8,128)(2,1)S(1)} collective-permute-done((bf16[128,256]{1,0:T(8,128)(2,1)S(1)}, bf16[128,256]{1,0:T(8,128)(2,1)S(1)}, u32[]{:S(2)}, u32[]{:S(2)}) %collective-permute-start.14) | collective-permute-done | bytes 65568 | tf_op jit(solution)/shard_map/ppermute | solution.py:201
  40.6 1.6 %collective-permute-done.19.r_2_ = bf16[384,256]{1,0:T(8,128)(2,1)S(1)} collective-permute-done((bf16[384,256]{1,0:T(8,128)(2,1)S(1)}, bf16[384,256]{1,0:T(8,128)(2,1)S(1)}, u32[]{:S(2)}, u32[]{:S(2)}) %collective-permute-start.19) | collective-permute-done | bytes 196640 | tf_op jit(solution)/shard_map/ppermute | solution.py:197
  42.2 1.5 %collective-permute-start.20 = (bf16[256,256]{1,0:T(8,128)(2,1)S(1)}, bf16[256,256]{1,0:T(8,128)(2,1)S(1)}, u32[]{:S(2)}, u32[]{:S(2)}) collective-permute-start(bf16[256,256]{1,0:T(8,128)(2,1)S(1)} %pad_maximum_fusion.2), channel_id=1, source_target_pairs={{0,1},{1,0},{2,3},{3,2},{4,5},{5,4},{6,7},{7,6},{8,9},{9,8},{10,11... | collective-permute-start | bytes 393224 | tf_op jit(solution)/shard_map/ppermute | solution.py:201
  43.8 1.5 %shard_map.97 = (f32[1024,128]{1,0:T(8,128)S(1)}, bf16[128,768]{1,0:T(8,128)(2,1)S(1)}) custom-call(s32[1]{0:T(128)} %bitcast.place.r_0_, bf16[128,768]{1,0:T(8,128)(2,1)S(1)} %get-tuple-element.43.r_1_, bf16[1024,768]{1,0:T(8,128)(2,1)S(1)} %get-tuple-element.40.r_5_.r_2_.r_3_, f32[1024,128]{1,0:T(8,128)S(1)} %get-tuple-element.44.r_3_, ...), custom_call_target="tpu_custom_call" | custom-call | flops 402653184 | bytes 5111808 | tf_op jit(solution)/shard_map/pallas_call | solution.py:26
  45.4 1.7 %collective-permute-start.25 = (bf16[128,768]{1,0:T(8,128)(2,1)S(1)}, bf16[128,768]{1,0:T(8,128)(2,1)S(1)}, u32[]{:S(2)}, u32[]{:S(2)}) collective-permute-start(bf16[128,768]{1,0:T(8,128)(2,1)S(1)} %get-tuple-element.45.r_8_.refs_4_), channel_id=1, source_target_pairs={{0,1},{1,0},{2,3},{3,2},{4,5},{5,4},{6,7},{7,6},{8,9},{9,8},{10,11... | collective-permute-start | bytes 589832 | tf_op jit(solution)/shard_map/ppermute | solution.py:201
  47.2 1.1 %collective-permute-done.21 = bf16[256,256]{1,0:T(8,128)(2,1)S(1)} collective-permute-done((bf16[256,256]{1,0:T(8,128)(2,1)S(1)}, bf16[256,256]{1,0:T(8,128)(2,1)S(1)}, u32[]{:S(2)}, u32[]{:S(2)}) %collective-permute-start.21) | collective-permute-done | bytes 131104 | tf_op jit(solution)/shard_map/ppermute | solution.py:197
  48.4 0.4 collective-permute-start.24
  48.8 1.5 %collective-permute-done.22.r_1_.refs_0_ = bf16[128,256]{1,0:T(8,128)(2,1)S(1)} collective-permute-done((bf16[128,256]{1,0:T(8,128)(2,1)S(1)}, bf16[128,256]{1,0:T(8,128)(2,1)S(1)}, u32[]{:S(2)}, u32[]{:S(2)}) %collective-permute-start.22) | collective-permute-done | bytes 65568 | tf_op jit(solution)/shard_map/ppermute | solution.py:197
  50.6 3.1 %collective-permute-start.26 = (bf16[384,256]{1,0:T(8,128)(2,1)S(1)}, bf16[384,256]{1,0:T(8,128)(2,1)S(1)}, u32[]{:S(2)}, u32[]{:S(2)}) collective-permute-start(bf16[384,256]{1,0:T(8,128)(2,1)S(1)} %shard_map.99), channel_id=1, source_target_pairs={{1,2},{3,0},{5,6},{7,4},{9,10},{11,8},{13,14},{15,12},{0,1},{2,3},... | collective-permute-start | bytes 589832 | tf_op jit(solution)/shard_map/ppermute | solution.py:197
  53.8 1.2 %collective-permute-done.23.r_2_ = bf16[128,256]{1,0:T(8,128)(2,1)S(1)} collective-permute-done((bf16[128,256]{1,0:T(8,128)(2,1)S(1)}, bf16[128,256]{1,0:T(8,128)(2,1)S(1)}, u32[]{:S(2)}, u32[]{:S(2)}) %collective-permute-start.23) | collective-permute-done | bytes 65568 | tf_op jit(solution)/shard_map/ppermute | solution.py:201
  54.9 0.4 shard_map.98
  55.3 1.9 %collective-permute-done.26.r_2_ = bf16[384,256]{1,0:T(8,128)(2,1)S(1)} collective-permute-done((bf16[384,256]{1,0:T(8,128)(2,1)S(1)}, bf16[384,256]{1,0:T(8,128)(2,1)S(1)}, u32[]{:S(2)}, u32[]{:S(2)}) %collective-permute-start.26) | collective-permute-done | bytes 196640 | tf_op jit(solution)/shard_map/ppermute | solution.py:197
  57.3 0.8 %collective-permute-start.28 = (bf16[256,256]{1,0:T(8,128)(2,1)S(1)}, bf16[256,256]{1,0:T(8,128)(2,1)S(1)}, u32[]{:S(2)}, u32[]{:S(2)}) collective-permute-start(bf16[256,256]{1,0:T(8,128)(2,1)S(1)} %add_convert_fusion.2), channel_id=1, source_target_pairs={{0,5},{2,7},{4,1},{6,3},{8,13},{10,15},{12,9},{14,11},{1,0},{3,2},... | collective-permute-start | bytes 393224 | tf_op jit(solution)/shard_map/ppermute | solution.py:197
  58.1 0.5 collective-permute-done.27.r_3_
  58.7 2.0 %collective-permute-done.28 = bf16[256,256]{1,0:T(8,128)(2,1)S(1)} collective-permute-done((bf16[256,256]{1,0:T(8,128)(2,1)S(1)}, bf16[256,256]{1,0:T(8,128)(2,1)S(1)}, u32[]{:S(2)}, u32[]{:S(2)}) %collective-permute-start.28) | collective-permute-done | bytes 131104 | tf_op jit(solution)/shard_map/ppermute | solution.py:197
  60.6 1.7 %collective-permute-start.29 = (bf16[128,256]{1,0:T(8,128)(2,1)S(1)}, bf16[128,256]{1,0:T(8,128)(2,1)S(1)}, u32[]{:S(2)}, u32[]{:S(2)}) collective-permute-start(bf16[128,256]{1,0:T(8,128)(2,1)S(1)} %add_convert_fusion.6), channel_id=1, source_target_pairs={{1,8},{3,10},{5,12},{7,14},{9,0},{11,2},{13,4},{15,6},{0,1},{2,3},... | collective-permute-start | bytes 196616 | tf_op jit(solution)/shard_map/ppermute | solution.py:197
  62.5 2.7 %collective-permute-done.29.r_1_ = bf16[128,256]{1,0:T(8,128)(2,1)S(1)} collective-permute-done((bf16[128,256]{1,0:T(8,128)(2,1)S(1)}, bf16[128,256]{1,0:T(8,128)(2,1)S(1)}, u32[]{:S(2)}, u32[]{:S(2)}) %collective-permute-start.29) | collective-permute-done | bytes 65568 | tf_op jit(solution)/shard_map/ppermute | solution.py:197
  65.3 0.9 %shard_map.101.r_6_ = f32[1024,128]{1,0:T(8,128)S(1)} custom-call(s32[1]{0:T(128)} %bitcast.place.r_0_, bf16[128,768]{1,0:T(8,128)(2,1)S(1)} %get-tuple-element.47.r_1_, bf16[1024,768]{1,0:T(8,128)(2,1)S(1)} %get-tuple-element.34.after.r_2_.r_5_, f32[1024,128]{1,0:T(8,128)S(1)} %get-tuple-element.48.r_3_, bf16[4,256,256]{2,1,0:T(8,128)(2,1)S(1)} %copy-done), custom_call_target="tpu_custom_call" | custom-call | flops 201326592 | bytes 3342336 | tf_op jit(solution)/shard_map/pallas_call | solution.py:26
  66.2 0.5 shard_map.102.r_4_
  66.7 1.0 %shard_map.103 = bf16[1024,128]{1,0:T(8,128)(2,1)} custom-call(s32[1]{0:T(128)} %bitcast.place.r_0_, bf16[128,256]{1,0:T(8,128)(2,1)S(1)} %collective-permute-done.29.r_1_, bf16[128,256]{1,0:T(8,128)(2,1)S(1)} %collective-permute-done.30.r_2_, bf16[1024,768]{1,0:T(8,128)(2,1)S(1)} %get-tuple-element.40.r_5_.r_2_.r_3_, f32[1024,128]{1,0:T(8,128)S(1)} %shard_map.102.r_4_), custom_call_target="tpu_custom_call" | custom-call | flops 67108864 | bytes 2490368 | tf_op jit(solution)/shard_map/pallas_call | solution.py:26
  (68 shorter events, 4.1 us)
Async XLA Ops:
  2.3 1.5 %collective-permute-start = (bf16[384,128]{1,0:T(8,128)(2,1)S(1)}, bf16[384,128]{1,0:T(8,128)(2,1)S(1)}, u32[]{:S(2)}, u32[]{:S(2)}) collective-permute-start(bf16[384,128]{1,0:T(8,128)(2,1)S(1)} %shard_map.82.own), channel_id=1, source_target_pairs={{0,1},{1,0},{2,3},{3,2},{4,5},{5,4},{6,7},{7,6},{8,9},{9,8},{10,11... | collective-permute-start | bytes 294920 | tf_op jit(solution)/shard_map/ppermute | solution.py:201
  5.0 3.0 %collective-permute-start.7 = (bf16[3072,128]{1,0:T(8,128)(2,1)S(1)}, bf16[3072,128]{1,0:T(8,128)(2,1)S(1)}, u32[]{:S(2)}, u32[]{:S(2)}) collective-permute-start(bf16[3072,128]{1,0:T(8,128)(2,1)S(1)} %shard_map.85), channel_id=1, source_target_pairs={{0,1},{1,0},{2,3},{3,2},{4,5},{5,4},{6,7},{7,6},{8,9},{9,8},{10,11... | collective-permute-start | bytes 2359304 | tf_op jit(solution)/shard_map/ppermute | solution.py:201
  5.4 6.6 %collective-permute-start.1 = (bf16[384,256]{1,0:T(8,128)(2,1)S(1)}, bf16[384,256]{1,0:T(8,128)(2,1)S(1)}, u32[]{:S(2)}, u32[]{:S(2)}) collective-permute-start(bf16[384,256]{1,0:T(8,128)(2,1)S(1)} %shard_map.83.r_1_), channel_id=1, source_target_pairs={{0,3},{2,1},{4,7},{6,5},{8,11},{10,9},{12,15},{14,13},{1,0},{3,2},... | collective-permute-start | bytes 589832 | tf_op jit(solution)/shard_map/ppermute | solution.py:197
  10.2 12.5 %collective-permute-start.8 = (bf16[768,768]{1,0:T(8,128)(2,1)S(1)}, bf16[768,768]{1,0:T(8,128)(2,1)S(1)}, u32[]{:S(2)}, u32[]{:S(2)}) collective-permute-start(bf16[768,768]{1,0:T(8,128)(2,1)S(1)} %get-tuple-element.31), channel_id=1, source_target_pairs={{0,1},{1,0},{2,3},{3,2},{4,5},{5,4},{6,7},{7,6},{8,9},{9,8},{10,11... | collective-permute-start | bytes 3538952 | tf_op jit(solution)/shard_map/ppermute | solution.py:201
  11.5 7.6 %collective-permute-start.16 = (bf16[3072,128]{1,0:T(8,128)(2,1)S(1)}, bf16[3072,128]{1,0:T(8,128)(2,1)S(1)}, u32[]{:S(2)}, u32[]{:S(2)}) collective-permute-start(bf16[3072,128]{1,0:T(8,128)(2,1)S(1)} %shard_map.91), channel_id=1, source_target_pairs={{0,1},{1,0},{2,3},{3,2},{4,5},{5,4},{6,7},{7,6},{8,9},{9,8},{10,11... | collective-permute-start | bytes 2359304 | tf_op jit(solution)/shard_map/ppermute | solution.py:201
  12.0 2.4 %collective-permute-start.2 = (bf16[256,256]{1,0:T(8,128)(2,1)S(1)}, bf16[256,256]{1,0:T(8,128)(2,1)S(1)}, u32[]{:S(2)}, u32[]{:S(2)}) collective-permute-start(bf16[256,256]{1,0:T(8,128)(2,1)S(1)} %pad_maximum_fusion), channel_id=1, source_target_pairs={{0,1},{1,0},{2,3},{3,2},{4,5},{5,4},{6,7},{7,6},{8,9},{9,8},{10,11... | collective-permute-start | bytes 393224 | tf_op jit(solution)/shard_map/ppermute | solution.py:201
  12.2 5.0 %collective-permute-start.3 = (bf16[256,256]{1,0:T(8,128)(2,1)S(1)}, bf16[256,256]{1,0:T(8,128)(2,1)S(1)}, u32[]{:S(2)}, u32[]{:S(2)}) collective-permute-start(bf16[256,256]{1,0:T(8,128)(2,1)S(1)} %add_convert_fusion.5), channel_id=1, source_target_pairs={{1,4},{3,6},{5,0},{7,2},{9,12},{11,14},{13,8},{15,10},{0,1},{2,3},... | collective-permute-start | bytes 393224 | tf_op jit(solution)/shard_map/ppermute | solution.py:197
  17.2 5.8 %collective-permute-start.4 = (bf16[128,256]{1,0:T(8,128)(2,1)S(1)}, bf16[128,256]{1,0:T(8,128)(2,1)S(1)}, u32[]{:S(2)}, u32[]{:S(2)}) collective-permute-start(bf16[128,256]{1,0:T(8,128)(2,1)S(1)} %add_convert_fusion.9), channel_id=1, source_target_pairs={{0,9},{2,11},{4,13},{6,15},{8,1},{10,3},{12,5},{14,7},{1,0},{3,2},... | collective-permute-start | bytes 196616 | tf_op jit(solution)/shard_map/ppermute | solution.py:197
  18.9 2.9 %copy-start = (bf16[4,256,256]{2,1,0:T(8,128)(2,1)S(1)}, bf16[4,256,256]{2,1,0:T(8,128)(2,1)}, u32[]{:S(2)}) copy-start(bf16[4,256,256]{2,1,0:T(8,128)(2,1)} %r_4_.2) | copy-start | bytes 1572868
  18.9 2.9 %copy-start.1 = (bf16[2048,128]{1,0:T(8,128)(2,1)S(1)}, bf16[2048,128]{1,0:T(8,128)(2,1)}, u32[]{:S(2)}) copy-start(bf16[2048,128]{1,0:T(8,128)(2,1)} %z) | copy-start | bytes 1572868
  19.0 4.1 %collective-permute-start.6 = (bf16[128,256]{1,0:T(8,128)(2,1)S(1)}, bf16[128,256]{1,0:T(8,128)(2,1)S(1)}, u32[]{:S(2)}, u32[]{:S(2)}) collective-permute-start(bf16[128,256]{1,0:T(8,128)(2,1)S(1)} %slice.124.r_3_), channel_id=1, source_target_pairs={{0,1},{1,0},{2,3},{3,2},{4,5},{5,4},{6,7},{7,6},{8,9},{9,8},{10,11... | collective-permute-start | bytes 196616 | tf_op jit(solution)/shard_map/ppermute | solution.py:201
  21.3 14.8 %collective-permute-start.17 = (bf16[768,768]{1,0:T(8,128)(2,1)S(1)}, bf16[768,768]{1,0:T(8,128)(2,1)S(1)}, u32[]{:S(2)}, u32[]{:S(2)}) collective-permute-start(bf16[768,768]{1,0:T(8,128)(2,1)S(1)} %get-tuple-element.37), channel_id=1, source_target_pairs={{0,1},{1,0},{2,3},{3,2},{4,5},{5,4},{6,7},{7,6},{8,9},{9,8},{10,11... | collective-permute-start | bytes 3538952 | tf_op jit(solution)/shard_map/ppermute | solution.py:201
  22.6 2.0 %collective-permute-start.9 = (bf16[128,768]{1,0:T(8,128)(2,1)S(1)}, bf16[128,768]{1,0:T(8,128)(2,1)S(1)}, u32[]{:S(2)}, u32[]{:S(2)}) collective-permute-start(bf16[128,768]{1,0:T(8,128)(2,1)S(1)} %get-tuple-element.35.r_8_.refs_4_), channel_id=1, source_target_pairs={{0,1},{1,0},{2,3},{3,2},{4,5},{5,4},{6,7},{7,6},{8,9},{9,8},{10,11... | collective-permute-start | bytes 589832 | tf_op jit(solution)/shard_map/ppermute | solution.py:201
  24.9 5.1 %collective-permute-start.10 = (bf16[384,256]{1,0:T(8,128)(2,1)S(1)}, bf16[384,256]{1,0:T(8,128)(2,1)S(1)}, u32[]{:S(2)}, u32[]{:S(2)}) collective-permute-start(bf16[384,256]{1,0:T(8,128)(2,1)S(1)} %shard_map.89), channel_id=1, source_target_pairs={{1,2},{3,0},{5,6},{7,4},{9,10},{11,8},{13,14},{15,12},{0,1},{2,3},... | collective-permute-start | bytes 589832 | tf_op jit(solution)/shard_map/ppermute | solution.py:197
  25.3 2.1 %collective-permute-start.5 = (bf16[128,256]{1,0:T(8,128)(2,1)S(1)}, bf16[128,256]{1,0:T(8,128)(2,1)S(1)}, u32[]{:S(2)}, u32[]{:S(2)}) collective-permute-start(bf16[128,256]{1,0:T(8,128)(2,1)S(1)} %collective-permute-done.4.r_1_.refs_0_), channel_id=1, source_target_pairs={{0,1},{1,0},{2,3},{3,2},{4,5},{5,4},{6,7},{7,6},{8,9},{9,8},{10,11... | collective-permute-start | bytes 196616 | tf_op jit(solution)/shard_map/ppermute | solution.py:201
  30.1 2.4 %collective-permute-start.11 = (bf16[256,256]{1,0:T(8,128)(2,1)S(1)}, bf16[256,256]{1,0:T(8,128)(2,1)S(1)}, u32[]{:S(2)}, u32[]{:S(2)}) collective-permute-start(bf16[256,256]{1,0:T(8,128)(2,1)S(1)} %pad_maximum_fusion.1), channel_id=1, source_target_pairs={{0,1},{1,0},{2,3},{3,2},{4,5},{5,4},{6,7},{7,6},{8,9},{9,8},{10,11... | collective-permute-start | bytes 393224 | tf_op jit(solution)/shard_map/ppermute | solution.py:201
  30.2 3.2 %collective-permute-start.12 = (bf16[256,256]{1,0:T(8,128)(2,1)S(1)}, bf16[256,256]{1,0:T(8,128)(2,1)S(1)}, u32[]{:S(2)}, u32[]{:S(2)}) collective-permute-start(bf16[256,256]{1,0:T(8,128)(2,1)S(1)} %add_convert_fusion.4), channel_id=1, source_target_pairs={{0,5},{2,7},{4,1},{6,3},{8,13},{10,15},{12,9},{14,11},{1,0},{3,2},... | collective-permute-start | bytes 393224 | tf_op jit(solution)/shard_map/ppermute | solution.py:197
  32.4 4.0 %collective-permute-start.18 = (bf16[128,768]{1,0:T(8,128)(2,1)S(1)}, bf16[128,768]{1,0:T(8,128)(2,1)S(1)}, u32[]{:S(2)}, u32[]{:S(2)}) collective-permute-start(bf16[128,768]{1,0:T(8,128)(2,1)S(1)} %get-tuple-element.41.r_8_.refs_4_), channel_id=1, source_target_pairs={{0,1},{1,0},{2,3},{3,2},{4,5},{5,4},{6,7},{7,6},{8,9},{9,8},{10,11... | collective-permute-start | bytes 589832 | tf_op jit(solution)/shard_map/ppermute | solution.py:201
  33.4 4.9 %collective-permute-start.13 = (bf16[128,256]{1,0:T(8,128)(2,1)S(1)}, bf16[128,256]{1,0:T(8,128)(2,1)S(1)}, u32[]{:S(2)}, u32[]{:S(2)}) collective-permute-start(bf16[128,256]{1,0:T(8,128)(2,1)S(1)} %add_convert_fusion.8), channel_id=1, source_target_pairs={{1,8},{3,10},{5,12},{7,14},{9,0},{11,2},{13,4},{15,6},{0,1},{2,3},... | collective-permute-start | bytes 196616 | tf_op jit(solution)/shard_map/ppermute | solution.py:197
  35.2 3.1 %collective-permute-start.15 = (bf16[128,256]{1,0:T(8,128)(2,1)S(1)}, bf16[128,256]{1,0:T(8,128)(2,1)S(1)}, u32[]{:S(2)}, u32[]{:S(2)}) collective-permute-start(bf16[128,256]{1,0:T(8,128)(2,1)S(1)} %slice.130.r_3_), channel_id=1, source_target_pairs={{0,1},{1,0},{2,3},{3,2},{4,5},{5,4},{6,7},{7,6},{8,9},{9,8},{10,11... | collective-permute-start | bytes 196616 | tf_op jit(solution)/shard_map/ppermute | solution.py:201
  38.6 3.5 %collective-permute-start.19 = (bf16[384,256]{1,0:T(8,128)(2,1)S(1)}, bf16[384,256]{1,0:T(8,128)(2,1)S(1)}, u32[]{:S(2)}, u32[]{:S(2)}) collective-permute-start(bf16[384,256]{1,0:T(8,128)(2,1)S(1)} %shard_map.95), channel_id=1, source_target_pairs={{0,3},{2,1},{4,7},{6,5},{8,11},{10,9},{12,15},{14,13},{1,0},{3,2},... | collective-permute-start | bytes 589832 | tf_op jit(solution)/shard_map/ppermute | solution.py:197
  39.0 1.3 %collective-permute-start.14 = (bf16[128,256]{1,0:T(8,128)(2,1)S(1)}, bf16[128,256]{1,0:T(8,128)(2,1)S(1)}, u32[]{:S(2)}, u32[]{:S(2)}) collective-permute-start(bf16[128,256]{1,0:T(8,128)(2,1)S(1)} %collective-permute-done.13.r_1_.refs_0_), channel_id=1, source_target_pairs={{0,1},{1,0},{2,3},{3,2},{4,5},{5,4},{6,7},{7,6},{8,9},{9,8},{10,11... | collective-permute-start | bytes 196616 | tf_op jit(solution)/shard_map/ppermute | solution.py:201
  42.2 4.9 %collective-permute-start.20 = (bf16[256,256]{1,0:T(8,128)(2,1)S(1)}, bf16[256,256]{1,0:T(8,128)(2,1)S(1)}, u32[]{:S(2)}, u32[]{:S(2)}) collective-permute-start(bf16[256,256]{1,0:T(8,128)(2,1)S(1)} %pad_maximum_fusion.2), channel_id=1, source_target_pairs={{0,1},{1,0},{2,3},{3,2},{4,5},{5,4},{6,7},{7,6},{8,9},{9,8},{10,11... | collective-permute-start | bytes 393224 | tf_op jit(solution)/shard_map/ppermute | solution.py:201
  43.8 4.4 %collective-permute-start.21 = (bf16[256,256]{1,0:T(8,128)(2,1)S(1)}, bf16[256,256]{1,0:T(8,128)(2,1)S(1)}, u32[]{:S(2)}, u32[]{:S(2)}) collective-permute-start(bf16[256,256]{1,0:T(8,128)(2,1)S(1)} %add_convert_fusion.3), channel_id=1, source_target_pairs={{1,4},{3,6},{5,0},{7,2},{9,12},{11,14},{13,8},{15,10},{0,1},{2,3},... | collective-permute-start | bytes 393224 | tf_op jit(solution)/shard_map/ppermute | solution.py:197
  45.4 3.4 %collective-permute-start.25 = (bf16[128,768]{1,0:T(8,128)(2,1)S(1)}, bf16[128,768]{1,0:T(8,128)(2,1)S(1)}, u32[]{:S(2)}, u32[]{:S(2)}) collective-permute-start(bf16[128,768]{1,0:T(8,128)(2,1)S(1)} %get-tuple-element.45.r_8_.refs_4_), channel_id=1, source_target_pairs={{0,1},{1,0},{2,3},{3,2},{4,5},{5,4},{6,7},{7,6},{8,9},{9,8},{10,11... | collective-permute-start | bytes 589832 | tf_op jit(solution)/shard_map/ppermute | solution.py:201
  48.2 2.0 %collective-permute-start.22 = (bf16[128,256]{1,0:T(8,128)(2,1)S(1)}, bf16[128,256]{1,0:T(8,128)(2,1)S(1)}, u32[]{:S(2)}, u32[]{:S(2)}) collective-permute-start(bf16[128,256]{1,0:T(8,128)(2,1)S(1)} %add_convert_fusion.7), channel_id=1, source_target_pairs={{0,9},{2,11},{4,13},{6,15},{8,1},{10,3},{12,5},{14,7},{1,0},{3,2},... | collective-permute-start | bytes 196616 | tf_op jit(solution)/shard_map/ppermute | solution.py:197
  48.4 1.9 %collective-permute-start.24 = (bf16[128,256]{1,0:T(8,128)(2,1)S(1)}, bf16[128,256]{1,0:T(8,128)(2,1)S(1)}, u32[]{:S(2)}, u32[]{:S(2)}) collective-permute-start(bf16[128,256]{1,0:T(8,128)(2,1)S(1)} %slice.136.r_3_), channel_id=1, source_target_pairs={{0,1},{1,0},{2,3},{3,2},{4,5},{5,4},{6,7},{7,6},{8,9},{9,8},{10,11... | collective-permute-start | bytes 196616 | tf_op jit(solution)/shard_map/ppermute | solution.py:201
  50.6 6.6 %collective-permute-start.26 = (bf16[384,256]{1,0:T(8,128)(2,1)S(1)}, bf16[384,256]{1,0:T(8,128)(2,1)S(1)}, u32[]{:S(2)}, u32[]{:S(2)}) collective-permute-start(bf16[384,256]{1,0:T(8,128)(2,1)S(1)} %shard_map.99), channel_id=1, source_target_pairs={{1,2},{3,0},{5,6},{7,4},{9,10},{11,8},{13,14},{15,12},{0,1},{2,3},... | collective-permute-start | bytes 589832 | tf_op jit(solution)/shard_map/ppermute | solution.py:197
  53.7 1.3 %collective-permute-start.23 = (bf16[128,256]{1,0:T(8,128)(2,1)S(1)}, bf16[128,256]{1,0:T(8,128)(2,1)S(1)}, u32[]{:S(2)}, u32[]{:S(2)}) collective-permute-start(bf16[128,256]{1,0:T(8,128)(2,1)S(1)} %collective-permute-done.22.r_1_.refs_0_), channel_id=1, source_target_pairs={{0,1},{1,0},{2,3},{3,2},{4,5},{5,4},{6,7},{7,6},{8,9},{9,8},{10,11... | collective-permute-start | bytes 196616 | tf_op jit(solution)/shard_map/ppermute | solution.py:201
  57.2 1.4 %collective-permute-start.27 = (bf16[256,256]{1,0:T(8,128)(2,1)S(1)}, bf16[256,256]{1,0:T(8,128)(2,1)S(1)}, u32[]{:S(2)}, u32[]{:S(2)}) collective-permute-start(bf16[256,256]{1,0:T(8,128)(2,1)S(1)} %pad_maximum_fusion.3), channel_id=1, source_target_pairs={{0,1},{1,0},{2,3},{3,2},{4,5},{5,4},{6,7},{7,6},{8,9},{9,8},{10,11... | collective-permute-start | bytes 393224 | tf_op jit(solution)/shard_map/ppermute | solution.py:201
  57.3 3.3 %collective-permute-start.28 = (bf16[256,256]{1,0:T(8,128)(2,1)S(1)}, bf16[256,256]{1,0:T(8,128)(2,1)S(1)}, u32[]{:S(2)}, u32[]{:S(2)}) collective-permute-start(bf16[256,256]{1,0:T(8,128)(2,1)S(1)} %add_convert_fusion.2), channel_id=1, source_target_pairs={{0,5},{2,7},{4,1},{6,3},{8,13},{10,15},{12,9},{14,11},{1,0},{3,2},... | collective-permute-start | bytes 393224 | tf_op jit(solution)/shard_map/ppermute | solution.py:197
  60.6 4.6 %collective-permute-start.29 = (bf16[128,256]{1,0:T(8,128)(2,1)S(1)}, bf16[128,256]{1,0:T(8,128)(2,1)S(1)}, u32[]{:S(2)}, u32[]{:S(2)}) collective-permute-start(bf16[128,256]{1,0:T(8,128)(2,1)S(1)} %add_convert_fusion.6), channel_id=1, source_target_pairs={{1,8},{3,10},{5,12},{7,14},{9,0},{11,2},{13,4},{15,6},{0,1},{2,3},... | collective-permute-start | bytes 196616 | tf_op jit(solution)/shard_map/ppermute | solution.py:197
  62.4 3.8 %collective-permute-start.31 = (bf16[128,256]{1,0:T(8,128)(2,1)S(1)}, bf16[128,256]{1,0:T(8,128)(2,1)S(1)}, u32[]{:S(2)}, u32[]{:S(2)}) collective-permute-start(bf16[128,256]{1,0:T(8,128)(2,1)S(1)} %slice.142.r_1_), channel_id=1, source_target_pairs={{0,1},{1,0},{2,3},{3,2},{4,5},{5,4},{6,7},{7,6},{8,9},{9,8},{10,11... | collective-permute-start | bytes 196616 | tf_op jit(solution)/shard_map/ppermute | solution.py:201
  65.3 1.4 %collective-permute-start.30 = (bf16[128,256]{1,0:T(8,128)(2,1)S(1)}, bf16[128,256]{1,0:T(8,128)(2,1)S(1)}, u32[]{:S(2)}, u32[]{:S(2)}) collective-permute-start(bf16[128,256]{1,0:T(8,128)(2,1)S(1)} %collective-permute-done.29.r_1_), channel_id=1, source_target_pairs={{0,1},{1,0},{2,3},{3,2},{4,5},{5,4},{6,7},{7,6},{8,9},{9,8},{10,11... | collective-permute-start | bytes 196616 | tf_op jit(solution)/shard_map/ppermute | solution.py:201

commit v6 on v5

v6 whole, which is shorter than its diff:
```python
import jax
import jax.numpy as jnp
from jax import lax
from jax.experimental import pallas as pl
from jax.experimental.pallas import tpu as pltpu
from jax.sharding import PartitionSpec as P


PASSES = 2
LEVELS = 3
CHUNKS = 4
BLOCKS = tuple((i, j) for i in range(LEVELS) for j in range(i + 1))
BF = jnp.bfloat16
F32 = jnp.float32
VMEM_BYTES = 12 * 2**20


def mm(a, b, ca, cb):
    return lax.dot_general(a, b, (((ca,), (cb,)), ((), ())), preferred_element_type=F32)


def call(kernel, outs, args, flops, scratch=(), far=0):
    vm = pl.BlockSpec(memory_space=pltpu.VMEM)
    hbm = pl.BlockSpec(memory_space=pltpu.HBM)
    near, distant = args[: len(args) - far], args[len(args) - far :]
    moved = sum(a.size * a.dtype.itemsize for a in args[1:]) + sum(o.size * o.dtype.itemsize for o in outs)
    return pl.pallas_call(
        kernel,
        out_shape=outs,
        in_specs=[pl.BlockSpec(memory_space=pltpu.SMEM)] + [vm] * (len(args) - 1 - far) + [hbm] * far,
        out_specs=[vm] * len(outs),
        scratch_shapes=list(scratch),
        cost_estimate=pl.CostEstimate(flops=flops, bytes_accessed=moved, transcendentals=0),
        compiler_params=pltpu.CompilerParams(vmem_limit_bytes=VMEM_BYTES),
    )(*near, *(pltpu.with_memory_space_constraint(a, pltpu.HBM) for a in distant))


def at(start, size):
    return pl.ds(pl.multiple_of(start, size), size)


def first_kernel(place, *refs):
    sources, out, buffers, sems = refs[: LEVELS + 1], refs[LEVELS + 1], refs[LEVELS + 2 : -1], refs[-1]
    rows = sources[0].shape[0] // CHUNKS
    copies = [
        [
            pltpu.make_async_copy(a.at[pl.ds(j * rows, rows), :], b.at[pl.ds(j * rows, rows), :], sems.at[i, j])
            for j in range(CHUNKS)
        ]
        for i, (a, b) in enumerate(zip(sources, buffers))
    ]
    for group in copies:
        for copy in group:
            copy.start()
    for copy in copies[0]:
        copy.wait()
    zt = buffers[0][...].T
    c = zt.shape[0]
    for level in range(LEVELS):
        for copy in copies[1 + level]:
            copy.wait()
        out[level * c : (level + 1) * c, :] = mm(zt, buffers[1 + level][...], 1, 0).astype(BF)


def pack_kernel(place, *refs):
    sources, out = refs[:LEVELS], refs[LEVELS]
    half = out.shape[0] // LEVELS
    for i, a in enumerate(sources):
        out[i * half : (i + 1) * half, :] = a[at((1 - place[0]) * half, half), :]


def beside_kernel(place, left, right, out):
    k = left.shape[1]
    out[:, :k] = left[...]
    out[:, k:] = right[...]


def join_kernel(place, own, other, out):
    k = own.shape[1]
    me = place[0]
    out[:, at(me * k, k)] = own[...]
    out[:, at((1 - me) * k, k)] = other[...]


def gram_kernel(place, other, *refs):
    own, (full, gram) = refs[:LEVELS], refs[LEVELS:]
    half, k = other.shape[0] // LEVELS, other.shape[1]
    me = place[0]
    for level in range(LEVELS):
        full[:, at((2 * level + me) * k, k)] = own[level][at(me * half, half), :]
        full[:, at((2 * level + 1 - me) * k, k)] = other[level * half : (level + 1) * half, :]
    wide = 2 * k
    for n, (i, j) in enumerate(BLOCKS):
        if j == 0:
            left = full[:, i * wide : (i + 1) * wide].T
        gram[n * wide : (n + 1) * wide, :] = mm(left, full[:, j * wide : (j + 1) * wide], 1, 0).astype(BF)


def whole_kernel(place, mine, other, out):
    k = mine.shape[1]
    for n, (i, j) in enumerate(BLOCKS):
        block = add(mine[n * k : (n + 1) * k, :], other[n * k : (n + 1) * k, :])
        out[i * k : (i + 1) * k, j * k : (j + 1) * k] = block
        if j < i:
            out[j * k : (j + 1) * k, i * k : (i + 1) * k] = block.T


def join_siblings(one, more, two, three, joined):
    k = one.shape[1]
    joined[:, :k] = add(one[...], more[...])
    joined[:, k : 2 * k] = two[...]
    joined[:, 2 * k :] = three[...]


def next_kernel(place, one, more, two, three, gram, here, there, out, joined):
    join_siblings(one, more, two, three, joined)
    c, k = one.shape
    for level in range(LEVELS):
        cols = slice(level * k, (level + 1) * k)
        total = here[:, cols].astype(F32) + there[:, cols].astype(F32) + mm(joined[...], gram[:, cols], 1, 0)
        out[level * c : (level + 1) * c, :] = total.astype(BF)


def again_kernel(holder, place, early, mine, other, gram, here, there, out, joined):
    @pl.when(place[0] == holder)
    def _():
        out[...] = early[...]
        joined[...] = mine[...]

    @pl.when(place[0] != holder)
    def _():
        joined[...] = other[...]
        c, k = out.shape[0] // LEVELS, out.shape[1]
        for level in range(LEVELS):
            cols = slice(level * k, (level + 1) * k)
            total = here[:, cols].astype(F32) + there[:, cols].astype(F32) + mm(joined[...], gram[:, cols], 1, 0)
            out[level * c : (level + 1) * c, :] = total.astype(BF)


def sum_kernel(source, place, summed, received, relayed, out):
    n = out.shape[0]

    @pl.when(place[0] == source)
    def _():
        out[...] = add(summed[:n, :], relayed[:n, :])

    @pl.when(place[0] != source)
    def _():
        out[...] = add(summed[:n, :], received[:n, :])


def leaf_terms(z, leaves, flipped, out):
    size = leaves.shape[1]
    for q in range(leaves.shape[0]):
        rows = slice(q * size, (q + 1) * size)
        out[rows, :] = mm(leaves[q], z[rows, :], 0 if flipped else 1, 0)


def start_kernel(place, z, leaves, after, y, s):
    half = y.shape[0]
    leaf_terms(z[at(place[0] * half, half), :], leaves, True, y)
    s[...] = mm(y[...].astype(BF).T, after[...], 1, 0).astype(BF)


def project_kernel(place, y, after, s):
    s[...] = mm(y[...].astype(BF).T, after[...], 1, 0).astype(BF)


def field_kernel(flipped, place, q, factor, was, leaves, y):
    z = (mm(factor[...], q[...], 1, 1) + was[...]).astype(BF)
    leaf_terms(z, leaves, flipped, y)


def siblings_kernel(place, one, more, two, three, joined):
    join_siblings(one, more, two, three, joined)


def last_kernel(holder, place, mine, other, factor, was, out, joined):
    @pl.when(place[0] == holder)
    def _():
        joined[...] = mine[...]

    @pl.when(place[0] != holder)
    def _():
        joined[...] = other[...]

    out[...] = (mm(factor[...], joined[...], 1, 1) + was[...]).astype(BF)


def one_way(value, mask, source):
    chips = lax.axis_size(("rows", "cols"))
    away = [(2 * p + source, 2 * (p ^ mask) + 1 - source) for p in range(chips)]
    home = [(2 * p + 1 - source, 2 * p + source) for p in range(chips)]
    return lax.ppermute(value, ("rows", "cols", "rank"), away + home)


def over_rank(value):
    return lax.ppermute(value, "rank", [(0, 1), (1, 0)])


def add(a, b):
    return (a.astype(F32) + b.astype(F32)).astype(BF)


def gathered(place, packed, summed, source):
    chips = lax.axis_size(("rows", "cols"))
    stride = 1
    while stride < chips // 2**LEVELS:
        received = one_way(packed, stride, source)
        relayed = over_rank(received)
        packed = add(summed, received)
        shape = jax.ShapeDtypeStruct(packed.shape, BF)
        (summed,) = call(
            lambda *r, source=source: sum_kernel(source, *r), [shape], (place, summed, received, relayed), 0
        )
        source, stride = 1 - source, 2 * stride
    return packed, summed, source, stride


def siblings_of(packed, summed, source, stride, received=None):
    c = packed.shape[0] // LEVELS
    if received is None:
        received = one_way(packed[: 2 * c], stride, source)
    three = one_way(summed[2 * c :], stride, 1 - source)
    both = add(summed[: 2 * c], received)
    one = one_way(both[:c], 6 * stride, 1 - source)
    more = one_way(both[:c], 4 * stride, 1 - source)
    two = one_way(both[c:], 2 * stride, 1 - source)
    return one, more, two, three


def local(probes, basis_one, basis_two, basis_three, coeff_one, coeff_two, coeff_three, leaves):
    place = lax.axis_index("rank").reshape(1)
    n, c = probes.shape
    half = n // 2
    k = basis_one.shape[1]
    wide = 2 * k * LEVELS
    S = jax.ShapeDtypeStruct
    p_shape, y_shape, s_shape = S((LEVELS * c, 2 * k), BF), S((half, c), F32), S((c, wide), BF)
    sems = pltpu.SemaphoreType.DMA
    uppers = (basis_one, basis_two, basis_three)
    lowers = (coeff_one, coeff_two, coeff_three)

    def prepared(factors):
        (sent,) = call(pack_kernel, [S((LEVELS * half, k), BF)], (place, *factors), 0)
        other = over_rank(sent)
        full, gram = call(
            gram_kernel,
            [S((half, wide), BF), S((len(BLOCKS) * 2 * k, 2 * k), BF)],
            (place, other, *factors),
            half * wide * wide * 3 // 2,
        )
        other = over_rank(gram)
        (gram,) = call(whole_kernel, [S((wide, wide), BF)], (place, gram, other), 0)
        return full, gram

    buffers = [pltpu.VMEM(a.shape, BF) for a in (probes, *uppers)]
    (own,) = call(
        first_kernel,
        [S((LEVELS * c, k), BF)],
        (place, probes, *uppers),
        2 * n * LEVELS * k * c,
        [*buffers, sems((LEVELS + 1, CHUNKS))],
        LEVELS + 1,
    )
    other = over_rank(own)
    (summed,) = call(join_kernel, [p_shape], (place, own, other), 0)
    packed, received = summed, None
    if lax.axis_size(("rows", "cols")) == 2**LEVELS:
        left = one_way(own[: 2 * c], 1, 0)
        right = one_way(other[: 2 * c], 1, 0)
        (received,) = call(beside_kernel, [S((2 * c, 2 * k), BF)], (place, left, right), 0)
    lower, lower_gram = prepared(lowers)
    upper, upper_gram = prepared(uppers)
    field_flops = 4 * half * wide * c
    y, s = call(start_kernel, [y_shape, s_shape], (place, probes, leaves, lower), field_flops // 2)
    applies = 2 * PASSES
    source = 0
    for step in range(applies):
        flipped = step % 2 == 0
        packed, summed, source, stride = gathered(place, packed, summed, source)
        pieces = siblings_of(packed, summed, source, stride, received)
        received = None
        if step + 1 == applies:
            (q,) = call(siblings_kernel, [s_shape], (place, *pieces), 0)
            other = over_rank(q)
            (out,) = call(
                lambda *r: last_kernel(source, *r),
                [S((half, c), BF)],
                (place, q, other, upper, y),
                field_flops // 2,
                [pltpu.VMEM((c, wide), BF)],
            )
            return out
        there = over_rank(s)
        gram = lower_gram if flipped else upper_gram
        factor, after = (lower, upper) if flipped else (upper, lower)
        packed, q = call(next_kernel, [p_shape, s_shape], (place, *pieces, gram, s, there), 2 * wide * wide * c)
        other = over_rank(q)
        summed, q = call(
            lambda *r: again_kernel(source, *r),
            [p_shape, s_shape],
            (place, packed, q, other, gram, s, there),
            2 * wide * wide * c,
        )
        (y,) = call(lambda *r: field_kernel(not flipped, *r), [y_shape], (place, q, factor, y, leaves), field_flops // 2)
        if step + 2 < applies:
            (s,) = call(project_kernel, [s_shape], (place, y, after), field_flops // 2)


def solution(mesh):
    rows = P(("parts", "rows", "cols"), None)
    split = P(("parts", "rows", "cols"), "rank")
    every = ("parts", "rows", "cols", "rank")
    in_specs = (rows,) + (split,) * 6 + (P(every, None, None),)

    return jax.shard_map(local, mesh=mesh, in_specs=in_specs, out_specs=P(every, None), check_vma=False)
```

time: 67.9 us -> 62.4 us (0.919)
  Pallas kernels: 17.4 us -> 12.3 us
  local copies, waits for them, and re-layouts: 0.09 us -> 3.39 us
  waiting for transfers between devices: 26.2 us -> 23.5 us
  other arithmetic: 0.86 us -> 0.14 us
    ppermute x20 -> x12, starting transfers between devices: 9 us -> 2.46 us  [over_rank(): return lax.ppermute(value, 'rank', [(0, 1), (1, 0)])]
    ppermute x12 -> x21, starting transfers between devices: 13.8 us -> 20 us  [one_way(): return lax.ppermute(value, ('rows', 'cols', 'rank'), away + home)]
    pallas_call x22 -> x23, Pallas kernels: 17.4 us -> 12.3 us  [call(): pl.pallas_call(kernel, out_shape=outs, in_specs=[pl.BlockSpec(memory_spac...]
    ppermute x20 -> x12, waiting for transfers between devices: 7.88 us -> 2.8 us  [over_rank(): return lax.ppermute(value, 'rank', [(0, 1), (1, 0)])]
    unnamed x4 -> x22, local copies, waits for them, and re-layouts: 0.01 us -> 3.28 us
    ppermute x12 -> x21, waiting for transfers between devices: 18.3 us -> 20.7 us  [one_way(): return lax.ppermute(value, ('rows', 'cols', 'rank'), away + home)]
  transfers between devices with their start and end apart: 32 -> 33, of which waited for: 17 -> 19; matrix products, arithmetic and copies ran while one was open for 1% -> 0% of each run, Pallas kernels for 18% -> 16%
where the time goes in v6:
time: 62.4 us; the launch traced here: 62.1 us
  waiting for transfers between devices  23.5 us (38%)
  starting transfers between devices  22.5 us (36%)
  Pallas kernels  12.3 us (20%)
  local copies, waits for them, and re-layouts  3.39 us (5%)
    ppermute x21, waiting for transfers between devices, one_way(): return lax.ppermute(value, ('rows', 'cols', 'rank'), away + home)  20.7 us
    ppermute x21, starting transfers between devices, one_way(): return lax.ppermute(value, ('rows', 'cols', 'rank'), away + home)  20 us
    pallas_call x23, Pallas kernels, call(): pl.pallas_call(kernel, out_shape=outs, in_specs=[pl.BlockSpec(memory_spac...  12.3 us
    unnamed x22, local copies, waits for them, and re-layouts  3.28 us
    ppermute x12, waiting for transfers between devices, over_rank(): return lax.ppermute(value, 'rank', [(0, 1), (1, 0)])  2.8 us
    ppermute x12, starting transfers between devices, over_rank(): return lax.ppermute(value, 'rank', [(0, 1), (1, 0)])  2.46 us
  transfers between devices with their start and end apart: 33, of which 19 were waited for; matrix products, arithmetic and copies ran while one was open for 0% of the time, Pallas kernels for 16%

profile of v6, /device:TPU:0, one launch (start us, length us, event | category | flops | bytes accessed | tf_op | source)
XLA Modules:
  0.0 62.1 jit_solution(18291021592352657514)
XLA Ops:
  0.0 1.2 %copy-done.8 = bf16[2048,128]{1,0:T(8,128)(2,1)S(1)} copy-done((bf16[2048,128]{1,0:T(8,128)(2,1)S(1)}, bf16[2048,128]{1,0:T(8,128)(2,1)}, u32[]{:S(2)}) %copy-start.8) | copy-done | bytes 524312
  1.2 1.0 %copy-done.9 = bf16[2048,128]{1,0:T(8,128)(2,1)S(1)} copy-done((bf16[2048,128]{1,0:T(8,128)(2,1)S(1)}, bf16[2048,128]{1,0:T(8,128)(2,1)}, u32[]{:S(2)}) %copy-start.9) | copy-done | bytes 524312
  2.2 1.0 %copy-done.10 = bf16[2048,128]{1,0:T(8,128)(2,1)S(1)} copy-done((bf16[2048,128]{1,0:T(8,128)(2,1)S(1)}, bf16[2048,128]{1,0:T(8,128)(2,1)}, u32[]{:S(2)}) %copy-start.10) | copy-done | bytes 524312
  3.3 0.6 collective-permute-start.7
  4.0 1.7 %collective-permute-done.7.other = bf16[3072,128]{1,0:T(8,128)(2,1)S(1)} collective-permute-done((bf16[3072,128]{1,0:T(8,128)(2,1)S(1)}, bf16[3072,128]{1,0:T(8,128)(2,1)S(1)}, u32[]{:S(2)}, u32[]{:S(2)}) %collective-permute-start.7) | collective-permute-done | bytes 786464 | tf_op jit(solution)/shard_map/ppermute | solution.py:198
  5.8 1.3 %shard_map.86 = (bf16[1024,768]{1,0:T(8,128)(2,1)S(1)}, bf16[1536,256]{1,0:T(8,128)(2,1)S(1)}) custom-call(s32[1]{0:T(128)} %bitcast.place.r_0_, bf16[3072,128]{1,0:T(8,128)(2,1)S(1)} %collective-permute-done.7.other, bf16[2048,128]{1,0:T(8,128)(2,1)S(1)} %copy-done.8, bf16[2048,128]{1,0:T(8,128)(2,1)S(1)} %copy-done.9, bf16[2048,128]{1,0:T(8,128)(2,1)S(1)} %copy-done.10), custom_call_target="tpu_custom_call" | custom-call | flops 905969664 | bytes 4718592 | tf_op jit(solution)/shard_map/pallas_call | solution.py:27
  7.2 0.4 collective-permute-start.8
  7.6 2.3 %shard_map.82.own = bf16[384,128]{1,0:T(8,128)(2,1)S(1)} custom-call(s32[1]{0:T(128)} %bitcast.place.r_0_, bf16[2048,128]{1,0:T(8,128)(2,1)} %z.1, bf16[2048,128]{1,0:T(8,128)(2,1)} %refs_0_.9, bf16[2048,128]{1,0:T(8,128)(2,1)} %refs_1_.9, bf16[2048,128]{1,0:T(8,128)(2,1)} %refs_2_.9), custom_call_target="tpu_custom_call" | custom-call | flops 201326592 | bytes 2195456 | tf_op jit(solution)/shard_map/pallas_call | solution.py:27
  10.2 2.6 %collective-permute-start.1 = (bf16[256,128]{1,0:T(8,128)(2,1)S(1)}, bf16[256,128]{1,0:T(8,128)(2,1)S(1)}, u32[]{:S(2)}, u32[]{:S(2)}) collective-permute-start(bf16[256,128]{1,0:T(8,128)(2,1)S(1)} %slice.89), channel_id=1, source_target_pairs={{0,3},{2,1},{4,7},{6,5},{8,11},{10,9},{12,15},{14,13},{1,0},{3,2},... | collective-permute-start | bytes 196616 | tf_op jit(solution)/shard_map/ppermute | solution.py:194
  12.8 1.1 %collective-permute-start.2 = (bf16[256,128]{1,0:T(8,128)(2,1)S(1)}, bf16[256,128]{1,0:T(8,128)(2,1)S(1)}, u32[]{:S(2)}, u32[]{:S(2)}) collective-permute-start(bf16[256,128]{1,0:T(8,128)(2,1)S(1)} %slice.90), channel_id=1, source_target_pairs={{0,3},{2,1},{4,7},{6,5},{8,11},{10,9},{12,15},{14,13},{1,0},{3,2},... | collective-permute-start | bytes 196616 | tf_op jit(solution)/shard_map/ppermute | solution.py:194
  14.0 0.7 %collective-permute-done.1.left = bf16[256,128]{1,0:T(8,128)(2,1)S(1)} collective-permute-done((bf16[256,128]{1,0:T(8,128)(2,1)S(1)}, bf16[256,128]{1,0:T(8,128)(2,1)S(1)}, u32[]{:S(2)}, u32[]{:S(2)}) %collective-permute-start.1) | collective-permute-done | bytes 65568 | tf_op jit(solution)/shard_map/ppermute | solution.py:194
  14.7 1.3 %collective-permute-done.2.right = bf16[256,128]{1,0:T(8,128)(2,1)S(1)} collective-permute-done((bf16[256,128]{1,0:T(8,128)(2,1)S(1)}, bf16[256,128]{1,0:T(8,128)(2,1)S(1)}, u32[]{:S(2)}, u32[]{:S(2)}) %collective-permute-start.2) | collective-permute-done | bytes 65568 | tf_op jit(solution)/shard_map/ppermute | solution.py:194
  16.1 0.7 %shard_map.88 = (f32[1024,128]{1,0:T(8,128)S(1)}, bf16[128,768]{1,0:T(8,128)(2,1)S(1)}) custom-call(s32[1]{0:T(128)} %bitcast.place.r_0_, bf16[2048,128]{1,0:T(8,128)(2,1)S(1)} %copy-done.7, bf16[4,256,256]{2,1,0:T(8,128)(2,1)S(1)} %copy-done, bf16[1024,768]{1,0:T(8,128)(2,1)S(1)} %get-tuple-element.24.after.r_2_), custom_call_target="tpu_custom_call" | custom-call | flops 201326592 | bytes 3342336 | tf_op jit(solution)/shard_map/pallas_call | solution.py:27
  17.0 0.5 collective-permute-start.3
  17.7 3.5 %collective-permute-start.4 = (bf16[128,256]{1,0:T(8,128)(2,1)S(1)}, bf16[128,256]{1,0:T(8,128)(2,1)S(1)}, u32[]{:S(2)}, u32[]{:S(2)}) collective-permute-start(bf16[128,256]{1,0:T(8,128)(2,1)S(1)} %get-tuple-element.48), channel_id=1, source_target_pairs={{1,8},{3,10},{5,12},{7,14},{9,0},{11,2},{13,4},{15,6},{0,1},{2,3},... | collective-permute-start | bytes 196616 | tf_op jit(solution)/shard_map/ppermute | solution.py:194
  21.3 1.3 %shard_map.92 = (bf16[1024,768]{1,0:T(8,128)(2,1)S(1)}, bf16[1536,256]{1,0:T(8,128)(2,1)S(1)}) custom-call(s32[1]{0:T(128)} %bitcast.place.r_0_, bf16[3072,128]{1,0:T(8,128)(2,1)S(1)} %collective-permute-done.16.other, bf16[2048,128]{1,0:T(8,128)(2,1)S(1)} %copy-done.2, bf16[2048,128]{1,0:T(8,128)(2,1)S(1)} %copy-done.4, bf16[2048,128]{1,0:T(8,128)(2,1)S(1)} %copy-done.6), custom_call_target="tpu_custom_call" | custom-call | flops 905969664 | bytes 4718592 | tf_op jit(solution)/shard_map/pallas_call | solution.py:27
  23.1 1.2 %collective-permute-done.4.more = bf16[128,256]{1,0:T(8,128)(2,1)S(1)} collective-permute-done((bf16[128,256]{1,0:T(8,128)(2,1)S(1)}, bf16[128,256]{1,0:T(8,128)(2,1)S(1)}, u32[]{:S(2)}, u32[]{:S(2)}) %collective-permute-start.4) | collective-permute-done | bytes 65568 | tf_op jit(solution)/shard_map/ppermute | solution.py:194
  24.3 0.7 %collective-permute-done.5.two = bf16[128,256]{1,0:T(8,128)(2,1)S(1)} collective-permute-done((bf16[128,256]{1,0:T(8,128)(2,1)S(1)}, bf16[128,256]{1,0:T(8,128)(2,1)S(1)}, u32[]{:S(2)}, u32[]{:S(2)}) %collective-permute-start.5) | collective-permute-done | bytes 65568 | tf_op jit(solution)/shard_map/ppermute | solution.py:194
  25.0 0.3 shard_map.89
  25.4 2.6 %collective-permute-start.11 = (bf16[256,256]{1,0:T(8,128)(2,1)S(1)}, bf16[256,256]{1,0:T(8,128)(2,1)S(1)}, u32[]{:S(2)}, u32[]{:S(2)}) collective-permute-start(bf16[256,256]{1,0:T(8,128)(2,1)S(1)} %slice.74), channel_id=1, source_target_pairs={{0,3},{2,1},{4,7},{6,5},{8,11},{10,9},{12,15},{14,13},{1,0},{3,2},... | collective-permute-start | bytes 393224 | tf_op jit(solution)/shard_map/ppermute | solution.py:194
  28.0 0.9 %shard_map.94.y.r_3_ = f32[1024,128]{1,0:T(8,128)S(1)} custom-call(s32[1]{0:T(128)} %bitcast.place.r_0_, bf16[128,768]{1,0:T(8,128)(2,1)S(1)} %get-tuple-element.30.r_1_, bf16[1024,768]{1,0:T(8,128)(2,1)S(1)} %get-tuple-element.24.after.r_2_, f32[1024,128]{1,0:T(8,128)S(1)} %get-tuple-element.31.r_3_, bf16[4,256,256]{2,1,0:T(8,128)(2,1)S(1)} %copy-done), custom_call_target="tpu_custom_call" | custom-call | flops 201326592 | bytes 3342336 | tf_op jit(solution)/shard_map/pallas_call | solution.py:27
  28.9 0.4 shard_map.95.here.r_5_
  29.4 1.1 %collective-permute-done.11 = bf16[256,256]{1,0:T(8,128)(2,1)S(1)} collective-permute-done((bf16[256,256]{1,0:T(8,128)(2,1)S(1)}, bf16[256,256]{1,0:T(8,128)(2,1)S(1)}, u32[]{:S(2)}, u32[]{:S(2)}) %collective-permute-start.11) | collective-permute-done | bytes 131104 | tf_op jit(solution)/shard_map/ppermute | solution.py:194
  30.8 1.6 %collective-permute-start.13 = (bf16[128,256]{1,0:T(8,128)(2,1)S(1)}, bf16[128,256]{1,0:T(8,128)(2,1)S(1)}, u32[]{:S(2)}, u32[]{:S(2)}) collective-permute-start(bf16[128,256]{1,0:T(8,128)(2,1)S(1)} %get-tuple-element.46), channel_id=1, source_target_pairs={{1,8},{3,10},{5,12},{7,14},{9,0},{11,2},{13,4},{15,6},{0,1},{2,3},... | collective-permute-start | bytes 196616 | tf_op jit(solution)/shard_map/ppermute | solution.py:194
  32.4 0.4 collective-permute-start.15
  33.1 3.2 %collective-permute-done.12.one = bf16[128,256]{1,0:T(8,128)(2,1)S(1)} collective-permute-done((bf16[128,256]{1,0:T(8,128)(2,1)S(1)}, bf16[128,256]{1,0:T(8,128)(2,1)S(1)}, u32[]{:S(2)}, u32[]{:S(2)}) %collective-permute-start.12) | collective-permute-done | bytes 65568 | tf_op jit(solution)/shard_map/ppermute | solution.py:194
  36.3 0.7 %collective-permute-done.13.more = bf16[128,256]{1,0:T(8,128)(2,1)S(1)} collective-permute-done((bf16[128,256]{1,0:T(8,128)(2,1)S(1)}, bf16[128,256]{1,0:T(8,128)(2,1)S(1)}, u32[]{:S(2)}, u32[]{:S(2)}) %collective-permute-start.13) | collective-permute-done | bytes 65568 | tf_op jit(solution)/shard_map/ppermute | solution.py:194
  37.1 0.3 shard_map.96
  37.5 1.2 %collective-permute-start.20 = (bf16[256,256]{1,0:T(8,128)(2,1)S(1)}, bf16[256,256]{1,0:T(8,128)(2,1)S(1)}, u32[]{:S(2)}, u32[]{:S(2)}) collective-permute-start(bf16[256,256]{1,0:T(8,128)(2,1)S(1)} %slice.79), channel_id=1, source_target_pairs={{0,3},{2,1},{4,7},{6,5},{8,11},{10,9},{12,15},{14,13},{1,0},{3,2},... | collective-permute-start | bytes 393224 | tf_op jit(solution)/shard_map/ppermute | solution.py:194
  38.9 0.9 %shard_map.98.y.r_3_ = f32[1024,128]{1,0:T(8,128)S(1)} custom-call(s32[1]{0:T(128)} %bitcast.place.r_0_, bf16[128,768]{1,0:T(8,128)(2,1)S(1)} %get-tuple-element.36.r_1_, bf16[1024,768]{1,0:T(8,128)(2,1)S(1)} %get-tuple-element.32.after.r_2_.r_3_, f32[1024,128]{1,0:T(8,128)S(1)} %shard_map.94.y.r_3_, bf16[4,256,256]{2,1,0:T(8,128)(2,1)S(1)} %copy-done), custom_call_target="tpu_custom_call" | custom-call | flops 201326592 | bytes 3342336 | tf_op jit(solution)/shard_map/pallas_call | solution.py:27
  39.8 0.4 shard_map.99.here.r_5_
  40.2 0.5 collective-permute-start.25
  40.7 0.5 collective-permute-done.20
  41.3 1.3 %collective-permute-start.21 = (bf16[128,256]{1,0:T(8,128)(2,1)S(1)}, bf16[128,256]{1,0:T(8,128)(2,1)S(1)}, u32[]{:S(2)}, u32[]{:S(2)}) collective-permute-start(bf16[128,256]{1,0:T(8,128)(2,1)S(1)} %get-tuple-element.44), channel_id=1, source_target_pairs={{1,12},{3,14},{5,8},{7,10},{9,4},{11,6},{13,0},{15,2},{0,1},{2,3},... | collective-permute-start | bytes 196616 | tf_op jit(solution)/shard_map/ppermute | solution.py:194
  42.5 1.1 %collective-permute-start.22 = (bf16[128,256]{1,0:T(8,128)(2,1)S(1)}, bf16[128,256]{1,0:T(8,128)(2,1)S(1)}, u32[]{:S(2)}, u32[]{:S(2)}) collective-permute-start(bf16[128,256]{1,0:T(8,128)(2,1)S(1)} %get-tuple-element.44), channel_id=1, source_target_pairs={{1,8},{3,10},{5,12},{7,14},{9,0},{11,2},{13,4},{15,6},{0,1},{2,3},... | collective-permute-start | bytes 196616 | tf_op jit(solution)/shard_map/ppermute | solution.py:194
  43.8 3.1 %collective-permute-done.21.one = bf16[128,256]{1,0:T(8,128)(2,1)S(1)} collective-permute-done((bf16[128,256]{1,0:T(8,128)(2,1)S(1)}, bf16[128,256]{1,0:T(8,128)(2,1)S(1)}, u32[]{:S(2)}, u32[]{:S(2)}) %collective-permute-start.21) | collective-permute-done | bytes 65568 | tf_op jit(solution)/shard_map/ppermute | solution.py:194
  46.9 1.3 %collective-permute-done.22.more = bf16[128,256]{1,0:T(8,128)(2,1)S(1)} collective-permute-done((bf16[128,256]{1,0:T(8,128)(2,1)S(1)}, bf16[128,256]{1,0:T(8,128)(2,1)S(1)}, u32[]{:S(2)}, u32[]{:S(2)}) %collective-permute-start.22) | collective-permute-done | bytes 65568 | tf_op jit(solution)/shard_map/ppermute | solution.py:194
  48.2 0.3 shard_map.100
  48.7 1.1 %collective-permute-start.27 = (bf16[256,256]{1,0:T(8,128)(2,1)S(1)}, bf16[256,256]{1,0:T(8,128)(2,1)S(1)}, u32[]{:S(2)}, u32[]{:S(2)}) collective-permute-start(bf16[256,256]{1,0:T(8,128)(2,1)S(1)} %slice.84), channel_id=1, source_target_pairs={{0,3},{2,1},{4,7},{6,5},{8,11},{10,9},{12,15},{14,13},{1,0},{3,2},... | collective-permute-start | bytes 393224 | tf_op jit(solution)/shard_map/ppermute | solution.py:194
  50.1 2.2 %collective-permute-done.27 = bf16[256,256]{1,0:T(8,128)(2,1)S(1)} collective-permute-done((bf16[256,256]{1,0:T(8,128)(2,1)S(1)}, bf16[256,256]{1,0:T(8,128)(2,1)S(1)}, u32[]{:S(2)}, u32[]{:S(2)}) %collective-permute-start.27) | collective-permute-done | bytes 131104 | tf_op jit(solution)/shard_map/ppermute | solution.py:194
  52.4 1.3 %collective-permute-start.28 = (bf16[128,256]{1,0:T(8,128)(2,1)S(1)}, bf16[128,256]{1,0:T(8,128)(2,1)S(1)}, u32[]{:S(2)}, u32[]{:S(2)}) collective-permute-start(bf16[128,256]{1,0:T(8,128)(2,1)S(1)} %get-tuple-element.42), channel_id=1, source_target_pairs={{1,12},{3,14},{5,8},{7,10},{9,4},{11,6},{13,0},{15,2},{0,1},{2,3},... | collective-permute-start | bytes 196616 | tf_op jit(solution)/shard_map/ppermute | solution.py:194
  53.7 0.7 %collective-permute-start.29 = (bf16[128,256]{1,0:T(8,128)(2,1)S(1)}, bf16[128,256]{1,0:T(8,128)(2,1)S(1)}, u32[]{:S(2)}, u32[]{:S(2)}) collective-permute-start(bf16[128,256]{1,0:T(8,128)(2,1)S(1)} %get-tuple-element.42), channel_id=1, source_target_pairs={{1,8},{3,10},{5,12},{7,14},{9,0},{11,2},{13,4},{15,6},{0,1},{2,3},... | collective-permute-start | bytes 196616 | tf_op jit(solution)/shard_map/ppermute | solution.py:194
  54.4 0.5 collective-permute-start.30
  54.9 3.0 %collective-permute-done.28.one = bf16[128,256]{1,0:T(8,128)(2,1)S(1)} collective-permute-done((bf16[128,256]{1,0:T(8,128)(2,1)S(1)}, bf16[128,256]{1,0:T(8,128)(2,1)S(1)}, u32[]{:S(2)}, u32[]{:S(2)}) %collective-permute-start.28) | collective-permute-done | bytes 65568 | tf_op jit(solution)/shard_map/ppermute | solution.py:194
  58.0 1.3 %collective-permute-done.29.more = bf16[128,256]{1,0:T(8,128)(2,1)S(1)} collective-permute-done((bf16[128,256]{1,0:T(8,128)(2,1)S(1)}, bf16[128,256]{1,0:T(8,128)(2,1)S(1)}, u32[]{:S(2)}, u32[]{:S(2)}) %collective-permute-start.29) | collective-permute-done | bytes 65568 | tf_op jit(solution)/shard_map/ppermute | solution.py:194
  59.4 0.9 %shard_map.103.r_4_ = f32[1024,128]{1,0:T(8,128)S(1)} custom-call(s32[1]{0:T(128)} %bitcast.place.r_0_, bf16[128,768]{1,0:T(8,128)(2,1)S(1)} %get-tuple-element.40.r_1_, bf16[1024,768]{1,0:T(8,128)(2,1)S(1)} %get-tuple-element.24.after.r_2_, f32[1024,128]{1,0:T(8,128)S(1)} %shard_map.98.y.r_3_, bf16[4,256,256]{2,1,0:T(8,128)(2,1)S(1)} %copy-done), custom_call_target="tpu_custom_call" | custom-call | flops 201326592 | bytes 3342336 | tf_op jit(solution)/shard_map/pallas_call | solution.py:27
  60.3 0.5 collective-permute-done.32.r_2_
  60.8 1.3 %shard_map.104 = bf16[1024,128]{1,0:T(8,128)(2,1)} custom-call(s32[1]{0:T(128)} %bitcast.place.r_0_, bf16[128,768]{1,0:T(8,128)(2,1)S(1)} %shard_map.102.r_1_, bf16[128,768]{1,0:T(8,128)(2,1)S(1)} %collective-permute-done.32.r_2_, bf16[1024,768]{1,0:T(8,128)(2,1)S(1)} %get-tuple-element.32.after.r_2_.r_3_, f32[1024,128]{1,0:T(8,128)S(1)} %shard_map.103.r_4_), custom_call_target="tpu_custom_call" | custom-call | flops 201326592 | bytes 2752512 | tf_op jit(solution)/shard_map/pallas_call | solution.py:27
  (80 shorter events, 3.4 us)
Async XLA Ops:
  0.0 3.9 %copy-start.1 = (bf16[2048,128]{1,0:T(8,128)(2,1)S(1)}, bf16[2048,128]{1,0:T(8,128)(2,1)}, u32[]{:S(2)}) copy-start(bf16[2048,128]{1,0:T(8,128)(2,1)} %refs_0_.9) | copy-start | bytes 1572868
  0.0 3.9 %copy-start.3 = (bf16[2048,128]{1,0:T(8,128)(2,1)S(1)}, bf16[2048,128]{1,0:T(8,128)(2,1)}, u32[]{:S(2)}) copy-start(bf16[2048,128]{1,0:T(8,128)(2,1)} %refs_1_.9) | copy-start | bytes 1572868
  0.0 3.9 %copy-start.5 = (bf16[2048,128]{1,0:T(8,128)(2,1)S(1)}, bf16[2048,128]{1,0:T(8,128)(2,1)}, u32[]{:S(2)}) copy-start(bf16[2048,128]{1,0:T(8,128)(2,1)} %refs_2_.9) | copy-start | bytes 1572868
  0.0 1.2 %copy-start.8 = (bf16[2048,128]{1,0:T(8,128)(2,1)S(1)}, bf16[2048,128]{1,0:T(8,128)(2,1)}, u32[]{:S(2)}) copy-start(bf16[2048,128]{1,0:T(8,128)(2,1)} %refs_0_.7) | copy-start | bytes 1572868
  1.2 1.0 %copy-start.9 = (bf16[2048,128]{1,0:T(8,128)(2,1)S(1)}, bf16[2048,128]{1,0:T(8,128)(2,1)}, u32[]{:S(2)}) copy-start(bf16[2048,128]{1,0:T(8,128)(2,1)} %refs_1_.7) | copy-start | bytes 1572868
  2.2 1.0 %copy-start.10 = (bf16[2048,128]{1,0:T(8,128)(2,1)S(1)}, bf16[2048,128]{1,0:T(8,128)(2,1)}, u32[]{:S(2)}) copy-start(bf16[2048,128]{1,0:T(8,128)(2,1)} %refs_2_.7) | copy-start | bytes 1572868
  3.3 2.5 %collective-permute-start.7 = (bf16[3072,128]{1,0:T(8,128)(2,1)S(1)}, bf16[3072,128]{1,0:T(8,128)(2,1)S(1)}, u32[]{:S(2)}, u32[]{:S(2)}) collective-permute-start(bf16[3072,128]{1,0:T(8,128)(2,1)S(1)} %shard_map.85), channel_id=1, source_target_pairs={{0,1},{1,0},{2,3},{3,2},{4,5},{5,4},{6,7},{7,6},{8,9},{9,8},{10,11... | collective-permute-start | bytes 2359304 | tf_op jit(solution)/shard_map/ppermute | solution.py:198
  3.9 17.3 %collective-permute-start.16 = (bf16[3072,128]{1,0:T(8,128)(2,1)S(1)}, bf16[3072,128]{1,0:T(8,128)(2,1)S(1)}, u32[]{:S(2)}, u32[]{:S(2)}) collective-permute-start(bf16[3072,128]{1,0:T(8,128)(2,1)S(1)} %shard_map.91), channel_id=1, source_target_pairs={{0,1},{1,0},{2,3},{3,2},{4,5},{5,4},{6,7},{7,6},{8,9},{9,8},{10,11... | collective-permute-start | bytes 2359304 | tf_op jit(solution)/shard_map/ppermute | solution.py:198
  7.1 9.0 %copy-start = (bf16[4,256,256]{2,1,0:T(8,128)(2,1)S(1)}, bf16[4,256,256]{2,1,0:T(8,128)(2,1)}, u32[]{:S(2)}) copy-start(bf16[4,256,256]{2,1,0:T(8,128)(2,1)} %r_4_.5) | copy-start | bytes 1572868
  7.1 9.0 %copy-start.7 = (bf16[2048,128]{1,0:T(8,128)(2,1)S(1)}, bf16[2048,128]{1,0:T(8,128)(2,1)}, u32[]{:S(2)}) copy-start(bf16[2048,128]{1,0:T(8,128)(2,1)} %z.1) | copy-start | bytes 1572868
  7.2 15.5 %collective-permute-start.8 = (bf16[1536,256]{1,0:T(8,128)(2,1)S(1)}, bf16[1536,256]{1,0:T(8,128)(2,1)S(1)}, u32[]{:S(2)}, u32[]{:S(2)}) collective-permute-start(bf16[1536,256]{1,0:T(8,128)(2,1)S(1)} %get-tuple-element.23.mine), channel_id=1, source_target_pairs={{0,1},{1,0},{2,3},{3,2},{4,5},{5,4},{6,7},{7,6},{8,9},{9,8},{10,11... | collective-permute-start | bytes 2359304 | tf_op jit(solution)/shard_map/ppermute | solution.py:198
  9.9 2.9 %collective-permute-start = (bf16[384,128]{1,0:T(8,128)(2,1)S(1)}, bf16[384,128]{1,0:T(8,128)(2,1)S(1)}, u32[]{:S(2)}, u32[]{:S(2)}) collective-permute-start(bf16[384,128]{1,0:T(8,128)(2,1)S(1)} %shard_map.82.own), channel_id=1, source_target_pairs={{0,1},{1,0},{2,3},{3,2},{4,5},{5,4},{6,7},{7,6},{8,9},{9,8},{10,11... | collective-permute-start | bytes 294920 | tf_op jit(solution)/shard_map/ppermute | solution.py:198
  10.2 4.5 %collective-permute-start.1 = (bf16[256,128]{1,0:T(8,128)(2,1)S(1)}, bf16[256,128]{1,0:T(8,128)(2,1)S(1)}, u32[]{:S(2)}, u32[]{:S(2)}) collective-permute-start(bf16[256,128]{1,0:T(8,128)(2,1)S(1)} %slice.89), channel_id=1, source_target_pairs={{0,3},{2,1},{4,7},{6,5},{8,11},{10,9},{12,15},{14,13},{1,0},{3,2},... | collective-permute-start | bytes 196616 | tf_op jit(solution)/shard_map/ppermute | solution.py:194
  12.8 3.2 %collective-permute-start.2 = (bf16[256,128]{1,0:T(8,128)(2,1)S(1)}, bf16[256,128]{1,0:T(8,128)(2,1)S(1)}, u32[]{:S(2)}, u32[]{:S(2)}) collective-permute-start(bf16[256,128]{1,0:T(8,128)(2,1)S(1)} %slice.90), channel_id=1, source_target_pairs={{0,3},{2,1},{4,7},{6,5},{8,11},{10,9},{12,15},{14,13},{1,0},{3,2},... | collective-permute-start | bytes 196616 | tf_op jit(solution)/shard_map/ppermute | solution.py:194
  13.9 3.7 %collective-permute-start.6 = (bf16[128,256]{1,0:T(8,128)(2,1)S(1)}, bf16[128,256]{1,0:T(8,128)(2,1)S(1)}, u32[]{:S(2)}, u32[]{:S(2)}) collective-permute-start(bf16[128,256]{1,0:T(8,128)(2,1)S(1)} %slice.93), channel_id=1, source_target_pairs={{1,2},{3,0},{5,6},{7,4},{9,10},{11,8},{13,14},{15,12},{0,1},{2,3},... | collective-permute-start | bytes 196616 | tf_op jit(solution)/shard_map/ppermute | solution.py:194
  16.1 5.2 %copy-start.2 = (bf16[2048,128]{1,0:T(8,128)(2,1)S(1)}, bf16[2048,128]{1,0:T(8,128)(2,1)}, u32[]{:S(2)}) copy-start(bf16[2048,128]{1,0:T(8,128)(2,1)} %refs_0_.9) | copy-start | bytes 1572868
  16.1 5.2 %copy-start.4 = (bf16[2048,128]{1,0:T(8,128)(2,1)S(1)}, bf16[2048,128]{1,0:T(8,128)(2,1)}, u32[]{:S(2)}) copy-start(bf16[2048,128]{1,0:T(8,128)(2,1)} %refs_1_.9) | copy-start | bytes 1572868
  16.1 5.2 %copy-start.6 = (bf16[2048,128]{1,0:T(8,128)(2,1)S(1)}, bf16[2048,128]{1,0:T(8,128)(2,1)}, u32[]{:S(2)}) copy-start(bf16[2048,128]{1,0:T(8,128)(2,1)} %refs_2_.9) | copy-start | bytes 1572868
  16.9 8.1 %collective-permute-start.9 = (bf16[128,768]{1,0:T(8,128)(2,1)S(1)}, bf16[128,768]{1,0:T(8,128)(2,1)S(1)}, u32[]{:S(2)}, u32[]{:S(2)}) collective-permute-start(bf16[128,768]{1,0:T(8,128)(2,1)S(1)} %get-tuple-element.25.here.r_5_), channel_id=1, source_target_pairs={{0,1},{1,0},{2,3},{3,2},{4,5},{5,4},{6,7},{7,6},{8,9},{9,8},{10,11... | collective-permute-start | bytes 589832 | tf_op jit(solution)/shard_map/ppermute | solution.py:198
  17.0 6.1 %collective-permute-start.3 = (bf16[128,256]{1,0:T(8,128)(2,1)S(1)}, bf16[128,256]{1,0:T(8,128)(2,1)S(1)}, u32[]{:S(2)}, u32[]{:S(2)}) collective-permute-start(bf16[128,256]{1,0:T(8,128)(2,1)S(1)} %get-tuple-element.48), channel_id=1, source_target_pairs={{1,12},{3,14},{5,8},{7,10},{9,4},{11,6},{13,0},{15,2},{0,1},{2,3},... | collective-permute-start | bytes 196616 | tf_op jit(solution)/shard_map/ppermute | solution.py:194
  17.7 6.6 %collective-permute-start.4 = (bf16[128,256]{1,0:T(8,128)(2,1)S(1)}, bf16[128,256]{1,0:T(8,128)(2,1)S(1)}, u32[]{:S(2)}, u32[]{:S(2)}) collective-permute-start(bf16[128,256]{1,0:T(8,128)(2,1)S(1)} %get-tuple-element.48), channel_id=1, source_target_pairs={{1,8},{3,10},{5,12},{7,14},{9,0},{11,2},{13,4},{15,6},{0,1},{2,3},... | collective-permute-start | bytes 196616 | tf_op jit(solution)/shard_map/ppermute | solution.py:194
  21.2 3.8 %collective-permute-start.5 = (bf16[128,256]{1,0:T(8,128)(2,1)S(1)}, bf16[128,256]{1,0:T(8,128)(2,1)S(1)}, u32[]{:S(2)}, u32[]{:S(2)}) collective-permute-start(bf16[128,256]{1,0:T(8,128)(2,1)S(1)} %get-tuple-element.47), channel_id=1, source_target_pairs={{1,4},{3,6},{5,0},{7,2},{9,12},{11,14},{13,8},{15,10},{0,1},{2,3},... | collective-permute-start | bytes 196616 | tf_op jit(solution)/shard_map/ppermute | solution.py:194
  22.6 9.8 %collective-permute-start.17 = (bf16[1536,256]{1,0:T(8,128)(2,1)S(1)}, bf16[1536,256]{1,0:T(8,128)(2,1)S(1)}, u32[]{:S(2)}, u32[]{:S(2)}) collective-permute-start(bf16[1536,256]{1,0:T(8,128)(2,1)S(1)} %get-tuple-element.29.mine), channel_id=1, source_target_pairs={{0,1},{1,0},{2,3},{3,2},{4,5},{5,4},{6,7},{7,6},{8,9},{9,8},{10,11... | collective-permute-start | bytes 2359304 | tf_op jit(solution)/shard_map/ppermute | solution.py:198
  25.3 2.7 %collective-permute-start.10 = (bf16[128,768]{1,0:T(8,128)(2,1)S(1)}, bf16[128,768]{1,0:T(8,128)(2,1)S(1)}, u32[]{:S(2)}, u32[]{:S(2)}) collective-permute-start(bf16[128,768]{1,0:T(8,128)(2,1)S(1)} %get-tuple-element.27.r_2_), channel_id=1, source_target_pairs={{0,1},{1,0},{2,3},{3,2},{4,5},{5,4},{6,7},{7,6},{8,9},{9,8},{10,11... | collective-permute-start | bytes 589832 | tf_op jit(solution)/shard_map/ppermute | solution.py:198
  25.4 5.1 %collective-permute-start.11 = (bf16[256,256]{1,0:T(8,128)(2,1)S(1)}, bf16[256,256]{1,0:T(8,128)(2,1)S(1)}, u32[]{:S(2)}, u32[]{:S(2)}) collective-permute-start(bf16[256,256]{1,0:T(8,128)(2,1)S(1)} %slice.74), channel_id=1, source_target_pairs={{0,3},{2,1},{4,7},{6,5},{8,11},{10,9},{12,15},{14,13},{1,0},{3,2},... | collective-permute-start | bytes 393224 | tf_op jit(solution)/shard_map/ppermute | solution.py:194
  29.3 7.7 %collective-permute-start.18 = (bf16[128,768]{1,0:T(8,128)(2,1)S(1)}, bf16[128,768]{1,0:T(8,128)(2,1)S(1)}, u32[]{:S(2)}, u32[]{:S(2)}) collective-permute-start(bf16[128,768]{1,0:T(8,128)(2,1)S(1)} %shard_map.95.here.r_5_), channel_id=1, source_target_pairs={{0,1},{1,0},{2,3},{3,2},{4,5},{5,4},{6,7},{7,6},{8,9},{9,8},{10,11... | collective-permute-start | bytes 589832 | tf_op jit(solution)/shard_map/ppermute | solution.py:198
  30.6 5.7 %collective-permute-start.12 = (bf16[128,256]{1,0:T(8,128)(2,1)S(1)}, bf16[128,256]{1,0:T(8,128)(2,1)S(1)}, u32[]{:S(2)}, u32[]{:S(2)}) collective-permute-start(bf16[128,256]{1,0:T(8,128)(2,1)S(1)} %get-tuple-element.46), channel_id=1, source_target_pairs={{1,12},{3,14},{5,8},{7,10},{9,4},{11,6},{13,0},{15,2},{0,1},{2,3},... | collective-permute-start | bytes 196616 | tf_op jit(solution)/shard_map/ppermute | solution.py:194
  30.8 6.3 %collective-permute-start.13 = (bf16[128,256]{1,0:T(8,128)(2,1)S(1)}, bf16[128,256]{1,0:T(8,128)(2,1)S(1)}, u32[]{:S(2)}, u32[]{:S(2)}) collective-permute-start(bf16[128,256]{1,0:T(8,128)(2,1)S(1)} %get-tuple-element.46), channel_id=1, source_target_pairs={{1,8},{3,10},{5,12},{7,14},{9,0},{11,2},{13,4},{15,6},{0,1},{2,3},... | collective-permute-start | bytes 196616 | tf_op jit(solution)/shard_map/ppermute | solution.py:194
  32.3 4.7 %collective-permute-start.14 = (bf16[128,256]{1,0:T(8,128)(2,1)S(1)}, bf16[128,256]{1,0:T(8,128)(2,1)S(1)}, u32[]{:S(2)}, u32[]{:S(2)}) collective-permute-start(bf16[128,256]{1,0:T(8,128)(2,1)S(1)} %get-tuple-element.45), channel_id=1, source_target_pairs={{1,4},{3,6},{5,0},{7,2},{9,12},{11,14},{13,8},{15,10},{0,1},{2,3},... | collective-permute-start | bytes 196616 | tf_op jit(solution)/shard_map/ppermute | solution.py:194
  32.4 4.7 %collective-permute-start.15 = (bf16[128,256]{1,0:T(8,128)(2,1)S(1)}, bf16[128,256]{1,0:T(8,128)(2,1)S(1)}, u32[]{:S(2)}, u32[]{:S(2)}) collective-permute-start(bf16[128,256]{1,0:T(8,128)(2,1)S(1)} %slice.77), channel_id=1, source_target_pairs={{1,2},{3,0},{5,6},{7,4},{9,10},{11,8},{13,14},{15,12},{0,1},{2,3},... | collective-permute-start | bytes 196616 | tf_op jit(solution)/shard_map/ppermute | solution.py:194
  37.4 1.5 %collective-permute-start.19 = (bf16[128,768]{1,0:T(8,128)(2,1)S(1)}, bf16[128,768]{1,0:T(8,128)(2,1)S(1)}, u32[]{:S(2)}, u32[]{:S(2)}) collective-permute-start(bf16[128,768]{1,0:T(8,128)(2,1)S(1)} %get-tuple-element.34.r_2_), channel_id=1, source_target_pairs={{0,1},{1,0},{2,3},{3,2},{4,5},{5,4},{6,7},{7,6},{8,9},{9,8},{10,11... | collective-permute-start | bytes 589832 | tf_op jit(solution)/shard_map/ppermute | solution.py:198
  37.5 3.7 %collective-permute-start.20 = (bf16[256,256]{1,0:T(8,128)(2,1)S(1)}, bf16[256,256]{1,0:T(8,128)(2,1)S(1)}, u32[]{:S(2)}, u32[]{:S(2)}) collective-permute-start(bf16[256,256]{1,0:T(8,128)(2,1)S(1)} %slice.79), channel_id=1, source_target_pairs={{0,3},{2,1},{4,7},{6,5},{8,11},{10,9},{12,15},{14,13},{1,0},{3,2},... | collective-permute-start | bytes 393224 | tf_op jit(solution)/shard_map/ppermute | solution.py:194
  40.2 8.0 %collective-permute-start.25 = (bf16[128,768]{1,0:T(8,128)(2,1)S(1)}, bf16[128,768]{1,0:T(8,128)(2,1)S(1)}, u32[]{:S(2)}, u32[]{:S(2)}) collective-permute-start(bf16[128,768]{1,0:T(8,128)(2,1)S(1)} %shard_map.99.here.r_5_), channel_id=1, source_target_pairs={{0,1},{1,0},{2,3},{3,2},{4,5},{5,4},{6,7},{7,6},{8,9},{9,8},{10,11... | collective-permute-start | bytes 589832 | tf_op jit(solution)/shard_map/ppermute | solution.py:198
  41.3 5.6 %collective-permute-start.21 = (bf16[128,256]{1,0:T(8,128)(2,1)S(1)}, bf16[128,256]{1,0:T(8,128)(2,1)S(1)}, u32[]{:S(2)}, u32[]{:S(2)}) collective-permute-start(bf16[128,256]{1,0:T(8,128)(2,1)S(1)} %get-tuple-element.44), channel_id=1, source_target_pairs={{1,12},{3,14},{5,8},{7,10},{9,4},{11,6},{13,0},{15,2},{0,1},{2,3},... | collective-permute-start | bytes 196616 | tf_op jit(solution)/shard_map/ppermute | solution.py:194
  42.5 5.7 %collective-permute-start.22 = (bf16[128,256]{1,0:T(8,128)(2,1)S(1)}, bf16[128,256]{1,0:T(8,128)(2,1)S(1)}, u32[]{:S(2)}, u32[]{:S(2)}) collective-permute-start(bf16[128,256]{1,0:T(8,128)(2,1)S(1)} %get-tuple-element.44), channel_id=1, source_target_pairs={{1,8},{3,10},{5,12},{7,14},{9,0},{11,2},{13,4},{15,6},{0,1},{2,3},... | collective-permute-start | bytes 196616 | tf_op jit(solution)/shard_map/ppermute | solution.py:194
  43.6 4.6 %collective-permute-start.23 = (bf16[128,256]{1,0:T(8,128)(2,1)S(1)}, bf16[128,256]{1,0:T(8,128)(2,1)S(1)}, u32[]{:S(2)}, u32[]{:S(2)}) collective-permute-start(bf16[128,256]{1,0:T(8,128)(2,1)S(1)} %get-tuple-element.43), channel_id=1, source_target_pairs={{1,4},{3,6},{5,0},{7,2},{9,12},{11,14},{13,8},{15,10},{0,1},{2,3},... | collective-permute-start | bytes 196616 | tf_op jit(solution)/shard_map/ppermute | solution.py:194
  43.7 4.5 %collective-permute-start.24 = (bf16[128,256]{1,0:T(8,128)(2,1)S(1)}, bf16[128,256]{1,0:T(8,128)(2,1)S(1)}, u32[]{:S(2)}, u32[]{:S(2)}) collective-permute-start(bf16[128,256]{1,0:T(8,128)(2,1)S(1)} %slice.82), channel_id=1, source_target_pairs={{1,2},{3,0},{5,6},{7,4},{9,10},{11,8},{13,14},{15,12},{0,1},{2,3},... | collective-permute-start | bytes 196616 | tf_op jit(solution)/shard_map/ppermute | solution.py:194
  48.6 1.5 %collective-permute-start.26 = (bf16[128,768]{1,0:T(8,128)(2,1)S(1)}, bf16[128,768]{1,0:T(8,128)(2,1)S(1)}, u32[]{:S(2)}, u32[]{:S(2)}) collective-permute-start(bf16[128,768]{1,0:T(8,128)(2,1)S(1)} %get-tuple-element.38.r_2_), channel_id=1, source_target_pairs={{0,1},{1,0},{2,3},{3,2},{4,5},{5,4},{6,7},{7,6},{8,9},{9,8},{10,11... | collective-permute-start | bytes 589832 | tf_op jit(solution)/shard_map/ppermute | solution.py:198
  48.7 3.6 %collective-permute-start.27 = (bf16[256,256]{1,0:T(8,128)(2,1)S(1)}, bf16[256,256]{1,0:T(8,128)(2,1)S(1)}, u32[]{:S(2)}, u32[]{:S(2)}) collective-permute-start(bf16[256,256]{1,0:T(8,128)(2,1)S(1)} %slice.84), channel_id=1, source_target_pairs={{0,3},{2,1},{4,7},{6,5},{8,11},{10,9},{12,15},{14,13},{1,0},{3,2},... | collective-permute-start | bytes 393224 | tf_op jit(solution)/shard_map/ppermute | solution.py:194
  52.4 5.6 %collective-permute-start.28 = (bf16[128,256]{1,0:T(8,128)(2,1)S(1)}, bf16[128,256]{1,0:T(8,128)(2,1)S(1)}, u32[]{:S(2)}, u32[]{:S(2)}) collective-permute-start(bf16[128,256]{1,0:T(8,128)(2,1)S(1)} %get-tuple-element.42), channel_id=1, source_target_pairs={{1,12},{3,14},{5,8},{7,10},{9,4},{11,6},{13,0},{15,2},{0,1},{2,3},... | collective-permute-start | bytes 196616 | tf_op jit(solution)/shard_map/ppermute | solution.py:194
  53.7 5.6 %collective-permute-start.29 = (bf16[128,256]{1,0:T(8,128)(2,1)S(1)}, bf16[128,256]{1,0:T(8,128)(2,1)S(1)}, u32[]{:S(2)}, u32[]{:S(2)}) collective-permute-start(bf16[128,256]{1,0:T(8,128)(2,1)S(1)} %get-tuple-element.42), channel_id=1, source_target_pairs={{1,8},{3,10},{5,12},{7,14},{9,0},{11,2},{13,4},{15,6},{0,1},{2,3},... | collective-permute-start | bytes 196616 | tf_op jit(solution)/shard_map/ppermute | solution.py:194
  54.4 4.9 %collective-permute-start.30 = (bf16[128,256]{1,0:T(8,128)(2,1)S(1)}, bf16[128,256]{1,0:T(8,128)(2,1)S(1)}, u32[]{:S(2)}, u32[]{:S(2)}) collective-permute-start(bf16[128,256]{1,0:T(8,128)(2,1)S(1)} %get-tuple-element.41), channel_id=1, source_target_pairs={{1,4},{3,6},{5,0},{7,2},{9,12},{11,14},{13,8},{15,10},{0,1},{2,3},... | collective-permute-start | bytes 196616 | tf_op jit(solution)/shard_map/ppermute | solution.py:194
  54.9 4.4 %collective-permute-start.31 = (bf16[128,256]{1,0:T(8,128)(2,1)S(1)}, bf16[128,256]{1,0:T(8,128)(2,1)S(1)}, u32[]{:S(2)}, u32[]{:S(2)}) collective-permute-start(bf16[128,256]{1,0:T(8,128)(2,1)S(1)} %slice.87), channel_id=1, source_target_pairs={{1,2},{3,0},{5,6},{7,4},{9,10},{11,8},{13,14},{15,12},{0,1},{2,3},... | collective-permute-start | bytes 196616 | tf_op jit(solution)/shard_map/ppermute | solution.py:194
  59.3 1.5 %collective-permute-start.32 = (bf16[128,768]{1,0:T(8,128)(2,1)S(1)}, bf16[128,768]{1,0:T(8,128)(2,1)S(1)}, u32[]{:S(2)}, u32[]{:S(2)}) collective-permute-start(bf16[128,768]{1,0:T(8,128)(2,1)S(1)} %shard_map.102.r_1_), channel_id=1, source_target_pairs={{0,1},{1,0},{2,3},{3,2},{4,5},{5,4},{6,7},{7,6},{8,9},{9,8},{10,11... | collective-permute-start | bytes 589832 | tf_op jit(solution)/shard_map/ppermute | solution.py:198

commit v7 on v6

--- a/solution.py
+++ b/solution.py
@@ -121,20 +121,28 @@
         out[level * c : (level + 1) * c, :] = total.astype(BF)
 
 
-def again_kernel(holder, place, early, mine, other, gram, here, there, out, joined):
+def again_kernel(holder, place, early, other, gram, here, there, out):
     @pl.when(place[0] == holder)
     def _():
         out[...] = early[...]
-        joined[...] = mine[...]
 
     @pl.when(place[0] != holder)
     def _():
-        joined[...] = other[...]
         c, k = out.shape[0] // LEVELS, out.shape[1]
         for level in range(LEVELS):
             cols = slice(level * k, (level + 1) * k)
-            total = here[:, cols].astype(F32) + there[:, cols].astype(F32) + mm(joined[...], gram[:, cols], 1, 0)
+            total = here[:, cols].astype(F32) + there[:, cols].astype(F32) + mm(other[...], gram[:, cols], 1, 0)
             out[level * c : (level + 1) * c, :] = total.astype(BF)
+
+
+def pick_kernel(holder, place, mine, other, out):
+    @pl.when(place[0] == holder)
+    def _():
+        out[...] = mine[...]
+
+    @pl.when(place[0] != holder)
+    def _():
+        out[...] = other[...]
 
 
 def sum_kernel(source, place, summed, received, relayed, out):
@@ -297,12 +305,10 @@
         factor, after = (lower, upper) if flipped else (upper, lower)
         packed, q = call(next_kernel, [p_shape, s_shape], (place, *pieces, gram, s, there), 2 * wide * wide * c)
         other = over_rank(q)
-        summed, q = call(
-            lambda *r: again_kernel(source, *r),
-            [p_shape, s_shape],
-            (place, packed, q, other, gram, s, there),
-            2 * wide * wide * c,
+        (summed,) = call(
+            lambda *r: again_kernel(source, *r), [p_shape], (place, packed, other, gram, s, there), 2 * wide * wide * c
         )
+        (q,) = call(lambda *r: pick_kernel(source, *r), [s_shape], (place, q, other), 0)
         (y,) = call(lambda *r: field_kernel(not flipped, *r), [y_shape], (place, q, factor, y, leaves), field_flops // 2)
         if step + 2 < applies:
             (s,) = call(project_kernel, [s_shape], (place, y, after), field_flops // 2)

time: 62.4 us -> 63.1 us (1.011)
  starting transfers between devices: 22.5 us -> 28.3 us
  waiting for transfers between devices: 23.5 us -> 18.4 us
    ppermute x21, starting transfers between devices: 20 us -> 25.8 us  [one_way(): return lax.ppermute(value, ('rows', 'cols', 'rank'), away + home)]
    ppermute x21, waiting for transfers between devices: 20.7 us -> 16.1 us  [one_way(): return lax.ppermute(value, ('rows', 'cols', 'rank'), away + home)]
    pallas_call x23 -> x26, Pallas kernels: 12.3 us -> 12.3 us  [call(): pl.pallas_call(kernel, out_shape=outs, in_specs=[pl.BlockSpec(memory_spac...]
  transfers between devices with their start and end apart: 33 -> 33, of which waited for: 19 -> 15; matrix products, arithmetic and copies ran while one was open for 0% -> 0% of each run, Pallas kernels for 16% -> 16%
where the time goes in v7:
time: 63.1 us; the launch traced here: 62.9 us
  starting transfers between devices  28.3 us (45%)
  waiting for transfers between devices  18.4 us (29%)
  Pallas kernels  12.3 us (19%)
  local copies, waits for them, and re-layouts  3.39 us (5%)
    ppermute x21, starting transfers between devices, one_way(): return lax.ppermute(value, ('rows', 'cols', 'rank'), away + home)  25.8 us
    ppermute x21, waiting for transfers between devices, one_way(): return lax.ppermute(value, ('rows', 'cols', 'rank'), away + home)  16.1 us
    pallas_call x26, Pallas kernels, call(): pl.pallas_call(kernel, out_shape=outs, in_specs=[pl.BlockSpec(memory_spac...  12.3 us
    unnamed x22, local copies, waits for them, and re-layouts  3.28 us
    ppermute x12, starting transfers between devices, over_rank(): return lax.ppermute(value, 'rank', [(0, 1), (1, 0)])  2.53 us
    ppermute x12, waiting for transfers between devices, over_rank(): return lax.ppermute(value, 'rank', [(0, 1), (1, 0)])  2.28 us
  transfers between devices with their start and end apart: 33, of which 15 were waited for; matrix products, arithmetic and copies ran while one was open for 0% of the time, Pallas kernels for 16%

profile of v7, /device:TPU:0, one launch (start us, length us, event | category | flops | bytes accessed | tf_op | source)
XLA Modules:
  0.0 62.9 jit_solution(9338632018412796538)
XLA Ops:
  0.0 1.2 %copy-done.8 = bf16[2048,128]{1,0:T(8,128)(2,1)S(1)} copy-done((bf16[2048,128]{1,0:T(8,128)(2,1)S(1)}, bf16[2048,128]{1,0:T(8,128)(2,1)}, u32[]{:S(2)}) %copy-start.8) | copy-done | bytes 524312
  1.2 1.0 %copy-done.9 = bf16[2048,128]{1,0:T(8,128)(2,1)S(1)} copy-done((bf16[2048,128]{1,0:T(8,128)(2,1)S(1)}, bf16[2048,128]{1,0:T(8,128)(2,1)}, u32[]{:S(2)}) %copy-start.9) | copy-done | bytes 524312
  2.2 1.0 %copy-done.10 = bf16[2048,128]{1,0:T(8,128)(2,1)S(1)} copy-done((bf16[2048,128]{1,0:T(8,128)(2,1)S(1)}, bf16[2048,128]{1,0:T(8,128)(2,1)}, u32[]{:S(2)}) %copy-start.10) | copy-done | bytes 524312
  3.3 0.6 collective-permute-start.7
  4.0 1.7 %collective-permute-done.7.other = bf16[3072,128]{1,0:T(8,128)(2,1)S(1)} collective-permute-done((bf16[3072,128]{1,0:T(8,128)(2,1)S(1)}, bf16[3072,128]{1,0:T(8,128)(2,1)S(1)}, u32[]{:S(2)}, u32[]{:S(2)}) %collective-permute-start.7) | collective-permute-done | bytes 786464 | tf_op jit(solution)/shard_map/ppermute | solution.py:206
  5.8 1.3 %shard_map.86 = (bf16[1024,768]{1,0:T(8,128)(2,1)S(1)}, bf16[1536,256]{1,0:T(8,128)(2,1)S(1)}) custom-call(s32[1]{0:T(128)} %bitcast.place.r_0_, bf16[3072,128]{1,0:T(8,128)(2,1)S(1)} %collective-permute-done.7.other, bf16[2048,128]{1,0:T(8,128)(2,1)S(1)} %copy-done.8, bf16[2048,128]{1,0:T(8,128)(2,1)S(1)} %copy-done.9, bf16[2048,128]{1,0:T(8,128)(2,1)S(1)} %copy-done.10), custom_call_target="tpu_custom_call" | custom-call | flops 905969664 | bytes 4718592 | tf_op jit(solution)/shard_map/pallas_call | solution.py:27
  7.2 0.4 collective-permute-start.8
  7.6 2.3 %shard_map.82.own = bf16[384,128]{1,0:T(8,128)(2,1)S(1)} custom-call(s32[1]{0:T(128)} %bitcast.place.r_0_, bf16[2048,128]{1,0:T(8,128)(2,1)} %z.1, bf16[2048,128]{1,0:T(8,128)(2,1)} %refs_0_.9, bf16[2048,128]{1,0:T(8,128)(2,1)} %refs_1_.9, bf16[2048,128]{1,0:T(8,128)(2,1)} %refs_2_.9), custom_call_target="tpu_custom_call" | custom-call | flops 201326592 | bytes 2195456 | tf_op jit(solution)/shard_map/pallas_call | solution.py:27
  10.2 2.6 %collective-permute-start.1 = (bf16[256,128]{1,0:T(8,128)(2,1)S(1)}, bf16[256,128]{1,0:T(8,128)(2,1)S(1)}, u32[]{:S(2)}, u32[]{:S(2)}) collective-permute-start(bf16[256,128]{1,0:T(8,128)(2,1)S(1)} %slice.89), channel_id=1, source_target_pairs={{0,3},{2,1},{4,7},{6,5},{8,11},{10,9},{12,15},{14,13},{1,0},{3,2},... | collective-permute-start | bytes 196616 | tf_op jit(solution)/shard_map/ppermute | solution.py:202
  12.8 1.1 %collective-permute-start.2 = (bf16[256,128]{1,0:T(8,128)(2,1)S(1)}, bf16[256,128]{1,0:T(8,128)(2,1)S(1)}, u32[]{:S(2)}, u32[]{:S(2)}) collective-permute-start(bf16[256,128]{1,0:T(8,128)(2,1)S(1)} %slice.90), channel_id=1, source_target_pairs={{0,3},{2,1},{4,7},{6,5},{8,11},{10,9},{12,15},{14,13},{1,0},{3,2},... | collective-permute-start | bytes 196616 | tf_op jit(solution)/shard_map/ppermute | solution.py:202
  14.0 0.7 %collective-permute-done.1.left = bf16[256,128]{1,0:T(8,128)(2,1)S(1)} collective-permute-done((bf16[256,128]{1,0:T(8,128)(2,1)S(1)}, bf16[256,128]{1,0:T(8,128)(2,1)S(1)}, u32[]{:S(2)}, u32[]{:S(2)}) %collective-permute-start.1) | collective-permute-done | bytes 65568 | tf_op jit(solution)/shard_map/ppermute | solution.py:202
  14.7 1.3 %collective-permute-done.2.right = bf16[256,128]{1,0:T(8,128)(2,1)S(1)} collective-permute-done((bf16[256,128]{1,0:T(8,128)(2,1)S(1)}, bf16[256,128]{1,0:T(8,128)(2,1)S(1)}, u32[]{:S(2)}, u32[]{:S(2)}) %collective-permute-start.2) | collective-permute-done | bytes 65568 | tf_op jit(solution)/shard_map/ppermute | solution.py:202
  16.1 0.7 %shard_map.88 = (f32[1024,128]{1,0:T(8,128)S(1)}, bf16[128,768]{1,0:T(8,128)(2,1)S(1)}) custom-call(s32[1]{0:T(128)} %bitcast.place.r_0_, bf16[2048,128]{1,0:T(8,128)(2,1)S(1)} %copy-done.7, bf16[4,256,256]{2,1,0:T(8,128)(2,1)S(1)} %copy-done, bf16[1024,768]{1,0:T(8,128)(2,1)S(1)} %get-tuple-element.18.after.r_2_), custom_call_target="tpu_custom_call" | custom-call | flops 201326592 | bytes 3342336 | tf_op jit(solution)/shard_map/pallas_call | solution.py:27
  17.0 0.5 collective-permute-start.4
  17.7 2.5 %collective-permute-start.3 = (bf16[128,256]{1,0:T(8,128)(2,1)S(1)}, bf16[128,256]{1,0:T(8,128)(2,1)S(1)}, u32[]{:S(2)}, u32[]{:S(2)}) collective-permute-start(bf16[128,256]{1,0:T(8,128)(2,1)S(1)} %get-tuple-element.36), channel_id=1, source_target_pairs={{1,12},{3,14},{5,8},{7,10},{9,4},{11,6},{13,0},{15,2},{0,1},{2,3},... | collective-permute-start | bytes 196616 | tf_op jit(solution)/shard_map/ppermute | solution.py:202
  20.2 1.4 %collective-permute-start.5 = (bf16[128,256]{1,0:T(8,128)(2,1)S(1)}, bf16[128,256]{1,0:T(8,128)(2,1)S(1)}, u32[]{:S(2)}, u32[]{:S(2)}) collective-permute-start(bf16[128,256]{1,0:T(8,128)(2,1)S(1)} %get-tuple-element.35), channel_id=1, source_target_pairs={{1,4},{3,6},{5,0},{7,2},{9,12},{11,14},{13,8},{15,10},{0,1},{2,3},... | collective-permute-start | bytes 196616 | tf_op jit(solution)/shard_map/ppermute | solution.py:202
  21.6 1.3 %shard_map.92 = (bf16[1024,768]{1,0:T(8,128)(2,1)S(1)}, bf16[1536,256]{1,0:T(8,128)(2,1)S(1)}) custom-call(s32[1]{0:T(128)} %bitcast.place.r_0_, bf16[3072,128]{1,0:T(8,128)(2,1)S(1)} %collective-permute-done.16.other, bf16[2048,128]{1,0:T(8,128)(2,1)S(1)} %copy-done.2, bf16[2048,128]{1,0:T(8,128)(2,1)S(1)} %copy-done.4, bf16[2048,128]{1,0:T(8,128)(2,1)S(1)} %copy-done.6), custom_call_target="tpu_custom_call" | custom-call | flops 905969664 | bytes 4718592 | tf_op jit(solution)/shard_map/pallas_call | solution.py:27
  23.6 1.0 %collective-permute-done.5.two = bf16[128,256]{1,0:T(8,128)(2,1)S(1)} collective-permute-done((bf16[128,256]{1,0:T(8,128)(2,1)S(1)}, bf16[128,256]{1,0:T(8,128)(2,1)S(1)}, u32[]{:S(2)}, u32[]{:S(2)}) %collective-permute-start.5) | collective-permute-done | bytes 65568 | tf_op jit(solution)/shard_map/ppermute | solution.py:202
  25.0 2.5 %collective-permute-start.11 = (bf16[256,256]{1,0:T(8,128)(2,1)S(1)}, bf16[256,256]{1,0:T(8,128)(2,1)S(1)}, u32[]{:S(2)}, u32[]{:S(2)}) collective-permute-start(bf16[256,256]{1,0:T(8,128)(2,1)S(1)} %slice.74), channel_id=1, source_target_pairs={{0,3},{2,1},{4,7},{6,5},{8,11},{10,9},{12,15},{14,13},{1,0},{3,2},... | collective-permute-start | bytes 393224 | tf_op jit(solution)/shard_map/ppermute | solution.py:202
  27.6 0.9 %shard_map.95.y.r_3_ = f32[1024,128]{1,0:T(8,128)S(1)} custom-call(s32[1]{0:T(128)} %bitcast.place.r_0_, bf16[128,768]{1,0:T(8,128)(2,1)S(1)} %shard_map.94.r_1_, bf16[1024,768]{1,0:T(8,128)(2,1)S(1)} %get-tuple-element.18.after.r_2_, f32[1024,128]{1,0:T(8,128)S(1)} %get-tuple-element.23.r_3_, bf16[4,256,256]{2,1,0:T(8,128)(2,1)S(1)} %copy-done), custom_call_target="tpu_custom_call" | custom-call | flops 201326592 | bytes 3342336 | tf_op jit(solution)/shard_map/pallas_call | solution.py:27
  28.5 0.4 shard_map.96.here.r_4_
  29.0 1.1 %collective-permute-done.11 = bf16[256,256]{1,0:T(8,128)(2,1)S(1)} collective-permute-done((bf16[256,256]{1,0:T(8,128)(2,1)S(1)}, bf16[256,256]{1,0:T(8,128)(2,1)S(1)}, u32[]{:S(2)}, u32[]{:S(2)}) %collective-permute-start.11) | collective-permute-done | bytes 131104 | tf_op jit(solution)/shard_map/ppermute | solution.py:202
  30.3 1.0 %collective-permute-start.13 = (bf16[128,256]{1,0:T(8,128)(2,1)S(1)}, bf16[128,256]{1,0:T(8,128)(2,1)S(1)}, u32[]{:S(2)}, u32[]{:S(2)}) collective-permute-start(bf16[128,256]{1,0:T(8,128)(2,1)S(1)} %get-tuple-element.34), channel_id=1, source_target_pairs={{1,8},{3,10},{5,12},{7,14},{9,0},{11,2},{13,4},{15,6},{0,1},{2,3},... | collective-permute-start | bytes 196616 | tf_op jit(solution)/shard_map/ppermute | solution.py:202
  31.3 1.4 %collective-permute-start.12 = (bf16[128,256]{1,0:T(8,128)(2,1)S(1)}, bf16[128,256]{1,0:T(8,128)(2,1)S(1)}, u32[]{:S(2)}, u32[]{:S(2)}) collective-permute-start(bf16[128,256]{1,0:T(8,128)(2,1)S(1)} %get-tuple-element.34), channel_id=1, source_target_pairs={{1,12},{3,14},{5,8},{7,10},{9,4},{11,6},{13,0},{15,2},{0,1},{2,3},... | collective-permute-start | bytes 196616 | tf_op jit(solution)/shard_map/ppermute | solution.py:202
  32.7 1.4 %collective-permute-start.15 = (bf16[128,256]{1,0:T(8,128)(2,1)S(1)}, bf16[128,256]{1,0:T(8,128)(2,1)S(1)}, u32[]{:S(2)}, u32[]{:S(2)}) collective-permute-start(bf16[128,256]{1,0:T(8,128)(2,1)S(1)} %slice.97), channel_id=1, source_target_pairs={{1,2},{3,0},{5,6},{7,4},{9,10},{11,8},{13,14},{15,12},{0,1},{2,3},... | collective-permute-start | bytes 196616 | tf_op jit(solution)/shard_map/ppermute | solution.py:202
  34.4 0.5 collective-permute-done.13.more
  34.9 2.1 %collective-permute-done.12.one = bf16[128,256]{1,0:T(8,128)(2,1)S(1)} collective-permute-done((bf16[128,256]{1,0:T(8,128)(2,1)S(1)}, bf16[128,256]{1,0:T(8,128)(2,1)S(1)}, u32[]{:S(2)}, u32[]{:S(2)}) %collective-permute-start.12) | collective-permute-done | bytes 65568 | tf_op jit(solution)/shard_map/ppermute | solution.py:202
  37.4 1.6 %collective-permute-start.20 = (bf16[256,256]{1,0:T(8,128)(2,1)S(1)}, bf16[256,256]{1,0:T(8,128)(2,1)S(1)}, u32[]{:S(2)}, u32[]{:S(2)}) collective-permute-start(bf16[256,256]{1,0:T(8,128)(2,1)S(1)} %slice.79), channel_id=1, source_target_pairs={{0,3},{2,1},{4,7},{6,5},{8,11},{10,9},{12,15},{14,13},{1,0},{3,2},... | collective-permute-start | bytes 393224 | tf_op jit(solution)/shard_map/ppermute | solution.py:202
  39.1 0.9 %shard_map.100.y.r_3_ = f32[1024,128]{1,0:T(8,128)S(1)} custom-call(s32[1]{0:T(128)} %bitcast.place.r_0_, bf16[128,768]{1,0:T(8,128)(2,1)S(1)} %shard_map.99.r_1_, bf16[1024,768]{1,0:T(8,128)(2,1)S(1)} %get-tuple-element.24.after.r_2_.r_3_, f32[1024,128]{1,0:T(8,128)S(1)} %shard_map.95.y.r_3_, bf16[4,256,256]{2,1,0:T(8,128)(2,1)S(1)} %copy-done), custom_call_target="tpu_custom_call" | custom-call | flops 201326592 | bytes 3342336 | tf_op jit(solution)/shard_map/pallas_call | solution.py:27
  40.0 0.4 shard_map.101.here.r_4_
  40.7 0.9 %collective-permute-done.20 = bf16[256,256]{1,0:T(8,128)(2,1)S(1)} collective-permute-done((bf16[256,256]{1,0:T(8,128)(2,1)S(1)}, bf16[256,256]{1,0:T(8,128)(2,1)S(1)}, u32[]{:S(2)}, u32[]{:S(2)}) %collective-permute-start.20) | collective-permute-done | bytes 131104 | tf_op jit(solution)/shard_map/ppermute | solution.py:202
  41.6 0.8 %collective-permute-start.23 = (bf16[128,256]{1,0:T(8,128)(2,1)S(1)}, bf16[128,256]{1,0:T(8,128)(2,1)S(1)}, u32[]{:S(2)}, u32[]{:S(2)}) collective-permute-start(bf16[128,256]{1,0:T(8,128)(2,1)S(1)} %get-tuple-element.31), channel_id=1, source_target_pairs={{1,4},{3,6},{5,0},{7,2},{9,12},{11,14},{13,8},{15,10},{0,1},{2,3},... | collective-permute-start | bytes 196616 | tf_op jit(solution)/shard_map/ppermute | solution.py:202
  42.5 0.5 collective-permute-start.22
  43.0 1.2 %collective-permute-start.21 = (bf16[128,256]{1,0:T(8,128)(2,1)S(1)}, bf16[128,256]{1,0:T(8,128)(2,1)S(1)}, u32[]{:S(2)}, u32[]{:S(2)}) collective-permute-start(bf16[128,256]{1,0:T(8,128)(2,1)S(1)} %get-tuple-element.32), channel_id=1, source_target_pairs={{1,12},{3,14},{5,8},{7,10},{9,4},{11,6},{13,0},{15,2},{0,1},{2,3},... | collective-permute-start | bytes 196616 | tf_op jit(solution)/shard_map/ppermute | solution.py:202
  44.2 1.4 %collective-permute-start.24 = (bf16[128,256]{1,0:T(8,128)(2,1)S(1)}, bf16[128,256]{1,0:T(8,128)(2,1)S(1)}, u32[]{:S(2)}, u32[]{:S(2)}) collective-permute-start(bf16[128,256]{1,0:T(8,128)(2,1)S(1)} %slice.101), channel_id=1, source_target_pairs={{1,2},{3,0},{5,6},{7,4},{9,10},{11,8},{13,14},{15,12},{0,1},{2,3},... | collective-permute-start | bytes 196616 | tf_op jit(solution)/shard_map/ppermute | solution.py:202
  45.6 1.5 %collective-permute-done.22.more = bf16[128,256]{1,0:T(8,128)(2,1)S(1)} collective-permute-done((bf16[128,256]{1,0:T(8,128)(2,1)S(1)}, bf16[128,256]{1,0:T(8,128)(2,1)S(1)}, u32[]{:S(2)}, u32[]{:S(2)}) %collective-permute-start.22) | collective-permute-done | bytes 65568 | tf_op jit(solution)/shard_map/ppermute | solution.py:202
  47.1 1.5 %collective-permute-done.21.one = bf16[128,256]{1,0:T(8,128)(2,1)S(1)} collective-permute-done((bf16[128,256]{1,0:T(8,128)(2,1)S(1)}, bf16[128,256]{1,0:T(8,128)(2,1)S(1)}, u32[]{:S(2)}, u32[]{:S(2)}) %collective-permute-start.21) | collective-permute-done | bytes 65568 | tf_op jit(solution)/shard_map/ppermute | solution.py:202
  49.0 1.6 %collective-permute-start.27 = (bf16[256,256]{1,0:T(8,128)(2,1)S(1)}, bf16[256,256]{1,0:T(8,128)(2,1)S(1)}, u32[]{:S(2)}, u32[]{:S(2)}) collective-permute-start(bf16[256,256]{1,0:T(8,128)(2,1)S(1)} %slice.84), channel_id=1, source_target_pairs={{0,3},{2,1},{4,7},{6,5},{8,11},{10,9},{12,15},{14,13},{1,0},{3,2},... | collective-permute-start | bytes 393224 | tf_op jit(solution)/shard_map/ppermute | solution.py:202
  50.6 2.5 %collective-permute-done.27 = bf16[256,256]{1,0:T(8,128)(2,1)S(1)} collective-permute-done((bf16[256,256]{1,0:T(8,128)(2,1)S(1)}, bf16[256,256]{1,0:T(8,128)(2,1)S(1)}, u32[]{:S(2)}, u32[]{:S(2)}) %collective-permute-start.27) | collective-permute-done | bytes 131104 | tf_op jit(solution)/shard_map/ppermute | solution.py:202
  53.1 0.9 %collective-permute-start.30 = (bf16[128,256]{1,0:T(8,128)(2,1)S(1)}, bf16[128,256]{1,0:T(8,128)(2,1)S(1)}, u32[]{:S(2)}, u32[]{:S(2)}) collective-permute-start(bf16[128,256]{1,0:T(8,128)(2,1)S(1)} %get-tuple-element.29), channel_id=1, source_target_pairs={{1,4},{3,6},{5,0},{7,2},{9,12},{11,14},{13,8},{15,10},{0,1},{2,3},... | collective-permute-start | bytes 196616 | tf_op jit(solution)/shard_map/ppermute | solution.py:202
  54.0 0.5 collective-permute-start.29
  54.5 1.8 %collective-permute-start.28 = (bf16[128,256]{1,0:T(8,128)(2,1)S(1)}, bf16[128,256]{1,0:T(8,128)(2,1)S(1)}, u32[]{:S(2)}, u32[]{:S(2)}) collective-permute-start(bf16[128,256]{1,0:T(8,128)(2,1)S(1)} %get-tuple-element.30), channel_id=1, source_target_pairs={{1,12},{3,14},{5,8},{7,10},{9,4},{11,6},{13,0},{15,2},{0,1},{2,3},... | collective-permute-start | bytes 196616 | tf_op jit(solution)/shard_map/ppermute | solution.py:202
  56.3 0.8 %collective-permute-start.31 = (bf16[128,256]{1,0:T(8,128)(2,1)S(1)}, bf16[128,256]{1,0:T(8,128)(2,1)S(1)}, u32[]{:S(2)}, u32[]{:S(2)}) collective-permute-start(bf16[128,256]{1,0:T(8,128)(2,1)S(1)} %slice.105), channel_id=1, source_target_pairs={{1,2},{3,0},{5,6},{7,4},{9,10},{11,8},{13,14},{15,12},{0,1},{2,3},... | collective-permute-start | bytes 196616 | tf_op jit(solution)/shard_map/ppermute | solution.py:202
  57.2 1.4 %collective-permute-done.29.more = bf16[128,256]{1,0:T(8,128)(2,1)S(1)} collective-permute-done((bf16[128,256]{1,0:T(8,128)(2,1)S(1)}, bf16[128,256]{1,0:T(8,128)(2,1)S(1)}, u32[]{:S(2)}, u32[]{:S(2)}) %collective-permute-start.29) | collective-permute-done | bytes 65568 | tf_op jit(solution)/shard_map/ppermute | solution.py:202
  58.6 1.5 %collective-permute-done.28.one = bf16[128,256]{1,0:T(8,128)(2,1)S(1)} collective-permute-done((bf16[128,256]{1,0:T(8,128)(2,1)S(1)}, bf16[128,256]{1,0:T(8,128)(2,1)S(1)}, u32[]{:S(2)}, u32[]{:S(2)}) %collective-permute-start.28) | collective-permute-done | bytes 65568 | tf_op jit(solution)/shard_map/ppermute | solution.py:202
  60.2 0.9 %shard_map.106.r_4_ = f32[1024,128]{1,0:T(8,128)S(1)} custom-call(s32[1]{0:T(128)} %bitcast.place.r_0_, bf16[128,768]{1,0:T(8,128)(2,1)S(1)} %shard_map.105.r_1_, bf16[1024,768]{1,0:T(8,128)(2,1)S(1)} %get-tuple-element.18.after.r_2_, f32[1024,128]{1,0:T(8,128)S(1)} %shard_map.100.y.r_3_, bf16[4,256,256]{2,1,0:T(8,128)(2,1)S(1)} %copy-done), custom_call_target="tpu_custom_call" | custom-call | flops 201326592 | bytes 3342336 | tf_op jit(solution)/shard_map/pallas_call | solution.py:27
  61.1 0.5 collective-permute-done.32.r_2_
  61.6 1.3 %shard_map.107 = bf16[1024,128]{1,0:T(8,128)(2,1)} custom-call(s32[1]{0:T(128)} %bitcast.place.r_0_, bf16[128,768]{1,0:T(8,128)(2,1)S(1)} %shard_map.104.r_1_, bf16[128,768]{1,0:T(8,128)(2,1)S(1)} %collective-permute-done.32.r_2_, bf16[1024,768]{1,0:T(8,128)(2,1)S(1)} %get-tuple-element.24.after.r_2_.r_3_, f32[1024,128]{1,0:T(8,128)S(1)} %shard_map.106.r_4_), custom_call_target="tpu_custom_call" | custom-call | flops 201326592 | bytes 2752512 | tf_op jit(solution)/shard_map/pallas_call | solution.py:27
  (83 shorter events, 4.1 us)
Async XLA Ops:
  0.0 3.9 %copy-start.5 = (bf16[2048,128]{1,0:T(8,128)(2,1)S(1)}, bf16[2048,128]{1,0:T(8,128)(2,1)}, u32[]{:S(2)}) copy-start(bf16[2048,128]{1,0:T(8,128)(2,1)} %refs_2_.9) | copy-start | bytes 1572868
  0.0 3.9 %copy-start.3 = (bf16[2048,128]{1,0:T(8,128)(2,1)S(1)}, bf16[2048,128]{1,0:T(8,128)(2,1)}, u32[]{:S(2)}) copy-start(bf16[2048,128]{1,0:T(8,128)(2,1)} %refs_1_.9) | copy-start | bytes 1572868
  0.0 3.9 %copy-start.1 = (bf16[2048,128]{1,0:T(8,128)(2,1)S(1)}, bf16[2048,128]{1,0:T(8,128)(2,1)}, u32[]{:S(2)}) copy-start(bf16[2048,128]{1,0:T(8,128)(2,1)} %refs_0_.9) | copy-start | bytes 1572868
  0.0 1.2 %copy-start.8 = (bf16[2048,128]{1,0:T(8,128)(2,1)S(1)}, bf16[2048,128]{1,0:T(8,128)(2,1)}, u32[]{:S(2)}) copy-start(bf16[2048,128]{1,0:T(8,128)(2,1)} %refs_0_.7) | copy-start | bytes 1572868
  1.2 1.0 %copy-start.9 = (bf16[2048,128]{1,0:T(8,128)(2,1)S(1)}, bf16[2048,128]{1,0:T(8,128)(2,1)}, u32[]{:S(2)}) copy-start(bf16[2048,128]{1,0:T(8,128)(2,1)} %refs_1_.7) | copy-start | bytes 1572868
  2.2 1.0 %copy-start.10 = (bf16[2048,128]{1,0:T(8,128)(2,1)S(1)}, bf16[2048,128]{1,0:T(8,128)(2,1)}, u32[]{:S(2)}) copy-start(bf16[2048,128]{1,0:T(8,128)(2,1)} %refs_2_.7) | copy-start | bytes 1572868
  3.3 2.5 %collective-permute-start.7 = (bf16[3072,128]{1,0:T(8,128)(2,1)S(1)}, bf16[3072,128]{1,0:T(8,128)(2,1)S(1)}, u32[]{:S(2)}, u32[]{:S(2)}) collective-permute-start(bf16[3072,128]{1,0:T(8,128)(2,1)S(1)} %shard_map.85), channel_id=1, source_target_pairs={{0,1},{1,0},{2,3},{3,2},{4,5},{5,4},{6,7},{7,6},{8,9},{9,8},{10,11... | collective-permute-start | bytes 2359304 | tf_op jit(solution)/shard_map/ppermute | solution.py:206
  3.9 16.2 %collective-permute-start.16 = (bf16[3072,128]{1,0:T(8,128)(2,1)S(1)}, bf16[3072,128]{1,0:T(8,128)(2,1)S(1)}, u32[]{:S(2)}, u32[]{:S(2)}) collective-permute-start(bf16[3072,128]{1,0:T(8,128)(2,1)S(1)} %shard_map.91), channel_id=1, source_target_pairs={{0,1},{1,0},{2,3},{3,2},{4,5},{5,4},{6,7},{7,6},{8,9},{9,8},{10,11... | collective-permute-start | bytes 2359304 | tf_op jit(solution)/shard_map/ppermute | solution.py:206
  7.1 9.0 %copy-start = (bf16[4,256,256]{2,1,0:T(8,128)(2,1)S(1)}, bf16[4,256,256]{2,1,0:T(8,128)(2,1)}, u32[]{:S(2)}) copy-start(bf16[4,256,256]{2,1,0:T(8,128)(2,1)} %r_4_.5) | copy-start | bytes 1572868
  7.1 9.0 %copy-start.7 = (bf16[2048,128]{1,0:T(8,128)(2,1)S(1)}, bf16[2048,128]{1,0:T(8,128)(2,1)}, u32[]{:S(2)}) copy-start(bf16[2048,128]{1,0:T(8,128)(2,1)} %z.1) | copy-start | bytes 1572868
  7.2 15.7 %collective-permute-start.8 = (bf16[1536,256]{1,0:T(8,128)(2,1)S(1)}, bf16[1536,256]{1,0:T(8,128)(2,1)S(1)}, u32[]{:S(2)}, u32[]{:S(2)}) collective-permute-start(bf16[1536,256]{1,0:T(8,128)(2,1)S(1)} %get-tuple-element.17.mine), channel_id=1, source_target_pairs={{0,1},{1,0},{2,3},{3,2},{4,5},{5,4},{6,7},{7,6},{8,9},{9,8},{10,11... | collective-permute-start | bytes 2359304 | tf_op jit(solution)/shard_map/ppermute | solution.py:206
  9.9 2.9 %collective-permute-start = (bf16[384,128]{1,0:T(8,128)(2,1)S(1)}, bf16[384,128]{1,0:T(8,128)(2,1)S(1)}, u32[]{:S(2)}, u32[]{:S(2)}) collective-permute-start(bf16[384,128]{1,0:T(8,128)(2,1)S(1)} %shard_map.82.own), channel_id=1, source_target_pairs={{0,1},{1,0},{2,3},{3,2},{4,5},{5,4},{6,7},{7,6},{8,9},{9,8},{10,11... | collective-permute-start | bytes 294920 | tf_op jit(solution)/shard_map/ppermute | solution.py:206
  10.2 4.5 %collective-permute-start.1 = (bf16[256,128]{1,0:T(8,128)(2,1)S(1)}, bf16[256,128]{1,0:T(8,128)(2,1)S(1)}, u32[]{:S(2)}, u32[]{:S(2)}) collective-permute-start(bf16[256,128]{1,0:T(8,128)(2,1)S(1)} %slice.89), channel_id=1, source_target_pairs={{0,3},{2,1},{4,7},{6,5},{8,11},{10,9},{12,15},{14,13},{1,0},{3,2},... | collective-permute-start | bytes 196616 | tf_op jit(solution)/shard_map/ppermute | solution.py:202
  12.8 3.2 %collective-permute-start.2 = (bf16[256,128]{1,0:T(8,128)(2,1)S(1)}, bf16[256,128]{1,0:T(8,128)(2,1)S(1)}, u32[]{:S(2)}, u32[]{:S(2)}) collective-permute-start(bf16[256,128]{1,0:T(8,128)(2,1)S(1)} %slice.90), channel_id=1, source_target_pairs={{0,3},{2,1},{4,7},{6,5},{8,11},{10,9},{12,15},{14,13},{1,0},{3,2},... | collective-permute-start | bytes 196616 | tf_op jit(solution)/shard_map/ppermute | solution.py:202
  13.9 3.7 %collective-permute-start.6 = (bf16[128,256]{1,0:T(8,128)(2,1)S(1)}, bf16[128,256]{1,0:T(8,128)(2,1)S(1)}, u32[]{:S(2)}, u32[]{:S(2)}) collective-permute-start(bf16[128,256]{1,0:T(8,128)(2,1)S(1)} %slice.93), channel_id=1, source_target_pairs={{1,2},{3,0},{5,6},{7,4},{9,10},{11,8},{13,14},{15,12},{0,1},{2,3},... | collective-permute-start | bytes 196616 | tf_op jit(solution)/shard_map/ppermute | solution.py:202
  16.1 5.5 %copy-start.2 = (bf16[2048,128]{1,0:T(8,128)(2,1)S(1)}, bf16[2048,128]{1,0:T(8,128)(2,1)}, u32[]{:S(2)}) copy-start(bf16[2048,128]{1,0:T(8,128)(2,1)} %refs_0_.9) | copy-start | bytes 1572868
  16.1 5.5 %copy-start.4 = (bf16[2048,128]{1,0:T(8,128)(2,1)S(1)}, bf16[2048,128]{1,0:T(8,128)(2,1)}, u32[]{:S(2)}) copy-start(bf16[2048,128]{1,0:T(8,128)(2,1)} %refs_1_.9) | copy-start | bytes 1572868
  16.1 5.5 %copy-start.6 = (bf16[2048,128]{1,0:T(8,128)(2,1)S(1)}, bf16[2048,128]{1,0:T(8,128)(2,1)}, u32[]{:S(2)}) copy-start(bf16[2048,128]{1,0:T(8,128)(2,1)} %refs_2_.9) | copy-start | bytes 1572868
  16.9 7.7 %collective-permute-start.9 = (bf16[128,768]{1,0:T(8,128)(2,1)S(1)}, bf16[128,768]{1,0:T(8,128)(2,1)S(1)}, u32[]{:S(2)}, u32[]{:S(2)}) collective-permute-start(bf16[128,768]{1,0:T(8,128)(2,1)S(1)} %get-tuple-element.19.here.r_4_), channel_id=1, source_target_pairs={{0,1},{1,0},{2,3},{3,2},{4,5},{5,4},{6,7},{7,6},{8,9},{9,8},{10,11... | collective-permute-start | bytes 589832 | tf_op jit(solution)/shard_map/ppermute | solution.py:206
  17.0 7.6 %collective-permute-start.4 = (bf16[128,256]{1,0:T(8,128)(2,1)S(1)}, bf16[128,256]{1,0:T(8,128)(2,1)S(1)}, u32[]{:S(2)}, u32[]{:S(2)}) collective-permute-start(bf16[128,256]{1,0:T(8,128)(2,1)S(1)} %get-tuple-element.36), channel_id=1, source_target_pairs={{1,8},{3,10},{5,12},{7,14},{9,0},{11,2},{13,4},{15,6},{0,1},{2,3},... | collective-permute-start | bytes 196616 | tf_op jit(solution)/shard_map/ppermute | solution.py:202
  17.7 6.9 %collective-permute-start.3 = (bf16[128,256]{1,0:T(8,128)(2,1)S(1)}, bf16[128,256]{1,0:T(8,128)(2,1)S(1)}, u32[]{:S(2)}, u32[]{:S(2)}) collective-permute-start(bf16[128,256]{1,0:T(8,128)(2,1)S(1)} %get-tuple-element.36), channel_id=1, source_target_pairs={{1,12},{3,14},{5,8},{7,10},{9,4},{11,6},{13,0},{15,2},{0,1},{2,3},... | collective-permute-start | bytes 196616 | tf_op jit(solution)/shard_map/ppermute | solution.py:202
  20.2 4.4 %collective-permute-start.5 = (bf16[128,256]{1,0:T(8,128)(2,1)S(1)}, bf16[128,256]{1,0:T(8,128)(2,1)S(1)}, u32[]{:S(2)}, u32[]{:S(2)}) collective-permute-start(bf16[128,256]{1,0:T(8,128)(2,1)S(1)} %get-tuple-element.35), channel_id=1, source_target_pairs={{1,4},{3,6},{5,0},{7,2},{9,12},{11,14},{13,8},{15,10},{0,1},{2,3},... | collective-permute-start | bytes 196616 | tf_op jit(solution)/shard_map/ppermute | solution.py:202
  22.9 9.8 %collective-permute-start.17 = (bf16[1536,256]{1,0:T(8,128)(2,1)S(1)}, bf16[1536,256]{1,0:T(8,128)(2,1)S(1)}, u32[]{:S(2)}, u32[]{:S(2)}) collective-permute-start(bf16[1536,256]{1,0:T(8,128)(2,1)S(1)} %get-tuple-element.22.mine), channel_id=1, source_target_pairs={{0,1},{1,0},{2,3},{3,2},{4,5},{5,4},{6,7},{7,6},{8,9},{9,8},{10,11... | collective-permute-start | bytes 2359304 | tf_op jit(solution)/shard_map/ppermute | solution.py:206
  24.9 2.6 %collective-permute-start.10 = (bf16[128,768]{1,0:T(8,128)(2,1)S(1)}, bf16[128,768]{1,0:T(8,128)(2,1)S(1)}, u32[]{:S(2)}, u32[]{:S(2)}) collective-permute-start(bf16[128,768]{1,0:T(8,128)(2,1)S(1)} %get-tuple-element.21.r_1_), channel_id=1, source_target_pairs={{0,1},{1,0},{2,3},{3,2},{4,5},{5,4},{6,7},{7,6},{8,9},{9,8},{10,11... | collective-permute-start | bytes 589832 | tf_op jit(solution)/shard_map/ppermute | solution.py:206
  25.0 5.0 %collective-permute-start.11 = (bf16[256,256]{1,0:T(8,128)(2,1)S(1)}, bf16[256,256]{1,0:T(8,128)(2,1)S(1)}, u32[]{:S(2)}, u32[]{:S(2)}) collective-permute-start(bf16[256,256]{1,0:T(8,128)(2,1)S(1)} %slice.74), channel_id=1, source_target_pairs={{0,3},{2,1},{4,7},{6,5},{8,11},{10,9},{12,15},{14,13},{1,0},{3,2},... | collective-permute-start | bytes 393224 | tf_op jit(solution)/shard_map/ppermute | solution.py:202
  28.9 8.1 %collective-permute-start.18 = (bf16[128,768]{1,0:T(8,128)(2,1)S(1)}, bf16[128,768]{1,0:T(8,128)(2,1)S(1)}, u32[]{:S(2)}, u32[]{:S(2)}) collective-permute-start(bf16[128,768]{1,0:T(8,128)(2,1)S(1)} %shard_map.96.here.r_4_), channel_id=1, source_target_pairs={{0,1},{1,0},{2,3},{3,2},{4,5},{5,4},{6,7},{7,6},{8,9},{9,8},{10,11... | collective-permute-start | bytes 589832 | tf_op jit(solution)/shard_map/ppermute | solution.py:206
  30.1 4.3 %collective-permute-start.14 = (bf16[128,256]{1,0:T(8,128)(2,1)S(1)}, bf16[128,256]{1,0:T(8,128)(2,1)S(1)}, u32[]{:S(2)}, u32[]{:S(2)}) collective-permute-start(bf16[128,256]{1,0:T(8,128)(2,1)S(1)} %get-tuple-element.33), channel_id=1, source_target_pairs={{1,4},{3,6},{5,0},{7,2},{9,12},{11,14},{13,8},{15,10},{0,1},{2,3},... | collective-permute-start | bytes 196616 | tf_op jit(solution)/shard_map/ppermute | solution.py:202
  30.3 4.6 %collective-permute-start.13 = (bf16[128,256]{1,0:T(8,128)(2,1)S(1)}, bf16[128,256]{1,0:T(8,128)(2,1)S(1)}, u32[]{:S(2)}, u32[]{:S(2)}) collective-permute-start(bf16[128,256]{1,0:T(8,128)(2,1)S(1)} %get-tuple-element.34), channel_id=1, source_target_pairs={{1,8},{3,10},{5,12},{7,14},{9,0},{11,2},{13,4},{15,6},{0,1},{2,3},... | collective-permute-start | bytes 196616 | tf_op jit(solution)/shard_map/ppermute | solution.py:202
  31.3 5.7 %collective-permute-start.12 = (bf16[128,256]{1,0:T(8,128)(2,1)S(1)}, bf16[128,256]{1,0:T(8,128)(2,1)S(1)}, u32[]{:S(2)}, u32[]{:S(2)}) collective-permute-start(bf16[128,256]{1,0:T(8,128)(2,1)S(1)} %get-tuple-element.34), channel_id=1, source_target_pairs={{1,12},{3,14},{5,8},{7,10},{9,4},{11,6},{13,0},{15,2},{0,1},{2,3},... | collective-permute-start | bytes 196616 | tf_op jit(solution)/shard_map/ppermute | solution.py:202
  32.7 4.3 %collective-permute-start.15 = (bf16[128,256]{1,0:T(8,128)(2,1)S(1)}, bf16[128,256]{1,0:T(8,128)(2,1)S(1)}, u32[]{:S(2)}, u32[]{:S(2)}) collective-permute-start(bf16[128,256]{1,0:T(8,128)(2,1)S(1)} %slice.97), channel_id=1, source_target_pairs={{1,2},{3,0},{5,6},{7,4},{9,10},{11,8},{13,14},{15,12},{0,1},{2,3},... | collective-permute-start | bytes 196616 | tf_op jit(solution)/shard_map/ppermute | solution.py:202
  37.3 1.7 %collective-permute-start.19 = (bf16[128,768]{1,0:T(8,128)(2,1)S(1)}, bf16[128,768]{1,0:T(8,128)(2,1)S(1)}, u32[]{:S(2)}, u32[]{:S(2)}) collective-permute-start(bf16[128,768]{1,0:T(8,128)(2,1)S(1)} %get-tuple-element.26.r_1_), channel_id=1, source_target_pairs={{0,1},{1,0},{2,3},{3,2},{4,5},{5,4},{6,7},{7,6},{8,9},{9,8},{10,11... | collective-permute-start | bytes 589832 | tf_op jit(solution)/shard_map/ppermute | solution.py:206
  37.4 4.2 %collective-permute-start.20 = (bf16[256,256]{1,0:T(8,128)(2,1)S(1)}, bf16[256,256]{1,0:T(8,128)(2,1)S(1)}, u32[]{:S(2)}, u32[]{:S(2)}) collective-permute-start(bf16[256,256]{1,0:T(8,128)(2,1)S(1)} %slice.79), channel_id=1, source_target_pairs={{0,3},{2,1},{4,7},{6,5},{8,11},{10,9},{12,15},{14,13},{1,0},{3,2},... | collective-permute-start | bytes 393224 | tf_op jit(solution)/shard_map/ppermute | solution.py:202
  40.4 8.1 %collective-permute-start.25 = (bf16[128,768]{1,0:T(8,128)(2,1)S(1)}, bf16[128,768]{1,0:T(8,128)(2,1)S(1)}, u32[]{:S(2)}, u32[]{:S(2)}) collective-permute-start(bf16[128,768]{1,0:T(8,128)(2,1)S(1)} %shard_map.101.here.r_4_), channel_id=1, source_target_pairs={{0,1},{1,0},{2,3},{3,2},{4,5},{5,4},{6,7},{7,6},{8,9},{9,8},{10,11... | collective-permute-start | bytes 589832 | tf_op jit(solution)/shard_map/ppermute | solution.py:206
  41.6 3.9 %collective-permute-start.23 = (bf16[128,256]{1,0:T(8,128)(2,1)S(1)}, bf16[128,256]{1,0:T(8,128)(2,1)S(1)}, u32[]{:S(2)}, u32[]{:S(2)}) collective-permute-start(bf16[128,256]{1,0:T(8,128)(2,1)S(1)} %get-tuple-element.31), channel_id=1, source_target_pairs={{1,4},{3,6},{5,0},{7,2},{9,12},{11,14},{13,8},{15,10},{0,1},{2,3},... | collective-permute-start | bytes 196616 | tf_op jit(solution)/shard_map/ppermute | solution.py:202
  42.5 4.6 %collective-permute-start.22 = (bf16[128,256]{1,0:T(8,128)(2,1)S(1)}, bf16[128,256]{1,0:T(8,128)(2,1)S(1)}, u32[]{:S(2)}, u32[]{:S(2)}) collective-permute-start(bf16[128,256]{1,0:T(8,128)(2,1)S(1)} %get-tuple-element.32), channel_id=1, source_target_pairs={{1,8},{3,10},{5,12},{7,14},{9,0},{11,2},{13,4},{15,6},{0,1},{2,3},... | collective-permute-start | bytes 196616 | tf_op jit(solution)/shard_map/ppermute | solution.py:202
  43.0 5.5 %collective-permute-start.21 = (bf16[128,256]{1,0:T(8,128)(2,1)S(1)}, bf16[128,256]{1,0:T(8,128)(2,1)S(1)}, u32[]{:S(2)}, u32[]{:S(2)}) collective-permute-start(bf16[128,256]{1,0:T(8,128)(2,1)S(1)} %get-tuple-element.32), channel_id=1, source_target_pairs={{1,12},{3,14},{5,8},{7,10},{9,4},{11,6},{13,0},{15,2},{0,1},{2,3},... | collective-permute-start | bytes 196616 | tf_op jit(solution)/shard_map/ppermute | solution.py:202
  44.2 4.4 %collective-permute-start.24 = (bf16[128,256]{1,0:T(8,128)(2,1)S(1)}, bf16[128,256]{1,0:T(8,128)(2,1)S(1)}, u32[]{:S(2)}, u32[]{:S(2)}) collective-permute-start(bf16[128,256]{1,0:T(8,128)(2,1)S(1)} %slice.101), channel_id=1, source_target_pairs={{1,2},{3,0},{5,6},{7,4},{9,10},{11,8},{13,14},{15,12},{0,1},{2,3},... | collective-permute-start | bytes 196616 | tf_op jit(solution)/shard_map/ppermute | solution.py:202
  48.9 1.7 %collective-permute-start.26 = (bf16[128,768]{1,0:T(8,128)(2,1)S(1)}, bf16[128,768]{1,0:T(8,128)(2,1)S(1)}, u32[]{:S(2)}, u32[]{:S(2)}) collective-permute-start(bf16[128,768]{1,0:T(8,128)(2,1)S(1)} %get-tuple-element.28.r_1_), channel_id=1, source_target_pairs={{0,1},{1,0},{2,3},{3,2},{4,5},{5,4},{6,7},{7,6},{8,9},{9,8},{10,11... | collective-permute-start | bytes 589832 | tf_op jit(solution)/shard_map/ppermute | solution.py:206
  49.0 4.1 %collective-permute-start.27 = (bf16[256,256]{1,0:T(8,128)(2,1)S(1)}, bf16[256,256]{1,0:T(8,128)(2,1)S(1)}, u32[]{:S(2)}, u32[]{:S(2)}) collective-permute-start(bf16[256,256]{1,0:T(8,128)(2,1)S(1)} %slice.84), channel_id=1, source_target_pairs={{0,3},{2,1},{4,7},{6,5},{8,11},{10,9},{12,15},{14,13},{1,0},{3,2},... | collective-permute-start | bytes 393224 | tf_op jit(solution)/shard_map/ppermute | solution.py:202
  53.1 4.0 %collective-permute-start.30 = (bf16[128,256]{1,0:T(8,128)(2,1)S(1)}, bf16[128,256]{1,0:T(8,128)(2,1)S(1)}, u32[]{:S(2)}, u32[]{:S(2)}) collective-permute-start(bf16[128,256]{1,0:T(8,128)(2,1)S(1)} %get-tuple-element.29), channel_id=1, source_target_pairs={{1,4},{3,6},{5,0},{7,2},{9,12},{11,14},{13,8},{15,10},{0,1},{2,3},... | collective-permute-start | bytes 196616 | tf_op jit(solution)/shard_map/ppermute | solution.py:202
  54.0 4.6 %collective-permute-start.29 = (bf16[128,256]{1,0:T(8,128)(2,1)S(1)}, bf16[128,256]{1,0:T(8,128)(2,1)S(1)}, u32[]{:S(2)}, u32[]{:S(2)}) collective-permute-start(bf16[128,256]{1,0:T(8,128)(2,1)S(1)} %get-tuple-element.30), channel_id=1, source_target_pairs={{1,8},{3,10},{5,12},{7,14},{9,0},{11,2},{13,4},{15,6},{0,1},{2,3},... | collective-permute-start | bytes 196616 | tf_op jit(solution)/shard_map/ppermute | solution.py:202
  54.5 5.5 %collective-permute-start.28 = (bf16[128,256]{1,0:T(8,128)(2,1)S(1)}, bf16[128,256]{1,0:T(8,128)(2,1)S(1)}, u32[]{:S(2)}, u32[]{:S(2)}) collective-permute-start(bf16[128,256]{1,0:T(8,128)(2,1)S(1)} %get-tuple-element.30), channel_id=1, source_target_pairs={{1,12},{3,14},{5,8},{7,10},{9,4},{11,6},{13,0},{15,2},{0,1},{2,3},... | collective-permute-start | bytes 196616 | tf_op jit(solution)/shard_map/ppermute | solution.py:202
  56.3 3.8 %collective-permute-start.31 = (bf16[128,256]{1,0:T(8,128)(2,1)S(1)}, bf16[128,256]{1,0:T(8,128)(2,1)S(1)}, u32[]{:S(2)}, u32[]{:S(2)}) collective-permute-start(bf16[128,256]{1,0:T(8,128)(2,1)S(1)} %slice.105), channel_id=1, source_target_pairs={{1,2},{3,0},{5,6},{7,4},{9,10},{11,8},{13,14},{15,12},{0,1},{2,3},... | collective-permute-start | bytes 196616 | tf_op jit(solution)/shard_map/ppermute | solution.py:202
  60.1 1.5 %collective-permute-start.32 = (bf16[128,768]{1,0:T(8,128)(2,1)S(1)}, bf16[128,768]{1,0:T(8,128)(2,1)S(1)}, u32[]{:S(2)}, u32[]{:S(2)}) collective-permute-start(bf16[128,768]{1,0:T(8,128)(2,1)S(1)} %shard_map.104.r_1_), channel_id=1, source_target_pairs={{0,1},{1,0},{2,3},{3,2},{4,5},{5,4},{6,7},{7,6},{8,9},{9,8},{10,11... | collective-permute-start | bytes 589832 | tf_op jit(solution)/shard_map/ppermute | solution.py:206

commit v8 on v7

--- a/solution.py
+++ b/solution.py
@@ -8,7 +8,6 @@
 
 PASSES = 2
 LEVELS = 3
-CHUNKS = 4
 BLOCKS = tuple((i, j) for i in range(LEVELS) for j in range(i + 1))
 BF = jnp.bfloat16
 F32 = jnp.float32
@@ -41,24 +40,14 @@
 
 def first_kernel(place, *refs):
     sources, out, buffers, sems = refs[: LEVELS + 1], refs[LEVELS + 1], refs[LEVELS + 2 : -1], refs[-1]
-    rows = sources[0].shape[0] // CHUNKS
-    copies = [
-        [
-            pltpu.make_async_copy(a.at[pl.ds(j * rows, rows), :], b.at[pl.ds(j * rows, rows), :], sems.at[i, j])
-            for j in range(CHUNKS)
-        ]
-        for i, (a, b) in enumerate(zip(sources, buffers))
-    ]
-    for group in copies:
-        for copy in group:
-            copy.start()
-    for copy in copies[0]:
-        copy.wait()
+    copies = [pltpu.make_async_copy(a, b, sems.at[i]) for i, (a, b) in enumerate(zip(sources, buffers))]
+    for copy in copies:
+        copy.start()
+    copies[0].wait()
     zt = buffers[0][...].T
     c = zt.shape[0]
     for level in range(LEVELS):
-        for copy in copies[1 + level]:
-            copy.wait()
+        copies[1 + level].wait()
         out[level * c : (level + 1) * c, :] = mm(zt, buffers[1 + level][...], 1, 0).astype(BF)
 
 
@@ -179,20 +168,20 @@
     leaf_terms(z, leaves, flipped, y)
 
 
-def siblings_kernel(place, one, more, two, three, joined):
-    join_siblings(one, more, two, three, joined)
+def siblings_kernel(place, one, more, two, out):
+    k = one.shape[1]
+    out[:, :k] = add(one[...], more[...])
+    out[:, k:] = two[...]
+
+
+def most_kernel(holder, place, three, other, factor, was, y, joined):
+    pick_kernel(holder, place, three, other, joined)
+    y[...] = mm(factor[:, -joined.shape[1] :], joined[...], 1, 1) + was[...]
 
 
 def last_kernel(holder, place, mine, other, factor, was, out, joined):
-    @pl.when(place[0] == holder)
-    def _():
-        joined[...] = mine[...]
-
-    @pl.when(place[0] != holder)
-    def _():
-        joined[...] = other[...]
-
-    out[...] = (mm(factor[...], joined[...], 1, 1) + was[...]).astype(BF)
+    pick_kernel(holder, place, mine, other, joined)
+    out[...] = (mm(factor[:, : joined.shape[1]], joined[...], 1, 1) + was[...]).astype(BF)
 
 
 def one_way(value, mask, source):
@@ -268,7 +257,7 @@
         [S((LEVELS * c, k), BF)],
         (place, probes, *uppers),
         2 * n * LEVELS * k * c,
-        [*buffers, sems((LEVELS + 1, CHUNKS))],
+        [*buffers, sems((LEVELS + 1,))],
         LEVELS + 1,
     )
     other = over_rank(own)
@@ -290,14 +279,23 @@
         pieces = siblings_of(packed, summed, source, stride, received)
         received = None
         if step + 1 == applies:
-            (q,) = call(siblings_kernel, [s_shape], (place, *pieces), 0)
+            one, more, two, three = pieces
+            other = over_rank(three)
+            (y,) = call(
+                lambda *r: most_kernel(source, *r),
+                [y_shape],
+                (place, three, other, upper, y),
+                field_flops // 6,
+                [pltpu.VMEM((c, 2 * k), BF)],
+            )
+            (q,) = call(siblings_kernel, [S((c, 4 * k), BF)], (place, one, more, two), 0)
             other = over_rank(q)
             (out,) = call(
                 lambda *r: last_kernel(source, *r),
                 [S((half, c), BF)],
                 (place, q, other, upper, y),
-                field_flops // 2,
-                [pltpu.VMEM((c, wide), BF)],
+                field_flops // 3,
+                [pltpu.VMEM((c, 4 * k), BF)],
             )
             return out
         there = over_rank(s)

time: 63.1 us -> 63.1 us (level)
    ppermute x12 -> x13, starting transfers between devices: 2.53 us -> 3.05 us  [over_rank(): return lax.ppermute(value, 'rank', [(0, 1), (1, 0)])]
    ppermute x12 -> x13, waiting for transfers between devices: 2.28 us -> 1.79 us  [over_rank(): return lax.ppermute(value, 'rank', [(0, 1), (1, 0)])]
    pallas_call x26 -> x27, Pallas kernels: 12.3 us -> 12.3 us  [call(): pl.pallas_call(kernel, out_shape=outs, in_specs=[pl.BlockSpec(memory_spac...]
  transfers between devices with their start and end apart: 33 -> 34, of which waited for: 15 -> 14; matrix products, arithmetic and copies ran while one was open for 0% -> 0% of each run, Pallas kernels for 16% -> 17%
where the time goes in v8:
time: 63.1 us; the launch traced here: 62.9 us
  starting transfers between devices  28.8 us (46%)
  waiting for transfers between devices  17.9 us (28%)
  Pallas kernels  12.3 us (19%)
  local copies, waits for them, and re-layouts  3.39 us (5%)
    ppermute x21, starting transfers between devices, one_way(): return lax.ppermute(value, ('rows', 'cols', 'rank'), away + home)  25.8 us
    ppermute x21, waiting for transfers between devices, one_way(): return lax.ppermute(value, ('rows', 'cols', 'rank'), away + home)  16.1 us
    pallas_call x27, Pallas kernels, call(): pl.pallas_call(kernel, out_shape=outs, in_specs=[pl.BlockSpec(memory_spac...  12.3 us
    unnamed x22, local copies, waits for them, and re-layouts  3.28 us
    ppermute x13, starting transfers between devices, over_rank(): return lax.ppermute(value, 'rank', [(0, 1), (1, 0)])  3.05 us
    ppermute x13, waiting for transfers between devices, over_rank(): return lax.ppermute(value, 'rank', [(0, 1), (1, 0)])  1.79 us
  transfers between devices with their start and end apart: 34, of which 14 were waited for; matrix products, arithmetic and copies ran while one was open for 0% of the time, Pallas kernels for 17%

profile of v8, /device:TPU:0, one launch (start us, length us, event | category | flops | bytes accessed | tf_op | source)
XLA Modules:
  0.0 62.9 jit_solution(13235683958173288661)
XLA Ops:
  0.0 1.2 %copy-done.8 = bf16[2048,128]{1,0:T(8,128)(2,1)S(1)} copy-done((bf16[2048,128]{1,0:T(8,128)(2,1)S(1)}, bf16[2048,128]{1,0:T(8,128)(2,1)}, u32[]{:S(2)}) %copy-start.8) | copy-done | bytes 524312
  1.2 1.0 %copy-done.9 = bf16[2048,128]{1,0:T(8,128)(2,1)S(1)} copy-done((bf16[2048,128]{1,0:T(8,128)(2,1)S(1)}, bf16[2048,128]{1,0:T(8,128)(2,1)}, u32[]{:S(2)}) %copy-start.9) | copy-done | bytes 524312
  2.2 1.0 %copy-done.10 = bf16[2048,128]{1,0:T(8,128)(2,1)S(1)} copy-done((bf16[2048,128]{1,0:T(8,128)(2,1)S(1)}, bf16[2048,128]{1,0:T(8,128)(2,1)}, u32[]{:S(2)}) %copy-start.10) | copy-done | bytes 524312
  3.3 0.6 collective-permute-start.7
  4.0 1.7 %collective-permute-done.7.other = bf16[3072,128]{1,0:T(8,128)(2,1)S(1)} collective-permute-done((bf16[3072,128]{1,0:T(8,128)(2,1)S(1)}, bf16[3072,128]{1,0:T(8,128)(2,1)S(1)}, u32[]{:S(2)}, u32[]{:S(2)}) %collective-permute-start.7) | collective-permute-done | bytes 786464 | tf_op jit(solution)/shard_map/ppermute | solution.py:195
  5.8 1.3 %shard_map.86 = (bf16[1024,768]{1,0:T(8,128)(2,1)S(1)}, bf16[1536,256]{1,0:T(8,128)(2,1)S(1)}) custom-call(s32[1]{0:T(128)} %bitcast.place.r_0_, bf16[3072,128]{1,0:T(8,128)(2,1)S(1)} %collective-permute-done.7.other, bf16[2048,128]{1,0:T(8,128)(2,1)S(1)} %copy-done.8, bf16[2048,128]{1,0:T(8,128)(2,1)S(1)} %copy-done.9, bf16[2048,128]{1,0:T(8,128)(2,1)S(1)} %copy-done.10), custom_call_target="tpu_custom_call" | custom-call | flops 905969664 | bytes 4718592 | tf_op jit(solution)/shard_map/pallas_call | solution.py:26
  7.2 0.4 collective-permute-start.8
  7.6 2.1 %shard_map.82.own = bf16[384,128]{1,0:T(8,128)(2,1)S(1)} custom-call(s32[1]{0:T(128)} %bitcast.place.r_0_, bf16[2048,128]{1,0:T(8,128)(2,1)} %z.1, bf16[2048,128]{1,0:T(8,128)(2,1)} %refs_0_.9, bf16[2048,128]{1,0:T(8,128)(2,1)} %refs_1_.9, bf16[2048,128]{1,0:T(8,128)(2,1)} %refs_2_.9), custom_call_target="tpu_custom_call" | custom-call | flops 201326592 | bytes 2195456 | tf_op jit(solution)/shard_map/pallas_call | solution.py:26
  10.0 2.6 %collective-permute-start.1 = (bf16[256,128]{1,0:T(8,128)(2,1)S(1)}, bf16[256,128]{1,0:T(8,128)(2,1)S(1)}, u32[]{:S(2)}, u32[]{:S(2)}) collective-permute-start(bf16[256,128]{1,0:T(8,128)(2,1)S(1)} %slice.89), channel_id=1, source_target_pairs={{0,3},{2,1},{4,7},{6,5},{8,11},{10,9},{12,15},{14,13},{1,0},{3,2},... | collective-permute-start | bytes 196616 | tf_op jit(solution)/shard_map/ppermute | solution.py:191
  12.6 1.1 %collective-permute-start.2 = (bf16[256,128]{1,0:T(8,128)(2,1)S(1)}, bf16[256,128]{1,0:T(8,128)(2,1)S(1)}, u32[]{:S(2)}, u32[]{:S(2)}) collective-permute-start(bf16[256,128]{1,0:T(8,128)(2,1)S(1)} %slice.90), channel_id=1, source_target_pairs={{0,3},{2,1},{4,7},{6,5},{8,11},{10,9},{12,15},{14,13},{1,0},{3,2},... | collective-permute-start | bytes 196616 | tf_op jit(solution)/shard_map/ppermute | solution.py:191
  13.8 0.7 %collective-permute-done.1.left = bf16[256,128]{1,0:T(8,128)(2,1)S(1)} collective-permute-done((bf16[256,128]{1,0:T(8,128)(2,1)S(1)}, bf16[256,128]{1,0:T(8,128)(2,1)S(1)}, u32[]{:S(2)}, u32[]{:S(2)}) %collective-permute-start.1) | collective-permute-done | bytes 65568 | tf_op jit(solution)/shard_map/ppermute | solution.py:191
  14.5 1.3 %collective-permute-done.2.right = bf16[256,128]{1,0:T(8,128)(2,1)S(1)} collective-permute-done((bf16[256,128]{1,0:T(8,128)(2,1)S(1)}, bf16[256,128]{1,0:T(8,128)(2,1)S(1)}, u32[]{:S(2)}, u32[]{:S(2)}) %collective-permute-start.2) | collective-permute-done | bytes 65568 | tf_op jit(solution)/shard_map/ppermute | solution.py:191
  16.0 0.7 %shard_map.88 = (f32[1024,128]{1,0:T(8,128)S(1)}, bf16[128,768]{1,0:T(8,128)(2,1)S(1)}) custom-call(s32[1]{0:T(128)} %bitcast.place.r_0_, bf16[2048,128]{1,0:T(8,128)(2,1)S(1)} %copy-done.7, bf16[4,256,256]{2,1,0:T(8,128)(2,1)S(1)} %copy-done, bf16[1024,768]{1,0:T(8,128)(2,1)S(1)} %get-tuple-element.18.after.r_2_), custom_call_target="tpu_custom_call" | custom-call | flops 201326592 | bytes 3342336 | tf_op jit(solution)/shard_map/pallas_call | solution.py:26
  16.8 0.5 collective-permute-start.4
  17.5 2.5 %collective-permute-start.3 = (bf16[128,256]{1,0:T(8,128)(2,1)S(1)}, bf16[128,256]{1,0:T(8,128)(2,1)S(1)}, u32[]{:S(2)}, u32[]{:S(2)}) collective-permute-start(bf16[128,256]{1,0:T(8,128)(2,1)S(1)} %get-tuple-element.36), channel_id=1, source_target_pairs={{1,12},{3,14},{5,8},{7,10},{9,4},{11,6},{13,0},{15,2},{0,1},{2,3},... | collective-permute-start | bytes 196616 | tf_op jit(solution)/shard_map/ppermute | solution.py:191
  20.0 1.4 %collective-permute-start.5 = (bf16[128,256]{1,0:T(8,128)(2,1)S(1)}, bf16[128,256]{1,0:T(8,128)(2,1)S(1)}, u32[]{:S(2)}, u32[]{:S(2)}) collective-permute-start(bf16[128,256]{1,0:T(8,128)(2,1)S(1)} %get-tuple-element.35), channel_id=1, source_target_pairs={{1,4},{3,6},{5,0},{7,2},{9,12},{11,14},{13,8},{15,10},{0,1},{2,3},... | collective-permute-start | bytes 196616 | tf_op jit(solution)/shard_map/ppermute | solution.py:191
  21.4 1.3 %shard_map.92 = (bf16[1024,768]{1,0:T(8,128)(2,1)S(1)}, bf16[1536,256]{1,0:T(8,128)(2,1)S(1)}) custom-call(s32[1]{0:T(128)} %bitcast.place.r_0_, bf16[3072,128]{1,0:T(8,128)(2,1)S(1)} %collective-permute-done.16.other, bf16[2048,128]{1,0:T(8,128)(2,1)S(1)} %copy-done.2, bf16[2048,128]{1,0:T(8,128)(2,1)S(1)} %copy-done.4, bf16[2048,128]{1,0:T(8,128)(2,1)S(1)} %copy-done.6), custom_call_target="tpu_custom_call" | custom-call | flops 905969664 | bytes 4718592 | tf_op jit(solution)/shard_map/pallas_call | solution.py:26
  22.7 0.4 collective-permute-start.17
  23.4 1.0 %collective-permute-done.5.two = bf16[128,256]{1,0:T(8,128)(2,1)S(1)} collective-permute-done((bf16[128,256]{1,0:T(8,128)(2,1)S(1)}, bf16[128,256]{1,0:T(8,128)(2,1)S(1)}, u32[]{:S(2)}, u32[]{:S(2)}) %collective-permute-start.5) | collective-permute-done | bytes 65568 | tf_op jit(solution)/shard_map/ppermute | solution.py:191
  24.9 2.5 %collective-permute-start.11 = (bf16[256,256]{1,0:T(8,128)(2,1)S(1)}, bf16[256,256]{1,0:T(8,128)(2,1)S(1)}, u32[]{:S(2)}, u32[]{:S(2)}) collective-permute-start(bf16[256,256]{1,0:T(8,128)(2,1)S(1)} %slice.74), channel_id=1, source_target_pairs={{0,3},{2,1},{4,7},{6,5},{8,11},{10,9},{12,15},{14,13},{1,0},{3,2},... | collective-permute-start | bytes 393224 | tf_op jit(solution)/shard_map/ppermute | solution.py:191
  27.4 0.9 %shard_map.95.y.r_3_ = f32[1024,128]{1,0:T(8,128)S(1)} custom-call(s32[1]{0:T(128)} %bitcast.place.r_0_, bf16[128,768]{1,0:T(8,128)(2,1)S(1)} %shard_map.94.r_1_, bf16[1024,768]{1,0:T(8,128)(2,1)S(1)} %get-tuple-element.18.after.r_2_, f32[1024,128]{1,0:T(8,128)S(1)} %get-tuple-element.23.r_3_, bf16[4,256,256]{2,1,0:T(8,128)(2,1)S(1)} %copy-done), custom_call_target="tpu_custom_call" | custom-call | flops 201326592 | bytes 3342336 | tf_op jit(solution)/shard_map/pallas_call | solution.py:26
  28.3 0.4 shard_map.96.here.r_4_
  28.8 1.1 %collective-permute-done.11 = bf16[256,256]{1,0:T(8,128)(2,1)S(1)} collective-permute-done((bf16[256,256]{1,0:T(8,128)(2,1)S(1)}, bf16[256,256]{1,0:T(8,128)(2,1)S(1)}, u32[]{:S(2)}, u32[]{:S(2)}) %collective-permute-start.11) | collective-permute-done | bytes 131104 | tf_op jit(solution)/shard_map/ppermute | solution.py:191
  30.1 1.0 %collective-permute-start.13 = (bf16[128,256]{1,0:T(8,128)(2,1)S(1)}, bf16[128,256]{1,0:T(8,128)(2,1)S(1)}, u32[]{:S(2)}, u32[]{:S(2)}) collective-permute-start(bf16[128,256]{1,0:T(8,128)(2,1)S(1)} %get-tuple-element.34), channel_id=1, source_target_pairs={{1,8},{3,10},{5,12},{7,14},{9,0},{11,2},{13,4},{15,6},{0,1},{2,3},... | collective-permute-start | bytes 196616 | tf_op jit(solution)/shard_map/ppermute | solution.py:191
  31.1 1.4 %collective-permute-start.12 = (bf16[128,256]{1,0:T(8,128)(2,1)S(1)}, bf16[128,256]{1,0:T(8,128)(2,1)S(1)}, u32[]{:S(2)}, u32[]{:S(2)}) collective-permute-start(bf16[128,256]{1,0:T(8,128)(2,1)S(1)} %get-tuple-element.34), channel_id=1, source_target_pairs={{1,12},{3,14},{5,8},{7,10},{9,4},{11,6},{13,0},{15,2},{0,1},{2,3},... | collective-permute-start | bytes 196616 | tf_op jit(solution)/shard_map/ppermute | solution.py:191
  32.5 1.4 %collective-permute-start.15 = (bf16[128,256]{1,0:T(8,128)(2,1)S(1)}, bf16[128,256]{1,0:T(8,128)(2,1)S(1)}, u32[]{:S(2)}, u32[]{:S(2)}) collective-permute-start(bf16[128,256]{1,0:T(8,128)(2,1)S(1)} %slice.97), channel_id=1, source_target_pairs={{1,2},{3,0},{5,6},{7,4},{9,10},{11,8},{13,14},{15,12},{0,1},{2,3},... | collective-permute-start | bytes 196616 | tf_op jit(solution)/shard_map/ppermute | solution.py:191
  34.2 0.5 collective-permute-done.13.more
  34.7 2.1 %collective-permute-done.12.one = bf16[128,256]{1,0:T(8,128)(2,1)S(1)} collective-permute-done((bf16[128,256]{1,0:T(8,128)(2,1)S(1)}, bf16[128,256]{1,0:T(8,128)(2,1)S(1)}, u32[]{:S(2)}, u32[]{:S(2)}) %collective-permute-start.12) | collective-permute-done | bytes 65568 | tf_op jit(solution)/shard_map/ppermute | solution.py:191
  37.3 1.6 %collective-permute-start.20 = (bf16[256,256]{1,0:T(8,128)(2,1)S(1)}, bf16[256,256]{1,0:T(8,128)(2,1)S(1)}, u32[]{:S(2)}, u32[]{:S(2)}) collective-permute-start(bf16[256,256]{1,0:T(8,128)(2,1)S(1)} %slice.79), channel_id=1, source_target_pairs={{0,3},{2,1},{4,7},{6,5},{8,11},{10,9},{12,15},{14,13},{1,0},{3,2},... | collective-permute-start | bytes 393224 | tf_op jit(solution)/shard_map/ppermute | solution.py:191
  39.0 0.9 %shard_map.100.y.r_3_ = f32[1024,128]{1,0:T(8,128)S(1)} custom-call(s32[1]{0:T(128)} %bitcast.place.r_0_, bf16[128,768]{1,0:T(8,128)(2,1)S(1)} %shard_map.99.r_1_, bf16[1024,768]{1,0:T(8,128)(2,1)S(1)} %get-tuple-element.24.after.r_2_.r_3_, f32[1024,128]{1,0:T(8,128)S(1)} %shard_map.95.y.r_3_, bf16[4,256,256]{2,1,0:T(8,128)(2,1)S(1)} %copy-done), custom_call_target="tpu_custom_call" | custom-call | flops 201326592 | bytes 3342336 | tf_op jit(solution)/shard_map/pallas_call | solution.py:26
  40.6 0.9 %collective-permute-done.20 = bf16[256,256]{1,0:T(8,128)(2,1)S(1)} collective-permute-done((bf16[256,256]{1,0:T(8,128)(2,1)S(1)}, bf16[256,256]{1,0:T(8,128)(2,1)S(1)}, u32[]{:S(2)}, u32[]{:S(2)}) %collective-permute-start.20) | collective-permute-done | bytes 131104 | tf_op jit(solution)/shard_map/ppermute | solution.py:191
  41.5 0.8 %collective-permute-start.23 = (bf16[128,256]{1,0:T(8,128)(2,1)S(1)}, bf16[128,256]{1,0:T(8,128)(2,1)S(1)}, u32[]{:S(2)}, u32[]{:S(2)}) collective-permute-start(bf16[128,256]{1,0:T(8,128)(2,1)S(1)} %get-tuple-element.31), channel_id=1, source_target_pairs={{1,4},{3,6},{5,0},{7,2},{9,12},{11,14},{13,8},{15,10},{0,1},{2,3},... | collective-permute-start | bytes 196616 | tf_op jit(solution)/shard_map/ppermute | solution.py:191
  42.3 0.5 collective-permute-start.22
  42.8 1.2 %collective-permute-start.21 = (bf16[128,256]{1,0:T(8,128)(2,1)S(1)}, bf16[128,256]{1,0:T(8,128)(2,1)S(1)}, u32[]{:S(2)}, u32[]{:S(2)}) collective-permute-start(bf16[128,256]{1,0:T(8,128)(2,1)S(1)} %get-tuple-element.32), channel_id=1, source_target_pairs={{1,12},{3,14},{5,8},{7,10},{9,4},{11,6},{13,0},{15,2},{0,1},{2,3},... | collective-permute-start | bytes 196616 | tf_op jit(solution)/shard_map/ppermute | solution.py:191
  44.0 1.4 %collective-permute-start.24 = (bf16[128,256]{1,0:T(8,128)(2,1)S(1)}, bf16[128,256]{1,0:T(8,128)(2,1)S(1)}, u32[]{:S(2)}, u32[]{:S(2)}) collective-permute-start(bf16[128,256]{1,0:T(8,128)(2,1)S(1)} %slice.101), channel_id=1, source_target_pairs={{1,2},{3,0},{5,6},{7,4},{9,10},{11,8},{13,14},{15,12},{0,1},{2,3},... | collective-permute-start | bytes 196616 | tf_op jit(solution)/shard_map/ppermute | solution.py:191
  45.4 1.5 %collective-permute-done.22.more = bf16[128,256]{1,0:T(8,128)(2,1)S(1)} collective-permute-done((bf16[128,256]{1,0:T(8,128)(2,1)S(1)}, bf16[128,256]{1,0:T(8,128)(2,1)S(1)}, u32[]{:S(2)}, u32[]{:S(2)}) %collective-permute-start.22) | collective-permute-done | bytes 65568 | tf_op jit(solution)/shard_map/ppermute | solution.py:191
  46.9 1.4 %collective-permute-done.21.one = bf16[128,256]{1,0:T(8,128)(2,1)S(1)} collective-permute-done((bf16[128,256]{1,0:T(8,128)(2,1)S(1)}, bf16[128,256]{1,0:T(8,128)(2,1)S(1)}, u32[]{:S(2)}, u32[]{:S(2)}) %collective-permute-start.21) | collective-permute-done | bytes 65568 | tf_op jit(solution)/shard_map/ppermute | solution.py:191
  48.8 1.6 %collective-permute-start.27 = (bf16[256,256]{1,0:T(8,128)(2,1)S(1)}, bf16[256,256]{1,0:T(8,128)(2,1)S(1)}, u32[]{:S(2)}, u32[]{:S(2)}) collective-permute-start(bf16[256,256]{1,0:T(8,128)(2,1)S(1)} %slice.84), channel_id=1, source_target_pairs={{0,3},{2,1},{4,7},{6,5},{8,11},{10,9},{12,15},{14,13},{1,0},{3,2},... | collective-permute-start | bytes 393224 | tf_op jit(solution)/shard_map/ppermute | solution.py:191
  50.4 2.5 %collective-permute-done.27 = bf16[256,256]{1,0:T(8,128)(2,1)S(1)} collective-permute-done((bf16[256,256]{1,0:T(8,128)(2,1)S(1)}, bf16[256,256]{1,0:T(8,128)(2,1)S(1)}, u32[]{:S(2)}, u32[]{:S(2)}) %collective-permute-start.27) | collective-permute-done | bytes 131104 | tf_op jit(solution)/shard_map/ppermute | solution.py:191
  53.0 0.9 %collective-permute-start.30 = (bf16[128,256]{1,0:T(8,128)(2,1)S(1)}, bf16[128,256]{1,0:T(8,128)(2,1)S(1)}, u32[]{:S(2)}, u32[]{:S(2)}) collective-permute-start(bf16[128,256]{1,0:T(8,128)(2,1)S(1)} %get-tuple-element.29), channel_id=1, source_target_pairs={{1,4},{3,6},{5,0},{7,2},{9,12},{11,14},{13,8},{15,10},{0,1},{2,3},... | collective-permute-start | bytes 196616 | tf_op jit(solution)/shard_map/ppermute | solution.py:191
  53.8 0.5 collective-permute-start.29
  54.4 1.8 %collective-permute-start.28 = (bf16[128,256]{1,0:T(8,128)(2,1)S(1)}, bf16[128,256]{1,0:T(8,128)(2,1)S(1)}, u32[]{:S(2)}, u32[]{:S(2)}) collective-permute-start(bf16[128,256]{1,0:T(8,128)(2,1)S(1)} %get-tuple-element.30), channel_id=1, source_target_pairs={{1,12},{3,14},{5,8},{7,10},{9,4},{11,6},{13,0},{15,2},{0,1},{2,3},... | collective-permute-start | bytes 196616 | tf_op jit(solution)/shard_map/ppermute | solution.py:191
  56.2 0.8 %collective-permute-start.32 = (bf16[128,256]{1,0:T(8,128)(2,1)S(1)}, bf16[128,256]{1,0:T(8,128)(2,1)S(1)}, u32[]{:S(2)}, u32[]{:S(2)}) collective-permute-start(bf16[128,256]{1,0:T(8,128)(2,1)S(1)} %slice.105), channel_id=1, source_target_pairs={{1,2},{3,0},{5,6},{7,4},{9,10},{11,8},{13,14},{15,12},{0,1},{2,3},... | collective-permute-start | bytes 196616 | tf_op jit(solution)/shard_map/ppermute | solution.py:191
  57.0 1.4 %collective-permute-done.29.more = bf16[128,256]{1,0:T(8,128)(2,1)S(1)} collective-permute-done((bf16[128,256]{1,0:T(8,128)(2,1)S(1)}, bf16[128,256]{1,0:T(8,128)(2,1)S(1)}, u32[]{:S(2)}, u32[]{:S(2)}) %collective-permute-start.29) | collective-permute-done | bytes 65568 | tf_op jit(solution)/shard_map/ppermute | solution.py:191
  58.4 1.5 %collective-permute-done.28.one = bf16[128,256]{1,0:T(8,128)(2,1)S(1)} collective-permute-done((bf16[128,256]{1,0:T(8,128)(2,1)S(1)}, bf16[128,256]{1,0:T(8,128)(2,1)S(1)}, u32[]{:S(2)}, u32[]{:S(2)}) %collective-permute-start.28) | collective-permute-done | bytes 65568 | tf_op jit(solution)/shard_map/ppermute | solution.py:191
  60.0 0.5 collective-permute-start.33
  60.5 0.9 %shard_map.106.r_4_ = f32[1024,128]{1,0:T(8,128)S(1)} custom-call(s32[1]{0:T(128)} %bitcast.place.r_0_, bf16[128,768]{1,0:T(8,128)(2,1)S(1)} %shard_map.105.r_1_, bf16[1024,768]{1,0:T(8,128)(2,1)S(1)} %get-tuple-element.18.after.r_2_, f32[1024,128]{1,0:T(8,128)S(1)} %shard_map.100.y.r_3_, bf16[4,256,256]{2,1,0:T(8,128)(2,1)S(1)} %copy-done), custom_call_target="tpu_custom_call" | custom-call | flops 201326592 | bytes 3342336 | tf_op jit(solution)/shard_map/pallas_call | solution.py:26
  61.8 1.2 %shard_map.108 = bf16[1024,128]{1,0:T(8,128)(2,1)} custom-call(s32[1]{0:T(128)} %bitcast.place.r_0_, bf16[128,512]{1,0:T(8,128)(2,1)S(1)} %shard_map.104.r_1_, bf16[128,512]{1,0:T(8,128)(2,1)S(1)} %collective-permute-done.31.r_2_, bf16[1024,768]{1,0:T(8,128)(2,1)S(1)} %get-tuple-element.24.after.r_2_.r_3_, f32[1024,128]{1,0:T(8,128)S(1)} %shard_map.107.r_4_), custom_call_target="tpu_custom_call" | custom-call | flops 134217728 | bytes 2621440 | tf_op jit(solution)/shard_map/pallas_call | solution.py:26
  (86 shorter events, 4.4 us)
Async XLA Ops:
  0.0 3.9 %copy-start.5 = (bf16[2048,128]{1,0:T(8,128)(2,1)S(1)}, bf16[2048,128]{1,0:T(8,128)(2,1)}, u32[]{:S(2)}) copy-start(bf16[2048,128]{1,0:T(8,128)(2,1)} %refs_2_.9) | copy-start | bytes 1572868
  0.0 3.9 %copy-start.3 = (bf16[2048,128]{1,0:T(8,128)(2,1)S(1)}, bf16[2048,128]{1,0:T(8,128)(2,1)}, u32[]{:S(2)}) copy-start(bf16[2048,128]{1,0:T(8,128)(2,1)} %refs_1_.9) | copy-start | bytes 1572868
  0.0 3.9 %copy-start.1 = (bf16[2048,128]{1,0:T(8,128)(2,1)S(1)}, bf16[2048,128]{1,0:T(8,128)(2,1)}, u32[]{:S(2)}) copy-start(bf16[2048,128]{1,0:T(8,128)(2,1)} %refs_0_.9) | copy-start | bytes 1572868
  0.0 1.2 %copy-start.8 = (bf16[2048,128]{1,0:T(8,128)(2,1)S(1)}, bf16[2048,128]{1,0:T(8,128)(2,1)}, u32[]{:S(2)}) copy-start(bf16[2048,128]{1,0:T(8,128)(2,1)} %refs_0_.7) | copy-start | bytes 1572868
  1.2 1.0 %copy-start.9 = (bf16[2048,128]{1,0:T(8,128)(2,1)S(1)}, bf16[2048,128]{1,0:T(8,128)(2,1)}, u32[]{:S(2)}) copy-start(bf16[2048,128]{1,0:T(8,128)(2,1)} %refs_1_.7) | copy-start | bytes 1572868
  2.2 1.0 %copy-start.10 = (bf16[2048,128]{1,0:T(8,128)(2,1)S(1)}, bf16[2048,128]{1,0:T(8,128)(2,1)}, u32[]{:S(2)}) copy-start(bf16[2048,128]{1,0:T(8,128)(2,1)} %refs_2_.7) | copy-start | bytes 1572868
  3.3 2.5 %collective-permute-start.7 = (bf16[3072,128]{1,0:T(8,128)(2,1)S(1)}, bf16[3072,128]{1,0:T(8,128)(2,1)S(1)}, u32[]{:S(2)}, u32[]{:S(2)}) collective-permute-start(bf16[3072,128]{1,0:T(8,128)(2,1)S(1)} %shard_map.85), channel_id=1, source_target_pairs={{0,1},{1,0},{2,3},{3,2},{4,5},{5,4},{6,7},{7,6},{8,9},{9,8},{10,11... | collective-permute-start | bytes 2359304 | tf_op jit(solution)/shard_map/ppermute | solution.py:195
  3.9 16.1 %collective-permute-start.16 = (bf16[3072,128]{1,0:T(8,128)(2,1)S(1)}, bf16[3072,128]{1,0:T(8,128)(2,1)S(1)}, u32[]{:S(2)}, u32[]{:S(2)}) collective-permute-start(bf16[3072,128]{1,0:T(8,128)(2,1)S(1)} %shard_map.91), channel_id=1, source_target_pairs={{0,1},{1,0},{2,3},{3,2},{4,5},{5,4},{6,7},{7,6},{8,9},{9,8},{10,11... | collective-permute-start | bytes 2359304 | tf_op jit(solution)/shard_map/ppermute | solution.py:195
  7.1 8.8 %copy-start = (bf16[4,256,256]{2,1,0:T(8,128)(2,1)S(1)}, bf16[4,256,256]{2,1,0:T(8,128)(2,1)}, u32[]{:S(2)}) copy-start(bf16[4,256,256]{2,1,0:T(8,128)(2,1)} %r_4_.5) | copy-start | bytes 1572868
  7.1 8.8 %copy-start.7 = (bf16[2048,128]{1,0:T(8,128)(2,1)S(1)}, bf16[2048,128]{1,0:T(8,128)(2,1)}, u32[]{:S(2)}) copy-start(bf16[2048,128]{1,0:T(8,128)(2,1)} %z.1) | copy-start | bytes 1572868
  7.2 15.6 %collective-permute-start.8 = (bf16[1536,256]{1,0:T(8,128)(2,1)S(1)}, bf16[1536,256]{1,0:T(8,128)(2,1)S(1)}, u32[]{:S(2)}, u32[]{:S(2)}) collective-permute-start(bf16[1536,256]{1,0:T(8,128)(2,1)S(1)} %get-tuple-element.17.mine), channel_id=1, source_target_pairs={{0,1},{1,0},{2,3},{3,2},{4,5},{5,4},{6,7},{7,6},{8,9},{9,8},{10,11... | collective-permute-start | bytes 2359304 | tf_op jit(solution)/shard_map/ppermute | solution.py:195
  9.7 2.9 %collective-permute-start = (bf16[384,128]{1,0:T(8,128)(2,1)S(1)}, bf16[384,128]{1,0:T(8,128)(2,1)S(1)}, u32[]{:S(2)}, u32[]{:S(2)}) collective-permute-start(bf16[384,128]{1,0:T(8,128)(2,1)S(1)} %shard_map.82.own), channel_id=1, source_target_pairs={{0,1},{1,0},{2,3},{3,2},{4,5},{5,4},{6,7},{7,6},{8,9},{9,8},{10,11... | collective-permute-start | bytes 294920 | tf_op jit(solution)/shard_map/ppermute | solution.py:195
  10.0 4.5 %collective-permute-start.1 = (bf16[256,128]{1,0:T(8,128)(2,1)S(1)}, bf16[256,128]{1,0:T(8,128)(2,1)S(1)}, u32[]{:S(2)}, u32[]{:S(2)}) collective-permute-start(bf16[256,128]{1,0:T(8,128)(2,1)S(1)} %slice.89), channel_id=1, source_target_pairs={{0,3},{2,1},{4,7},{6,5},{8,11},{10,9},{12,15},{14,13},{1,0},{3,2},... | collective-permute-start | bytes 196616 | tf_op jit(solution)/shard_map/ppermute | solution.py:191
  12.6 3.2 %collective-permute-start.2 = (bf16[256,128]{1,0:T(8,128)(2,1)S(1)}, bf16[256,128]{1,0:T(8,128)(2,1)S(1)}, u32[]{:S(2)}, u32[]{:S(2)}) collective-permute-start(bf16[256,128]{1,0:T(8,128)(2,1)S(1)} %slice.90), channel_id=1, source_target_pairs={{0,3},{2,1},{4,7},{6,5},{8,11},{10,9},{12,15},{14,13},{1,0},{3,2},... | collective-permute-start | bytes 196616 | tf_op jit(solution)/shard_map/ppermute | solution.py:191
  13.8 3.7 %collective-permute-start.6 = (bf16[128,256]{1,0:T(8,128)(2,1)S(1)}, bf16[128,256]{1,0:T(8,128)(2,1)S(1)}, u32[]{:S(2)}, u32[]{:S(2)}) collective-permute-start(bf16[128,256]{1,0:T(8,128)(2,1)S(1)} %slice.93), channel_id=1, source_target_pairs={{1,2},{3,0},{5,6},{7,4},{9,10},{11,8},{13,14},{15,12},{0,1},{2,3},... | collective-permute-start | bytes 196616 | tf_op jit(solution)/shard_map/ppermute | solution.py:191
  15.9 5.5 %copy-start.2 = (bf16[2048,128]{1,0:T(8,128)(2,1)S(1)}, bf16[2048,128]{1,0:T(8,128)(2,1)}, u32[]{:S(2)}) copy-start(bf16[2048,128]{1,0:T(8,128)(2,1)} %refs_0_.9) | copy-start | bytes 1572868
  15.9 5.5 %copy-start.4 = (bf16[2048,128]{1,0:T(8,128)(2,1)S(1)}, bf16[2048,128]{1,0:T(8,128)(2,1)}, u32[]{:S(2)}) copy-start(bf16[2048,128]{1,0:T(8,128)(2,1)} %refs_1_.9) | copy-start | bytes 1572868
  15.9 5.5 %copy-start.6 = (bf16[2048,128]{1,0:T(8,128)(2,1)S(1)}, bf16[2048,128]{1,0:T(8,128)(2,1)}, u32[]{:S(2)}) copy-start(bf16[2048,128]{1,0:T(8,128)(2,1)} %refs_2_.9) | copy-start | bytes 1572868
  16.7 7.7 %collective-permute-start.9 = (bf16[128,768]{1,0:T(8,128)(2,1)S(1)}, bf16[128,768]{1,0:T(8,128)(2,1)S(1)}, u32[]{:S(2)}, u32[]{:S(2)}) collective-permute-start(bf16[128,768]{1,0:T(8,128)(2,1)S(1)} %get-tuple-element.19.here.r_4_), channel_id=1, source_target_pairs={{0,1},{1,0},{2,3},{3,2},{4,5},{5,4},{6,7},{7,6},{8,9},{9,8},{10,11... | collective-permute-start | bytes 589832 | tf_op jit(solution)/shard_map/ppermute | solution.py:195
  16.8 7.6 %collective-permute-start.4 = (bf16[128,256]{1,0:T(8,128)(2,1)S(1)}, bf16[128,256]{1,0:T(8,128)(2,1)S(1)}, u32[]{:S(2)}, u32[]{:S(2)}) collective-permute-start(bf16[128,256]{1,0:T(8,128)(2,1)S(1)} %get-tuple-element.36), channel_id=1, source_target_pairs={{1,8},{3,10},{5,12},{7,14},{9,0},{11,2},{13,4},{15,6},{0,1},{2,3},... | collective-permute-start | bytes 196616 | tf_op jit(solution)/shard_map/ppermute | solution.py:191
  17.5 6.9 %collective-permute-start.3 = (bf16[128,256]{1,0:T(8,128)(2,1)S(1)}, bf16[128,256]{1,0:T(8,128)(2,1)S(1)}, u32[]{:S(2)}, u32[]{:S(2)}) collective-permute-start(bf16[128,256]{1,0:T(8,128)(2,1)S(1)} %get-tuple-element.36), channel_id=1, source_target_pairs={{1,12},{3,14},{5,8},{7,10},{9,4},{11,6},{13,0},{15,2},{0,1},{2,3},... | collective-permute-start | bytes 196616 | tf_op jit(solution)/shard_map/ppermute | solution.py:191
  20.0 4.4 %collective-permute-start.5 = (bf16[128,256]{1,0:T(8,128)(2,1)S(1)}, bf16[128,256]{1,0:T(8,128)(2,1)S(1)}, u32[]{:S(2)}, u32[]{:S(2)}) collective-permute-start(bf16[128,256]{1,0:T(8,128)(2,1)S(1)} %get-tuple-element.35), channel_id=1, source_target_pairs={{1,4},{3,6},{5,0},{7,2},{9,12},{11,14},{13,8},{15,10},{0,1},{2,3},... | collective-permute-start | bytes 196616 | tf_op jit(solution)/shard_map/ppermute | solution.py:191
  22.7 9.8 %collective-permute-start.17 = (bf16[1536,256]{1,0:T(8,128)(2,1)S(1)}, bf16[1536,256]{1,0:T(8,128)(2,1)S(1)}, u32[]{:S(2)}, u32[]{:S(2)}) collective-permute-start(bf16[1536,256]{1,0:T(8,128)(2,1)S(1)} %get-tuple-element.22.mine), channel_id=1, source_target_pairs={{0,1},{1,0},{2,3},{3,2},{4,5},{5,4},{6,7},{7,6},{8,9},{9,8},{10,11... | collective-permute-start | bytes 2359304 | tf_op jit(solution)/shard_map/ppermute | solution.py:195
  24.8 2.6 %collective-permute-start.10 = (bf16[128,768]{1,0:T(8,128)(2,1)S(1)}, bf16[128,768]{1,0:T(8,128)(2,1)S(1)}, u32[]{:S(2)}, u32[]{:S(2)}) collective-permute-start(bf16[128,768]{1,0:T(8,128)(2,1)S(1)} %get-tuple-element.21.r_1_), channel_id=1, source_target_pairs={{0,1},{1,0},{2,3},{3,2},{4,5},{5,4},{6,7},{7,6},{8,9},{9,8},{10,11... | collective-permute-start | bytes 589832 | tf_op jit(solution)/shard_map/ppermute | solution.py:195
  24.9 5.0 %collective-permute-start.11 = (bf16[256,256]{1,0:T(8,128)(2,1)S(1)}, bf16[256,256]{1,0:T(8,128)(2,1)S(1)}, u32[]{:S(2)}, u32[]{:S(2)}) collective-permute-start(bf16[256,256]{1,0:T(8,128)(2,1)S(1)} %slice.74), channel_id=1, source_target_pairs={{0,3},{2,1},{4,7},{6,5},{8,11},{10,9},{12,15},{14,13},{1,0},{3,2},... | collective-permute-start | bytes 393224 | tf_op jit(solution)/shard_map/ppermute | solution.py:191
  28.7 8.1 %collective-permute-start.18 = (bf16[128,768]{1,0:T(8,128)(2,1)S(1)}, bf16[128,768]{1,0:T(8,128)(2,1)S(1)}, u32[]{:S(2)}, u32[]{:S(2)}) collective-permute-start(bf16[128,768]{1,0:T(8,128)(2,1)S(1)} %shard_map.96.here.r_4_), channel_id=1, source_target_pairs={{0,1},{1,0},{2,3},{3,2},{4,5},{5,4},{6,7},{7,6},{8,9},{9,8},{10,11... | collective-permute-start | bytes 589832 | tf_op jit(solution)/shard_map/ppermute | solution.py:195
  29.9 4.3 %collective-permute-start.14 = (bf16[128,256]{1,0:T(8,128)(2,1)S(1)}, bf16[128,256]{1,0:T(8,128)(2,1)S(1)}, u32[]{:S(2)}, u32[]{:S(2)}) collective-permute-start(bf16[128,256]{1,0:T(8,128)(2,1)S(1)} %get-tuple-element.33), channel_id=1, source_target_pairs={{1,4},{3,6},{5,0},{7,2},{9,12},{11,14},{13,8},{15,10},{0,1},{2,3},... | collective-permute-start | bytes 196616 | tf_op jit(solution)/shard_map/ppermute | solution.py:191
  30.1 4.6 %collective-permute-start.13 = (bf16[128,256]{1,0:T(8,128)(2,1)S(1)}, bf16[128,256]{1,0:T(8,128)(2,1)S(1)}, u32[]{:S(2)}, u32[]{:S(2)}) collective-permute-start(bf16[128,256]{1,0:T(8,128)(2,1)S(1)} %get-tuple-element.34), channel_id=1, source_target_pairs={{1,8},{3,10},{5,12},{7,14},{9,0},{11,2},{13,4},{15,6},{0,1},{2,3},... | collective-permute-start | bytes 196616 | tf_op jit(solution)/shard_map/ppermute | solution.py:191
  31.1 5.7 %collective-permute-start.12 = (bf16[128,256]{1,0:T(8,128)(2,1)S(1)}, bf16[128,256]{1,0:T(8,128)(2,1)S(1)}, u32[]{:S(2)}, u32[]{:S(2)}) collective-permute-start(bf16[128,256]{1,0:T(8,128)(2,1)S(1)} %get-tuple-element.34), channel_id=1, source_target_pairs={{1,12},{3,14},{5,8},{7,10},{9,4},{11,6},{13,0},{15,2},{0,1},{2,3},... | collective-permute-start | bytes 196616 | tf_op jit(solution)/shard_map/ppermute | solution.py:191
  32.5 4.3 %collective-permute-start.15 = (bf16[128,256]{1,0:T(8,128)(2,1)S(1)}, bf16[128,256]{1,0:T(8,128)(2,1)S(1)}, u32[]{:S(2)}, u32[]{:S(2)}) collective-permute-start(bf16[128,256]{1,0:T(8,128)(2,1)S(1)} %slice.97), channel_id=1, source_target_pairs={{1,2},{3,0},{5,6},{7,4},{9,10},{11,8},{13,14},{15,12},{0,1},{2,3},... | collective-permute-start | bytes 196616 | tf_op jit(solution)/shard_map/ppermute | solution.py:191
  37.2 1.7 %collective-permute-start.19 = (bf16[128,768]{1,0:T(8,128)(2,1)S(1)}, bf16[128,768]{1,0:T(8,128)(2,1)S(1)}, u32[]{:S(2)}, u32[]{:S(2)}) collective-permute-start(bf16[128,768]{1,0:T(8,128)(2,1)S(1)} %get-tuple-element.26.r_1_), channel_id=1, source_target_pairs={{0,1},{1,0},{2,3},{3,2},{4,5},{5,4},{6,7},{7,6},{8,9},{9,8},{10,11... | collective-permute-start | bytes 589832 | tf_op jit(solution)/shard_map/ppermute | solution.py:195
  37.3 4.2 %collective-permute-start.20 = (bf16[256,256]{1,0:T(8,128)(2,1)S(1)}, bf16[256,256]{1,0:T(8,128)(2,1)S(1)}, u32[]{:S(2)}, u32[]{:S(2)}) collective-permute-start(bf16[256,256]{1,0:T(8,128)(2,1)S(1)} %slice.79), channel_id=1, source_target_pairs={{0,3},{2,1},{4,7},{6,5},{8,11},{10,9},{12,15},{14,13},{1,0},{3,2},... | collective-permute-start | bytes 393224 | tf_op jit(solution)/shard_map/ppermute | solution.py:191
  40.3 8.1 %collective-permute-start.25 = (bf16[128,768]{1,0:T(8,128)(2,1)S(1)}, bf16[128,768]{1,0:T(8,128)(2,1)S(1)}, u32[]{:S(2)}, u32[]{:S(2)}) collective-permute-start(bf16[128,768]{1,0:T(8,128)(2,1)S(1)} %shard_map.101.here.r_4_), channel_id=1, source_target_pairs={{0,1},{1,0},{2,3},{3,2},{4,5},{5,4},{6,7},{7,6},{8,9},{9,8},{10,11... | collective-permute-start | bytes 589832 | tf_op jit(solution)/shard_map/ppermute | solution.py:195
  41.5 3.9 %collective-permute-start.23 = (bf16[128,256]{1,0:T(8,128)(2,1)S(1)}, bf16[128,256]{1,0:T(8,128)(2,1)S(1)}, u32[]{:S(2)}, u32[]{:S(2)}) collective-permute-start(bf16[128,256]{1,0:T(8,128)(2,1)S(1)} %get-tuple-element.31), channel_id=1, source_target_pairs={{1,4},{3,6},{5,0},{7,2},{9,12},{11,14},{13,8},{15,10},{0,1},{2,3},... | collective-permute-start | bytes 196616 | tf_op jit(solution)/shard_map/ppermute | solution.py:191
  42.3 4.6 %collective-permute-start.22 = (bf16[128,256]{1,0:T(8,128)(2,1)S(1)}, bf16[128,256]{1,0:T(8,128)(2,1)S(1)}, u32[]{:S(2)}, u32[]{:S(2)}) collective-permute-start(bf16[128,256]{1,0:T(8,128)(2,1)S(1)} %get-tuple-element.32), channel_id=1, source_target_pairs={{1,8},{3,10},{5,12},{7,14},{9,0},{11,2},{13,4},{15,6},{0,1},{2,3},... | collective-permute-start | bytes 196616 | tf_op jit(solution)/shard_map/ppermute | solution.py:191
  42.8 5.5 %collective-permute-start.21 = (bf16[128,256]{1,0:T(8,128)(2,1)S(1)}, bf16[128,256]{1,0:T(8,128)(2,1)S(1)}, u32[]{:S(2)}, u32[]{:S(2)}) collective-permute-start(bf16[128,256]{1,0:T(8,128)(2,1)S(1)} %get-tuple-element.32), channel_id=1, source_target_pairs={{1,12},{3,14},{5,8},{7,10},{9,4},{11,6},{13,0},{15,2},{0,1},{2,3},... | collective-permute-start | bytes 196616 | tf_op jit(solution)/shard_map/ppermute | solution.py:191
  44.0 4.4 %collective-permute-start.24 = (bf16[128,256]{1,0:T(8,128)(2,1)S(1)}, bf16[128,256]{1,0:T(8,128)(2,1)S(1)}, u32[]{:S(2)}, u32[]{:S(2)}) collective-permute-start(bf16[128,256]{1,0:T(8,128)(2,1)S(1)} %slice.101), channel_id=1, source_target_pairs={{1,2},{3,0},{5,6},{7,4},{9,10},{11,8},{13,14},{15,12},{0,1},{2,3},... | collective-permute-start | bytes 196616 | tf_op jit(solution)/shard_map/ppermute | solution.py:191
  48.7 1.7 %collective-permute-start.26 = (bf16[128,768]{1,0:T(8,128)(2,1)S(1)}, bf16[128,768]{1,0:T(8,128)(2,1)S(1)}, u32[]{:S(2)}, u32[]{:S(2)}) collective-permute-start(bf16[128,768]{1,0:T(8,128)(2,1)S(1)} %get-tuple-element.28.r_1_), channel_id=1, source_target_pairs={{0,1},{1,0},{2,3},{3,2},{4,5},{5,4},{6,7},{7,6},{8,9},{9,8},{10,11... | collective-permute-start | bytes 589832 | tf_op jit(solution)/shard_map/ppermute | solution.py:195
  48.8 4.1 %collective-permute-start.27 = (bf16[256,256]{1,0:T(8,128)(2,1)S(1)}, bf16[256,256]{1,0:T(8,128)(2,1)S(1)}, u32[]{:S(2)}, u32[]{:S(2)}) collective-permute-start(bf16[256,256]{1,0:T(8,128)(2,1)S(1)} %slice.84), channel_id=1, source_target_pairs={{0,3},{2,1},{4,7},{6,5},{8,11},{10,9},{12,15},{14,13},{1,0},{3,2},... | collective-permute-start | bytes 393224 | tf_op jit(solution)/shard_map/ppermute | solution.py:191
  53.0 4.0 %collective-permute-start.30 = (bf16[128,256]{1,0:T(8,128)(2,1)S(1)}, bf16[128,256]{1,0:T(8,128)(2,1)S(1)}, u32[]{:S(2)}, u32[]{:S(2)}) collective-permute-start(bf16[128,256]{1,0:T(8,128)(2,1)S(1)} %get-tuple-element.29), channel_id=1, source_target_pairs={{1,4},{3,6},{5,0},{7,2},{9,12},{11,14},{13,8},{15,10},{0,1},{2,3},... | collective-permute-start | bytes 196616 | tf_op jit(solution)/shard_map/ppermute | solution.py:191
  53.8 4.6 %collective-permute-start.29 = (bf16[128,256]{1,0:T(8,128)(2,1)S(1)}, bf16[128,256]{1,0:T(8,128)(2,1)S(1)}, u32[]{:S(2)}, u32[]{:S(2)}) collective-permute-start(bf16[128,256]{1,0:T(8,128)(2,1)S(1)} %get-tuple-element.30), channel_id=1, source_target_pairs={{1,8},{3,10},{5,12},{7,14},{9,0},{11,2},{13,4},{15,6},{0,1},{2,3},... | collective-permute-start | bytes 196616 | tf_op jit(solution)/shard_map/ppermute | solution.py:191
  54.4 5.5 %collective-permute-start.28 = (bf16[128,256]{1,0:T(8,128)(2,1)S(1)}, bf16[128,256]{1,0:T(8,128)(2,1)S(1)}, u32[]{:S(2)}, u32[]{:S(2)}) collective-permute-start(bf16[128,256]{1,0:T(8,128)(2,1)S(1)} %get-tuple-element.30), channel_id=1, source_target_pairs={{1,12},{3,14},{5,8},{7,10},{9,4},{11,6},{13,0},{15,2},{0,1},{2,3},... | collective-permute-start | bytes 196616 | tf_op jit(solution)/shard_map/ppermute | solution.py:191
  56.2 3.9 %collective-permute-start.32 = (bf16[128,256]{1,0:T(8,128)(2,1)S(1)}, bf16[128,256]{1,0:T(8,128)(2,1)S(1)}, u32[]{:S(2)}, u32[]{:S(2)}) collective-permute-start(bf16[128,256]{1,0:T(8,128)(2,1)S(1)} %slice.105), channel_id=1, source_target_pairs={{1,2},{3,0},{5,6},{7,4},{9,10},{11,8},{13,14},{15,12},{0,1},{2,3},... | collective-permute-start | bytes 196616 | tf_op jit(solution)/shard_map/ppermute | solution.py:191
  59.9 1.8 %collective-permute-start.31 = (bf16[128,512]{1,0:T(8,128)(2,1)S(1)}, bf16[128,512]{1,0:T(8,128)(2,1)S(1)}, u32[]{:S(2)}, u32[]{:S(2)}) collective-permute-start(bf16[128,512]{1,0:T(8,128)(2,1)S(1)} %shard_map.104.r_1_), channel_id=1, source_target_pairs={{0,1},{1,0},{2,3},{3,2},{4,5},{5,4},{6,7},{7,6},{8,9},{9,8},{10,11... | collective-permute-start | bytes 393224 | tf_op jit(solution)/shard_map/ppermute | solution.py:195
  60.0 1.4 %collective-permute-start.33 = (bf16[128,256]{1,0:T(8,128)(2,1)S(1)}, bf16[128,256]{1,0:T(8,128)(2,1)S(1)}, u32[]{:S(2)}, u32[]{:S(2)}) collective-permute-start(bf16[128,256]{1,0:T(8,128)(2,1)S(1)} %collective-permute-done.32.r_1_), channel_id=1, source_target_pairs={{0,1},{1,0},{2,3},{3,2},{4,5},{5,4},{6,7},{7,6},{8,9},{9,8},{10,11... | collective-permute-start | bytes 196616 | tf_op jit(solution)/shard_map/ppermute | solution.py:195

commit v9 on v8

--- a/solution.py
+++ b/solution.py
@@ -18,7 +18,7 @@
     return lax.dot_general(a, b, (((ca,), (cb,)), ((), ())), preferred_element_type=F32)
 
 
-def call(kernel, outs, args, flops, scratch=(), far=0):
+def call(kernel, outs, args, flops, scratch=(), far=0, keep=True):
     vm = pl.BlockSpec(memory_space=pltpu.VMEM)
     hbm = pl.BlockSpec(memory_space=pltpu.HBM)
     near, distant = args[: len(args) - far], args[len(args) - far :]
@@ -27,7 +27,7 @@
         kernel,
         out_shape=outs,
         in_specs=[pl.BlockSpec(memory_space=pltpu.SMEM)] + [vm] * (len(args) - 1 - far) + [hbm] * far,
-        out_specs=[vm] * len(outs),
+        out_specs=[vm if keep else hbm] * len(outs),
         scratch_shapes=list(scratch),
         cost_estimate=pl.CostEstimate(flops=flops, bytes_accessed=moved, transcendentals=0),
         compiler_params=pltpu.CompilerParams(vmem_limit_bytes=VMEM_BYTES),
@@ -101,13 +101,20 @@
     joined[:, 2 * k :] = three[...]
 
 
-def next_kernel(place, one, more, two, three, gram, here, there, out, joined):
+def base_kernel(place, three, gram, here, there, out):
+    c, k = three.shape
+    for level in range(LEVELS):
+        cols = slice(level * k, (level + 1) * k)
+        total = here[:, cols].astype(F32) + there[:, cols].astype(F32)
+        out[level * c : (level + 1) * c, :] = total + mm(three[...], gram[-k:, cols], 1, 0)
+
+
+def next_kernel(place, one, more, two, three, gram, base, out, joined):
     join_siblings(one, more, two, three, joined)
     c, k = one.shape
     for level in range(LEVELS):
-        cols = slice(level * k, (level + 1) * k)
-        total = here[:, cols].astype(F32) + there[:, cols].astype(F32) + mm(joined[...], gram[:, cols], 1, 0)
-        out[level * c : (level + 1) * c, :] = total.astype(BF)
+        rows, cols = slice(level * c, (level + 1) * c), slice(level * k, (level + 1) * k)
+        out[rows, :] = (base[rows, :] + mm(joined[:, : 2 * k], gram[: 2 * k, cols], 1, 0)).astype(BF)
 
 
 def again_kernel(holder, place, early, other, gram, here, there, out):
@@ -179,9 +186,18 @@
     y[...] = mm(factor[:, -joined.shape[1] :], joined[...], 1, 1) + was[...]
 
 
-def last_kernel(holder, place, mine, other, factor, was, out, joined):
+def last_kernel(holder, place, mine, other, factor, was, out, joined, rows, sems):
     pick_kernel(holder, place, mine, other, joined)
-    out[...] = (mm(factor[:, : joined.shape[1]], joined[...], 1, 1) + was[...]).astype(BF)
+    parts = sems.shape[0]
+    size = rows.shape[0] // parts
+    copies = []
+    for i in range(parts):
+        part = pl.ds(i * size, size)
+        rows[part, :] = (mm(factor[part, : joined.shape[1]], joined[...], 1, 1) + was[part, :]).astype(BF)
+        copies.append(pltpu.make_async_copy(rows.at[part, :], out.at[part, :], sems.at[i]))
+        copies[-1].start()
+    for copy in copies:
+        copy.wait()
 
 
 def one_way(value, mask, source):
@@ -214,15 +230,24 @@
     return packed, summed, source, stride
 
 
-def siblings_of(packed, summed, source, stride, received=None):
+def add_kernel(place, one, two, out):
+    out[...] = add(one[...], two[...])
+
+
+def siblings_of(place, packed, summed, source, stride, received=None):
     c = packed.shape[0] // LEVELS
     if received is None:
-        received = one_way(packed[: 2 * c], stride, source)
+        received = one_way(packed[:c], stride, source)
+        below = one_way(packed[c : 2 * c], stride, source)
+    else:
+        received, below = received[:c], received[c:]
     three = one_way(summed[2 * c :], stride, 1 - source)
-    both = add(summed[: 2 * c], received)
-    one = one_way(both[:c], 6 * stride, 1 - source)
-    more = one_way(both[:c], 4 * stride, 1 - source)
-    two = one_way(both[c:], 2 * stride, 1 - source)
+    both = add(summed[:c], received)
+    one = one_way(both, 6 * stride, 1 - source)
+    more = one_way(both, 4 * stride, 1 - source)
+    shape = jax.ShapeDtypeStruct(below.shape, BF)
+    (under,) = call(add_kernel, [shape], (place, summed[c : 2 * c], below), 0)
+    two = one_way(under, 2 * stride, 1 - source)
     return one, more, two, three
 
 
@@ -276,7 +301,7 @@
     for step in range(applies):
         flipped = step % 2 == 0
         packed, summed, source, stride = gathered(place, packed, summed, source)
-        pieces = siblings_of(packed, summed, source, stride, received)
+        pieces = siblings_of(place, packed, summed, source, stride, received)
         received = None
         if step + 1 == applies:
             one, more, two, three = pieces
@@ -295,13 +320,15 @@
                 [S((half, c), BF)],
                 (place, q, other, upper, y),
                 field_flops // 3,
-                [pltpu.VMEM((c, 4 * k), BF)],
+                [pltpu.VMEM((c, 4 * k), BF), pltpu.VMEM((half, c), BF), sems((2,))],
+                keep=False,
             )
             return out
         there = over_rank(s)
         gram = lower_gram if flipped else upper_gram
         factor, after = (lower, upper) if flipped else (upper, lower)
-        packed, q = call(next_kernel, [p_shape, s_shape], (place, *pieces, gram, s, there), 2 * wide * wide * c)
+        (base,) = call(base_kernel, [S(p_shape.shape, F32)], (place, pieces[3], gram, s, there), wide * wide * c)
+        packed, q = call(next_kernel, [p_shape, s_shape], (place, *pieces, gram, base), 2 * wide * wide * c)
         other = over_rank(q)
         (summed,) = call(
             lambda *r: again_kernel(source, *r), [p_shape], (place, packed, other, gram, s, there), 2 * wide * wide * c

time: 63.1 us -> 66 us (1.046)
  waiting for transfers between devices: 17.9 us -> 19.9 us
    ppermute x13, waiting for transfers between devices: 1.79 us -> 3 us  [over_rank(): return lax.ppermute(value, 'rank', [(0, 1), (1, 0)])]
    ppermute x13, starting transfers between devices: 3.05 us -> 3.92 us  [over_rank(): return lax.ppermute(value, 'rank', [(0, 1), (1, 0)])]
    ppermute x21 -> x24, waiting for transfers between devices: 16.1 us -> 16.9 us  [one_way(): return lax.ppermute(value, ('rows', 'cols', 'rank'), away + home)]
    pallas_call x27 -> x34, Pallas kernels: 12.3 us -> 12.8 us  [call(): pl.pallas_call(kernel, out_shape=outs, in_specs=[pl.BlockSpec(memory_spac...]
    ppermute x21 -> x24, starting transfers between devices: 25.8 us -> 25.3 us  [one_way(): return lax.ppermute(value, ('rows', 'cols', 'rank'), away + home)]
  transfers between devices with their start and end apart: 34 -> 37, of which waited for: 14 -> 15; matrix products, arithmetic and copies ran while one was open for 0% -> 0% of each run, Pallas kernels for 17% -> 17%
where the time goes in v9:
time: 66 us; the launch traced here: 65.8 us
  starting transfers between devices  29.2 us (44%)
  waiting for transfers between devices  19.9 us (30%)
  Pallas kernels  12.8 us (19%)
  local copies, waits for them, and re-layouts  3.38 us (5%)
    ppermute x24, starting transfers between devices, one_way(): return lax.ppermute(value, ('rows', 'cols', 'rank'), away + home)  25.3 us
    ppermute x24, waiting for transfers between devices, one_way(): return lax.ppermute(value, ('rows', 'cols', 'rank'), away + home)  16.9 us
    pallas_call x34, Pallas kernels, call(): pl.pallas_call(kernel, out_shape=outs, in_specs=[pl.BlockSpec(memory_spac...  12.8 us
    ppermute x13, starting transfers between devices, over_rank(): return lax.ppermute(value, 'rank', [(0, 1), (1, 0)])  3.92 us
    unnamed x22, local copies, waits for them, and re-layouts  3.28 us
    ppermute x13, waiting for transfers between devices, over_rank(): return lax.ppermute(value, 'rank', [(0, 1), (1, 0)])  3 us
  transfers between devices with their start and end apart: 37, of which 15 were waited for; matrix products, arithmetic and copies ran while one was open for 0% of the time, Pallas kernels for 17%

profile of v9, /device:TPU:0, one launch (start us, length us, event | category | flops | bytes accessed | tf_op | source)
XLA Modules:
  0.0 65.8 jit_solution(13774298068910982763)
XLA Ops:
  0.0 1.2 %copy-done.8 = bf16[2048,128]{1,0:T(8,128)(2,1)S(1)} copy-done((bf16[2048,128]{1,0:T(8,128)(2,1)S(1)}, bf16[2048,128]{1,0:T(8,128)(2,1)}, u32[]{:S(2)}) %copy-start.8) | copy-done | bytes 524312
  1.2 1.0 %copy-done.9 = bf16[2048,128]{1,0:T(8,128)(2,1)S(1)} copy-done((bf16[2048,128]{1,0:T(8,128)(2,1)S(1)}, bf16[2048,128]{1,0:T(8,128)(2,1)}, u32[]{:S(2)}) %copy-start.9) | copy-done | bytes 524312
  2.2 1.0 %copy-done.10 = bf16[2048,128]{1,0:T(8,128)(2,1)S(1)} copy-done((bf16[2048,128]{1,0:T(8,128)(2,1)S(1)}, bf16[2048,128]{1,0:T(8,128)(2,1)}, u32[]{:S(2)}) %copy-start.10) | copy-done | bytes 524312
  3.3 0.6 collective-permute-start.7
  4.0 1.7 %collective-permute-done.7.other = bf16[3072,128]{1,0:T(8,128)(2,1)S(1)} collective-permute-done((bf16[3072,128]{1,0:T(8,128)(2,1)S(1)}, bf16[3072,128]{1,0:T(8,128)(2,1)S(1)}, u32[]{:S(2)}, u32[]{:S(2)}) %collective-permute-start.7) | collective-permute-done | bytes 786464 | tf_op jit(solution)/shard_map/ppermute | solution.py:211
  5.8 1.3 %shard_map.87 = (bf16[1024,768]{1,0:T(8,128)(2,1)S(1)}, bf16[1536,256]{1,0:T(8,128)(2,1)S(1)}) custom-call(s32[1]{0:T(128)} %bitcast.place.r_0_, bf16[3072,128]{1,0:T(8,128)(2,1)S(1)} %collective-permute-done.7.other, bf16[2048,128]{1,0:T(8,128)(2,1)S(1)} %copy-done.8, bf16[2048,128]{1,0:T(8,128)(2,1)S(1)} %copy-done.9, bf16[2048,128]{1,0:T(8,128)(2,1)S(1)} %copy-done.10), custom_call_target="tpu_custom_call" | custom-call | flops 905969664 | bytes 4718592 | tf_op jit(solution)/shard_map/pallas_call | solution.py:26
  7.2 0.4 collective-permute-start.8
  7.6 2.1 %shard_map.82.own = bf16[384,128]{1,0:T(8,128)(2,1)S(1)} custom-call(s32[1]{0:T(128)} %bitcast.place.r_0_, bf16[2048,128]{1,0:T(8,128)(2,1)} %z.1, bf16[2048,128]{1,0:T(8,128)(2,1)} %refs_0_.9, bf16[2048,128]{1,0:T(8,128)(2,1)} %refs_1_.9, bf16[2048,128]{1,0:T(8,128)(2,1)} %refs_2_.9), custom_call_target="tpu_custom_call" | custom-call | flops 201326592 | bytes 2195456 | tf_op jit(solution)/shard_map/pallas_call | solution.py:26
  10.0 2.6 %collective-permute-start.1 = (bf16[256,128]{1,0:T(8,128)(2,1)S(1)}, bf16[256,128]{1,0:T(8,128)(2,1)S(1)}, u32[]{:S(2)}, u32[]{:S(2)}) collective-permute-start(bf16[256,128]{1,0:T(8,128)(2,1)S(1)} %slice.89), channel_id=1, source_target_pairs={{0,3},{2,1},{4,7},{6,5},{8,11},{10,9},{12,15},{14,13},{1,0},{3,2},... | collective-permute-start | bytes 196616 | tf_op jit(solution)/shard_map/ppermute | solution.py:207
  12.6 1.1 %collective-permute-start.2 = (bf16[256,128]{1,0:T(8,128)(2,1)S(1)}, bf16[256,128]{1,0:T(8,128)(2,1)S(1)}, u32[]{:S(2)}, u32[]{:S(2)}) collective-permute-start(bf16[256,128]{1,0:T(8,128)(2,1)S(1)} %slice.90), channel_id=1, source_target_pairs={{0,3},{2,1},{4,7},{6,5},{8,11},{10,9},{12,15},{14,13},{1,0},{3,2},... | collective-permute-start | bytes 196616 | tf_op jit(solution)/shard_map/ppermute | solution.py:207
  13.8 0.7 %collective-permute-done.1.left = bf16[256,128]{1,0:T(8,128)(2,1)S(1)} collective-permute-done((bf16[256,128]{1,0:T(8,128)(2,1)S(1)}, bf16[256,128]{1,0:T(8,128)(2,1)S(1)}, u32[]{:S(2)}, u32[]{:S(2)}) %collective-permute-start.1) | collective-permute-done | bytes 65568 | tf_op jit(solution)/shard_map/ppermute | solution.py:207
  14.5 1.3 %collective-permute-done.2.right = bf16[256,128]{1,0:T(8,128)(2,1)S(1)} collective-permute-done((bf16[256,128]{1,0:T(8,128)(2,1)S(1)}, bf16[256,128]{1,0:T(8,128)(2,1)S(1)}, u32[]{:S(2)}, u32[]{:S(2)}) %collective-permute-start.2) | collective-permute-done | bytes 65568 | tf_op jit(solution)/shard_map/ppermute | solution.py:207
  15.9 0.7 %shard_map.89 = (f32[1024,128]{1,0:T(8,128)S(1)}, bf16[128,768]{1,0:T(8,128)(2,1)S(1)}) custom-call(s32[1]{0:T(128)} %bitcast.place.r_0_, bf16[2048,128]{1,0:T(8,128)(2,1)S(1)} %copy-done.7, bf16[4,256,256]{2,1,0:T(8,128)(2,1)S(1)} %copy-done, bf16[1024,768]{1,0:T(8,128)(2,1)S(1)} %get-tuple-element.18.after.r_2_), custom_call_target="tpu_custom_call" | custom-call | flops 201326592 | bytes 3342336 | tf_op jit(solution)/shard_map/pallas_call | solution.py:26
  16.8 0.5 collective-permute-start.4
  17.5 2.6 %collective-permute-start.3 = (bf16[128,256]{1,0:T(8,128)(2,1)S(1)}, bf16[128,256]{1,0:T(8,128)(2,1)S(1)}, u32[]{:S(2)}, u32[]{:S(2)}) collective-permute-start(bf16[128,256]{1,0:T(8,128)(2,1)S(1)} %add_convert_fusion.3), channel_id=1, source_target_pairs={{1,12},{3,14},{5,8},{7,10},{9,4},{11,6},{13,0},{15,2},{0,1},{2,3},... | collective-permute-start | bytes 196616 | tf_op jit(solution)/shard_map/ppermute | solution.py:207
  20.1 1.3 %collective-permute-start.5 = (bf16[128,256]{1,0:T(8,128)(2,1)S(1)}, bf16[128,256]{1,0:T(8,128)(2,1)S(1)}, u32[]{:S(2)}, u32[]{:S(2)}) collective-permute-start(bf16[128,256]{1,0:T(8,128)(2,1)S(1)} %shard_map.85), channel_id=1, source_target_pairs={{1,4},{3,6},{5,0},{7,2},{9,12},{11,14},{13,8},{15,10},{0,1},{2,3},... | collective-permute-start | bytes 196616 | tf_op jit(solution)/shard_map/ppermute | solution.py:207
  21.4 1.3 %shard_map.95 = (bf16[1024,768]{1,0:T(8,128)(2,1)S(1)}, bf16[1536,256]{1,0:T(8,128)(2,1)S(1)}) custom-call(s32[1]{0:T(128)} %bitcast.place.r_0_, bf16[3072,128]{1,0:T(8,128)(2,1)S(1)} %collective-permute-done.17.other, bf16[2048,128]{1,0:T(8,128)(2,1)S(1)} %copy-done.2, bf16[2048,128]{1,0:T(8,128)(2,1)S(1)} %copy-done.4, bf16[2048,128]{1,0:T(8,128)(2,1)S(1)} %copy-done.6), custom_call_target="tpu_custom_call" | custom-call | flops 905969664 | bytes 4718592 | tf_op jit(solution)/shard_map/pallas_call | solution.py:26
  22.8 0.4 collective-permute-start.18
  23.7 0.7 %collective-permute-done.5.two = bf16[128,256]{1,0:T(8,128)(2,1)S(1)} collective-permute-done((bf16[128,256]{1,0:T(8,128)(2,1)S(1)}, bf16[128,256]{1,0:T(8,128)(2,1)S(1)}, u32[]{:S(2)}, u32[]{:S(2)}) %collective-permute-start.5) | collective-permute-done | bytes 65568 | tf_op jit(solution)/shard_map/ppermute | solution.py:207
  24.8 2.5 %collective-permute-start.14 = (bf16[128,256]{1,0:T(8,128)(2,1)S(1)}, bf16[128,256]{1,0:T(8,128)(2,1)S(1)}, u32[]{:S(2)}, u32[]{:S(2)}) collective-permute-start(bf16[128,256]{1,0:T(8,128)(2,1)S(1)} %get-tuple-element.39), channel_id=1, source_target_pairs={{0,3},{2,1},{4,7},{6,5},{8,11},{10,9},{12,15},{14,13},{1,0},{3,2},... | collective-permute-start | bytes 196616 | tf_op jit(solution)/shard_map/ppermute | solution.py:207
  27.4 1.8 %collective-permute-done.14.two = bf16[128,256]{1,0:T(8,128)(2,1)S(1)} collective-permute-done((bf16[128,256]{1,0:T(8,128)(2,1)S(1)}, bf16[128,256]{1,0:T(8,128)(2,1)S(1)}, u32[]{:S(2)}, u32[]{:S(2)}) %collective-permute-start.14) | collective-permute-done | bytes 65568 | tf_op jit(solution)/shard_map/ppermute | solution.py:207
  29.3 1.1 %collective-permute-start.16 = (bf16[128,256]{1,0:T(8,128)(2,1)S(1)}, bf16[128,256]{1,0:T(8,128)(2,1)S(1)}, u32[]{:S(2)}, u32[]{:S(2)}) collective-permute-start(bf16[128,256]{1,0:T(8,128)(2,1)S(1)} %get-tuple-element.37), channel_id=1, source_target_pairs={{1,2},{3,0},{5,6},{7,4},{9,10},{11,8},{13,14},{15,12},{0,1},{2,3},... | collective-permute-start | bytes 196616 | tf_op jit(solution)/shard_map/ppermute | solution.py:207
  30.5 0.9 %shard_map.98.y.r_3_ = f32[1024,128]{1,0:T(8,128)S(1)} custom-call(s32[1]{0:T(128)} %bitcast.place.r_0_, bf16[128,768]{1,0:T(8,128)(2,1)S(1)} %shard_map.97.r_1_, bf16[1024,768]{1,0:T(8,128)(2,1)S(1)} %get-tuple-element.18.after.r_2_, f32[1024,128]{1,0:T(8,128)S(1)} %get-tuple-element.23.r_3_, bf16[4,256,256]{2,1,0:T(8,128)(2,1)S(1)} %copy-done), custom_call_target="tpu_custom_call" | custom-call | flops 201326592 | bytes 3342336 | tf_op jit(solution)/shard_map/pallas_call | solution.py:26
  31.3 0.4 shard_map.99.here.r_4_
  31.8 1.1 %collective-permute-start.19 = (bf16[128,768]{1,0:T(8,128)(2,1)S(1)}, bf16[128,768]{1,0:T(8,128)(2,1)S(1)}, u32[]{:S(2)}, u32[]{:S(2)}) collective-permute-start(bf16[128,768]{1,0:T(8,128)(2,1)S(1)} %shard_map.99.here.r_4_), channel_id=1, source_target_pairs={{0,1},{1,0},{2,3},{3,2},{4,5},{5,4},{6,7},{7,6},{8,9},{9,8},{10,11... | collective-permute-start | bytes 589832 | tf_op jit(solution)/shard_map/ppermute | solution.py:211
  33.0 2.4 %collective-permute-start.12 = (bf16[128,256]{1,0:T(8,128)(2,1)S(1)}, bf16[128,256]{1,0:T(8,128)(2,1)S(1)}, u32[]{:S(2)}, u32[]{:S(2)}) collective-permute-start(bf16[128,256]{1,0:T(8,128)(2,1)S(1)} %add_convert_fusion.2), channel_id=1, source_target_pairs={{1,12},{3,14},{5,8},{7,10},{9,4},{11,6},{13,0},{15,2},{0,1},{2,3},... | collective-permute-start | bytes 196616 | tf_op jit(solution)/shard_map/ppermute | solution.py:207
  35.9 3.1 %collective-permute-done.13.more = bf16[128,256]{1,0:T(8,128)(2,1)S(1)} collective-permute-done((bf16[128,256]{1,0:T(8,128)(2,1)S(1)}, bf16[128,256]{1,0:T(8,128)(2,1)S(1)}, u32[]{:S(2)}, u32[]{:S(2)}) %collective-permute-start.13) | collective-permute-done | bytes 65568 | tf_op jit(solution)/shard_map/ppermute | solution.py:207
  39.6 1.2 %collective-permute-done.20.r_2_ = bf16[128,768]{1,0:T(8,128)(2,1)S(1)} collective-permute-done((bf16[128,768]{1,0:T(8,128)(2,1)S(1)}, bf16[128,768]{1,0:T(8,128)(2,1)S(1)}, u32[]{:S(2)}, u32[]{:S(2)}) %collective-permute-start.20) | collective-permute-done | bytes 196640 | tf_op jit(solution)/shard_map/ppermute | solution.py:211
  40.8 0.6 collective-permute-done.24.two
  41.4 2.2 %collective-permute-start.25 = (bf16[128,256]{1,0:T(8,128)(2,1)S(1)}, bf16[128,256]{1,0:T(8,128)(2,1)S(1)}, u32[]{:S(2)}, u32[]{:S(2)}) collective-permute-start(bf16[128,256]{1,0:T(8,128)(2,1)S(1)} %shard_map.103), channel_id=1, source_target_pairs={{1,4},{3,6},{5,0},{7,2},{9,12},{11,14},{13,8},{15,10},{0,1},{2,3},... | collective-permute-start | bytes 196616 | tf_op jit(solution)/shard_map/ppermute | solution.py:207
  43.8 0.9 %shard_map.105.y.r_3_ = f32[1024,128]{1,0:T(8,128)S(1)} custom-call(s32[1]{0:T(128)} %bitcast.place.r_0_, bf16[128,768]{1,0:T(8,128)(2,1)S(1)} %shard_map.104.r_1_, bf16[1024,768]{1,0:T(8,128)(2,1)S(1)} %get-tuple-element.24.after.r_2_.r_3_, f32[1024,128]{1,0:T(8,128)S(1)} %shard_map.98.y.r_3_, bf16[4,256,256]{2,1,0:T(8,128)(2,1)S(1)} %copy-done), custom_call_target="tpu_custom_call" | custom-call | flops 201326592 | bytes 3342336 | tf_op jit(solution)/shard_map/pallas_call | solution.py:26
  44.6 0.4 shard_map.106.here.r_4_
  45.2 0.5 collective-permute-start.23
  45.7 1.9 %collective-permute-start.22 = (bf16[128,256]{1,0:T(8,128)(2,1)S(1)}, bf16[128,256]{1,0:T(8,128)(2,1)S(1)}, u32[]{:S(2)}, u32[]{:S(2)}) collective-permute-start(bf16[128,256]{1,0:T(8,128)(2,1)S(1)} %add_convert_fusion.1), channel_id=1, source_target_pairs={{1,12},{3,14},{5,8},{7,10},{9,4},{11,6},{13,0},{15,2},{0,1},{2,3},... | collective-permute-start | bytes 196616 | tf_op jit(solution)/shard_map/ppermute | solution.py:207
  47.9 2.0 %collective-permute-done.23.more = bf16[128,256]{1,0:T(8,128)(2,1)S(1)} collective-permute-done((bf16[128,256]{1,0:T(8,128)(2,1)S(1)}, bf16[128,256]{1,0:T(8,128)(2,1)S(1)}, u32[]{:S(2)}, u32[]{:S(2)}) %collective-permute-start.23) | collective-permute-done | bytes 65568 | tf_op jit(solution)/shard_map/ppermute | solution.py:207
  49.8 1.5 %collective-permute-done.22.one = bf16[128,256]{1,0:T(8,128)(2,1)S(1)} collective-permute-done((bf16[128,256]{1,0:T(8,128)(2,1)S(1)}, bf16[128,256]{1,0:T(8,128)(2,1)S(1)}, u32[]{:S(2)}, u32[]{:S(2)}) %collective-permute-start.22) | collective-permute-done | bytes 65568 | tf_op jit(solution)/shard_map/ppermute | solution.py:207
  51.7 2.2 %collective-permute-start.32 = (bf16[128,256]{1,0:T(8,128)(2,1)S(1)}, bf16[128,256]{1,0:T(8,128)(2,1)S(1)}, u32[]{:S(2)}, u32[]{:S(2)}) collective-permute-start(bf16[128,256]{1,0:T(8,128)(2,1)S(1)} %get-tuple-element.31), channel_id=1, source_target_pairs={{0,3},{2,1},{4,7},{6,5},{8,11},{10,9},{12,15},{14,13},{1,0},{3,2},... | collective-permute-start | bytes 196616 | tf_op jit(solution)/shard_map/ppermute | solution.py:207
  54.0 1.8 %collective-permute-done.32.two = bf16[128,256]{1,0:T(8,128)(2,1)S(1)} collective-permute-done((bf16[128,256]{1,0:T(8,128)(2,1)S(1)}, bf16[128,256]{1,0:T(8,128)(2,1)S(1)}, u32[]{:S(2)}, u32[]{:S(2)}) %collective-permute-start.32) | collective-permute-done | bytes 65568 | tf_op jit(solution)/shard_map/ppermute | solution.py:207
  56.0 0.4 collective-permute-done.29
  56.4 0.8 %collective-permute-start.31 = (bf16[128,256]{1,0:T(8,128)(2,1)S(1)}, bf16[128,256]{1,0:T(8,128)(2,1)S(1)}, u32[]{:S(2)}, u32[]{:S(2)}) collective-permute-start(bf16[128,256]{1,0:T(8,128)(2,1)S(1)} %add_convert_fusion), channel_id=1, source_target_pairs={{1,8},{3,10},{5,12},{7,14},{9,0},{11,2},{13,4},{15,6},{0,1},{2,3},... | collective-permute-start | bytes 196616 | tf_op jit(solution)/shard_map/ppermute | solution.py:207
  57.2 1.6 %collective-permute-start.30 = (bf16[128,256]{1,0:T(8,128)(2,1)S(1)}, bf16[128,256]{1,0:T(8,128)(2,1)S(1)}, u32[]{:S(2)}, u32[]{:S(2)}) collective-permute-start(bf16[128,256]{1,0:T(8,128)(2,1)S(1)} %add_convert_fusion), channel_id=1, source_target_pairs={{1,12},{3,14},{5,8},{7,10},{9,4},{11,6},{13,0},{15,2},{0,1},{2,3},... | collective-permute-start | bytes 196616 | tf_op jit(solution)/shard_map/ppermute | solution.py:207
  58.9 1.0 %collective-permute-start.35 = (bf16[128,256]{1,0:T(8,128)(2,1)S(1)}, bf16[128,256]{1,0:T(8,128)(2,1)S(1)}, u32[]{:S(2)}, u32[]{:S(2)}) collective-permute-start(bf16[128,256]{1,0:T(8,128)(2,1)S(1)} %get-tuple-element.29), channel_id=1, source_target_pairs={{1,2},{3,0},{5,6},{7,4},{9,10},{11,8},{13,14},{15,12},{0,1},{2,3},... | collective-permute-start | bytes 196616 | tf_op jit(solution)/shard_map/ppermute | solution.py:207
  59.9 1.2 %collective-permute-done.31.more = bf16[128,256]{1,0:T(8,128)(2,1)S(1)} collective-permute-done((bf16[128,256]{1,0:T(8,128)(2,1)S(1)}, bf16[128,256]{1,0:T(8,128)(2,1)S(1)}, u32[]{:S(2)}, u32[]{:S(2)}) %collective-permute-start.31) | collective-permute-done | bytes 65568 | tf_op jit(solution)/shard_map/ppermute | solution.py:207
  61.1 1.7 %collective-permute-done.30.one = bf16[128,256]{1,0:T(8,128)(2,1)S(1)} collective-permute-done((bf16[128,256]{1,0:T(8,128)(2,1)S(1)}, bf16[128,256]{1,0:T(8,128)(2,1)S(1)}, u32[]{:S(2)}, u32[]{:S(2)}) %collective-permute-start.30) | collective-permute-done | bytes 65568 | tf_op jit(solution)/shard_map/ppermute | solution.py:207
  62.9 0.5 collective-permute-start.36
  63.4 0.9 %shard_map.113.r_4_ = f32[1024,128]{1,0:T(8,128)S(1)} custom-call(s32[1]{0:T(128)} %bitcast.place.r_0_, bf16[128,768]{1,0:T(8,128)(2,1)S(1)} %shard_map.112.r_1_, bf16[1024,768]{1,0:T(8,128)(2,1)S(1)} %get-tuple-element.18.after.r_2_, f32[1024,128]{1,0:T(8,128)S(1)} %shard_map.105.y.r_3_, bf16[4,256,256]{2,1,0:T(8,128)(2,1)S(1)} %copy-done), custom_call_target="tpu_custom_call" | custom-call | flops 201326592 | bytes 3342336 | tf_op jit(solution)/shard_map/pallas_call | solution.py:26
  64.3 0.3 shard_map.114.r_4_
  64.6 1.2 %shard_map.115 = bf16[1024,128]{1,0:T(8,128)(2,1)} custom-call(s32[1]{0:T(128)} %bitcast.place.r_0_, bf16[128,512]{1,0:T(8,128)(2,1)S(1)} %shard_map.111.r_1_, bf16[128,512]{1,0:T(8,128)(2,1)S(1)} %collective-permute-done.34.r_2_, bf16[1024,768]{1,0:T(8,128)(2,1)S(1)} %get-tuple-element.24.after.r_2_.r_3_, f32[1024,128]{1,0:T(8,128)S(1)} %shard_map.114.r_4_), custom_call_target="tpu_custom_call" | custom-call | flops 134217728 | bytes 2621440 | tf_op jit(solution)/shard_map/pallas_call | solution.py:26
  (96 shorter events, 4.5 us)
Async XLA Ops:
  0.0 3.9 %copy-start.5 = (bf16[2048,128]{1,0:T(8,128)(2,1)S(1)}, bf16[2048,128]{1,0:T(8,128)(2,1)}, u32[]{:S(2)}) copy-start(bf16[2048,128]{1,0:T(8,128)(2,1)} %refs_2_.9) | copy-start | bytes 1572868
  0.0 3.9 %copy-start.3 = (bf16[2048,128]{1,0:T(8,128)(2,1)S(1)}, bf16[2048,128]{1,0:T(8,128)(2,1)}, u32[]{:S(2)}) copy-start(bf16[2048,128]{1,0:T(8,128)(2,1)} %refs_1_.9) | copy-start | bytes 1572868
  0.0 3.9 %copy-start.1 = (bf16[2048,128]{1,0:T(8,128)(2,1)S(1)}, bf16[2048,128]{1,0:T(8,128)(2,1)}, u32[]{:S(2)}) copy-start(bf16[2048,128]{1,0:T(8,128)(2,1)} %refs_0_.9) | copy-start | bytes 1572868
  0.0 1.2 %copy-start.8 = (bf16[2048,128]{1,0:T(8,128)(2,1)S(1)}, bf16[2048,128]{1,0:T(8,128)(2,1)}, u32[]{:S(2)}) copy-start(bf16[2048,128]{1,0:T(8,128)(2,1)} %refs_0_.7) | copy-start | bytes 1572868
  1.2 1.0 %copy-start.9 = (bf16[2048,128]{1,0:T(8,128)(2,1)S(1)}, bf16[2048,128]{1,0:T(8,128)(2,1)}, u32[]{:S(2)}) copy-start(bf16[2048,128]{1,0:T(8,128)(2,1)} %refs_1_.7) | copy-start | bytes 1572868
  2.2 1.0 %copy-start.10 = (bf16[2048,128]{1,0:T(8,128)(2,1)S(1)}, bf16[2048,128]{1,0:T(8,128)(2,1)}, u32[]{:S(2)}) copy-start(bf16[2048,128]{1,0:T(8,128)(2,1)} %refs_2_.7) | copy-start | bytes 1572868
  3.3 2.5 %collective-permute-start.7 = (bf16[3072,128]{1,0:T(8,128)(2,1)S(1)}, bf16[3072,128]{1,0:T(8,128)(2,1)S(1)}, u32[]{:S(2)}, u32[]{:S(2)}) collective-permute-start(bf16[3072,128]{1,0:T(8,128)(2,1)S(1)} %shard_map.86), channel_id=1, source_target_pairs={{0,1},{1,0},{2,3},{3,2},{4,5},{5,4},{6,7},{7,6},{8,9},{9,8},{10,11... | collective-permute-start | bytes 2359304 | tf_op jit(solution)/shard_map/ppermute | solution.py:211
  3.9 16.1 %collective-permute-start.17 = (bf16[3072,128]{1,0:T(8,128)(2,1)S(1)}, bf16[3072,128]{1,0:T(8,128)(2,1)S(1)}, u32[]{:S(2)}, u32[]{:S(2)}) collective-permute-start(bf16[3072,128]{1,0:T(8,128)(2,1)S(1)} %shard_map.94), channel_id=1, source_target_pairs={{0,1},{1,0},{2,3},{3,2},{4,5},{5,4},{6,7},{7,6},{8,9},{9,8},{10,11... | collective-permute-start | bytes 2359304 | tf_op jit(solution)/shard_map/ppermute | solution.py:211
  7.1 8.8 %copy-start = (bf16[4,256,256]{2,1,0:T(8,128)(2,1)S(1)}, bf16[4,256,256]{2,1,0:T(8,128)(2,1)}, u32[]{:S(2)}) copy-start(bf16[4,256,256]{2,1,0:T(8,128)(2,1)} %r_4_.5) | copy-start | bytes 1572868
  7.1 8.7 %copy-start.7 = (bf16[2048,128]{1,0:T(8,128)(2,1)S(1)}, bf16[2048,128]{1,0:T(8,128)(2,1)}, u32[]{:S(2)}) copy-start(bf16[2048,128]{1,0:T(8,128)(2,1)} %z.1) | copy-start | bytes 1572868
  7.2 15.6 %collective-permute-start.8 = (bf16[1536,256]{1,0:T(8,128)(2,1)S(1)}, bf16[1536,256]{1,0:T(8,128)(2,1)S(1)}, u32[]{:S(2)}, u32[]{:S(2)}) collective-permute-start(bf16[1536,256]{1,0:T(8,128)(2,1)S(1)} %get-tuple-element.17.mine), channel_id=1, source_target_pairs={{0,1},{1,0},{2,3},{3,2},{4,5},{5,4},{6,7},{7,6},{8,9},{9,8},{10,11... | collective-permute-start | bytes 2359304 | tf_op jit(solution)/shard_map/ppermute | solution.py:211
  9.7 2.9 %collective-permute-start = (bf16[384,128]{1,0:T(8,128)(2,1)S(1)}, bf16[384,128]{1,0:T(8,128)(2,1)S(1)}, u32[]{:S(2)}, u32[]{:S(2)}) collective-permute-start(bf16[384,128]{1,0:T(8,128)(2,1)S(1)} %shard_map.82.own), channel_id=1, source_target_pairs={{0,1},{1,0},{2,3},{3,2},{4,5},{5,4},{6,7},{7,6},{8,9},{9,8},{10,11... | collective-permute-start | bytes 294920 | tf_op jit(solution)/shard_map/ppermute | solution.py:211
  10.0 4.5 %collective-permute-start.1 = (bf16[256,128]{1,0:T(8,128)(2,1)S(1)}, bf16[256,128]{1,0:T(8,128)(2,1)S(1)}, u32[]{:S(2)}, u32[]{:S(2)}) collective-permute-start(bf16[256,128]{1,0:T(8,128)(2,1)S(1)} %slice.89), channel_id=1, source_target_pairs={{0,3},{2,1},{4,7},{6,5},{8,11},{10,9},{12,15},{14,13},{1,0},{3,2},... | collective-permute-start | bytes 196616 | tf_op jit(solution)/shard_map/ppermute | solution.py:207
  12.6 3.2 %collective-permute-start.2 = (bf16[256,128]{1,0:T(8,128)(2,1)S(1)}, bf16[256,128]{1,0:T(8,128)(2,1)S(1)}, u32[]{:S(2)}, u32[]{:S(2)}) collective-permute-start(bf16[256,128]{1,0:T(8,128)(2,1)S(1)} %slice.90), channel_id=1, source_target_pairs={{0,3},{2,1},{4,7},{6,5},{8,11},{10,9},{12,15},{14,13},{1,0},{3,2},... | collective-permute-start | bytes 196616 | tf_op jit(solution)/shard_map/ppermute | solution.py:207
  13.8 3.7 %collective-permute-start.6 = (bf16[128,256]{1,0:T(8,128)(2,1)S(1)}, bf16[128,256]{1,0:T(8,128)(2,1)S(1)}, u32[]{:S(2)}, u32[]{:S(2)}) collective-permute-start(bf16[128,256]{1,0:T(8,128)(2,1)S(1)} %get-tuple-element.41), channel_id=1, source_target_pairs={{1,2},{3,0},{5,6},{7,4},{9,10},{11,8},{13,14},{15,12},{0,1},{2,3},... | collective-permute-start | bytes 196616 | tf_op jit(solution)/shard_map/ppermute | solution.py:207
  15.9 5.5 %copy-start.2 = (bf16[2048,128]{1,0:T(8,128)(2,1)S(1)}, bf16[2048,128]{1,0:T(8,128)(2,1)}, u32[]{:S(2)}) copy-start(bf16[2048,128]{1,0:T(8,128)(2,1)} %refs_0_.9) | copy-start | bytes 1572868
  15.9 5.5 %copy-start.4 = (bf16[2048,128]{1,0:T(8,128)(2,1)S(1)}, bf16[2048,128]{1,0:T(8,128)(2,1)}, u32[]{:S(2)}) copy-start(bf16[2048,128]{1,0:T(8,128)(2,1)} %refs_1_.9) | copy-start | bytes 1572868
  15.9 5.5 %copy-start.6 = (bf16[2048,128]{1,0:T(8,128)(2,1)S(1)}, bf16[2048,128]{1,0:T(8,128)(2,1)}, u32[]{:S(2)}) copy-start(bf16[2048,128]{1,0:T(8,128)(2,1)} %refs_2_.9) | copy-start | bytes 1572868
  16.7 6.8 %collective-permute-start.9 = (bf16[128,768]{1,0:T(8,128)(2,1)S(1)}, bf16[128,768]{1,0:T(8,128)(2,1)S(1)}, u32[]{:S(2)}, u32[]{:S(2)}) collective-permute-start(bf16[128,768]{1,0:T(8,128)(2,1)S(1)} %get-tuple-element.19.here.r_4_), channel_id=1, source_target_pairs={{0,1},{1,0},{2,3},{3,2},{4,5},{5,4},{6,7},{7,6},{8,9},{9,8},{10,11... | collective-permute-start | bytes 589832 | tf_op jit(solution)/shard_map/ppermute | solution.py:211
  16.8 7.6 %collective-permute-start.4 = (bf16[128,256]{1,0:T(8,128)(2,1)S(1)}, bf16[128,256]{1,0:T(8,128)(2,1)S(1)}, u32[]{:S(2)}, u32[]{:S(2)}) collective-permute-start(bf16[128,256]{1,0:T(8,128)(2,1)S(1)} %add_convert_fusion.3), channel_id=1, source_target_pairs={{1,8},{3,10},{5,12},{7,14},{9,0},{11,2},{13,4},{15,6},{0,1},{2,3},... | collective-permute-start | bytes 196616 | tf_op jit(solution)/shard_map/ppermute | solution.py:207
  17.5 6.9 %collective-permute-start.3 = (bf16[128,256]{1,0:T(8,128)(2,1)S(1)}, bf16[128,256]{1,0:T(8,128)(2,1)S(1)}, u32[]{:S(2)}, u32[]{:S(2)}) collective-permute-start(bf16[128,256]{1,0:T(8,128)(2,1)S(1)} %add_convert_fusion.3), channel_id=1, source_target_pairs={{1,12},{3,14},{5,8},{7,10},{9,4},{11,6},{13,0},{15,2},{0,1},{2,3},... | collective-permute-start | bytes 196616 | tf_op jit(solution)/shard_map/ppermute | solution.py:207
  20.1 4.3 %collective-permute-start.5 = (bf16[128,256]{1,0:T(8,128)(2,1)S(1)}, bf16[128,256]{1,0:T(8,128)(2,1)S(1)}, u32[]{:S(2)}, u32[]{:S(2)}) collective-permute-start(bf16[128,256]{1,0:T(8,128)(2,1)S(1)} %shard_map.85), channel_id=1, source_target_pairs={{1,4},{3,6},{5,0},{7,2},{9,12},{11,14},{13,8},{15,10},{0,1},{2,3},... | collective-permute-start | bytes 196616 | tf_op jit(solution)/shard_map/ppermute | solution.py:207
  22.8 10.2 %collective-permute-start.18 = (bf16[1536,256]{1,0:T(8,128)(2,1)S(1)}, bf16[1536,256]{1,0:T(8,128)(2,1)S(1)}, u32[]{:S(2)}, u32[]{:S(2)}) collective-permute-start(bf16[1536,256]{1,0:T(8,128)(2,1)S(1)} %get-tuple-element.22.mine), channel_id=1, source_target_pairs={{0,1},{1,0},{2,3},{3,2},{4,5},{5,4},{6,7},{7,6},{8,9},{9,8},{10,11... | collective-permute-start | bytes 2359304 | tf_op jit(solution)/shard_map/ppermute | solution.py:211
  24.7 2.6 %collective-permute-start.10 = (bf16[128,768]{1,0:T(8,128)(2,1)S(1)}, bf16[128,768]{1,0:T(8,128)(2,1)S(1)}, u32[]{:S(2)}, u32[]{:S(2)}) collective-permute-start(bf16[128,768]{1,0:T(8,128)(2,1)S(1)} %get-tuple-element.21.r_1_), channel_id=1, source_target_pairs={{0,1},{1,0},{2,3},{3,2},{4,5},{5,4},{6,7},{7,6},{8,9},{9,8},{10,11... | collective-permute-start | bytes 589832 | tf_op jit(solution)/shard_map/ppermute | solution.py:211
  24.8 4.4 %collective-permute-start.14 = (bf16[128,256]{1,0:T(8,128)(2,1)S(1)}, bf16[128,256]{1,0:T(8,128)(2,1)S(1)}, u32[]{:S(2)}, u32[]{:S(2)}) collective-permute-start(bf16[128,256]{1,0:T(8,128)(2,1)S(1)} %get-tuple-element.39), channel_id=1, source_target_pairs={{0,3},{2,1},{4,7},{6,5},{8,11},{10,9},{12,15},{14,13},{1,0},{3,2},... | collective-permute-start | bytes 196616 | tf_op jit(solution)/shard_map/ppermute | solution.py:207
  27.2 5.7 %collective-permute-start.11 = (bf16[128,256]{1,0:T(8,128)(2,1)S(1)}, bf16[128,256]{1,0:T(8,128)(2,1)S(1)}, u32[]{:S(2)}, u32[]{:S(2)}) collective-permute-start(bf16[128,256]{1,0:T(8,128)(2,1)S(1)} %get-tuple-element.40), channel_id=1, source_target_pairs={{0,3},{2,1},{4,7},{6,5},{8,11},{10,9},{12,15},{14,13},{1,0},{3,2},... | collective-permute-start | bytes 196616 | tf_op jit(solution)/shard_map/ppermute | solution.py:207
  29.2 6.7 %collective-permute-start.15 = (bf16[128,256]{1,0:T(8,128)(2,1)S(1)}, bf16[128,256]{1,0:T(8,128)(2,1)S(1)}, u32[]{:S(2)}, u32[]{:S(2)}) collective-permute-start(bf16[128,256]{1,0:T(8,128)(2,1)S(1)} %shard_map.93), channel_id=1, source_target_pairs={{1,4},{3,6},{5,0},{7,2},{9,12},{11,14},{13,8},{15,10},{0,1},{2,3},... | collective-permute-start | bytes 196616 | tf_op jit(solution)/shard_map/ppermute | solution.py:207
  29.3 6.4 %collective-permute-start.16 = (bf16[128,256]{1,0:T(8,128)(2,1)S(1)}, bf16[128,256]{1,0:T(8,128)(2,1)S(1)}, u32[]{:S(2)}, u32[]{:S(2)}) collective-permute-start(bf16[128,256]{1,0:T(8,128)(2,1)S(1)} %get-tuple-element.37), channel_id=1, source_target_pairs={{1,2},{3,0},{5,6},{7,4},{9,10},{11,8},{13,14},{15,12},{0,1},{2,3},... | collective-permute-start | bytes 196616 | tf_op jit(solution)/shard_map/ppermute | solution.py:207
  31.8 3.9 %collective-permute-start.19 = (bf16[128,768]{1,0:T(8,128)(2,1)S(1)}, bf16[128,768]{1,0:T(8,128)(2,1)S(1)}, u32[]{:S(2)}, u32[]{:S(2)}) collective-permute-start(bf16[128,768]{1,0:T(8,128)(2,1)S(1)} %shard_map.99.here.r_4_), channel_id=1, source_target_pairs={{0,1},{1,0},{2,3},{3,2},{4,5},{5,4},{6,7},{7,6},{8,9},{9,8},{10,11... | collective-permute-start | bytes 589832 | tf_op jit(solution)/shard_map/ppermute | solution.py:211
  32.9 6.0 %collective-permute-start.13 = (bf16[128,256]{1,0:T(8,128)(2,1)S(1)}, bf16[128,256]{1,0:T(8,128)(2,1)S(1)}, u32[]{:S(2)}, u32[]{:S(2)}) collective-permute-start(bf16[128,256]{1,0:T(8,128)(2,1)S(1)} %add_convert_fusion.2), channel_id=1, source_target_pairs={{1,8},{3,10},{5,12},{7,14},{9,0},{11,2},{13,4},{15,6},{0,1},{2,3},... | collective-permute-start | bytes 196616 | tf_op jit(solution)/shard_map/ppermute | solution.py:207
  33.0 6.0 %collective-permute-start.12 = (bf16[128,256]{1,0:T(8,128)(2,1)S(1)}, bf16[128,256]{1,0:T(8,128)(2,1)S(1)}, u32[]{:S(2)}, u32[]{:S(2)}) collective-permute-start(bf16[128,256]{1,0:T(8,128)(2,1)S(1)} %add_convert_fusion.2), channel_id=1, source_target_pairs={{1,12},{3,14},{5,8},{7,10},{9,4},{11,6},{13,0},{15,2},{0,1},{2,3},... | collective-permute-start | bytes 196616 | tf_op jit(solution)/shard_map/ppermute | solution.py:207
  39.3 1.5 %collective-permute-start.20 = (bf16[128,768]{1,0:T(8,128)(2,1)S(1)}, bf16[128,768]{1,0:T(8,128)(2,1)S(1)}, u32[]{:S(2)}, u32[]{:S(2)}) collective-permute-start(bf16[128,768]{1,0:T(8,128)(2,1)S(1)} %get-tuple-element.26.r_1_), channel_id=1, source_target_pairs={{0,1},{1,0},{2,3},{3,2},{4,5},{5,4},{6,7},{7,6},{8,9},{9,8},{10,11... | collective-permute-start | bytes 589832 | tf_op jit(solution)/shard_map/ppermute | solution.py:211
  39.4 2.0 %collective-permute-start.24 = (bf16[128,256]{1,0:T(8,128)(2,1)S(1)}, bf16[128,256]{1,0:T(8,128)(2,1)S(1)}, u32[]{:S(2)}, u32[]{:S(2)}) collective-permute-start(bf16[128,256]{1,0:T(8,128)(2,1)S(1)} %get-tuple-element.35), channel_id=1, source_target_pairs={{0,3},{2,1},{4,7},{6,5},{8,11},{10,9},{12,15},{14,13},{1,0},{3,2},... | collective-permute-start | bytes 196616 | tf_op jit(solution)/shard_map/ppermute | solution.py:207
  39.5 5.7 %collective-permute-start.21 = (bf16[128,256]{1,0:T(8,128)(2,1)S(1)}, bf16[128,256]{1,0:T(8,128)(2,1)S(1)}, u32[]{:S(2)}, u32[]{:S(2)}) collective-permute-start(bf16[128,256]{1,0:T(8,128)(2,1)S(1)} %get-tuple-element.36), channel_id=1, source_target_pairs={{0,3},{2,1},{4,7},{6,5},{8,11},{10,9},{12,15},{14,13},{1,0},{3,2},... | collective-permute-start | bytes 196616 | tf_op jit(solution)/shard_map/ppermute | solution.py:207
  41.4 6.4 %collective-permute-start.25 = (bf16[128,256]{1,0:T(8,128)(2,1)S(1)}, bf16[128,256]{1,0:T(8,128)(2,1)S(1)}, u32[]{:S(2)}, u32[]{:S(2)}) collective-permute-start(bf16[128,256]{1,0:T(8,128)(2,1)S(1)} %shard_map.103), channel_id=1, source_target_pairs={{1,4},{3,6},{5,0},{7,2},{9,12},{11,14},{13,8},{15,10},{0,1},{2,3},... | collective-permute-start | bytes 196616 | tf_op jit(solution)/shard_map/ppermute | solution.py:207
  43.7 4.0 %collective-permute-start.26 = (bf16[128,256]{1,0:T(8,128)(2,1)S(1)}, bf16[128,256]{1,0:T(8,128)(2,1)S(1)}, u32[]{:S(2)}, u32[]{:S(2)}) collective-permute-start(bf16[128,256]{1,0:T(8,128)(2,1)S(1)} %get-tuple-element.33), channel_id=1, source_target_pairs={{1,2},{3,0},{5,6},{7,4},{9,10},{11,8},{13,14},{15,12},{0,1},{2,3},... | collective-permute-start | bytes 196616 | tf_op jit(solution)/shard_map/ppermute | solution.py:207
  45.1 2.6 %collective-permute-start.27 = (bf16[128,768]{1,0:T(8,128)(2,1)S(1)}, bf16[128,768]{1,0:T(8,128)(2,1)S(1)}, u32[]{:S(2)}, u32[]{:S(2)}) collective-permute-start(bf16[128,768]{1,0:T(8,128)(2,1)S(1)} %shard_map.106.here.r_4_), channel_id=1, source_target_pairs={{0,1},{1,0},{2,3},{3,2},{4,5},{5,4},{6,7},{7,6},{8,9},{9,8},{10,11... | collective-permute-start | bytes 589832 | tf_op jit(solution)/shard_map/ppermute | solution.py:211
  45.2 4.6 %collective-permute-start.23 = (bf16[128,256]{1,0:T(8,128)(2,1)S(1)}, bf16[128,256]{1,0:T(8,128)(2,1)S(1)}, u32[]{:S(2)}, u32[]{:S(2)}) collective-permute-start(bf16[128,256]{1,0:T(8,128)(2,1)S(1)} %add_convert_fusion.1), channel_id=1, source_target_pairs={{1,8},{3,10},{5,12},{7,14},{9,0},{11,2},{13,4},{15,6},{0,1},{2,3},... | collective-permute-start | bytes 196616 | tf_op jit(solution)/shard_map/ppermute | solution.py:207
  45.7 5.6 %collective-permute-start.22 = (bf16[128,256]{1,0:T(8,128)(2,1)S(1)}, bf16[128,256]{1,0:T(8,128)(2,1)S(1)}, u32[]{:S(2)}, u32[]{:S(2)}) collective-permute-start(bf16[128,256]{1,0:T(8,128)(2,1)S(1)} %add_convert_fusion.1), channel_id=1, source_target_pairs={{1,12},{3,14},{5,8},{7,10},{9,4},{11,6},{13,0},{15,2},{0,1},{2,3},... | collective-permute-start | bytes 196616 | tf_op jit(solution)/shard_map/ppermute | solution.py:207
  51.6 2.4 %collective-permute-start.28 = (bf16[128,768]{1,0:T(8,128)(2,1)S(1)}, bf16[128,768]{1,0:T(8,128)(2,1)S(1)}, u32[]{:S(2)}, u32[]{:S(2)}) collective-permute-start(bf16[128,768]{1,0:T(8,128)(2,1)S(1)} %get-tuple-element.28.r_1_), channel_id=1, source_target_pairs={{0,1},{1,0},{2,3},{3,2},{4,5},{5,4},{6,7},{7,6},{8,9},{9,8},{10,11... | collective-permute-start | bytes 589832 | tf_op jit(solution)/shard_map/ppermute | solution.py:211
  51.7 4.1 %collective-permute-start.32 = (bf16[128,256]{1,0:T(8,128)(2,1)S(1)}, bf16[128,256]{1,0:T(8,128)(2,1)S(1)}, u32[]{:S(2)}, u32[]{:S(2)}) collective-permute-start(bf16[128,256]{1,0:T(8,128)(2,1)S(1)} %get-tuple-element.31), channel_id=1, source_target_pairs={{0,3},{2,1},{4,7},{6,5},{8,11},{10,9},{12,15},{14,13},{1,0},{3,2},... | collective-permute-start | bytes 196616 | tf_op jit(solution)/shard_map/ppermute | solution.py:207
  53.9 2.5 %collective-permute-start.29 = (bf16[128,256]{1,0:T(8,128)(2,1)S(1)}, bf16[128,256]{1,0:T(8,128)(2,1)S(1)}, u32[]{:S(2)}, u32[]{:S(2)}) collective-permute-start(bf16[128,256]{1,0:T(8,128)(2,1)S(1)} %get-tuple-element.32), channel_id=1, source_target_pairs={{0,3},{2,1},{4,7},{6,5},{8,11},{10,9},{12,15},{14,13},{1,0},{3,2},... | collective-permute-start | bytes 196616 | tf_op jit(solution)/shard_map/ppermute | solution.py:207
  55.8 4.1 %collective-permute-start.33 = (bf16[128,256]{1,0:T(8,128)(2,1)S(1)}, bf16[128,256]{1,0:T(8,128)(2,1)S(1)}, u32[]{:S(2)}, u32[]{:S(2)}) collective-permute-start(bf16[128,256]{1,0:T(8,128)(2,1)S(1)} %shard_map.110), channel_id=1, source_target_pairs={{1,4},{3,6},{5,0},{7,2},{9,12},{11,14},{13,8},{15,10},{0,1},{2,3},... | collective-permute-start | bytes 196616 | tf_op jit(solution)/shard_map/ppermute | solution.py:207
  56.4 4.6 %collective-permute-start.31 = (bf16[128,256]{1,0:T(8,128)(2,1)S(1)}, bf16[128,256]{1,0:T(8,128)(2,1)S(1)}, u32[]{:S(2)}, u32[]{:S(2)}) collective-permute-start(bf16[128,256]{1,0:T(8,128)(2,1)S(1)} %add_convert_fusion), channel_id=1, source_target_pairs={{1,8},{3,10},{5,12},{7,14},{9,0},{11,2},{13,4},{15,6},{0,1},{2,3},... | collective-permute-start | bytes 196616 | tf_op jit(solution)/shard_map/ppermute | solution.py:207
  57.2 5.5 %collective-permute-start.30 = (bf16[128,256]{1,0:T(8,128)(2,1)S(1)}, bf16[128,256]{1,0:T(8,128)(2,1)S(1)}, u32[]{:S(2)}, u32[]{:S(2)}) collective-permute-start(bf16[128,256]{1,0:T(8,128)(2,1)S(1)} %add_convert_fusion), channel_id=1, source_target_pairs={{1,12},{3,14},{5,8},{7,10},{9,4},{11,6},{13,0},{15,2},{0,1},{2,3},... | collective-permute-start | bytes 196616 | tf_op jit(solution)/shard_map/ppermute | solution.py:207
  58.9 4.0 %collective-permute-start.35 = (bf16[128,256]{1,0:T(8,128)(2,1)S(1)}, bf16[128,256]{1,0:T(8,128)(2,1)S(1)}, u32[]{:S(2)}, u32[]{:S(2)}) collective-permute-start(bf16[128,256]{1,0:T(8,128)(2,1)S(1)} %get-tuple-element.29), channel_id=1, source_target_pairs={{1,2},{3,0},{5,6},{7,4},{9,10},{11,8},{13,14},{15,12},{0,1},{2,3},... | collective-permute-start | bytes 196616 | tf_op jit(solution)/shard_map/ppermute | solution.py:207
  62.8 1.8 %collective-permute-start.34 = (bf16[128,512]{1,0:T(8,128)(2,1)S(1)}, bf16[128,512]{1,0:T(8,128)(2,1)S(1)}, u32[]{:S(2)}, u32[]{:S(2)}) collective-permute-start(bf16[128,512]{1,0:T(8,128)(2,1)S(1)} %shard_map.111.r_1_), channel_id=1, source_target_pairs={{0,1},{1,0},{2,3},{3,2},{4,5},{5,4},{6,7},{7,6},{8,9},{9,8},{10,11... | collective-permute-start | bytes 393224 | tf_op jit(solution)/shard_map/ppermute | solution.py:211
  62.9 1.4 %collective-permute-start.36 = (bf16[128,256]{1,0:T(8,128)(2,1)S(1)}, bf16[128,256]{1,0:T(8,128)(2,1)S(1)}, u32[]{:S(2)}, u32[]{:S(2)}) collective-permute-start(bf16[128,256]{1,0:T(8,128)(2,1)S(1)} %collective-permute-done.35.r_1_), channel_id=1, source_target_pairs={{0,1},{1,0},{2,3},{3,2},{4,5},{5,4},{6,7},{7,6},{8,9},{9,8},{10,11... | collective-permute-start | bytes 196616 | tf_op jit(solution)/shard_map/ppermute | solution.py:211

commit v10 on v9

--- a/solution.py
+++ b/solution.py
@@ -238,9 +238,7 @@
     c = packed.shape[0] // LEVELS
     if received is None:
         received = one_way(packed[:c], stride, source)
-        below = one_way(packed[c : 2 * c], stride, source)
-    else:
-        received, below = received[:c], received[c:]
+    below = one_way(packed[c : 2 * c], stride, source)
     three = one_way(summed[2 * c :], stride, 1 - source)
     both = add(summed[:c], received)
     one = one_way(both, 6 * stride, 1 - source)
@@ -289,9 +287,9 @@
     (summed,) = call(join_kernel, [p_shape], (place, own, other), 0)
     packed, received = summed, None
     if lax.axis_size(("rows", "cols")) == 2**LEVELS:
-        left = one_way(own[: 2 * c], 1, 0)
-        right = one_way(other[: 2 * c], 1, 0)
-        (received,) = call(beside_kernel, [S((2 * c, 2 * k), BF)], (place, left, right), 0)
+        left = one_way(own[:c], 1, 0)
+        right = one_way(other[:c], 1, 0)
+        (received,) = call(beside_kernel, [S((c, 2 * k), BF)], (place, left, right), 0)
     lower, lower_gram = prepared(lowers)
     upper, upper_gram = prepared(uppers)
     field_flops = 4 * half * wide * c

time: 66 us -> 66.2 us (level)
    ppermute x24 -> x25, waiting for transfers between devices: 16.9 us -> 17.7 us  [one_way(): return lax.ppermute(value, ('rows', 'cols', 'rank'), away + home)]
    ppermute x24 -> x25, starting transfers between devices: 25.3 us -> 25.7 us  [one_way(): return lax.ppermute(value, ('rows', 'cols', 'rank'), away + home)]
  transfers between devices with their start and end apart: 37 -> 38, of which waited for: 15 -> 15; matrix products, arithmetic and copies ran while one was open for 0% -> 0% of each run, Pallas kernels for 17% -> 17%
where the time goes in v10:
time: 66.2 us; the launch traced here: 65.9 us
  starting transfers between devices  29 us (44%)
  waiting for transfers between devices  20.2 us (31%)
  Pallas kernels  12.8 us (19%)
  local copies, waits for them, and re-layouts  3.36 us (5%)
    ppermute x25, starting transfers between devices, one_way(): return lax.ppermute(value, ('rows', 'cols', 'rank'), away + home)  25.7 us
    ppermute x25, waiting for transfers between devices, one_way(): return lax.ppermute(value, ('rows', 'cols', 'rank'), away + home)  17.7 us
    pallas_call x34, Pallas kernels, call(): pl.pallas_call(kernel, out_shape=outs, in_specs=[pl.BlockSpec(memory_spac...  12.8 us
    ppermute x13, starting transfers between devices, over_rank(): return lax.ppermute(value, 'rank', [(0, 1), (1, 0)])  3.32 us
    unnamed x22, local copies, waits for them, and re-layouts  3.28 us
    ppermute x13, waiting for transfers between devices, over_rank(): return lax.ppermute(value, 'rank', [(0, 1), (1, 0)])  2.49 us
  transfers between devices with their start and end apart: 38, of which 15 were waited for; matrix products, arithmetic and copies ran while one was open for 0% of the time, Pallas kernels for 17%

profile of v10, /device:TPU:0, one launch (start us, length us, event | category | flops | bytes accessed | tf_op | source)
XLA Modules:
  0.0 65.9 jit_solution(11317306464152064819)
XLA Ops:
  0.0 1.2 %copy-done.8 = bf16[2048,128]{1,0:T(8,128)(2,1)S(1)} copy-done((bf16[2048,128]{1,0:T(8,128)(2,1)S(1)}, bf16[2048,128]{1,0:T(8,128)(2,1)}, u32[]{:S(2)}) %copy-start.8) | copy-done | bytes 524312
  1.2 1.0 %copy-done.9 = bf16[2048,128]{1,0:T(8,128)(2,1)S(1)} copy-done((bf16[2048,128]{1,0:T(8,128)(2,1)S(1)}, bf16[2048,128]{1,0:T(8,128)(2,1)}, u32[]{:S(2)}) %copy-start.9) | copy-done | bytes 524312
  2.2 1.0 %copy-done.10 = bf16[2048,128]{1,0:T(8,128)(2,1)S(1)} copy-done((bf16[2048,128]{1,0:T(8,128)(2,1)S(1)}, bf16[2048,128]{1,0:T(8,128)(2,1)}, u32[]{:S(2)}) %copy-start.10) | copy-done | bytes 524312
  3.3 0.6 collective-permute-start.8
  4.0 1.7 %collective-permute-done.8.other = bf16[3072,128]{1,0:T(8,128)(2,1)S(1)} collective-permute-done((bf16[3072,128]{1,0:T(8,128)(2,1)S(1)}, bf16[3072,128]{1,0:T(8,128)(2,1)S(1)}, u32[]{:S(2)}, u32[]{:S(2)}) %collective-permute-start.8) | collective-permute-done | bytes 786464 | tf_op jit(solution)/shard_map/ppermute | solution.py:211
  5.8 1.3 %shard_map.87 = (bf16[1024,768]{1,0:T(8,128)(2,1)S(1)}, bf16[1536,256]{1,0:T(8,128)(2,1)S(1)}) custom-call(s32[1]{0:T(128)} %bitcast.place.r_0_, bf16[3072,128]{1,0:T(8,128)(2,1)S(1)} %collective-permute-done.8.other, bf16[2048,128]{1,0:T(8,128)(2,1)S(1)} %copy-done.8, bf16[2048,128]{1,0:T(8,128)(2,1)S(1)} %copy-done.9, bf16[2048,128]{1,0:T(8,128)(2,1)S(1)} %copy-done.10), custom_call_target="tpu_custom_call" | custom-call | flops 905969664 | bytes 4718592 | tf_op jit(solution)/shard_map/pallas_call | solution.py:26
  7.2 0.4 collective-permute-start.9
  7.6 2.1 %shard_map.82.own = bf16[384,128]{1,0:T(8,128)(2,1)S(1)} custom-call(s32[1]{0:T(128)} %bitcast.place.r_0_, bf16[2048,128]{1,0:T(8,128)(2,1)} %z.1, bf16[2048,128]{1,0:T(8,128)(2,1)} %refs_0_.9, bf16[2048,128]{1,0:T(8,128)(2,1)} %refs_1_.9, bf16[2048,128]{1,0:T(8,128)(2,1)} %refs_2_.9), custom_call_target="tpu_custom_call" | custom-call | flops 201326592 | bytes 2195456 | tf_op jit(solution)/shard_map/pallas_call | solution.py:26
  10.0 2.6 %collective-permute-start.1 = (bf16[128,128]{1,0:T(8,128)(2,1)S(1)}, bf16[128,128]{1,0:T(8,128)(2,1)S(1)}, u32[]{:S(2)}, u32[]{:S(2)}) collective-permute-start(bf16[128,128]{1,0:T(8,128)(2,1)S(1)} %slice.82), channel_id=1, source_target_pairs={{0,3},{2,1},{4,7},{6,5},{8,11},{10,9},{12,15},{14,13},{1,0},{3,2},... | collective-permute-start | bytes 98312 | tf_op jit(solution)/shard_map/ppermute | solution.py:207
  12.6 1.1 %collective-permute-start.2 = (bf16[128,128]{1,0:T(8,128)(2,1)S(1)}, bf16[128,128]{1,0:T(8,128)(2,1)S(1)}, u32[]{:S(2)}, u32[]{:S(2)}) collective-permute-start(bf16[128,128]{1,0:T(8,128)(2,1)S(1)} %slice.83), channel_id=1, source_target_pairs={{0,3},{2,1},{4,7},{6,5},{8,11},{10,9},{12,15},{14,13},{1,0},{3,2},... | collective-permute-start | bytes 98312 | tf_op jit(solution)/shard_map/ppermute | solution.py:207
  13.8 0.4 collective-permute-done.1.left
  14.2 1.7 %collective-permute-start.5 = (bf16[128,256]{1,0:T(8,128)(2,1)S(1)}, bf16[128,256]{1,0:T(8,128)(2,1)S(1)}, u32[]{:S(2)}, u32[]{:S(2)}) collective-permute-start(bf16[128,256]{1,0:T(8,128)(2,1)S(1)} %get-tuple-element.42.one), channel_id=1, source_target_pairs={{0,3},{2,1},{4,7},{6,5},{8,11},{10,9},{12,15},{14,13},{1,0},{3,2},... | collective-permute-start | bytes 196616 | tf_op jit(solution)/shard_map/ppermute | solution.py:207
  16.0 0.7 %shard_map.89 = (f32[1024,128]{1,0:T(8,128)S(1)}, bf16[128,768]{1,0:T(8,128)(2,1)S(1)}) custom-call(s32[1]{0:T(128)} %bitcast.place.r_0_, bf16[2048,128]{1,0:T(8,128)(2,1)S(1)} %copy-done.7, bf16[4,256,256]{2,1,0:T(8,128)(2,1)S(1)} %copy-done, bf16[1024,768]{1,0:T(8,128)(2,1)S(1)} %get-tuple-element.18.after.r_2_), custom_call_target="tpu_custom_call" | custom-call | flops 201326592 | bytes 3342336 | tf_op jit(solution)/shard_map/pallas_call | solution.py:26
  16.9 1.0 %collective-permute-done.5.two = bf16[128,256]{1,0:T(8,128)(2,1)S(1)} collective-permute-done((bf16[128,256]{1,0:T(8,128)(2,1)S(1)}, bf16[128,256]{1,0:T(8,128)(2,1)S(1)}, u32[]{:S(2)}, u32[]{:S(2)}) %collective-permute-start.5) | collective-permute-done | bytes 65568 | tf_op jit(solution)/shard_map/ppermute | solution.py:207
  18.2 2.4 %collective-permute-start.3 = (bf16[128,256]{1,0:T(8,128)(2,1)S(1)}, bf16[128,256]{1,0:T(8,128)(2,1)S(1)}, u32[]{:S(2)}, u32[]{:S(2)}) collective-permute-start(bf16[128,256]{1,0:T(8,128)(2,1)S(1)} %add_convert_fusion.3), channel_id=1, source_target_pairs={{1,12},{3,14},{5,8},{7,10},{9,4},{11,6},{13,0},{15,2},{0,1},{2,3},... | collective-permute-start | bytes 196616 | tf_op jit(solution)/shard_map/ppermute | solution.py:207
  20.7 1.7 %collective-permute-start.6 = (bf16[128,256]{1,0:T(8,128)(2,1)S(1)}, bf16[128,256]{1,0:T(8,128)(2,1)S(1)}, u32[]{:S(2)}, u32[]{:S(2)}) collective-permute-start(bf16[128,256]{1,0:T(8,128)(2,1)S(1)} %shard_map.85), channel_id=1, source_target_pairs={{1,4},{3,6},{5,0},{7,2},{9,12},{11,14},{13,8},{15,10},{0,1},{2,3},... | collective-permute-start | bytes 196616 | tf_op jit(solution)/shard_map/ppermute | solution.py:207
  22.4 1.3 %shard_map.95 = (bf16[1024,768]{1,0:T(8,128)(2,1)S(1)}, bf16[1536,256]{1,0:T(8,128)(2,1)S(1)}) custom-call(s32[1]{0:T(128)} %bitcast.place.r_0_, bf16[3072,128]{1,0:T(8,128)(2,1)S(1)} %collective-permute-done.18.other, bf16[2048,128]{1,0:T(8,128)(2,1)S(1)} %copy-done.2, bf16[2048,128]{1,0:T(8,128)(2,1)S(1)} %copy-done.4, bf16[2048,128]{1,0:T(8,128)(2,1)S(1)} %copy-done.6), custom_call_target="tpu_custom_call" | custom-call | flops 905969664 | bytes 4718592 | tf_op jit(solution)/shard_map/pallas_call | solution.py:26
  24.6 0.4 collective-permute-done.6.two
  25.4 1.2 %collective-permute-start.15 = (bf16[128,256]{1,0:T(8,128)(2,1)S(1)}, bf16[128,256]{1,0:T(8,128)(2,1)S(1)}, u32[]{:S(2)}, u32[]{:S(2)}) collective-permute-start(bf16[128,256]{1,0:T(8,128)(2,1)S(1)} %get-tuple-element.39), channel_id=1, source_target_pairs={{0,3},{2,1},{4,7},{6,5},{8,11},{10,9},{12,15},{14,13},{1,0},{3,2},... | collective-permute-start | bytes 196616 | tf_op jit(solution)/shard_map/ppermute | solution.py:207
  26.9 1.7 %collective-permute-done.15.two = bf16[128,256]{1,0:T(8,128)(2,1)S(1)} collective-permute-done((bf16[128,256]{1,0:T(8,128)(2,1)S(1)}, bf16[128,256]{1,0:T(8,128)(2,1)S(1)}, u32[]{:S(2)}, u32[]{:S(2)}) %collective-permute-start.15) | collective-permute-done | bytes 65568 | tf_op jit(solution)/shard_map/ppermute | solution.py:207
  28.6 1.2 %collective-permute-start.16 = (bf16[128,256]{1,0:T(8,128)(2,1)S(1)}, bf16[128,256]{1,0:T(8,128)(2,1)S(1)}, u32[]{:S(2)}, u32[]{:S(2)}) collective-permute-start(bf16[128,256]{1,0:T(8,128)(2,1)S(1)} %shard_map.93), channel_id=1, source_target_pairs={{1,4},{3,6},{5,0},{7,2},{9,12},{11,14},{13,8},{15,10},{0,1},{2,3},... | collective-permute-start | bytes 196616 | tf_op jit(solution)/shard_map/ppermute | solution.py:207
  29.8 1.0 %collective-permute-start.17 = (bf16[128,256]{1,0:T(8,128)(2,1)S(1)}, bf16[128,256]{1,0:T(8,128)(2,1)S(1)}, u32[]{:S(2)}, u32[]{:S(2)}) collective-permute-start(bf16[128,256]{1,0:T(8,128)(2,1)S(1)} %get-tuple-element.37), channel_id=1, source_target_pairs={{1,2},{3,0},{5,6},{7,4},{9,10},{11,8},{13,14},{15,12},{0,1},{2,3},... | collective-permute-start | bytes 196616 | tf_op jit(solution)/shard_map/ppermute | solution.py:207
  30.8 0.9 %shard_map.98.y.r_3_ = f32[1024,128]{1,0:T(8,128)S(1)} custom-call(s32[1]{0:T(128)} %bitcast.place.r_0_, bf16[128,768]{1,0:T(8,128)(2,1)S(1)} %shard_map.97.r_1_, bf16[1024,768]{1,0:T(8,128)(2,1)S(1)} %get-tuple-element.18.after.r_2_, f32[1024,128]{1,0:T(8,128)S(1)} %get-tuple-element.23.r_3_, bf16[4,256,256]{2,1,0:T(8,128)(2,1)S(1)} %copy-done), custom_call_target="tpu_custom_call" | custom-call | flops 201326592 | bytes 3342336 | tf_op jit(solution)/shard_map/pallas_call | solution.py:26
  31.7 0.4 shard_map.99.here.r_4_
  32.4 0.4 collective-permute-start.14
  32.8 1.3 %collective-permute-start.13 = (bf16[128,256]{1,0:T(8,128)(2,1)S(1)}, bf16[128,256]{1,0:T(8,128)(2,1)S(1)}, u32[]{:S(2)}, u32[]{:S(2)}) collective-permute-start(bf16[128,256]{1,0:T(8,128)(2,1)S(1)} %add_convert_fusion.2), channel_id=1, source_target_pairs={{1,12},{3,14},{5,8},{7,10},{9,4},{11,6},{13,0},{15,2},{0,1},{2,3},... | collective-permute-start | bytes 196616 | tf_op jit(solution)/shard_map/ppermute | solution.py:207
  34.6 2.4 %collective-permute-done.14.more = bf16[128,256]{1,0:T(8,128)(2,1)S(1)} collective-permute-done((bf16[128,256]{1,0:T(8,128)(2,1)S(1)}, bf16[128,256]{1,0:T(8,128)(2,1)S(1)}, u32[]{:S(2)}, u32[]{:S(2)}) %collective-permute-start.14) | collective-permute-done | bytes 65568 | tf_op jit(solution)/shard_map/ppermute | solution.py:207
  37.0 2.1 %collective-permute-done.13.one = bf16[128,256]{1,0:T(8,128)(2,1)S(1)} collective-permute-done((bf16[128,256]{1,0:T(8,128)(2,1)S(1)}, bf16[128,256]{1,0:T(8,128)(2,1)S(1)}, u32[]{:S(2)}, u32[]{:S(2)}) %collective-permute-start.13) | collective-permute-done | bytes 65568 | tf_op jit(solution)/shard_map/ppermute | solution.py:207
  39.5 0.8 %collective-permute-start.25 = (bf16[128,256]{1,0:T(8,128)(2,1)S(1)}, bf16[128,256]{1,0:T(8,128)(2,1)S(1)}, u32[]{:S(2)}, u32[]{:S(2)}) collective-permute-start(bf16[128,256]{1,0:T(8,128)(2,1)S(1)} %get-tuple-element.35), channel_id=1, source_target_pairs={{0,3},{2,1},{4,7},{6,5},{8,11},{10,9},{12,15},{14,13},{1,0},{3,2},... | collective-permute-start | bytes 196616 | tf_op jit(solution)/shard_map/ppermute | solution.py:207
  40.4 0.6 collective-permute-done.21.r_2_
  41.0 1.2 %collective-permute-done.25.two = bf16[128,256]{1,0:T(8,128)(2,1)S(1)} collective-permute-done((bf16[128,256]{1,0:T(8,128)(2,1)S(1)}, bf16[128,256]{1,0:T(8,128)(2,1)S(1)}, u32[]{:S(2)}, u32[]{:S(2)}) %collective-permute-start.25) | collective-permute-done | bytes 65568 | tf_op jit(solution)/shard_map/ppermute | solution.py:207
  42.2 1.6 %collective-permute-start.26 = (bf16[128,256]{1,0:T(8,128)(2,1)S(1)}, bf16[128,256]{1,0:T(8,128)(2,1)S(1)}, u32[]{:S(2)}, u32[]{:S(2)}) collective-permute-start(bf16[128,256]{1,0:T(8,128)(2,1)S(1)} %shard_map.103), channel_id=1, source_target_pairs={{1,4},{3,6},{5,0},{7,2},{9,12},{11,14},{13,8},{15,10},{0,1},{2,3},... | collective-permute-start | bytes 196616 | tf_op jit(solution)/shard_map/ppermute | solution.py:207
  43.9 0.9 %shard_map.105.y.r_3_ = f32[1024,128]{1,0:T(8,128)S(1)} custom-call(s32[1]{0:T(128)} %bitcast.place.r_0_, bf16[128,768]{1,0:T(8,128)(2,1)S(1)} %shard_map.104.r_1_, bf16[1024,768]{1,0:T(8,128)(2,1)S(1)} %get-tuple-element.24.after.r_2_.r_3_, f32[1024,128]{1,0:T(8,128)S(1)} %shard_map.98.y.r_3_, bf16[4,256,256]{2,1,0:T(8,128)(2,1)S(1)} %copy-done), custom_call_target="tpu_custom_call" | custom-call | flops 201326592 | bytes 3342336 | tf_op jit(solution)/shard_map/pallas_call | solution.py:26
  44.8 0.4 shard_map.106.here.r_4_
  45.2 0.7 %collective-permute-start.28 = (bf16[128,768]{1,0:T(8,128)(2,1)S(1)}, bf16[128,768]{1,0:T(8,128)(2,1)S(1)}, u32[]{:S(2)}, u32[]{:S(2)}) collective-permute-start(bf16[128,768]{1,0:T(8,128)(2,1)S(1)} %shard_map.106.here.r_4_), channel_id=1, source_target_pairs={{0,1},{1,0},{2,3},{3,2},{4,5},{5,4},{6,7},{7,6},{8,9},{9,8},{10,11... | collective-permute-start | bytes 589832 | tf_op jit(solution)/shard_map/ppermute | solution.py:211
  46.1 2.3 %collective-permute-start.23 = (bf16[128,256]{1,0:T(8,128)(2,1)S(1)}, bf16[128,256]{1,0:T(8,128)(2,1)S(1)}, u32[]{:S(2)}, u32[]{:S(2)}) collective-permute-start(bf16[128,256]{1,0:T(8,128)(2,1)S(1)} %add_convert_fusion.1), channel_id=1, source_target_pairs={{1,12},{3,14},{5,8},{7,10},{9,4},{11,6},{13,0},{15,2},{0,1},{2,3},... | collective-permute-start | bytes 196616 | tf_op jit(solution)/shard_map/ppermute | solution.py:207
  48.6 3.5 %collective-permute-done.24.more = bf16[128,256]{1,0:T(8,128)(2,1)S(1)} collective-permute-done((bf16[128,256]{1,0:T(8,128)(2,1)S(1)}, bf16[128,256]{1,0:T(8,128)(2,1)S(1)}, u32[]{:S(2)}, u32[]{:S(2)}) %collective-permute-start.24) | collective-permute-done | bytes 65568 | tf_op jit(solution)/shard_map/ppermute | solution.py:207
  52.4 1.2 %collective-permute-start.33 = (bf16[128,256]{1,0:T(8,128)(2,1)S(1)}, bf16[128,256]{1,0:T(8,128)(2,1)S(1)}, u32[]{:S(2)}, u32[]{:S(2)}) collective-permute-start(bf16[128,256]{1,0:T(8,128)(2,1)S(1)} %get-tuple-element.31), channel_id=1, source_target_pairs={{0,3},{2,1},{4,7},{6,5},{8,11},{10,9},{12,15},{14,13},{1,0},{3,2},... | collective-permute-start | bytes 196616 | tf_op jit(solution)/shard_map/ppermute | solution.py:207
  53.9 1.6 %collective-permute-done.33.two = bf16[128,256]{1,0:T(8,128)(2,1)S(1)} collective-permute-done((bf16[128,256]{1,0:T(8,128)(2,1)S(1)}, bf16[128,256]{1,0:T(8,128)(2,1)S(1)}, u32[]{:S(2)}, u32[]{:S(2)}) %collective-permute-start.33) | collective-permute-done | bytes 65568 | tf_op jit(solution)/shard_map/ppermute | solution.py:207
  55.5 1.2 %collective-permute-start.34 = (bf16[128,256]{1,0:T(8,128)(2,1)S(1)}, bf16[128,256]{1,0:T(8,128)(2,1)S(1)}, u32[]{:S(2)}, u32[]{:S(2)}) collective-permute-start(bf16[128,256]{1,0:T(8,128)(2,1)S(1)} %shard_map.110), channel_id=1, source_target_pairs={{1,4},{3,6},{5,0},{7,2},{9,12},{11,14},{13,8},{15,10},{0,1},{2,3},... | collective-permute-start | bytes 196616 | tf_op jit(solution)/shard_map/ppermute | solution.py:207
  56.8 0.7 %collective-permute-start.32 = (bf16[128,256]{1,0:T(8,128)(2,1)S(1)}, bf16[128,256]{1,0:T(8,128)(2,1)S(1)}, u32[]{:S(2)}, u32[]{:S(2)}) collective-permute-start(bf16[128,256]{1,0:T(8,128)(2,1)S(1)} %add_convert_fusion), channel_id=1, source_target_pairs={{1,8},{3,10},{5,12},{7,14},{9,0},{11,2},{13,4},{15,6},{0,1},{2,3},... | collective-permute-start | bytes 196616 | tf_op jit(solution)/shard_map/ppermute | solution.py:207
  57.4 1.7 %collective-permute-start.31 = (bf16[128,256]{1,0:T(8,128)(2,1)S(1)}, bf16[128,256]{1,0:T(8,128)(2,1)S(1)}, u32[]{:S(2)}, u32[]{:S(2)}) collective-permute-start(bf16[128,256]{1,0:T(8,128)(2,1)S(1)} %add_convert_fusion), channel_id=1, source_target_pairs={{1,12},{3,14},{5,8},{7,10},{9,4},{11,6},{13,0},{15,2},{0,1},{2,3},... | collective-permute-start | bytes 196616 | tf_op jit(solution)/shard_map/ppermute | solution.py:207
  59.1 0.9 %collective-permute-start.36 = (bf16[128,256]{1,0:T(8,128)(2,1)S(1)}, bf16[128,256]{1,0:T(8,128)(2,1)S(1)}, u32[]{:S(2)}, u32[]{:S(2)}) collective-permute-start(bf16[128,256]{1,0:T(8,128)(2,1)S(1)} %get-tuple-element.29), channel_id=1, source_target_pairs={{1,2},{3,0},{5,6},{7,4},{9,10},{11,8},{13,14},{15,12},{0,1},{2,3},... | collective-permute-start | bytes 196616 | tf_op jit(solution)/shard_map/ppermute | solution.py:207
  60.0 1.4 %collective-permute-done.32.more = bf16[128,256]{1,0:T(8,128)(2,1)S(1)} collective-permute-done((bf16[128,256]{1,0:T(8,128)(2,1)S(1)}, bf16[128,256]{1,0:T(8,128)(2,1)S(1)}, u32[]{:S(2)}, u32[]{:S(2)}) %collective-permute-start.32) | collective-permute-done | bytes 65568 | tf_op jit(solution)/shard_map/ppermute | solution.py:207
  61.4 1.5 %collective-permute-done.31.one = bf16[128,256]{1,0:T(8,128)(2,1)S(1)} collective-permute-done((bf16[128,256]{1,0:T(8,128)(2,1)S(1)}, bf16[128,256]{1,0:T(8,128)(2,1)S(1)}, u32[]{:S(2)}, u32[]{:S(2)}) %collective-permute-start.31) | collective-permute-done | bytes 65568 | tf_op jit(solution)/shard_map/ppermute | solution.py:207
  63.0 0.5 collective-permute-start.37
  63.6 0.9 %shard_map.113.r_4_ = f32[1024,128]{1,0:T(8,128)S(1)} custom-call(s32[1]{0:T(128)} %bitcast.place.r_0_, bf16[128,768]{1,0:T(8,128)(2,1)S(1)} %shard_map.112.r_1_, bf16[1024,768]{1,0:T(8,128)(2,1)S(1)} %get-tuple-element.18.after.r_2_, f32[1024,128]{1,0:T(8,128)S(1)} %shard_map.105.y.r_3_, bf16[4,256,256]{2,1,0:T(8,128)(2,1)S(1)} %copy-done), custom_call_target="tpu_custom_call" | custom-call | flops 201326592 | bytes 3342336 | tf_op jit(solution)/shard_map/pallas_call | solution.py:26
  64.8 1.2 %shard_map.115 = bf16[1024,128]{1,0:T(8,128)(2,1)} custom-call(s32[1]{0:T(128)} %bitcast.place.r_0_, bf16[128,512]{1,0:T(8,128)(2,1)S(1)} %shard_map.111.r_1_, bf16[128,512]{1,0:T(8,128)(2,1)S(1)} %collective-permute-done.35.r_2_, bf16[1024,768]{1,0:T(8,128)(2,1)S(1)} %get-tuple-element.24.after.r_2_.r_3_, f32[1024,128]{1,0:T(8,128)S(1)} %shard_map.114.r_4_), custom_call_target="tpu_custom_call" | custom-call | flops 134217728 | bytes 2621440 | tf_op jit(solution)/shard_map/pallas_call | solution.py:26
  (97 shorter events, 5.3 us)
Async XLA Ops:
  0.0 3.9 %copy-start.5 = (bf16[2048,128]{1,0:T(8,128)(2,1)S(1)}, bf16[2048,128]{1,0:T(8,128)(2,1)}, u32[]{:S(2)}) copy-start(bf16[2048,128]{1,0:T(8,128)(2,1)} %refs_2_.9) | copy-start | bytes 1572868
  0.0 3.9 %copy-start.3 = (bf16[2048,128]{1,0:T(8,128)(2,1)S(1)}, bf16[2048,128]{1,0:T(8,128)(2,1)}, u32[]{:S(2)}) copy-start(bf16[2048,128]{1,0:T(8,128)(2,1)} %refs_1_.9) | copy-start | bytes 1572868
  0.0 3.9 %copy-start.1 = (bf16[2048,128]{1,0:T(8,128)(2,1)S(1)}, bf16[2048,128]{1,0:T(8,128)(2,1)}, u32[]{:S(2)}) copy-start(bf16[2048,128]{1,0:T(8,128)(2,1)} %refs_0_.9) | copy-start | bytes 1572868
  0.0 1.2 %copy-start.8 = (bf16[2048,128]{1,0:T(8,128)(2,1)S(1)}, bf16[2048,128]{1,0:T(8,128)(2,1)}, u32[]{:S(2)}) copy-start(bf16[2048,128]{1,0:T(8,128)(2,1)} %refs_0_.7) | copy-start | bytes 1572868
  1.2 1.0 %copy-start.9 = (bf16[2048,128]{1,0:T(8,128)(2,1)S(1)}, bf16[2048,128]{1,0:T(8,128)(2,1)}, u32[]{:S(2)}) copy-start(bf16[2048,128]{1,0:T(8,128)(2,1)} %refs_1_.7) | copy-start | bytes 1572868
  3.3 2.5 %collective-permute-start.8 = (bf16[3072,128]{1,0:T(8,128)(2,1)S(1)}, bf16[3072,128]{1,0:T(8,128)(2,1)S(1)}, u32[]{:S(2)}, u32[]{:S(2)}) collective-permute-start(bf16[3072,128]{1,0:T(8,128)(2,1)S(1)} %shard_map.86), channel_id=1, source_target_pairs={{0,1},{1,0},{2,3},{3,2},{4,5},{5,4},{6,7},{7,6},{8,9},{9,8},{10,11... | collective-permute-start | bytes 2359304 | tf_op jit(solution)/shard_map/ppermute | solution.py:211
  3.9 16.7 %collective-permute-start.18 = (bf16[3072,128]{1,0:T(8,128)(2,1)S(1)}, bf16[3072,128]{1,0:T(8,128)(2,1)S(1)}, u32[]{:S(2)}, u32[]{:S(2)}) collective-permute-start(bf16[3072,128]{1,0:T(8,128)(2,1)S(1)} %shard_map.94), channel_id=1, source_target_pairs={{0,1},{1,0},{2,3},{3,2},{4,5},{5,4},{6,7},{7,6},{8,9},{9,8},{10,11... | collective-permute-start | bytes 2359304 | tf_op jit(solution)/shard_map/ppermute | solution.py:211
  7.1 8.9 %copy-start = (bf16[4,256,256]{2,1,0:T(8,128)(2,1)S(1)}, bf16[4,256,256]{2,1,0:T(8,128)(2,1)}, u32[]{:S(2)}) copy-start(bf16[4,256,256]{2,1,0:T(8,128)(2,1)} %r_4_.5) | copy-start | bytes 1572868
  7.1 8.9 %copy-start.7 = (bf16[2048,128]{1,0:T(8,128)(2,1)S(1)}, bf16[2048,128]{1,0:T(8,128)(2,1)}, u32[]{:S(2)}) copy-start(bf16[2048,128]{1,0:T(8,128)(2,1)} %z.1) | copy-start | bytes 1572868
  7.2 16.6 %collective-permute-start.9 = (bf16[1536,256]{1,0:T(8,128)(2,1)S(1)}, bf16[1536,256]{1,0:T(8,128)(2,1)S(1)}, u32[]{:S(2)}, u32[]{:S(2)}) collective-permute-start(bf16[1536,256]{1,0:T(8,128)(2,1)S(1)} %get-tuple-element.17.mine), channel_id=1, source_target_pairs={{0,1},{1,0},{2,3},{3,2},{4,5},{5,4},{6,7},{7,6},{8,9},{9,8},{10,11... | collective-permute-start | bytes 2359304 | tf_op jit(solution)/shard_map/ppermute | solution.py:211
  9.7 2.9 %collective-permute-start = (bf16[384,128]{1,0:T(8,128)(2,1)S(1)}, bf16[384,128]{1,0:T(8,128)(2,1)S(1)}, u32[]{:S(2)}, u32[]{:S(2)}) collective-permute-start(bf16[384,128]{1,0:T(8,128)(2,1)S(1)} %shard_map.82.own), channel_id=1, source_target_pairs={{0,1},{1,0},{2,3},{3,2},{4,5},{5,4},{6,7},{7,6},{8,9},{9,8},{10,11... | collective-permute-start | bytes 294920 | tf_op jit(solution)/shard_map/ppermute | solution.py:211
  10.0 4.2 %collective-permute-start.1 = (bf16[128,128]{1,0:T(8,128)(2,1)S(1)}, bf16[128,128]{1,0:T(8,128)(2,1)S(1)}, u32[]{:S(2)}, u32[]{:S(2)}) collective-permute-start(bf16[128,128]{1,0:T(8,128)(2,1)S(1)} %slice.82), channel_id=1, source_target_pairs={{0,3},{2,1},{4,7},{6,5},{8,11},{10,9},{12,15},{14,13},{1,0},{3,2},... | collective-permute-start | bytes 98312 | tf_op jit(solution)/shard_map/ppermute | solution.py:207
  12.6 3.3 %collective-permute-start.2 = (bf16[128,128]{1,0:T(8,128)(2,1)S(1)}, bf16[128,128]{1,0:T(8,128)(2,1)S(1)}, u32[]{:S(2)}, u32[]{:S(2)}) collective-permute-start(bf16[128,128]{1,0:T(8,128)(2,1)S(1)} %slice.83), channel_id=1, source_target_pairs={{0,3},{2,1},{4,7},{6,5},{8,11},{10,9},{12,15},{14,13},{1,0},{3,2},... | collective-permute-start | bytes 98312 | tf_op jit(solution)/shard_map/ppermute | solution.py:207
  13.8 4.5 %collective-permute-start.7 = (bf16[128,256]{1,0:T(8,128)(2,1)S(1)}, bf16[128,256]{1,0:T(8,128)(2,1)S(1)}, u32[]{:S(2)}, u32[]{:S(2)}) collective-permute-start(bf16[128,256]{1,0:T(8,128)(2,1)S(1)} %get-tuple-element.41), channel_id=1, source_target_pairs={{1,2},{3,0},{5,6},{7,4},{9,10},{11,8},{13,14},{15,12},{0,1},{2,3},... | collective-permute-start | bytes 196616 | tf_op jit(solution)/shard_map/ppermute | solution.py:207
  14.2 8.1 %copy-start.2 = (bf16[2048,128]{1,0:T(8,128)(2,1)S(1)}, bf16[2048,128]{1,0:T(8,128)(2,1)}, u32[]{:S(2)}) copy-start(bf16[2048,128]{1,0:T(8,128)(2,1)} %refs_0_.9) | copy-start | bytes 1572868
  14.2 8.1 %copy-start.4 = (bf16[2048,128]{1,0:T(8,128)(2,1)S(1)}, bf16[2048,128]{1,0:T(8,128)(2,1)}, u32[]{:S(2)}) copy-start(bf16[2048,128]{1,0:T(8,128)(2,1)} %refs_1_.9) | copy-start | bytes 1572868
  14.2 8.1 %copy-start.6 = (bf16[2048,128]{1,0:T(8,128)(2,1)S(1)}, bf16[2048,128]{1,0:T(8,128)(2,1)}, u32[]{:S(2)}) copy-start(bf16[2048,128]{1,0:T(8,128)(2,1)} %refs_2_.9) | copy-start | bytes 1572868
  14.2 3.6 %collective-permute-start.5 = (bf16[128,256]{1,0:T(8,128)(2,1)S(1)}, bf16[128,256]{1,0:T(8,128)(2,1)S(1)}, u32[]{:S(2)}, u32[]{:S(2)}) collective-permute-start(bf16[128,256]{1,0:T(8,128)(2,1)S(1)} %get-tuple-element.42.one), channel_id=1, source_target_pairs={{0,3},{2,1},{4,7},{6,5},{8,11},{10,9},{12,15},{14,13},{1,0},{3,2},... | collective-permute-start | bytes 196616 | tf_op jit(solution)/shard_map/ppermute | solution.py:207
  16.8 7.3 %collective-permute-start.10 = (bf16[128,768]{1,0:T(8,128)(2,1)S(1)}, bf16[128,768]{1,0:T(8,128)(2,1)S(1)}, u32[]{:S(2)}, u32[]{:S(2)}) collective-permute-start(bf16[128,768]{1,0:T(8,128)(2,1)S(1)} %get-tuple-element.19.here.r_4_), channel_id=1, source_target_pairs={{0,1},{1,0},{2,3},{3,2},{4,5},{5,4},{6,7},{7,6},{8,9},{9,8},{10,11... | collective-permute-start | bytes 589832 | tf_op jit(solution)/shard_map/ppermute | solution.py:211
  17.9 6.4 %collective-permute-start.4 = (bf16[128,256]{1,0:T(8,128)(2,1)S(1)}, bf16[128,256]{1,0:T(8,128)(2,1)S(1)}, u32[]{:S(2)}, u32[]{:S(2)}) collective-permute-start(bf16[128,256]{1,0:T(8,128)(2,1)S(1)} %add_convert_fusion.3), channel_id=1, source_target_pairs={{1,8},{3,10},{5,12},{7,14},{9,0},{11,2},{13,4},{15,6},{0,1},{2,3},... | collective-permute-start | bytes 196616 | tf_op jit(solution)/shard_map/ppermute | solution.py:207
  18.2 6.4 %collective-permute-start.3 = (bf16[128,256]{1,0:T(8,128)(2,1)S(1)}, bf16[128,256]{1,0:T(8,128)(2,1)S(1)}, u32[]{:S(2)}, u32[]{:S(2)}) collective-permute-start(bf16[128,256]{1,0:T(8,128)(2,1)S(1)} %add_convert_fusion.3), channel_id=1, source_target_pairs={{1,12},{3,14},{5,8},{7,10},{9,4},{11,6},{13,0},{15,2},{0,1},{2,3},... | collective-permute-start | bytes 196616 | tf_op jit(solution)/shard_map/ppermute | solution.py:207
  20.7 4.4 %collective-permute-start.6 = (bf16[128,256]{1,0:T(8,128)(2,1)S(1)}, bf16[128,256]{1,0:T(8,128)(2,1)S(1)}, u32[]{:S(2)}, u32[]{:S(2)}) collective-permute-start(bf16[128,256]{1,0:T(8,128)(2,1)S(1)} %shard_map.85), channel_id=1, source_target_pairs={{1,4},{3,6},{5,0},{7,2},{9,12},{11,14},{13,8},{15,10},{0,1},{2,3},... | collective-permute-start | bytes 196616 | tf_op jit(solution)/shard_map/ppermute | solution.py:207
  23.7 9.0 %collective-permute-start.19 = (bf16[1536,256]{1,0:T(8,128)(2,1)S(1)}, bf16[1536,256]{1,0:T(8,128)(2,1)S(1)}, u32[]{:S(2)}, u32[]{:S(2)}) collective-permute-start(bf16[1536,256]{1,0:T(8,128)(2,1)S(1)} %get-tuple-element.22.mine), channel_id=1, source_target_pairs={{0,1},{1,0},{2,3},{3,2},{4,5},{5,4},{6,7},{7,6},{8,9},{9,8},{10,11... | collective-permute-start | bytes 2359304 | tf_op jit(solution)/shard_map/ppermute | solution.py:211
  25.4 1.5 %collective-permute-start.11 = (bf16[128,768]{1,0:T(8,128)(2,1)S(1)}, bf16[128,768]{1,0:T(8,128)(2,1)S(1)}, u32[]{:S(2)}, u32[]{:S(2)}) collective-permute-start(bf16[128,768]{1,0:T(8,128)(2,1)S(1)} %get-tuple-element.21.r_1_), channel_id=1, source_target_pairs={{0,1},{1,0},{2,3},{3,2},{4,5},{5,4},{6,7},{7,6},{8,9},{9,8},{10,11... | collective-permute-start | bytes 589832 | tf_op jit(solution)/shard_map/ppermute | solution.py:211
  25.4 3.1 %collective-permute-start.15 = (bf16[128,256]{1,0:T(8,128)(2,1)S(1)}, bf16[128,256]{1,0:T(8,128)(2,1)S(1)}, u32[]{:S(2)}, u32[]{:S(2)}) collective-permute-start(bf16[128,256]{1,0:T(8,128)(2,1)S(1)} %get-tuple-element.39), channel_id=1, source_target_pairs={{0,3},{2,1},{4,7},{6,5},{8,11},{10,9},{12,15},{14,13},{1,0},{3,2},... | collective-permute-start | bytes 196616 | tf_op jit(solution)/shard_map/ppermute | solution.py:207
  26.7 5.7 %collective-permute-start.12 = (bf16[128,256]{1,0:T(8,128)(2,1)S(1)}, bf16[128,256]{1,0:T(8,128)(2,1)S(1)}, u32[]{:S(2)}, u32[]{:S(2)}) collective-permute-start(bf16[128,256]{1,0:T(8,128)(2,1)S(1)} %get-tuple-element.40), channel_id=1, source_target_pairs={{0,3},{2,1},{4,7},{6,5},{8,11},{10,9},{12,15},{14,13},{1,0},{3,2},... | collective-permute-start | bytes 196616 | tf_op jit(solution)/shard_map/ppermute | solution.py:207
  28.6 6.0 %collective-permute-start.16 = (bf16[128,256]{1,0:T(8,128)(2,1)S(1)}, bf16[128,256]{1,0:T(8,128)(2,1)S(1)}, u32[]{:S(2)}, u32[]{:S(2)}) collective-permute-start(bf16[128,256]{1,0:T(8,128)(2,1)S(1)} %shard_map.93), channel_id=1, source_target_pairs={{1,4},{3,6},{5,0},{7,2},{9,12},{11,14},{13,8},{15,10},{0,1},{2,3},... | collective-permute-start | bytes 196616 | tf_op jit(solution)/shard_map/ppermute | solution.py:207
  29.8 4.6 %collective-permute-start.17 = (bf16[128,256]{1,0:T(8,128)(2,1)S(1)}, bf16[128,256]{1,0:T(8,128)(2,1)S(1)}, u32[]{:S(2)}, u32[]{:S(2)}) collective-permute-start(bf16[128,256]{1,0:T(8,128)(2,1)S(1)} %get-tuple-element.37), channel_id=1, source_target_pairs={{1,2},{3,0},{5,6},{7,4},{9,10},{11,8},{13,14},{15,12},{0,1},{2,3},... | collective-permute-start | bytes 196616 | tf_op jit(solution)/shard_map/ppermute | solution.py:207
  32.1 2.2 %collective-permute-start.20 = (bf16[128,768]{1,0:T(8,128)(2,1)S(1)}, bf16[128,768]{1,0:T(8,128)(2,1)S(1)}, u32[]{:S(2)}, u32[]{:S(2)}) collective-permute-start(bf16[128,768]{1,0:T(8,128)(2,1)S(1)} %shard_map.99.here.r_4_), channel_id=1, source_target_pairs={{0,1},{1,0},{2,3},{3,2},{4,5},{5,4},{6,7},{7,6},{8,9},{9,8},{10,11... | collective-permute-start | bytes 589832 | tf_op jit(solution)/shard_map/ppermute | solution.py:211
  32.4 4.6 %collective-permute-start.14 = (bf16[128,256]{1,0:T(8,128)(2,1)S(1)}, bf16[128,256]{1,0:T(8,128)(2,1)S(1)}, u32[]{:S(2)}, u32[]{:S(2)}) collective-permute-start(bf16[128,256]{1,0:T(8,128)(2,1)S(1)} %add_convert_fusion.2), channel_id=1, source_target_pairs={{1,8},{3,10},{5,12},{7,14},{9,0},{11,2},{13,4},{15,6},{0,1},{2,3},... | collective-permute-start | bytes 196616 | tf_op jit(solution)/shard_map/ppermute | solution.py:207
  32.8 6.4 %collective-permute-start.13 = (bf16[128,256]{1,0:T(8,128)(2,1)S(1)}, bf16[128,256]{1,0:T(8,128)(2,1)S(1)}, u32[]{:S(2)}, u32[]{:S(2)}) collective-permute-start(bf16[128,256]{1,0:T(8,128)(2,1)S(1)} %add_convert_fusion.2), channel_id=1, source_target_pairs={{1,12},{3,14},{5,8},{7,10},{9,4},{11,6},{13,0},{15,2},{0,1},{2,3},... | collective-permute-start | bytes 196616 | tf_op jit(solution)/shard_map/ppermute | solution.py:207
  39.4 1.5 %collective-permute-start.21 = (bf16[128,768]{1,0:T(8,128)(2,1)S(1)}, bf16[128,768]{1,0:T(8,128)(2,1)S(1)}, u32[]{:S(2)}, u32[]{:S(2)}) collective-permute-start(bf16[128,768]{1,0:T(8,128)(2,1)S(1)} %get-tuple-element.26.r_1_), channel_id=1, source_target_pairs={{0,1},{1,0},{2,3},{3,2},{4,5},{5,4},{6,7},{7,6},{8,9},{9,8},{10,11... | collective-permute-start | bytes 589832 | tf_op jit(solution)/shard_map/ppermute | solution.py:211
  39.5 2.7 %collective-permute-start.25 = (bf16[128,256]{1,0:T(8,128)(2,1)S(1)}, bf16[128,256]{1,0:T(8,128)(2,1)S(1)}, u32[]{:S(2)}, u32[]{:S(2)}) collective-permute-start(bf16[128,256]{1,0:T(8,128)(2,1)S(1)} %get-tuple-element.35), channel_id=1, source_target_pairs={{0,3},{2,1},{4,7},{6,5},{8,11},{10,9},{12,15},{14,13},{1,0},{3,2},... | collective-permute-start | bytes 196616 | tf_op jit(solution)/shard_map/ppermute | solution.py:207
  40.3 5.7 %collective-permute-start.22 = (bf16[128,256]{1,0:T(8,128)(2,1)S(1)}, bf16[128,256]{1,0:T(8,128)(2,1)S(1)}, u32[]{:S(2)}, u32[]{:S(2)}) collective-permute-start(bf16[128,256]{1,0:T(8,128)(2,1)S(1)} %get-tuple-element.36), channel_id=1, source_target_pairs={{0,3},{2,1},{4,7},{6,5},{8,11},{10,9},{12,15},{14,13},{1,0},{3,2},... | collective-permute-start | bytes 196616 | tf_op jit(solution)/shard_map/ppermute | solution.py:207
  42.2 6.3 %collective-permute-start.26 = (bf16[128,256]{1,0:T(8,128)(2,1)S(1)}, bf16[128,256]{1,0:T(8,128)(2,1)S(1)}, u32[]{:S(2)}, u32[]{:S(2)}) collective-permute-start(bf16[128,256]{1,0:T(8,128)(2,1)S(1)} %shard_map.103), channel_id=1, source_target_pairs={{1,4},{3,6},{5,0},{7,2},{9,12},{11,14},{13,8},{15,10},{0,1},{2,3},... | collective-permute-start | bytes 196616 | tf_op jit(solution)/shard_map/ppermute | solution.py:207
  43.8 4.5 %collective-permute-start.27 = (bf16[128,256]{1,0:T(8,128)(2,1)S(1)}, bf16[128,256]{1,0:T(8,128)(2,1)S(1)}, u32[]{:S(2)}, u32[]{:S(2)}) collective-permute-start(bf16[128,256]{1,0:T(8,128)(2,1)S(1)} %get-tuple-element.33), channel_id=1, source_target_pairs={{1,2},{3,0},{5,6},{7,4},{9,10},{11,8},{13,14},{15,12},{0,1},{2,3},... | collective-permute-start | bytes 196616 | tf_op jit(solution)/shard_map/ppermute | solution.py:207
  45.2 3.1 %collective-permute-start.28 = (bf16[128,768]{1,0:T(8,128)(2,1)S(1)}, bf16[128,768]{1,0:T(8,128)(2,1)S(1)}, u32[]{:S(2)}, u32[]{:S(2)}) collective-permute-start(bf16[128,768]{1,0:T(8,128)(2,1)S(1)} %shard_map.106.here.r_4_), channel_id=1, source_target_pairs={{0,1},{1,0},{2,3},{3,2},{4,5},{5,4},{6,7},{7,6},{8,9},{9,8},{10,11... | collective-permute-start | bytes 589832 | tf_op jit(solution)/shard_map/ppermute | solution.py:211
  46.0 6.0 %collective-permute-start.24 = (bf16[128,256]{1,0:T(8,128)(2,1)S(1)}, bf16[128,256]{1,0:T(8,128)(2,1)S(1)}, u32[]{:S(2)}, u32[]{:S(2)}) collective-permute-start(bf16[128,256]{1,0:T(8,128)(2,1)S(1)} %add_convert_fusion.1), channel_id=1, source_target_pairs={{1,8},{3,10},{5,12},{7,14},{9,0},{11,2},{13,4},{15,6},{0,1},{2,3},... | collective-permute-start | bytes 196616 | tf_op jit(solution)/shard_map/ppermute | solution.py:207
  46.1 6.0 %collective-permute-start.23 = (bf16[128,256]{1,0:T(8,128)(2,1)S(1)}, bf16[128,256]{1,0:T(8,128)(2,1)S(1)}, u32[]{:S(2)}, u32[]{:S(2)}) collective-permute-start(bf16[128,256]{1,0:T(8,128)(2,1)S(1)} %add_convert_fusion.1), channel_id=1, source_target_pairs={{1,12},{3,14},{5,8},{7,10},{9,4},{11,6},{13,0},{15,2},{0,1},{2,3},... | collective-permute-start | bytes 196616 | tf_op jit(solution)/shard_map/ppermute | solution.py:207
  52.3 1.5 %collective-permute-start.29 = (bf16[128,768]{1,0:T(8,128)(2,1)S(1)}, bf16[128,768]{1,0:T(8,128)(2,1)S(1)}, u32[]{:S(2)}, u32[]{:S(2)}) collective-permute-start(bf16[128,768]{1,0:T(8,128)(2,1)S(1)} %get-tuple-element.28.r_1_), channel_id=1, source_target_pairs={{0,1},{1,0},{2,3},{3,2},{4,5},{5,4},{6,7},{7,6},{8,9},{9,8},{10,11... | collective-permute-start | bytes 589832 | tf_op jit(solution)/shard_map/ppermute | solution.py:211
  52.4 3.1 %collective-permute-start.33 = (bf16[128,256]{1,0:T(8,128)(2,1)S(1)}, bf16[128,256]{1,0:T(8,128)(2,1)S(1)}, u32[]{:S(2)}, u32[]{:S(2)}) collective-permute-start(bf16[128,256]{1,0:T(8,128)(2,1)S(1)} %get-tuple-element.31), channel_id=1, source_target_pairs={{0,3},{2,1},{4,7},{6,5},{8,11},{10,9},{12,15},{14,13},{1,0},{3,2},... | collective-permute-start | bytes 196616 | tf_op jit(solution)/shard_map/ppermute | solution.py:207
  53.6 3.1 %collective-permute-start.30 = (bf16[128,256]{1,0:T(8,128)(2,1)S(1)}, bf16[128,256]{1,0:T(8,128)(2,1)S(1)}, u32[]{:S(2)}, u32[]{:S(2)}) collective-permute-start(bf16[128,256]{1,0:T(8,128)(2,1)S(1)} %get-tuple-element.32), channel_id=1, source_target_pairs={{0,3},{2,1},{4,7},{6,5},{8,11},{10,9},{12,15},{14,13},{1,0},{3,2},... | collective-permute-start | bytes 196616 | tf_op jit(solution)/shard_map/ppermute | solution.py:207
  55.5 4.5 %collective-permute-start.34 = (bf16[128,256]{1,0:T(8,128)(2,1)S(1)}, bf16[128,256]{1,0:T(8,128)(2,1)S(1)}, u32[]{:S(2)}, u32[]{:S(2)}) collective-permute-start(bf16[128,256]{1,0:T(8,128)(2,1)S(1)} %shard_map.110), channel_id=1, source_target_pairs={{1,4},{3,6},{5,0},{7,2},{9,12},{11,14},{13,8},{15,10},{0,1},{2,3},... | collective-permute-start | bytes 196616 | tf_op jit(solution)/shard_map/ppermute | solution.py:207
  56.8 4.6 %collective-permute-start.32 = (bf16[128,256]{1,0:T(8,128)(2,1)S(1)}, bf16[128,256]{1,0:T(8,128)(2,1)S(1)}, u32[]{:S(2)}, u32[]{:S(2)}) collective-permute-start(bf16[128,256]{1,0:T(8,128)(2,1)S(1)} %add_convert_fusion), channel_id=1, source_target_pairs={{1,8},{3,10},{5,12},{7,14},{9,0},{11,2},{13,4},{15,6},{0,1},{2,3},... | collective-permute-start | bytes 196616 | tf_op jit(solution)/shard_map/ppermute | solution.py:207
  57.4 5.5 %collective-permute-start.31 = (bf16[128,256]{1,0:T(8,128)(2,1)S(1)}, bf16[128,256]{1,0:T(8,128)(2,1)S(1)}, u32[]{:S(2)}, u32[]{:S(2)}) collective-permute-start(bf16[128,256]{1,0:T(8,128)(2,1)S(1)} %add_convert_fusion), channel_id=1, source_target_pairs={{1,12},{3,14},{5,8},{7,10},{9,4},{11,6},{13,0},{15,2},{0,1},{2,3},... | collective-permute-start | bytes 196616 | tf_op jit(solution)/shard_map/ppermute | solution.py:207
  59.1 3.9 %collective-permute-start.36 = (bf16[128,256]{1,0:T(8,128)(2,1)S(1)}, bf16[128,256]{1,0:T(8,128)(2,1)S(1)}, u32[]{:S(2)}, u32[]{:S(2)}) collective-permute-start(bf16[128,256]{1,0:T(8,128)(2,1)S(1)} %get-tuple-element.29), channel_id=1, source_target_pairs={{1,2},{3,0},{5,6},{7,4},{9,10},{11,8},{13,14},{15,12},{0,1},{2,3},... | collective-permute-start | bytes 196616 | tf_op jit(solution)/shard_map/ppermute | solution.py:207
  63.0 1.8 %collective-permute-start.35 = (bf16[128,512]{1,0:T(8,128)(2,1)S(1)}, bf16[128,512]{1,0:T(8,128)(2,1)S(1)}, u32[]{:S(2)}, u32[]{:S(2)}) collective-permute-start(bf16[128,512]{1,0:T(8,128)(2,1)S(1)} %shard_map.111.r_1_), channel_id=1, source_target_pairs={{0,1},{1,0},{2,3},{3,2},{4,5},{5,4},{6,7},{7,6},{8,9},{9,8},{10,11... | collective-permute-start | bytes 393224 | tf_op jit(solution)/shard_map/ppermute | solution.py:211
  63.0 1.4 %collective-permute-start.37 = (bf16[128,256]{1,0:T(8,128)(2,1)S(1)}, bf16[128,256]{1,0:T(8,128)(2,1)S(1)}, u32[]{:S(2)}, u32[]{:S(2)}) collective-permute-start(bf16[128,256]{1,0:T(8,128)(2,1)S(1)} %collective-permute-done.36.r_1_), channel_id=1, source_target_pairs={{0,1},{1,0},{2,3},{3,2},{4,5},{5,4},{6,7},{7,6},{8,9},{9,8},{10,11... | collective-permute-start | bytes 196616 | tf_op jit(solution)/shard_map/ppermute | solution.py:211
  (1 other events, 1.0 us)
